TPU v7x, 32 devices: a whole 2x2x4 slice. The times are simulated.
32 devices in a mesh: groups: 2 (over x), tok: 16 (over z, y, core).
Axes of the slice: x: 2, y: 2, z: 4, core: 2. Of those that a mesh axis runs over, the one named last changes fastest.
Arguments:
- single: bfloat16 [512, 8, 768], P(('groups', 'tok')), parts along dimension 0, may hold values from -6 to 6
- pair: bfloat16 [512, 256, 128], P(('groups', 'tok')), parts along dimension 0, may hold values from -400 to 400, as said below
- chain: int32 [512], P(('groups', 'tok')), parts along dimension 0, may hold values from 0 to 7, never falling along the last dimension, each value on 1 to 64 neighbouring positions
- residue: int32 [512], P(('groups', 'tok')), parts along dimension 0, may hold values from 0 to 510, as said below
- valid: int32 [512], P(('groups', 'tok')), parts along dimension 0, may hold values 0 or 1
- w_query: bfloat16 [768, 768], replicated, may hold values from -0.21875 to 0.21875
- w_key: bfloat16 [768, 768], replicated, may hold values from -0.21875 to 0.21875
- w_value: bfloat16 [768, 768], replicated, may hold values from -0.21875 to 0.21875
- w_gate: bfloat16 [768, 768], replicated, may hold values from -0.21875 to 0.21875
- w_out: bfloat16 [768, 768], replicated, may hold values from -0.21875 to 0.21875
- w_pair: bfloat16 [128, 16], replicated, may hold values from -1.1953125 to 1.1953125
- rel_table: float32 [66, 16], replicated, may hold values from -6 to 6
Outputs:
- updated: bfloat16 [512, 8, 768], P(('groups', 'tok')), parts along dimension 0
There are 2 independent parts, one for each index of `groups`. A program takes and returns all parts, laid end to end along the dimension named above; an argument that names none is the same for every part. Nothing has to cross between parts.
Inputs may be any that keep to these rules, and one draw needn't show every extreme that they name: `pair`: pair entries are of order one, except possibly in a few query rows where two entries have many times the usual size. `residue`: starts at 0 and rises from each token to the next, by 1 or 2 except into the last token, which holds the largest value.
All inputs are finite; a program needn't handle non-finite values. No bound on the sum of `valid` on one device may be relied on, other than what follows from the above.
Results may differ from a plain program's by a relative error of at most 0.0045.
Values may be sent and summed in bfloat16 or wider, within the bound.
No kernel may reach another device: no remote copies, remote signals or barrier semaphores. Data moves between devices by JAX's collectives and lax.ppermute only.
A program may use at most 128 MiB of HBM per device.

v0:
```python
import math

import jax
import jax.numpy as jnp
from jax import lax
from jax.sharding import PartitionSpec as P

NORM_EPS = 1e-05
MASK_PENALTY = 10000.0


def layer_normed(values_in):
    mean_val = jnp.mean(values_in, axis=-1, keepdims=True)
    centred = values_in - mean_val
    spread = jnp.mean(centred * centred, axis=-1, keepdims=True)
    return centred * lax.rsqrt(spread + NORM_EPS)


def shards(
    single, pair, chain, residue, valid, w_query, w_key, w_value, w_gate, w_out, w_pair, rel_table
):
    local_tokens, sample_count, width = single.shape
    head_count = w_pair.shape[1]
    head_size = width // head_count
    total_keys = pair.shape[1]
    channels = pair.shape[2]
    rel_bins = rel_table.shape[0]
    rel_reach = (rel_bins - 2) // 2
    scale_factor = 1.0 / math.sqrt(head_size)
    bucket_ids = jnp.arange(rel_bins, dtype=jnp.int32)
    normed = layer_normed(single.astype(jnp.float32)).astype(jnp.bfloat16)
    flat_rows = normed.reshape(local_tokens * sample_count, width)

    def project(weight):
        return jnp.dot(flat_rows, weight, preferred_element_type=jnp.float32)

    query_proj = (
        project(w_query)
        .astype(jnp.bfloat16)
        .reshape(local_tokens, sample_count, head_count, head_size)
    )
    key_proj = project(w_key).astype(jnp.bfloat16).reshape(local_tokens, sample_count, width)
    value_proj = project(w_value).astype(jnp.bfloat16).reshape(local_tokens, sample_count, width)
    gate_proj = jax.nn.sigmoid(project(w_gate)).reshape(
        local_tokens, sample_count, head_count, head_size
    )
    bias_rows = jnp.dot(
        pair.reshape(local_tokens * total_keys, channels),
        w_pair,
        preferred_element_type=jnp.float32,
    ).reshape(local_tokens, total_keys, head_count)
    token_axis = lax.axis_size("tok")
    quarters = token_axis // head_count
    quarter_rows = local_tokens // quarters
    my_index = lax.axis_index("tok")
    my_quarter = my_index // head_count
    my_head = my_index % head_count
    query_split = query_proj.reshape(quarters, quarter_rows, sample_count, head_count, head_size)
    query_send = jnp.transpose(query_split, (0, 3, 1, 2, 4)).reshape(
        token_axis, quarter_rows, sample_count * head_size
    )
    both_heads = jnp.stack(
        [
            key_proj.reshape(local_tokens, sample_count, head_count, head_size),
            value_proj.reshape(local_tokens, sample_count, head_count, head_size),
        ],
        axis=3,
    )
    both_heads = jnp.transpose(both_heads, (2, 0, 1, 3, 4))
    kv_send = jnp.broadcast_to(both_heads[None], (quarters,) + both_heads.shape).reshape(
        token_axis, local_tokens, sample_count * 2 * head_size
    )
    query_got, kv_got = (
        lax.all_to_all(query_send, "tok", split_axis=0, concat_axis=1, tiled=True),
        lax.all_to_all(kv_send, "tok", split_axis=0, concat_axis=1, tiled=True),
    )
    bias_send = jnp.transpose(
        bias_rows.reshape(quarters, quarter_rows, total_keys, head_count), (0, 3, 1, 2)
    ).reshape(token_axis, quarter_rows, total_keys)
    meta_one = jnp.stack([chain, residue, valid], axis=0).astype(jnp.float32)
    meta_send = jnp.broadcast_to(meta_one[None], (token_axis, 3, local_tokens))
    bias_got, meta_got = (
        lax.all_to_all(bias_send, "tok", split_axis=0, concat_axis=1, tiled=True),
        lax.all_to_all(meta_send, "tok", split_axis=0, concat_axis=1, tiled=True),
    )
    query_rows = token_axis * quarter_rows
    query_all = query_got.reshape(query_rows, sample_count, head_size)
    kv_all = kv_got.reshape(total_keys, sample_count, 2, head_size)
    key_all = kv_all[:, :, 0]
    value_all = kv_all[:, :, 1]
    bias_all = bias_got.reshape(query_rows, total_keys)
    meta_int = jnp.transpose(meta_got.reshape(token_axis, 3, local_tokens), (1, 0, 2)).astype(
        jnp.int32
    )
    chain_keys = meta_int[0].reshape(total_keys)
    residue_keys = meta_int[1].reshape(total_keys)
    valid_keys = meta_int[2].reshape(total_keys)
    chain_query = lax.dynamic_slice_in_dim(
        meta_int[0].reshape(token_axis, quarters, quarter_rows), my_quarter, 1, 1
    ).reshape(query_rows)
    residue_query = lax.dynamic_slice_in_dim(
        meta_int[1].reshape(token_axis, quarters, quarter_rows), my_quarter, 1, 1
    ).reshape(query_rows)
    rel_column = lax.dynamic_slice_in_dim(rel_table, my_head, 1, 1)
    mask_keys = (valid_keys.astype(jnp.float32) - 1.0) * MASK_PENALTY
    block_rows = math.gcd(query_rows, 64)

    def head_block(block_index):
        start_row = block_index * block_rows
        query_block = lax.dynamic_slice_in_dim(query_all, start_row, block_rows, 0)
        bias_block = lax.dynamic_slice_in_dim(bias_all, start_row, block_rows, 0)
        chain_block = lax.dynamic_slice_in_dim(chain_query, start_row, block_rows, 0)
        residue_block = lax.dynamic_slice_in_dim(residue_query, start_row, block_rows, 0)
        same_chain = chain_block[:, None] == chain_keys[None, :]
        offset = (
            jnp.clip(residue_block[:, None] - residue_keys[None, :], -rel_reach, rel_reach)
            + rel_reach
        )
        bucket = jnp.where(same_chain, offset, rel_bins - 1)
        one_hot = (bucket[:, :, None] == bucket_ids).astype(jnp.float32)
        rel_bias = jnp.einsum("qkb,bh->qkh", one_hot, rel_column, precision=lax.Precision.HIGHEST)[
            :, :, 0
        ]
        total_bias = bias_block + rel_bias + mask_keys[None, :]
        scores = (
            jnp.einsum("qsd,ksd->sqk", query_block, key_all, preferred_element_type=jnp.float32)
            * scale_factor
            + total_bias[None]
        )
        top_score = jnp.max(scores, axis=-1, keepdims=True)
        probs = jnp.exp(scores - top_score)
        mass = jnp.sum(probs, axis=-1)
        weighted = jnp.einsum(
            "sqk,ksd->sqd",
            probs.astype(jnp.bfloat16),
            value_all,
            preferred_element_type=jnp.float32,
        )
        return jnp.transpose(weighted / mass[..., None], (1, 0, 2))

    attended_rows = lax.map(head_block, jnp.arange(query_rows // block_rows, dtype=jnp.int32))
    result_send = attended_rows.reshape(token_axis, quarter_rows, sample_count * head_size)
    result_got = lax.all_to_all(
        result_send.astype(jnp.bfloat16), "tok", split_axis=0, concat_axis=1, tiled=True
    ).astype(result_send.dtype)
    attended = jnp.transpose(
        result_got.reshape(quarters, head_count, quarter_rows, sample_count, head_size),
        (0, 2, 3, 1, 4),
    ).reshape(local_tokens, sample_count, head_count, head_size)
    gated = (gate_proj * attended).reshape(local_tokens * sample_count, width).astype(jnp.bfloat16)
    out_rows = jnp.dot(gated, w_out, preferred_element_type=jnp.float32).reshape(
        local_tokens, sample_count, width
    )
    return (single.astype(jnp.float32) + out_rows).astype(jnp.bfloat16)


def solution(mesh):
    placed = (
        P(("groups", "tok"), None, None),
        P(("groups", "tok"), None, None),
        P(("groups", "tok")),
        P(("groups", "tok")),
        P(("groups", "tok")),
        P(),
        P(),
        P(),
        P(),
        P(),
        P(),
        P(),
    )
    return jax.shard_map(
        shards,
        mesh=mesh,
        in_specs=placed,
        out_specs=P(("groups", "tok"), None, None),
        check_vma=False,
    )
```

profile of v0, /device:TPU:0, one launch (start us, length us, event | category | flops | bytes accessed | tf_op | source)
XLA Modules:
  0.0 108.9 jit_solution(10050591456605176731)
XLA Ops:
  0.0 0.8 add_convert_fusion
  0.8 0.6 broadcast_in_dim.12
  1.4 7.4 %all-to-all-start.3 = ((f32[16,3,16]{2,1,0:T(4,128)}), f32[16,3,16]{2,1,0:T(4,128)S(1)}, u32[]{:S(2)}, u32[]{:S(2)}) async-start(f32[16,3,16]{2,1,0:T(4,128)} %broadcast_in_dim.12), calls=%async_computation.3 | async-start | bytes 65536 | tf_op jit(solution)/shard_map/all_to_all | solution.py:84
  8.9 1.1 %convert_reduce_fusion = f32[16,8]{1,0:T(8,128)S(1)} fusion(bf16[16,8,768]{2,1,0:T(8,128)(2,1)} %param.14), kind=kLoop, calls=%fused_computation.36 | loop fusion | flops 196480 | bytes 197120 | tf_op jit(solution)/shard_map/reduce_sum | solution.py:13
  10.0 1.1 %fusion.28 = f32[16,8]{1,0:T(8,128)S(1)} fusion(bf16[16,8,768]{2,1,0:T(8,128)(2,1)} %param.14, f32[16,8]{1,0:T(8,128)S(1)} %broadcast_multiply_fusion), kind=kLoop, calls=%fused_computation.40 | loop fusion | flops 393088 | bytes 197632 | tf_op jit(solution)/shard_map/reduce_sum | solution.py:15
  11.1 1.3 %convolution_convert_fusion.1 = bf16[128,768]{1,0:T(8,128)(2,1)S(1)} fusion(bf16[768,768]{1,0:T(8,128)(2,1)S(1)} %copy-done, bf16[16,8,768]{2,1,0:T(8,128)(2,1)} %param.14, f32[16,8]{1,0:T(8,128)S(1)} %add_rsqrt_fusion, f32[16,8]{1,0:T(8,128)S(1)} %broadcast_multiply_fusion), kind=kOutput, calls=%fused_computation.30 | convolution fusion | flops 151486464 | bytes 1573888 | tf_op jit(solution)/shard_map/dot_general | solution.py:35
  12.9 0.6 stack_reshape_reshape.6
  13.5 1.0 copy.43
  14.5 0.6 reshape_reshape.4
  15.3 1.0 reshape.199
  16.3 6.1 %all-to-all-start = ((bf16[16,16,384]{2,1,0:T(8,128)(2,1)}), bf16[16,16,384]{2,1,0:T(8,128)(2,1)}, u32[]{:S(2)}, u32[]{:S(2)}) async-start(bf16[16,16,384]{2,1,0:T(8,128)(2,1)} %reshape.199), calls=%async_computation | async-start | bytes 393216 | tf_op jit(solution)/shard_map/all_to_all | solution.py:74
  22.4 1.6 %convolution_convert_fusion = bf16[128,768]{1,0:T(8,128)(2,1)S(1)} fusion(bf16[768,768]{1,0:T(8,128)(2,1)} %param.21, bf16[16,8,768]{2,1,0:T(8,128)(2,1)S(1)} %copy-done.1, f32[16,8]{1,0:T(8,128)S(1)} %add_rsqrt_fusion, f32[16,8]{1,0:T(8,128)S(1)} %broadcast_multiply_fusion), kind=kOutput, calls=%fused_computation.29 | convolution fusion | flops 151486464 | bytes 1573888 | tf_op jit(solution)/shard_map/dot_general | solution.py:35
  24.0 0.6 stack_reshape_reshape.7
  24.7 1.0 copy.44
  25.7 2.8 %maximum_bitcast_fusion = bf16[16,16,8,2,48]{4,3,2,1,0:T(2,128)(2,1)S(1)} fusion(bf16[16,8,16,1,48]{4,3,1,0,2:T(2,128)(2,1)S(1)} %copy.44, bf16[16,8,16,1,48]{4,3,1,0,2:T(2,128)(2,1)S(1)} %copy.43), kind=kLoop, calls=%fused_computation.34 | loop fusion | flops 786432 | bytes 786432 | tf_op jit(solution)/shard_map/transpose | solution.py:69
  28.5 2.0 %reshape_broadcast_in_dim.3 = bf16[16,16,768]{2,1,0:T(8,128)(2,1)} reshape(bf16[16,16,8,2,48]{4,3,2,1,0:T(2,128)(2,1)S(1)} %maximum_bitcast_fusion) | data formatting | bytes 786432 | tf_op jit(solution)/shard_map/reshape;broadcast_in_dim | solution.py:70
  30.5 0.9 all-to-all-done
  31.4 5.0 %all-to-all-start.1 = ((bf16[16,16,768]{2,1,0:T(8,128)(2,1)}), bf16[16,16,768]{2,1,0:T(8,128)(2,1)S(1)}, u32[]{:S(2)}, u32[]{:S(2)}) async-start(bf16[16,16,768]{2,1,0:T(8,128)(2,1)} %reshape_broadcast_in_dim.3), calls=%async_computation.1 | async-start | bytes 786432 | tf_op jit(solution)/shard_map/all_to_all | solution.py:75
  36.9 0.9 copy.46
  37.7 0.7 constant_dynamic-slice_fusion
  38.8 9.8 %all-to-all-done.1 = bf16[16,16,768]{2,1,0:T(8,128)(2,1)S(1)} async-done(((bf16[16,16,768]{2,1,0:T(8,128)(2,1)}), bf16[16,16,768]{2,1,0:T(8,128)(2,1)S(1)}, u32[]{:S(2)}, u32[]{:S(2)}) %all-to-all-start.1) | async-done | bytes 393248 | tf_op jit(solution)/shard_map/all_to_all | solution.py:75
  48.6 4.4 %all-to-all-start.2 = ((f32[16,16,256]{2,1,0:T(8,128)}), f32[16,16,256]{2,1,0:T(8,128)}, u32[]{:S(2)}, u32[]{:S(2)}) async-start(f32[16,16,256]{2,1,0:T(8,128)} %copy.46), calls=%async_computation.2 | async-start | bytes 524288 | tf_op jit(solution)/shard_map/all_to_all | solution.py:83
  53.1 1.4 %reshape.200 = bf16[256,8,48]{2,1,0:T(8,128)(2,1)S(1)} reshape(bf16[16,16,384]{2,1,0:T(8,128)(2,1)} %all-to-all-done) | data formatting | bytes 393216 | tf_op jit(solution)/shard_map/reshape | solution.py:87
  54.5 1.0 copy.48
  55.5 1.2 %reshape.201 = bf16[256,8,2,48]{3,2,1,0:T(2,128)(2,1)S(1)} reshape(bf16[16,16,768]{2,1,0:T(8,128)(2,1)S(1)} %all-to-all-done.1) | data formatting | bytes 786432 | tf_op jit(solution)/shard_map/reshape | solution.py:88
  56.8 2.3 %fusion.43 = (bf16[256,8,1,48]{3,2,1,0:T(2,128)(2,1)}, bf16[256,8,1,48]{3,2,1,0:T(2,128)(2,1)S(1)}) fusion(bf16[256,8,2,48]{3,2,1,0:T(2,128)(2,1)S(1)} %reshape.201), kind=kLoop, calls=%fused_computation.58 | loop fusion | bytes 786432 | tf_op jit(solution)/shard_map/slice | solution.py:90
  59.0 3.4 %copy.47 = bf16[256,8,1,48]{0,3,2,1:T(8,128)(2,1)} copy(bf16[256,8,1,48]{3,2,1,0:T(2,128)(2,1)} %get-tuple-element.188) | data formatting | bytes 393216 | tf_op jit(solution)/shard_map/slice | solution.py:90
  62.5 0.8 copy.45
  63.3 25.9 %while.12 = (s32[]{:T(128)}, bf16[4,64,8,48]{1,3,2,0:T(8,128)(2,1)S(1)}, s32[4]{0:T(128)S(1)}, bf16[256,8,48]{0,2,1:T(8,128)(2,1)S(1)}, bf16[256,8,48]{0,2,1:T(8...) while((s32[]{:T(128)}, ...), condition=%wide.wide.region_5.6_spmd.clone, body=%wide.wide.region_2.5_spmd.clone.sunk | while | flops 40279044 | bytes 5688351 | solution.py:141
  63.3 0.6 dynamic_slice.45
  64.8 0.6 iota_compare_fusion.3
  65.5 2.4 %fusion.76 = f32[1,64,256]{2,0,1:T(1,128)S(1)} fusion(pred[64,256,66]{1,0,2:T(32,128)(4,1)S(1)} %iota_compare_fusion.3, f32[66,1]{0,1:T(1,128)S(1)} %get-tuple-element.388), kind=kOutput, calls=%fused_computation.1.clone.clone.1 | convolution fusion | flops 12976128 | bytes 1147144 | tf_op jit(solution)/shard_map/while/body/eval_jaxpr/qkb,bh->qkh/dot_general | solution.py:121
  67.8 0.9 fusion.77
  69.8 0.6 dynamic_slice.45
  71.3 0.6 iota_compare_fusion.3
  71.9 2.4 %fusion.76 = f32[1,64,256]{2,0,1:T(1,128)S(1)} fusion(pred[64,256,66]{1,0,2:T(32,128)(4,1)S(1)} %iota_compare_fusion.3, f32[66,1]{0,1:T(1,128)S(1)} %get-tuple-element.388), kind=kOutput, calls=%fused_computation.1.clone.clone.1 | convolution fusion | flops 12976128 | bytes 1147144 | tf_op jit(solution)/shard_map/while/body/eval_jaxpr/qkb,bh->qkh/dot_general | solution.py:121
  74.3 0.9 fusion.77
  76.3 0.6 dynamic_slice.45
  77.8 0.6 iota_compare_fusion.3
  78.4 2.4 %fusion.76 = f32[1,64,256]{2,0,1:T(1,128)S(1)} fusion(pred[64,256,66]{1,0,2:T(32,128)(4,1)S(1)} %iota_compare_fusion.3, f32[66,1]{0,1:T(1,128)S(1)} %get-tuple-element.388), kind=kOutput, calls=%fused_computation.1.clone.clone.1 | convolution fusion | flops 12976128 | bytes 1147144 | tf_op jit(solution)/shard_map/while/body/eval_jaxpr/qkb,bh->qkh/dot_general | solution.py:121
  80.8 0.9 fusion.77
  82.8 0.6 dynamic_slice.45
  84.3 0.6 iota_compare_fusion.3
  84.9 2.4 %fusion.76 = f32[1,64,256]{2,0,1:T(1,128)S(1)} fusion(pred[64,256,66]{1,0,2:T(32,128)(4,1)S(1)} %iota_compare_fusion.3, f32[66,1]{0,1:T(1,128)S(1)} %get-tuple-element.388), kind=kOutput, calls=%fused_computation.1.clone.clone.1 | convolution fusion | flops 12976128 | bytes 1147144 | tf_op jit(solution)/shard_map/while/body/eval_jaxpr/qkb,bh->qkh/dot_general | solution.py:121
  87.3 0.9 fusion.77
  90.0 14.5 %all_to_all.20 = bf16[16,16,384]{2,1,0:T(8,128)(2,1)S(1)} all-to-all(bf16[16,16,384]{2,1,0:T(8,128)(2,1)S(1)} %convert_element_type.72), channel_id=1, replica_groups=mesh['groups'=2,'tok'=16] {'tok'}, dimensions={0} | all-to-all | bytes 393216 | tf_op jit(solution)/shard_map/all_to_all | solution.py:143
  104.8 0.6 copy.52
  105.9 3.0 %fusion.22 = bf16[16,8,768]{2,1,0:T(8,128)(2,1)} fusion(bf16[768,768]{1,0:T(8,128)(2,1)} %param.23, f32[128,768]{1,0:T(8,128)S(1)} %reshape.209, bf16[768,768]{1,0:T(8,128)(2,1)} %param.22, bf16[16,8,768]{2,1,0:T(8,128)(2,1)S(1)} %copy-done.1, f32[16,8]{1,0:T(8,128)S(1)} %add_rsqrt_fusion, f32[16,8]{1,0:T(8,128)S(1)} %broadcast_multiply_fusion), kind=kOutput, calls=%fused_computation.28 | convolution fusion | flops 303169536 | bytes 3146752 | tf_op jit(solution)/shard_map/dot_general | solution.py:151
  (71 shorter events, 8.1 us)
Async XLA Ops:
  0.0 11.1 %copy-start = (bf16[768,768]{1,0:T(8,128)(2,1)S(1)}, bf16[768,768]{1,0:T(8,128)(2,1)}, u32[]{:S(2)}) copy-start(bf16[768,768]{1,0:T(8,128)(2,1)} %param.20) | copy-start | bytes 3538948
  0.0 12.4 %copy-start.1 = (bf16[16,8,768]{2,1,0:T(8,128)(2,1)S(1)}, bf16[16,8,768]{2,1,0:T(8,128)(2,1)}, u32[]{:S(2)}) copy-start(bf16[16,8,768]{2,1,0:T(8,128)(2,1)} %param.14) | copy-start | bytes 589828
  1.4 14.9 %all-to-all-start.3 = ((f32[16,3,16]{2,1,0:T(4,128)}), f32[16,3,16]{2,1,0:T(4,128)S(1)}, u32[]{:S(2)}, u32[]{:S(2)}) async-start(f32[16,3,16]{2,1,0:T(4,128)} %broadcast_in_dim.12), calls=%async_computation.3 | async-start | bytes 65536 | tf_op jit(solution)/shard_map/all_to_all | solution.py:84
  8.8 3.6 %copy-start.3 = (bf16[768,768]{1,0:T(8,128)(2,1)S(1)}, bf16[768,768]{1,0:T(8,128)(2,1)}, u32[]{:S(2)}) copy-start(bf16[768,768]{1,0:T(8,128)(2,1)} %param.19) | copy-start | bytes 3538948
  16.3 15.1 %all-to-all-start = ((bf16[16,16,384]{2,1,0:T(8,128)(2,1)}), bf16[16,16,384]{2,1,0:T(8,128)(2,1)}, u32[]{:S(2)}, u32[]{:S(2)}) async-start(bf16[16,16,384]{2,1,0:T(8,128)(2,1)} %reshape.199), calls=%async_computation | async-start | bytes 393216 | tf_op jit(solution)/shard_map/all_to_all | solution.py:74
  28.5 8.0 %copy-start.4 = (bf16[16,256,128]{2,1,0:T(8,128)(2,1)S(1)}, bf16[16,256,128]{2,1,0:T(8,128)(2,1)}, u32[]{:S(2)}) copy-start(bf16[16,256,128]{2,1,0:T(8,128)(2,1)} %param.15) | copy-start | bytes 3145732
  28.5 8.0 %copy-start.9 = (bf16[128,16]{0,1:T(8,128)(2,1)S(1)}, bf16[128,16]{0,1:T(8,128)(2,1)}, u32[]{:S(2)}) copy-start(bf16[128,16]{0,1:T(8,128)(2,1)} %param.24) | copy-start | bytes 12292
  31.4 17.2 %all-to-all-start.1 = ((bf16[16,16,768]{2,1,0:T(8,128)(2,1)}), bf16[16,16,768]{2,1,0:T(8,128)(2,1)S(1)}, u32[]{:S(2)}, u32[]{:S(2)}) async-start(bf16[16,16,768]{2,1,0:T(8,128)(2,1)} %reshape_broadcast_in_dim.3), calls=%async_computation.1 | async-start | bytes 786432 | tf_op jit(solution)/shard_map/all_to_all | solution.py:75
  38.5 18.3 %copy-start.7 = (s32[1,16,16]{2,0,1:T(1,128)}, s32[1,16,16]{2,0,1:T(1,128)S(1)}, u32[]{:S(2)}) copy-start(s32[1,16,16]{2,0,1:T(1,128)S(1)} %get-tuple-element.190) | copy-start | bytes 3076
  38.5 18.3 %copy-start.8 = (s32[1,16,16]{2,0,1:T(1,128)}, s32[1,16,16]{2,0,1:T(1,128)S(1)}, u32[]{:S(2)}) copy-start(s32[1,16,16]{2,0,1:T(1,128)S(1)} %get-tuple-element.191) | copy-start | bytes 3076
  48.6 14.6 %all-to-all-start.2 = ((f32[16,16,256]{2,1,0:T(8,128)}), f32[16,16,256]{2,1,0:T(8,128)}, u32[]{:S(2)}, u32[]{:S(2)}) async-start(f32[16,16,256]{2,1,0:T(8,128)} %copy.46), calls=%async_computation.2 | async-start | bytes 524288 | tf_op jit(solution)/shard_map/all_to_all | solution.py:83
  59.0 4.3 %copy-start.2 = (bf16[256,8,48]{0,2,1:T(8,128)(2,1)S(1)}, bf16[256,8,48]{0,2,1:T(8,128)(2,1)}, u32[]{:S(2)}) copy-start(bf16[256,8,48]{0,2,1:T(8,128)(2,1)} %copy.48) | copy-start | bytes 589828
  59.0 4.3 %copy-start.5 = (bf16[4,64,8,48]{1,3,2,0:T(8,128)(2,1)S(1)}, bf16[4,64,8,48]{1,3,2,0:T(8,128)(2,1)}, u32[]{:S(2)}) copy-start(bf16[4,64,8,48]{1,3,2,0:T(8,128)(2,1)} %custom-call) | copy-start | bytes 589828
  67.8 1.7 %copy-start.6 = (bf16[256,8,48]{0,2,1:T(8,128)(2,1)S(1)}, bf16[256,8,48]{0,2,1:T(8,128)(2,1)}, u32[]{:S(2)}) copy-start(bf16[256,8,48]{0,2,1:T(8,128)(2,1)} %get-tuple-element.390) | copy-start | bytes 589828 | tf_op jit(solution)/shard_map/while
  74.3 1.7 %copy-start.6 = (bf16[256,8,48]{0,2,1:T(8,128)(2,1)S(1)}, bf16[256,8,48]{0,2,1:T(8,128)(2,1)}, u32[]{:S(2)}) copy-start(bf16[256,8,48]{0,2,1:T(8,128)(2,1)} %get-tuple-element.390) | copy-start | bytes 589828 | tf_op jit(solution)/shard_map/while
  80.8 1.7 %copy-start.6 = (bf16[256,8,48]{0,2,1:T(8,128)(2,1)S(1)}, bf16[256,8,48]{0,2,1:T(8,128)(2,1)}, u32[]{:S(2)}) copy-start(bf16[256,8,48]{0,2,1:T(8,128)(2,1)} %get-tuple-element.390) | copy-start | bytes 589828 | tf_op jit(solution)/shard_map/while
  87.3 1.7 %copy-start.6 = (bf16[256,8,48]{0,2,1:T(8,128)(2,1)S(1)}, bf16[256,8,48]{0,2,1:T(8,128)(2,1)}, u32[]{:S(2)}) copy-start(bf16[256,8,48]{0,2,1:T(8,128)(2,1)} %get-tuple-element.390) | copy-start | bytes 589828 | tf_op jit(solution)/shard_map/while
where the time goes:
time: 110 us; the launch traced here: 109 us
  local copies, waits for them, and re-layouts  24.9 us (23%)
  starting transfers between devices  22.9 us (21%)
  matrix products  19.1 us (17%)
  blocking collectives  14.5 us (13%)
  other arithmetic  13.5 us (12%)
  waiting for transfers between devices  10.7 us (10%)
  loops' own time  2.86 us (3%)
    all_to_all x1, blocking collectives, shards(): lax.all_to_all(result_send.astype(jnp.bfloat16), 'tok', split_axis=0, con...  14.5 us
    all_to_all x1, waiting for transfers between devices, shards(): lax.all_to_all(kv_send, 'tok', split_axis=0, concat_axis=1, tiled=True)  9.8 us
    dot_general x4, matrix products, head_block(): jnp.einsum('qkb,bh->qkh', one_hot, rel_column, precision=lax.Precision.HI...  9.43 us
    all_to_all x1, starting transfers between devices, shards(): lax.all_to_all(meta_send, 'tok', split_axis=0, concat_axis=1, tiled=True)  7.41 us
    all_to_all x1, starting transfers between devices, shards(): lax.all_to_all(query_send, 'tok', split_axis=0, concat_axis=1, tiled=True)  6.05 us
    slice x2, local copies, waits for them, and re-layouts, shards(): value_all = kv_all[:, :, 1]  5.7 us
    all_to_all x1, starting transfers between devices, shards(): lax.all_to_all(kv_send, 'tok', split_axis=0, concat_axis=1, tiled=True)  5.03 us
    all_to_all x1, starting transfers between devices, shards(): lax.all_to_all(bias_send, 'tok', split_axis=0, concat_axis=1, tiled=True)  4.37 us
  transfers between devices with their start and end apart: 4, of which 2 were waited for; matrix products, arithmetic and copies ran while one was open for 26% of the time, Pallas kernels for 0%

commit v1 on v0

v1 whole, which is shorter than its diff:
```python
import functools
import math

import jax
import jax.numpy as jnp
from jax import lax
from jax.experimental import pallas as pl
from jax.experimental.pallas import tpu as pltpu
from jax.sharding import PartitionSpec as P

NORM_EPS = 1e-05
MASK_PENALTY = 10000.0
F32 = jnp.float32
BF16 = jnp.bfloat16
CORES = 2
TILE = 256


def normed_rows(block):
    tokens, samples, width = block.shape
    values = block.astype(F32).reshape(tokens * samples, width)
    centred = values - jnp.mean(values, axis=-1, keepdims=True)
    spread = jnp.mean(centred * centred, axis=-1, keepdims=True)
    return (centred * lax.rsqrt(spread + NORM_EPS)).astype(BF16)


def sample_major(tokens, samples):
    rows = tokens * samples
    to = lax.broadcasted_iota(jnp.int32, (rows, rows), 0)
    frm = lax.broadcasted_iota(jnp.int32, (rows, rows), 1)
    want = (to % tokens) * samples + to // tokens
    return (want == frm).astype(F32).astype(BF16)


def token_major(tokens, samples):
    rows = tokens * samples
    to = lax.broadcasted_iota(jnp.int32, (rows, rows), 0)
    frm = lax.broadcasted_iota(jnp.int32, (rows, rows), 1)
    want = (to % samples) * tokens + to // samples
    return (want == frm).astype(F32).astype(BF16)


def matmul(a, b):
    return jnp.dot(a, b, preferred_element_type=F32)


def query_body(single_ref, wq_ref, wg_ref, q_ref, gate_ref):
    tokens, samples, _ = single_ref.shape
    rows = normed_rows(single_ref[...])
    rows = matmul(sample_major(tokens, samples), rows).astype(BF16)
    q_ref[...] = matmul(rows, wq_ref[...]).astype(BF16)
    gate_ref[...] = jax.nn.sigmoid(matmul(rows, wg_ref[...]))


def keys_values(blocks, wk, wv):
    tokens, samples, width = blocks[0].shape
    perm = sample_major(tokens, samples)
    parts = [
        matmul(perm, normed_rows(b)).astype(BF16).reshape(samples, tokens, width) for b in blocks
    ]
    rows = jnp.concatenate(parts, axis=1) if len(parts) > 1 else parts[0]
    shape = rows.shape
    rows = rows.reshape(shape[0] * shape[1], width)
    return (
        matmul(rows, wk).astype(BF16).reshape(shape),
        matmul(rows, wv).astype(BF16).reshape(shape),
    )


def kv_body(*refs):
    wk_ref, wv_ref, k_ref, v_ref = refs[-4:]
    keys, values = keys_values([r[...] for r in refs[:-4]], wk_ref[...], wv_ref[...])
    k_ref[...] = keys
    v_ref[...] = values


def bias_body(blk_ref, chain_ref, res_ref, pair_ref, wp_ref, tab_ref, meta_ref, out_ref):
    heads, queries, total = out_ref.shape
    channels = pair_ref.shape[2]
    bins = tab_ref.shape[0]
    reach = (bins - 2) // 2
    tokens = total // blk_ref.shape[0]
    weights = jnp.transpose(wp_ref[...].astype(F32)).astype(BF16)
    table = jnp.transpose(tab_ref[...])
    high = table.astype(BF16)
    rest = table - high.astype(F32)
    mid = rest.astype(BF16)
    low = (rest - mid.astype(F32)).astype(BF16)
    chain_keys = meta_ref[0:1, :]
    res_keys = meta_ref[1:2, :]
    mask = (meta_ref[2:3, :] - 1.0) * MASK_PENALTY
    bin_ids = lax.broadcasted_iota(jnp.int32, (bins, total), 0).astype(F32)
    for i in range(queries):
        rows = jnp.concatenate(
            [
                pair_ref[i, pl.ds(pl.multiple_of(blk_ref[b] * tokens, tokens), tokens), :]
                for b in range(blk_ref.shape[0])
            ],
            axis=0,
        )
        acc = lax.dot_general(weights, rows, (((1,), (1,)), ((), ())), preferred_element_type=F32)
        chain_q = chain_ref[i].astype(F32)
        res_q = res_ref[i].astype(F32)
        offset = jnp.clip(res_q - res_keys, -reach, reach) + reach
        bucket = jnp.where(chain_keys == chain_q, offset, float(bins - 1))
        hot = (bin_ids == bucket).astype(F32).astype(BF16)
        rel = (matmul(low, hot) + matmul(mid, hot)) + matmul(high, hot)
        out_ref[:, i, :] = acc + rel + mask


def attend_body(n_kv, heads, scale, *refs):
    kv_refs = refs[: 2 * n_kv]
    last = refs[2 * n_kv : 2 * n_kv + 4]
    q_ref, gate_ref, bias_ref, single_ref, wk_ref, wv_ref, wo_ref, out_ref = refs[2 * n_kv + 4 :]
    tokens, samples, width = single_ref.shape
    hs = width // heads
    blocks = [
        jnp.concatenate([last[0][...], last[1][...]], axis=0),
        jnp.concatenate([last[2][...], last[3][...]], axis=0),
    ]
    k_last, v_last = keys_values(blocks, wk_ref[...], wv_ref[...])
    total = bias_ref.shape[2]
    bias = bias_ref[...].reshape(heads * tokens, total)
    lane_head = lax.broadcasted_iota(jnp.int32, (tokens, width), 1) // hs
    spans = []
    for t in range(width // TILE):
        spans.append(((t * TILE) // hs, ((t + 1) * TILE - 1) // hs))
    gated = []
    for s in range(samples):
        keys = jnp.concatenate([r[s] for r in kv_refs[:n_kv]] + [k_last[s]], axis=0)
        values = jnp.concatenate([r[s] for r in kv_refs[n_kv:]] + [v_last[s]], axis=0)
        q = q_ref[pl.ds(s * tokens, tokens), :].astype(F32)
        per_head = [None] * heads
        for t, (h0, h1) in enumerate(spans):
            cut = slice(t * TILE, (t + 1) * TILE)
            qt = jnp.concatenate(
                [
                    jnp.where(lane_head[:, cut] == h, q[:, cut], 0.0).astype(BF16)
                    for h in range(h0, h1 + 1)
                ],
                axis=0,
            )
            st = lax.dot_general(
                qt, keys[:, cut], (((1,), (1,)), ((), ())), preferred_element_type=F32
            )
            for h in range(h0, h1 + 1):
                part = st[(h - h0) * tokens : (h - h0 + 1) * tokens]
                per_head[h] = part if per_head[h] is None else per_head[h] + part
        scores = jnp.concatenate(per_head, axis=0) * scale + bias
        top = jnp.max(scores, axis=-1, keepdims=True)
        probs = jnp.exp(scores - top)
        inv = 1.0 / jnp.sum(probs, axis=-1, keepdims=True)
        probs = probs.astype(BF16)
        attended = []
        for t, (h0, h1) in enumerate(spans):
            cut = slice(t * TILE, (t + 1) * TILE)
            ot = matmul(probs[h0 * tokens : (h1 + 1) * tokens], values[:, cut])
            ot = ot * inv[h0 * tokens : (h1 + 1) * tokens]
            got = ot[:tokens]
            for h in range(h0 + 1, h1 + 1):
                got = jnp.where(
                    lane_head[:, cut] == h, ot[(h - h0) * tokens : (h - h0 + 1) * tokens], got
                )
            attended.append(got)
        attended = jnp.concatenate(attended, axis=1)
        gated.append((gate_ref[pl.ds(s * tokens, tokens), :] * attended).astype(BF16))
    gated = jnp.concatenate(gated, axis=0)
    gated = matmul(token_major(tokens, samples), gated).astype(BF16)
    out = matmul(gated, wo_ref[...]).reshape(tokens, samples, width)
    out_ref[...] = (single_ref[...].astype(F32) + out).astype(BF16)


def call(body, out_shape, args, in_specs=None, flops=0, moved=0, name=None, limit=40 << 20):
    return pl.pallas_call(
        body,
        out_shape=out_shape,
        in_specs=in_specs or [pl.BlockSpec(memory_space=pltpu.VMEM)] * len(args),
        out_specs=jax.tree.map(lambda _: pl.BlockSpec(memory_space=pltpu.VMEM), out_shape),
        compiler_params=pltpu.CompilerParams(vmem_limit_bytes=limit),
        cost_estimate=pl.CostEstimate(flops=flops, bytes_accessed=moved, transcendentals=0),
        name=name,
    )(*args)


def shards(
    single, pair, chain, residue, valid, w_query, w_key, w_value, w_gate, w_out, w_pair, rel_table
):
    tokens, samples, width = single.shape
    heads = w_pair.shape[1]
    total = pair.shape[1]
    devices = lax.axis_size("tok")
    chips = devices // CORES
    half = chips // 2
    me = lax.axis_index("tok")
    core = me % CORES
    chip = me // CORES
    order = list(range(0, chips, 2)) + list(range(1, chips, 2))[::-1]
    place = jnp.where(chip % 2 == 0, chip // 2, chips - 1 - chip // 2)

    def ring(value, step):
        pairs = [
            (order[i] * CORES + c, order[(i + step) % chips] * CORES + c)
            for i in range(chips)
            for c in range(CORES)
        ]
        return lax.ppermute(value, "tok", pairs)

    def flip(value, bit):
        return lax.ppermute(value, "tok", [(d, d ^ bit) for d in range(devices)])

    steps = [(0, 0), (0, 1)]
    for k in range(1, half):
        steps += [(-k, 0), (k, 0), (-k, 1), (k, 1)]
    steps += [(half, 0), (half, 1)]
    rel_place = jnp.array([r for r, _ in steps], jnp.int32)
    rel_core = jnp.array([c for _, c in steps], jnp.int32)
    at = (place + rel_place + chips) % chips
    at_chip = jnp.where(at < half, 2 * at, 2 * (chips - 1 - at) + 1)
    blocks = at_chip * CORES + (core + rel_core) % CORES

    cw = ring(single, 1)
    ccw = ring(single, -1)
    partner = flip(single, 1)

    meta = jnp.stack([chain, residue, valid], axis=0).astype(F32).reshape(1, 3 * tokens)
    mine = lax.broadcasted_iota(jnp.int32, (devices, 3 * tokens), 0) == me
    meta = jnp.where(mine, meta, 0.0)
    bit = 1
    while bit < devices:
        meta = meta + flip(meta, bit)
        bit *= 2
    meta = jnp.take(meta, blocks, axis=0).reshape(devices, 3, tokens)
    meta = jnp.transpose(meta, (1, 0, 2)).reshape(3, total)

    rows = tokens * samples
    query, gate = call(
        query_body,
        (jax.ShapeDtypeStruct((rows, width), BF16), jax.ShapeDtypeStruct((rows, width), F32)),
        (single, w_query, w_gate),
        flops=4 * rows * width * width,
        moved=4 * width * width + 8 * rows * width,
        name="query",
    )
    smem = pl.BlockSpec(memory_space=pltpu.SMEM)
    vmem = pl.BlockSpec(memory_space=pltpu.VMEM)

    def kv(parts):
        n = len(parts)
        shape = jax.ShapeDtypeStruct((samples, n * tokens, width), BF16)
        return call(
            kv_body,
            (shape, shape),
            (*parts, w_key, w_value),
            flops=4 * n * rows * width * width,
            moved=4 * width * width + 6 * n * rows * width,
            name="kv",
        )

    kvs = [kv([single, partner])]
    for k in range(1, half):
        if k + 1 < half:
            cw_next, ccw_next = ring(cw, 1), ring(ccw, -1)
        else:
            cw_next = ring(cw[: tokens // 2], 1)
            ccw_next = ring(ccw[tokens // 2 :], -1)
        cw_other, ccw_other = flip(cw, 1), flip(ccw, 1)
        kvs.append(kv([cw, ccw, cw_other, ccw_other]))
        cw, ccw = cw_next, ccw_next
    bias = call(
        bias_body,
        jax.ShapeDtypeStruct((heads, tokens, total), F32),
        (blocks, chain, residue, pair, w_pair, rel_table, meta),
        in_specs=[smem, smem, smem, vmem, vmem, vmem, vmem],
        flops=2 * tokens * total * heads * 512,
        moved=pair.size * 2 + heads * tokens * total * 4,
        name="bias",
    )
    cw_other, ccw_other = flip(cw, 1), flip(ccw, 1)
    args = [k for k, _ in kvs] + [v for _, v in kvs]
    args += [cw, ccw, cw_other, ccw_other, query, gate, bias, single, w_key, w_value, w_out]
    return call(
        functools.partial(attend_body, len(kvs), heads, 1.0 / math.sqrt(width // heads)),
        jax.ShapeDtypeStruct(single.shape, BF16),
        args,
        flops=4 * rows * total * width,
        moved=4 * samples * total * width,
        name="attend",
        limit=60 << 20,
    )


def solution(mesh):
    placed = (
        P(("groups", "tok"), None, None),
        P(("groups", "tok"), None, None),
        P(("groups", "tok")),
        P(("groups", "tok")),
        P(("groups", "tok")),
        P(),
        P(),
        P(),
        P(),
        P(),
        P(),
        P(),
    )
    return jax.shard_map(
        shards,
        mesh=mesh,
        in_specs=placed,
        out_specs=P(("groups", "tok"), None, None),
        check_vma=False,
    )
```

time: 110 us -> 60.5 us (0.55)
  Pallas kernels: 0 us -> 21.4 us
  matrix products: 19.1 us -> 0 us
  blocking collectives: 14.5 us -> 0 us
  local copies, waits for them, and re-layouts: 24.9 us -> 12.2 us
  other arithmetic: 13.5 us -> 1.72 us
  starting transfers between devices: 22.9 us -> 17.4 us
  waiting for transfers between devices: 10.7 us -> 7.19 us
  loops' own time: 2.86 us -> 0 us
    all_to_all x4 -> x0, starting transfers between devices: 22.9 us -> none  [the longest x1 7.41 us: shards(): lax.all_to_all(meta_send, 'tok', split_axis=0, concat_axis=1, tiled=True)]
    pallas_call x0 -> x7, Pallas kernels: none -> 21.4 us  [call(): pl.pallas_call(body, out_shape=out_shape, in_specs=in_specs or [pl.BlockS...]
    dot_general x17 -> x0, matrix products: 19.1 us -> none  [the longest x4 9.43 us: head_block(): jnp.einsum('qkb,bh->qkh', one_hot, rel_column, precision=lax.Precision.HI...]
    ppermute x0 -> x21, starting transfers between devices: none -> 17.4 us  [the longest x8 9.13 us: ring(): return lax.ppermute(value, 'tok', pairs)]
    all_to_all x1 -> x0, blocking collectives: 14.5 us -> none  [shards(): lax.all_to_all(result_send.astype(jnp.bfloat16), 'tok', split_axis=0, con...]
    all_to_all x4 -> x0, waiting for transfers between devices: 10.7 us -> none  [the longest x1 9.8 us: shards(): lax.all_to_all(kv_send, 'tok', split_axis=0, concat_axis=1, tiled=True)]
    unnamed x19 -> x54, local copies, waits for them, and re-layouts: 1.04 us -> 11.3 us
    ppermute x0 -> x21, waiting for transfers between devices: none -> 7.19 us  [the longest x13 5.77 us: flip(): return lax.ppermute(value, 'tok', [(d, d ^ bit) for d in range(devices)])]
  transfers between devices with their start and end apart: 4 -> 21, of which waited for: 2 -> 5; matrix products, arithmetic and copies ran while one was open for 26% -> 5% of each run, Pallas kernels for 0% -> 20%
where the time goes in v1:
time: 60.5 us; the launch traced here: 60.2 us
  Pallas kernels  21.4 us (35%)
  starting transfers between devices  17.4 us (29%)
  local copies, waits for them, and re-layouts  12.2 us (20%)
  waiting for transfers between devices  7.19 us (12%)
  other arithmetic  1.72 us (3%)
    pallas_call x7, Pallas kernels, call(): pl.pallas_call(body, out_shape=out_shape, in_specs=in_specs or [pl.BlockS...  21.4 us
    unnamed x54, local copies, waits for them, and re-layouts  11.3 us
    ppermute x8, starting transfers between devices, ring(): return lax.ppermute(value, 'tok', pairs)  9.13 us
    ppermute x13, starting transfers between devices, flip(): return lax.ppermute(value, 'tok', [(d, d ^ bit) for d in range(devices)])  8.32 us
    ppermute x13, waiting for transfers between devices, flip(): return lax.ppermute(value, 'tok', [(d, d ^ bit) for d in range(devices)])  5.77 us
    ppermute x8, waiting for transfers between devices, ring(): return lax.ppermute(value, 'tok', pairs)  1.43 us
  transfers between devices with their start and end apart: 21, of which 5 were waited for; matrix products, arithmetic and copies ran while one was open for 5% of the time, Pallas kernels for 20%

profile of v1, /device:TPU:0, one launch (start us, length us, event | category | flops | bytes accessed | tf_op | source)
XLA Modules:
  0.0 60.2 jit_solution(11564569240221610512)
XLA Ops:
  0.0 3.1 %collective-permute-start.1 = (bf16[16,8,768]{2,1,0:T(8,128)(2,1)}, bf16[16,8,768]{2,1,0:T(8,128)(2,1)S(1)}, u32[]{:S(2)}, u32[]{:S(2)}) collective-permute-start(bf16[16,8,768]{2,1,0:T(8,128)(2,1)} %refs_15_.1), channel_id=1, source_target_pairs={{0,4},{1,5},{4,8},{5,9},{8,12},{9,13},{12,14},{13,15},{14,10},{15,... | collective-permute-start | bytes 589832 | tf_op jit(solution)/shard_map/ppermute | solution.py:206
  3.1 0.7 %add_convert_fusion = f32[3,16]{1,0:T(4,128)S(1)} fusion(s32[1,16]{1,0:T(1,128)} %bitcast.7, s32[1,16]{1,0:T(1,128)} %bitcast.6, s32[1,16]{1,0:T(1,128)} %bitcast.5), kind=kLoop, calls=%fused_computation.10 | loop fusion | flops 144 | bytes 384 | tf_op jit(solution)/shard_map/convert_element_type | solution.py:225
  3.8 0.1 convert_element_type.11
  3.9 0.1 broadcast_select_fusion
  3.9 0.5 collective-permute-start.17
  4.4 0.7 %compare_and_fusion = (pred[16]{0:T(512)(128)(4,1)S(1)}, s32[16]{0:T(128)S(1)}) fusion(s32[16]{0:T(128)} %constant.90.clone, s32[]{:T(128)S(6)} %select_n.55, s32[16]{0:T(128)} %constant.89.clone, s32[]{:T(128)S(6)} %select_n.52), kind=kLoop, calls=%fused_computation.11 | loop fusion | flops 624 | bytes 216 | tf_op jit(solution)/shard_map/jit(_take)/and | solution.py:232
  5.1 0.1 collective-permute-done.17
  5.3 2.0 %collective-permute-start.18 = (f32[16,48]{1,0:T(8,128)S(1)}, f32[16,48]{1,0:T(8,128)S(1)}, u32[]{:S(2)}, u32[]{:S(2)}) collective-permute-start(f32[16,48]{1,0:T(8,128)S(1)} %fusion), channel_id=1, source_target_pairs={{0,2},{1,3},{2,0},{3,1},{4,6},{5,7},{6,4},{7,5},{8,10},{9,11},{10,... | collective-permute-start | bytes 9224 | tf_op jit(solution)/shard_map/ppermute | solution.py:209
  7.3 0.8 %collective-permute-done.1.refs_0_ = bf16[16,8,768]{2,1,0:T(8,128)(2,1)S(1)} collective-permute-done((bf16[16,8,768]{2,1,0:T(8,128)(2,1)}, bf16[16,8,768]{2,1,0:T(8,128)(2,1)S(1)}, u32[]{:S(2)}, u32[]{:S(2)}) %collective-permute-start.1) | collective-permute-done | bytes 196640 | tf_op jit(solution)/shard_map/ppermute | solution.py:206
  8.1 1.8 %collective-permute-start.5 = (bf16[16,8,768]{2,1,0:T(8,128)(2,1)S(1)}, bf16[16,8,768]{2,1,0:T(8,128)(2,1)}, u32[]{:S(2)}, u32[]{:S(2)}) collective-permute-start(bf16[16,8,768]{2,1,0:T(8,128)(2,1)S(1)} %collective-permute-done.1.refs_0_), channel_id=1, source_target_pairs={{0,4},{1,5},{4,8},{5,9},{8,12},{9,13},{12,14},{13,15},{14,10},{15,... | collective-permute-start | bytes 589832 | tf_op jit(solution)/shard_map/ppermute | solution.py:206
  9.9 0.2 collective-permute-start.6
  10.1 0.1 fusion.6
  10.2 1.8 %collective-permute-start.19 = (f32[16,48]{1,0:T(8,128)S(1)}, f32[16,48]{1,0:T(8,128)S(1)}, u32[]{:S(2)}, u32[]{:S(2)}) collective-permute-start(f32[16,48]{1,0:T(8,128)S(1)} %fusion.6), channel_id=1, source_target_pairs={{0,4},{1,5},{2,6},{3,7},{4,0},{5,1},{6,2},{7,3},{8,12},{9,13},{10,... | collective-permute-start | bytes 9224 | tf_op jit(solution)/shard_map/ppermute | solution.py:209
  12.0 5.6 %collective-permute-done.19 = f32[16,48]{1,0:T(8,128)S(1)} collective-permute-done((f32[16,48]{1,0:T(8,128)S(1)}, f32[16,48]{1,0:T(8,128)S(1)}, u32[]{:S(2)}, u32[]{:S(2)}) %collective-permute-start.19) | collective-permute-done | bytes 3104 | tf_op jit(solution)/shard_map/ppermute | solution.py:209
  17.6 2.6 %collective-permute-start.20 = (f32[16,48]{1,0:T(8,128)S(1)}, f32[16,48]{1,0:T(8,128)S(1)}, u32[]{:S(2)}, u32[]{:S(2)}) collective-permute-start(f32[16,48]{1,0:T(8,128)S(1)} %add.70), channel_id=1, source_target_pairs={{0,8},{1,9},{2,10},{3,11},{4,12},{5,13},{6,14},{7,15},{8,0},{9,1},... | collective-permute-start | bytes 9224 | tf_op jit(solution)/shard_map/ppermute | solution.py:209
  20.2 0.9 %copy-done.2 = bf16[16,8,768]{2,1,0:T(8,128)(2,1)S(1)} copy-done((bf16[16,8,768]{2,1,0:T(8,128)(2,1)S(1)}, bf16[16,8,768]{2,1,0:T(8,128)(2,1)}, u32[]{:S(2)}) %copy-start.2) | copy-done | bytes 196632
  21.2 1.3 %copy-done.4 = bf16[768,768]{1,0:T(8,128)(2,1)S(1)} copy-done((bf16[768,768]{1,0:T(8,128)(2,1)S(1)}, bf16[768,768]{1,0:T(8,128)(2,1)}, u32[]{:S(2)}) %copy-start.4) | copy-done | bytes 1179672
  22.4 1.3 %copy-done.5 = bf16[768,768]{1,0:T(8,128)(2,1)S(1)} copy-done((bf16[768,768]{1,0:T(8,128)(2,1)S(1)}, bf16[768,768]{1,0:T(8,128)(2,1)}, u32[]{:S(2)}) %copy-start.5) | copy-done | bytes 1179672
  23.7 0.8 %query.1 = (bf16[128,768]{1,0:T(8,128)(2,1)S(1)}, f32[128,768]{1,0:T(8,128)S(1)}) custom-call(bf16[16,8,768]{2,1,0:T(8,128)(2,1)S(1)} %copy-done.2, bf16[768,768]{1,0:T(8,128)(2,1)S(1)} %copy-done.4, bf16[768,768]{1,0:T(8,128)(2,1)S(1)} %copy-done.5), custom_call_target="tpu_custom_call" | custom-call | flops 301989888 | bytes 3145728 | tf_op jit(solution)/shard_map/query/pallas_call | solution.py:174
  24.5 0.8 %copy-done.14 = f32[128,768]{1,0:T(8,128)} copy-done((f32[128,768]{1,0:T(8,128)}, f32[128,768]{1,0:T(8,128)S(1)}, u32[]{:S(2)}) %copy-start.14) | copy-done | bytes 393240
  25.3 0.7 %copy-done.17 = bf16[128,768]{1,0:T(8,128)(2,1)} copy-done((bf16[128,768]{1,0:T(8,128)(2,1)}, bf16[128,768]{1,0:T(8,128)(2,1)S(1)}, u32[]{:S(2)}) %copy-start.17) | copy-done | bytes 196632
  26.0 0.1 copy.20.tab_ref
  26.1 0.1 copy.19.wp_ref
  26.2 0.6 gather_fusion
  26.8 0.1 gather.7
  27.0 0.5 collective-permute-start.7
  27.5 1.7 %collective-permute-start.10 = (bf16[16,8,768]{2,1,0:T(8,128)(2,1)}, bf16[16,8,768]{2,1,0:T(8,128)(2,1)S(1)}, u32[]{:S(2)}, u32[]{:S(2)}) collective-permute-start(bf16[16,8,768]{2,1,0:T(8,128)(2,1)} %collective-permute-done.6.refs_1_), channel_id=1, source_target_pairs={{0,2},{1,3},{4,0},{5,1},{8,4},{9,5},{12,8},{13,9},{14,12},{15,13},... | collective-permute-start | bytes 589832 | tf_op jit(solution)/shard_map/ppermute | solution.py:206
  29.3 0.1 select_bitcast_fusion
  29.4 0.1 reshape.22.meta_ref
  29.5 1.2 %copy-done.6 = bf16[16,256,128]{2,1,0:T(8,128)(2,1)S(1)} copy-done((bf16[16,256,128]{2,1,0:T(8,128)(2,1)S(1)}, bf16[16,256,128]{2,1,0:T(8,128)(2,1)}, u32[]{:S(2)}) %copy-start.6) | copy-done | bytes 1048600
  30.7 1.3 %bias.1.refs_14_ = f32[16,16,256]{2,1,0:T(8,128)S(1)} custom-call(s32[16]{0:T(128)S(1)} %get-tuple-element.26.blk_ref, s32[16]{0:T(128)S(1)} %copy-done.18, s32[16]{0:T(128)S(1)} %copy-done.19, bf16[16,256,128]{2,1,0:T(8,128)(2,1)S(1)} %copy-done.6, bf16[128,16]{1,0:T(8,128)(2,1)S(1)} %copy.19.wp_ref, f32[66,16]{1,0:T(8,128)S(1)} %copy.20.tab_ref, ...), custom_call_target="tpu_custom_call" | custom-call | flops 67108864 | bytes 1310720 | tf_op jit(solution)/shard_map/bias/pallas_call | solution.py:174
  32.1 1.2 %kv.4 = (bf16[8,32,768]{2,1,0:T(8,128)(2,1)S(1)}, bf16[8,32,768]{2,1,0:T(8,128)(2,1)S(1)}) custom-call(bf16[16,8,768]{2,1,0:T(8,128)(2,1)S(1)} %copy-done.3, bf16[16,8,768]{2,1,0:T(8,128)(2,1)S(1)} %collective-permute-done.refs_1_, bf16[768,768]{1,0:T(8,128)(2,1)S(1)} %copy-done, bf16[768,768]{1,0:T(8,128)(2,1)S(1)} %copy-done.1), custom_call_target="tpu_custom_call" | custom-call | flops 603979776 | bytes 3538944 | tf_op jit(solution)/shard_map/kv/pallas_call | solution.py:174
  33.3 0.7 %copy-done.15 = bf16[8,32,768]{2,1,0:T(8,128)(2,1)} copy-done((bf16[8,32,768]{2,1,0:T(8,128)(2,1)}, bf16[8,32,768]{2,1,0:T(8,128)(2,1)S(1)}, u32[]{:S(2)}) %copy-start.15) | copy-done | bytes 393240
  34.0 0.5 collective-permute-done.9.refs_0_
  34.5 0.2 collective-permute-done.10.refs_1_
  34.6 0.3 collective-permute-start.12
  35.0 3.2 %kv.5 = (bf16[8,64,768]{2,1,0:T(8,128)(2,1)S(1)}, bf16[8,64,768]{2,1,0:T(8,128)(2,1)S(1)}) custom-call(bf16[16,8,768]{2,1,0:T(8,128)(2,1)S(1)} %collective-permute-done.1.refs_0_, bf16[16,8,768]{2,1,0:T(8,128)(2,1)} %collective-permute-done.2.refs_1_, bf16[16,8,768]{2,1,0:T(8,128)(2,1)} %collective-permute-done.3.refs_2_, ...), custom_call_target="tpu_custom_call" | custom-call | flops 1207959552 | bytes 4718592 | tf_op jit(solution)/shard_map/kv/pallas_call | solution.py:174
  38.2 0.9 %copy-done.8 = bf16[8,64,768]{2,1,0:T(8,128)(2,1)} copy-done((bf16[8,64,768]{2,1,0:T(8,128)(2,1)}, bf16[8,64,768]{2,1,0:T(8,128)(2,1)S(1)}, u32[]{:S(2)}) %copy-start.8) | copy-done | bytes 786456
  39.1 0.5 collective-permute-start.13
  39.6 1.8 %collective-permute-start.14 = (bf16[8,8,768]{2,1,0:T(8,128)(2,1)S(1)}, bf16[8,8,768]{2,1,0:T(8,128)(2,1)S(1)}, u32[]{:S(2)}, u32[]{:S(2)}) collective-permute-start(bf16[8,8,768]{2,1,0:T(8,128)(2,1)S(1)} %slice.11), channel_id=1, source_target_pairs={{0,2},{1,3},{4,0},{5,1},{8,4},{9,5},{12,8},{13,9},{14,12},{15,13},... | collective-permute-start | bytes 294920 | tf_op jit(solution)/shard_map/ppermute | solution.py:206
  41.4 3.3 %kv.6 = (bf16[8,64,768]{2,1,0:T(8,128)(2,1)S(1)}, bf16[8,64,768]{2,1,0:T(8,128)(2,1)S(1)}) custom-call(bf16[16,8,768]{2,1,0:T(8,128)(2,1)} %collective-permute-done.5.refs_0_, bf16[16,8,768]{2,1,0:T(8,128)(2,1)} %collective-permute-done.6.refs_1_, bf16[16,8,768]{2,1,0:T(8,128)(2,1)} %collective-permute-done.7.refs_2_, ...), custom_call_target="tpu_custom_call" | custom-call | flops 1207959552 | bytes 4718592 | tf_op jit(solution)/shard_map/kv/pallas_call | solution.py:174
  44.7 0.9 %copy-done.10 = bf16[8,64,768]{2,1,0:T(8,128)(2,1)} copy-done((bf16[8,64,768]{2,1,0:T(8,128)(2,1)}, bf16[8,64,768]{2,1,0:T(8,128)(2,1)S(1)}, u32[]{:S(2)}) %copy-start.10) | copy-done | bytes 786456
  45.6 0.5 collective-permute-start.16
  46.1 2.1 %kv.7 = (bf16[8,64,768]{2,1,0:T(8,128)(2,1)S(1)}, bf16[8,64,768]{2,1,0:T(8,128)(2,1)S(1)}) custom-call(bf16[16,8,768]{2,1,0:T(8,128)(2,1)S(1)} %collective-permute-done.9.refs_0_, bf16[16,8,768]{2,1,0:T(8,128)(2,1)S(1)} %collective-permute-done.10.refs_1_, bf16[16,8,768]{2,1,0:T(8,128)(2,1)S(1)} %collective-permute-done.11.refs_2_, ...), custom_call_target="tpu_custom_call" | custom-call | flops 1207959552 | bytes 4718592 | tf_op jit(solution)/shard_map/kv/pallas_call | solution.py:174
  48.2 0.9 %copy-done.12 = bf16[8,64,768]{2,1,0:T(8,128)(2,1)} copy-done((bf16[8,64,768]{2,1,0:T(8,128)(2,1)}, bf16[8,64,768]{2,1,0:T(8,128)(2,1)S(1)}, u32[]{:S(2)}) %copy-start.12) | copy-done | bytes 786456
  49.1 0.9 %copy-done.13 = bf16[8,64,768]{2,1,0:T(8,128)(2,1)} copy-done((bf16[8,64,768]{2,1,0:T(8,128)(2,1)}, bf16[8,64,768]{2,1,0:T(8,128)(2,1)S(1)}, u32[]{:S(2)}) %copy-start.13) | copy-done | bytes 786456
  50.0 0.6 %copy-done.22 = bf16[8,8,768]{2,1,0:T(8,128)(2,1)} copy-done((bf16[8,8,768]{2,1,0:T(8,128)(2,1)}, bf16[8,8,768]{2,1,0:T(8,128)(2,1)S(1)}, u32[]{:S(2)}) %copy-start.22) | copy-done | bytes 98328
  50.7 9.6 %attend.1 = bf16[16,8,768]{2,1,0:T(8,128)(2,1)} custom-call(bf16[8,32,768]{2,1,0:T(8,128)(2,1)} %copy-done.15, bf16[8,64,768]{2,1,0:T(8,128)(2,1)} %copy-done.8, bf16[8,64,768]{2,1,0:T(8,128)(2,1)} %copy-done.10, bf16[8,64,768]{2,1,0:T(8,128)(2,1)} %copy-done.12, bf16[8,32,768]{2,1,0:T(8,128)(2,1)} %copy-done.16, bf16[8,64,768]{2,1,0:T(8,128)(2,1)} %copy-done.9, ...), custom_call_target="tpu_custom_call" | custom-call | flops 100663296 | bytes 6291456 | tf_op jit(solution)/shard_map/attend/pallas_call | solution.py:174
  (73 shorter events, 0.5 us)
Async XLA Ops:
  0.0 8.1 %collective-permute-start.1 = (bf16[16,8,768]{2,1,0:T(8,128)(2,1)}, bf16[16,8,768]{2,1,0:T(8,128)(2,1)S(1)}, u32[]{:S(2)}, u32[]{:S(2)}) collective-permute-start(bf16[16,8,768]{2,1,0:T(8,128)(2,1)} %refs_15_.1), channel_id=1, source_target_pairs={{0,4},{1,5},{4,8},{5,9},{8,12},{9,13},{12,14},{13,15},{14,10},{15,... | collective-permute-start | bytes 589832 | tf_op jit(solution)/shard_map/ppermute | solution.py:206
  3.1 6.9 %collective-permute-start.2 = (bf16[16,8,768]{2,1,0:T(8,128)(2,1)}, bf16[16,8,768]{2,1,0:T(8,128)(2,1)}, u32[]{:S(2)}, u32[]{:S(2)}) collective-permute-start(bf16[16,8,768]{2,1,0:T(8,128)(2,1)} %refs_15_.1), channel_id=1, source_target_pairs={{0,2},{1,3},{4,0},{5,1},{8,4},{9,5},{12,8},{13,9},{14,12},{15,13},... | collective-permute-start | bytes 589832 | tf_op jit(solution)/shard_map/ppermute | solution.py:206
  3.1 24.0 %collective-permute-start = (bf16[16,8,768]{2,1,0:T(8,128)(2,1)}, bf16[16,8,768]{2,1,0:T(8,128)(2,1)S(1)}, u32[]{:S(2)}, u32[]{:S(2)}) collective-permute-start(bf16[16,8,768]{2,1,0:T(8,128)(2,1)} %refs_15_.1), channel_id=1, source_target_pairs={{0,1},{1,0},{2,3},{3,2},{4,5},{5,4},{6,7},{7,6},{8,9},{9,8},{10,11... | collective-permute-start | bytes 589832 | tf_op jit(solution)/shard_map/ppermute | solution.py:209
  3.9 1.3 %collective-permute-start.17 = (f32[16,48]{1,0:T(8,128)S(1)}, f32[16,48]{1,0:T(8,128)S(1)}, u32[]{:S(2)}, u32[]{:S(2)}) collective-permute-start(f32[16,48]{1,0:T(8,128)S(1)} %broadcast_select_fusion), channel_id=1, source_target_pairs={{0,1},{1,0},{2,3},{3,2},{4,5},{5,4},{6,7},{7,6},{8,9},{9,8},{10,11... | collective-permute-start | bytes 9224 | tf_op jit(solution)/shard_map/ppermute | solution.py:209
  5.3 4.8 %collective-permute-start.18 = (f32[16,48]{1,0:T(8,128)S(1)}, f32[16,48]{1,0:T(8,128)S(1)}, u32[]{:S(2)}, u32[]{:S(2)}) collective-permute-start(f32[16,48]{1,0:T(8,128)S(1)} %fusion), channel_id=1, source_target_pairs={{0,2},{1,3},{2,0},{3,1},{4,6},{5,7},{6,4},{7,5},{8,10},{9,11},{10,... | collective-permute-start | bytes 9224 | tf_op jit(solution)/shard_map/ppermute | solution.py:209
  8.1 18.8 %collective-permute-start.5 = (bf16[16,8,768]{2,1,0:T(8,128)(2,1)S(1)}, bf16[16,8,768]{2,1,0:T(8,128)(2,1)}, u32[]{:S(2)}, u32[]{:S(2)}) collective-permute-start(bf16[16,8,768]{2,1,0:T(8,128)(2,1)S(1)} %collective-permute-done.1.refs_0_), channel_id=1, source_target_pairs={{0,4},{1,5},{4,8},{5,9},{8,12},{9,13},{12,14},{13,15},{14,10},{15,... | collective-permute-start | bytes 589832 | tf_op jit(solution)/shard_map/ppermute | solution.py:206
  9.9 19.3 %collective-permute-start.3 = (bf16[16,8,768]{2,1,0:T(8,128)(2,1)S(1)}, bf16[16,8,768]{2,1,0:T(8,128)(2,1)}, u32[]{:S(2)}, u32[]{:S(2)}) collective-permute-start(bf16[16,8,768]{2,1,0:T(8,128)(2,1)S(1)} %collective-permute-done.1.refs_0_), channel_id=1, source_target_pairs={{0,1},{1,0},{2,3},{3,2},{4,5},{5,4},{6,7},{7,6},{8,9},{9,8},{10,11... | collective-permute-start | bytes 589832 | tf_op jit(solution)/shard_map/ppermute | solution.py:209
  9.9 17.6 %collective-permute-start.6 = (bf16[16,8,768]{2,1,0:T(8,128)(2,1)}, bf16[16,8,768]{2,1,0:T(8,128)(2,1)}, u32[]{:S(2)}, u32[]{:S(2)}) collective-permute-start(bf16[16,8,768]{2,1,0:T(8,128)(2,1)} %collective-permute-done.2.refs_1_), channel_id=1, source_target_pairs={{0,2},{1,3},{4,0},{5,1},{8,4},{9,5},{12,8},{13,9},{14,12},{15,13},... | collective-permute-start | bytes 589832 | tf_op jit(solution)/shard_map/ppermute | solution.py:206
  10.2 7.4 %collective-permute-start.19 = (f32[16,48]{1,0:T(8,128)S(1)}, f32[16,48]{1,0:T(8,128)S(1)}, u32[]{:S(2)}, u32[]{:S(2)}) collective-permute-start(f32[16,48]{1,0:T(8,128)S(1)} %fusion.6), channel_id=1, source_target_pairs={{0,4},{1,5},{2,6},{3,7},{4,0},{5,1},{6,2},{7,3},{8,12},{9,13},{10,... | collective-permute-start | bytes 9224 | tf_op jit(solution)/shard_map/ppermute | solution.py:209
  17.6 8.6 %collective-permute-start.20 = (f32[16,48]{1,0:T(8,128)S(1)}, f32[16,48]{1,0:T(8,128)S(1)}, u32[]{:S(2)}, u32[]{:S(2)}) collective-permute-start(f32[16,48]{1,0:T(8,128)S(1)} %add.70), channel_id=1, source_target_pairs={{0,8},{1,9},{2,10},{3,11},{4,12},{5,13},{6,14},{7,15},{8,0},{9,1},... | collective-permute-start | bytes 9224 | tf_op jit(solution)/shard_map/ppermute | solution.py:209
  20.2 0.9 %copy-start.2 = (bf16[16,8,768]{2,1,0:T(8,128)(2,1)S(1)}, bf16[16,8,768]{2,1,0:T(8,128)(2,1)}, u32[]{:S(2)}) copy-start(bf16[16,8,768]{2,1,0:T(8,128)(2,1)} %refs_15_.1) | copy-start | bytes 589828
  21.2 1.3 %copy-start.4 = (bf16[768,768]{1,0:T(8,128)(2,1)S(1)}, bf16[768,768]{1,0:T(8,128)(2,1)}, u32[]{:S(2)}) copy-start(bf16[768,768]{1,0:T(8,128)(2,1)} %wq_ref.1) | copy-start | bytes 3538948
  22.4 1.3 %copy-start.5 = (bf16[768,768]{1,0:T(8,128)(2,1)S(1)}, bf16[768,768]{1,0:T(8,128)(2,1)}, u32[]{:S(2)}) copy-start(bf16[768,768]{1,0:T(8,128)(2,1)} %wg_ref.1) | copy-start | bytes 3538948
  23.7 2.3 %copy-start.24 = (f32[66,16]{0,1:T(8,128)S(1)}, f32[66,16]{0,1:T(8,128)}, u32[]{:S(2)}) copy-start(f32[66,16]{0,1:T(8,128)} %param.25) | copy-start | bytes 12676
  23.7 2.4 %copy-start.25 = (bf16[128,16]{0,1:T(8,128)(2,1)S(1)}, bf16[128,16]{0,1:T(8,128)(2,1)}, u32[]{:S(2)}) copy-start(bf16[128,16]{0,1:T(8,128)(2,1)} %param.24) | copy-start | bytes 12292
  23.7 5.8 %copy-start.18 = (s32[16]{0:T(128)S(1)}, s32[16]{0:T(128)}, u32[]{:S(2)}) copy-start(s32[16]{0:T(128)} %chain_ref.1) | copy-start | bytes 196
  23.7 5.8 %copy-start.19 = (s32[16]{0:T(128)S(1)}, s32[16]{0:T(128)}, u32[]{:S(2)}) copy-start(s32[16]{0:T(128)} %res_ref.1) | copy-start | bytes 196
  23.7 8.3 %copy-start.1 = (bf16[768,768]{1,0:T(8,128)(2,1)S(1)}, bf16[768,768]{1,0:T(8,128)(2,1)}, u32[]{:S(2)}) copy-start(bf16[768,768]{1,0:T(8,128)(2,1)} %refs_17_.1) | copy-start | bytes 3538948
  24.5 0.8 %copy-start.14 = (f32[128,768]{1,0:T(8,128)}, f32[128,768]{1,0:T(8,128)S(1)}, u32[]{:S(2)}) copy-start(f32[128,768]{1,0:T(8,128)S(1)} %get-tuple-element.24.refs_13_) | copy-start | bytes 1179652
  25.3 0.7 %copy-start.17 = (bf16[128,768]{1,0:T(8,128)(2,1)}, bf16[128,768]{1,0:T(8,128)(2,1)S(1)}, u32[]{:S(2)}) copy-start(bf16[128,768]{1,0:T(8,128)(2,1)S(1)} %get-tuple-element.23.refs_12_) | copy-start | bytes 589828
  26.0 6.1 %copy-start = (bf16[768,768]{1,0:T(8,128)(2,1)S(1)}, bf16[768,768]{1,0:T(8,128)(2,1)}, u32[]{:S(2)}) copy-start(bf16[768,768]{1,0:T(8,128)(2,1)} %refs_16_.1) | copy-start | bytes 3538948
  26.0 6.1 %copy-start.3 = (bf16[16,8,768]{2,1,0:T(8,128)(2,1)S(1)}, bf16[16,8,768]{2,1,0:T(8,128)(2,1)}, u32[]{:S(2)}) copy-start(bf16[16,8,768]{2,1,0:T(8,128)(2,1)} %refs_15_.1) | copy-start | bytes 589828
  26.9 8.1 %collective-permute-start.4 = (bf16[16,8,768]{2,1,0:T(8,128)(2,1)}, bf16[16,8,768]{2,1,0:T(8,128)(2,1)}, u32[]{:S(2)}, u32[]{:S(2)}) collective-permute-start(bf16[16,8,768]{2,1,0:T(8,128)(2,1)} %collective-permute-done.2.refs_1_), channel_id=1, source_target_pairs={{0,1},{1,0},{2,3},{3,2},{4,5},{5,4},{6,7},{7,6},{8,9},{9,8},{10,11... | collective-permute-start | bytes 589832 | tf_op jit(solution)/shard_map/ppermute | solution.py:209
  26.9 7.5 %collective-permute-start.9 = (bf16[16,8,768]{2,1,0:T(8,128)(2,1)}, bf16[16,8,768]{2,1,0:T(8,128)(2,1)S(1)}, u32[]{:S(2)}, u32[]{:S(2)}) collective-permute-start(bf16[16,8,768]{2,1,0:T(8,128)(2,1)} %collective-permute-done.5.refs_0_), channel_id=1, source_target_pairs={{0,4},{1,5},{4,8},{5,9},{8,12},{9,13},{12,14},{13,15},{14,10},{15,... | collective-permute-start | bytes 589832 | tf_op jit(solution)/shard_map/ppermute | solution.py:206
  27.0 12.6 %collective-permute-start.7 = (bf16[16,8,768]{2,1,0:T(8,128)(2,1)}, bf16[16,8,768]{2,1,0:T(8,128)(2,1)}, u32[]{:S(2)}, u32[]{:S(2)}) collective-permute-start(bf16[16,8,768]{2,1,0:T(8,128)(2,1)} %collective-permute-done.5.refs_0_), channel_id=1, source_target_pairs={{0,1},{1,0},{2,3},{3,2},{4,5},{5,4},{6,7},{7,6},{8,9},{9,8},{10,11... | collective-permute-start | bytes 589832 | tf_op jit(solution)/shard_map/ppermute | solution.py:209
  27.5 7.1 %collective-permute-start.10 = (bf16[16,8,768]{2,1,0:T(8,128)(2,1)}, bf16[16,8,768]{2,1,0:T(8,128)(2,1)S(1)}, u32[]{:S(2)}, u32[]{:S(2)}) collective-permute-start(bf16[16,8,768]{2,1,0:T(8,128)(2,1)} %collective-permute-done.6.refs_1_), channel_id=1, source_target_pairs={{0,2},{1,3},{4,0},{5,1},{8,4},{9,5},{12,8},{13,9},{14,12},{15,13},... | collective-permute-start | bytes 589832 | tf_op jit(solution)/shard_map/ppermute | solution.py:206
  29.2 12.2 %collective-permute-start.8 = (bf16[16,8,768]{2,1,0:T(8,128)(2,1)}, bf16[16,8,768]{2,1,0:T(8,128)(2,1)}, u32[]{:S(2)}, u32[]{:S(2)}) collective-permute-start(bf16[16,8,768]{2,1,0:T(8,128)(2,1)} %collective-permute-done.6.refs_1_), channel_id=1, source_target_pairs={{0,1},{1,0},{2,3},{3,2},{4,5},{5,4},{6,7},{7,6},{8,9},{9,8},{10,11... | collective-permute-start | bytes 589832 | tf_op jit(solution)/shard_map/ppermute | solution.py:209
  29.5 1.2 %copy-start.6 = (bf16[16,256,128]{2,1,0:T(8,128)(2,1)S(1)}, bf16[16,256,128]{2,1,0:T(8,128)(2,1)}, u32[]{:S(2)}) copy-start(bf16[16,256,128]{2,1,0:T(8,128)(2,1)} %pair_ref.1) | copy-start | bytes 3145732
  32.1 1.2 %copy-start.7 = (f32[16,16,256]{2,1,0:T(8,128)}, f32[16,16,256]{2,1,0:T(8,128)S(1)}, u32[]{:S(2)}) copy-start(f32[16,16,256]{2,1,0:T(8,128)S(1)} %bias.1.refs_14_) | copy-start | bytes 786436
  33.3 0.7 %copy-start.15 = (bf16[8,32,768]{2,1,0:T(8,128)(2,1)}, bf16[8,32,768]{2,1,0:T(8,128)(2,1)S(1)}, u32[]{:S(2)}) copy-start(bf16[8,32,768]{2,1,0:T(8,128)(2,1)S(1)} %get-tuple-element.15.refs_0_) | copy-start | bytes 1179652
  34.0 4.2 %copy-start.16 = (bf16[8,32,768]{2,1,0:T(8,128)(2,1)}, bf16[8,32,768]{2,1,0:T(8,128)(2,1)S(1)}, u32[]{:S(2)}) copy-start(bf16[8,32,768]{2,1,0:T(8,128)(2,1)S(1)} %get-tuple-element.19.refs_4_) | copy-start | bytes 1179652
  34.5 11.7 %collective-permute-start.11 = (bf16[16,8,768]{2,1,0:T(8,128)(2,1)S(1)}, bf16[16,8,768]{2,1,0:T(8,128)(2,1)S(1)}, u32[]{:S(2)}, u32[]{:S(2)}) collective-permute-start(bf16[16,8,768]{2,1,0:T(8,128)(2,1)S(1)} %collective-permute-done.9.refs_0_), channel_id=1, source_target_pairs={{0,1},{1,0},{2,3},{3,2},{4,5},{5,4},{6,7},{7,6},{8,9},{9,8},{10,11... | collective-permute-start | bytes 589832 | tf_op jit(solution)/shard_map/ppermute | solution.py:209
  34.6 11.5 %collective-permute-start.12 = (bf16[16,8,768]{2,1,0:T(8,128)(2,1)S(1)}, bf16[16,8,768]{2,1,0:T(8,128)(2,1)S(1)}, u32[]{:S(2)}, u32[]{:S(2)}) collective-permute-start(bf16[16,8,768]{2,1,0:T(8,128)(2,1)S(1)} %collective-permute-done.10.refs_1_), channel_id=1, source_target_pairs={{0,1},{1,0},{2,3},{3,2},{4,5},{5,4},{6,7},{7,6},{8,9},{9,8},{10,11... | collective-permute-start | bytes 589832 | tf_op jit(solution)/shard_map/ppermute | solution.py:209
  38.2 0.9 %copy-start.8 = (bf16[8,64,768]{2,1,0:T(8,128)(2,1)}, bf16[8,64,768]{2,1,0:T(8,128)(2,1)S(1)}, u32[]{:S(2)}) copy-start(bf16[8,64,768]{2,1,0:T(8,128)(2,1)S(1)} %get-tuple-element.16.refs_1_) | copy-start | bytes 2359300
  39.1 5.6 %copy-start.9 = (bf16[8,64,768]{2,1,0:T(8,128)(2,1)}, bf16[8,64,768]{2,1,0:T(8,128)(2,1)S(1)}, u32[]{:S(2)}) copy-start(bf16[8,64,768]{2,1,0:T(8,128)(2,1)S(1)} %get-tuple-element.20.refs_5_) | copy-start | bytes 2359300
  39.1 6.5 %collective-permute-start.13 = (bf16[8,8,768]{2,1,0:T(8,128)(2,1)S(1)}, bf16[8,8,768]{2,1,0:T(8,128)(2,1)S(1)}, u32[]{:S(2)}, u32[]{:S(2)}) collective-permute-start(bf16[8,8,768]{2,1,0:T(8,128)(2,1)S(1)} %slice.10), channel_id=1, source_target_pairs={{0,4},{1,5},{4,8},{5,9},{8,12},{9,13},{12,14},{13,15},{14,10},{15,... | collective-permute-start | bytes 294920 | tf_op jit(solution)/shard_map/ppermute | solution.py:206
  39.6 6.0 %collective-permute-start.14 = (bf16[8,8,768]{2,1,0:T(8,128)(2,1)S(1)}, bf16[8,8,768]{2,1,0:T(8,128)(2,1)S(1)}, u32[]{:S(2)}, u32[]{:S(2)}) collective-permute-start(bf16[8,8,768]{2,1,0:T(8,128)(2,1)S(1)} %slice.11), channel_id=1, source_target_pairs={{0,2},{1,3},{4,0},{5,1},{8,4},{9,5},{12,8},{13,9},{14,12},{15,13},... | collective-permute-start | bytes 294920 | tf_op jit(solution)/shard_map/ppermute | solution.py:206
  44.7 0.9 %copy-start.10 = (bf16[8,64,768]{2,1,0:T(8,128)(2,1)}, bf16[8,64,768]{2,1,0:T(8,128)(2,1)S(1)}, u32[]{:S(2)}) copy-start(bf16[8,64,768]{2,1,0:T(8,128)(2,1)S(1)} %get-tuple-element.17.refs_2_) | copy-start | bytes 2359300
  45.6 2.6 %copy-start.11 = (bf16[8,64,768]{2,1,0:T(8,128)(2,1)}, bf16[8,64,768]{2,1,0:T(8,128)(2,1)S(1)}, u32[]{:S(2)}) copy-start(bf16[8,64,768]{2,1,0:T(8,128)(2,1)S(1)} %get-tuple-element.21.refs_6_) | copy-start | bytes 2359300
  45.6 2.6 %copy-start.20 = (bf16[8,8,768]{2,1,0:T(8,128)(2,1)}, bf16[8,8,768]{2,1,0:T(8,128)(2,1)S(1)}, u32[]{:S(2)}) copy-start(bf16[8,8,768]{2,1,0:T(8,128)(2,1)S(1)} %collective-permute-done.13.refs_8_) | copy-start | bytes 294916
  45.6 4.4 %collective-permute-start.15 = (bf16[8,8,768]{2,1,0:T(8,128)(2,1)S(1)}, bf16[8,8,768]{2,1,0:T(8,128)(2,1)S(1)}, u32[]{:S(2)}, u32[]{:S(2)}) collective-permute-start(bf16[8,8,768]{2,1,0:T(8,128)(2,1)S(1)} %collective-permute-done.13.refs_8_), channel_id=1, source_target_pairs={{0,1},{1,0},{2,3},{3,2},{4,5},{5,4},{6,7},{7,6},{8,9},{9,8},{10,11... | collective-permute-start | bytes 294920 | tf_op jit(solution)/shard_map/ppermute | solution.py:209
  45.6 2.6 %copy-start.21 = (bf16[8,8,768]{2,1,0:T(8,128)(2,1)}, bf16[8,8,768]{2,1,0:T(8,128)(2,1)S(1)}, u32[]{:S(2)}) copy-start(bf16[8,8,768]{2,1,0:T(8,128)(2,1)S(1)} %collective-permute-done.14.refs_9_) | copy-start | bytes 294916
  45.6 4.4 %collective-permute-start.16 = (bf16[8,8,768]{2,1,0:T(8,128)(2,1)S(1)}, bf16[8,8,768]{2,1,0:T(8,128)(2,1)S(1)}, u32[]{:S(2)}, u32[]{:S(2)}) collective-permute-start(bf16[8,8,768]{2,1,0:T(8,128)(2,1)S(1)} %collective-permute-done.14.refs_9_), channel_id=1, source_target_pairs={{0,1},{1,0},{2,3},{3,2},{4,5},{5,4},{6,7},{7,6},{8,9},{9,8},{10,11... | collective-permute-start | bytes 294920 | tf_op jit(solution)/shard_map/ppermute | solution.py:209
  48.2 0.9 %copy-start.12 = (bf16[8,64,768]{2,1,0:T(8,128)(2,1)}, bf16[8,64,768]{2,1,0:T(8,128)(2,1)S(1)}, u32[]{:S(2)}) copy-start(bf16[8,64,768]{2,1,0:T(8,128)(2,1)S(1)} %get-tuple-element.18.refs_3_) | copy-start | bytes 2359300
  49.1 0.9 %copy-start.13 = (bf16[8,64,768]{2,1,0:T(8,128)(2,1)}, bf16[8,64,768]{2,1,0:T(8,128)(2,1)S(1)}, u32[]{:S(2)}) copy-start(bf16[8,64,768]{2,1,0:T(8,128)(2,1)S(1)} %get-tuple-element.22.refs_7_) | copy-start | bytes 2359300
  50.0 0.6 %copy-start.22 = (bf16[8,8,768]{2,1,0:T(8,128)(2,1)}, bf16[8,8,768]{2,1,0:T(8,128)(2,1)S(1)}, u32[]{:S(2)}) copy-start(bf16[8,8,768]{2,1,0:T(8,128)(2,1)S(1)} %collective-permute-done.15.refs_10_) | copy-start | bytes 294916
  50.0 0.7 %copy-start.23 = (bf16[8,8,768]{2,1,0:T(8,128)(2,1)}, bf16[8,8,768]{2,1,0:T(8,128)(2,1)S(1)}, u32[]{:S(2)}) copy-start(bf16[8,8,768]{2,1,0:T(8,128)(2,1)S(1)} %collective-permute-done.16.refs_11_) | copy-start | bytes 294916

commit v2 on v1

v2 whole, which is shorter than its diff:
```python
import functools
import math

import jax
import jax.numpy as jnp
from jax import lax
from jax.experimental import pallas as pl
from jax.experimental.pallas import tpu as pltpu
from jax.sharding import PartitionSpec as P


NORM_EPS = 1e-05
MASK_PENALTY = 10000.0
F32 = jnp.float32
BF16 = jnp.bfloat16
CORES = 2
TILE = 256
VMEM = pl.BlockSpec(memory_space=pltpu.VMEM)
SMEM = pl.BlockSpec(memory_space=pltpu.SMEM)
VMEM = pl.BlockSpec(memory_space=pltpu.VMEM)
SMEM = pl.BlockSpec(memory_space=pltpu.SMEM)
VMEM = pl.BlockSpec(memory_space=pltpu.VMEM)
SMEM = pl.BlockSpec(memory_space=pltpu.SMEM)


def normed_rows(block):
    tokens, samples, width = block.shape
    values = block.astype(F32).reshape(tokens * samples, width)
    centred = values - jnp.mean(values, axis=-1, keepdims=True)
    spread = jnp.mean(centred * centred, axis=-1, keepdims=True)
    return (centred * lax.rsqrt(spread + NORM_EPS)).astype(BF16)


def sample_major(tokens, samples):
    rows = tokens * samples
    to = lax.broadcasted_iota(jnp.int32, (rows, rows), 0)
    frm = lax.broadcasted_iota(jnp.int32, (rows, rows), 1)
    want = (to % tokens) * samples + to // tokens
    return (want == frm).astype(F32).astype(BF16)


def token_major(tokens, samples):
    rows = tokens * samples
    to = lax.broadcasted_iota(jnp.int32, (rows, rows), 0)
    frm = lax.broadcasted_iota(jnp.int32, (rows, rows), 1)
    want = (to % samples) * tokens + to // samples
    return (want == frm).astype(F32).astype(BF16)


def matmul(a, b):
    return jnp.dot(a, b, preferred_element_type=F32)


META_ROWS = 8
RADIX = 128


def prep_body(single_ref, chain_ref, residue_ref, valid_ref, out_ref):
    tokens, samples, width = single_ref.shape
    rows = tokens * samples
    normed = normed_rows(single_ref[...])
    out_ref[pl.ds(0, rows), :] = matmul(sample_major(tokens, samples), normed).astype(BF16)
    residue = residue_ref[...]
    row = lax.broadcasted_iota(jnp.int32, (META_ROWS, tokens), 0)
    meta = jnp.where(row == 0, chain_ref[...], 0)
    meta = jnp.where(row == 1, residue // RADIX, meta)
    meta = jnp.where(row == 2, residue % RADIX, meta)
    meta = jnp.where(row == 3, valid_ref[...], meta)
    token = lax.broadcasted_iota(jnp.int32, (tokens, width), 0)
    lane = lax.broadcasted_iota(jnp.int32, (tokens, width), 1)
    spread = (lane % tokens == token).astype(F32).astype(BF16)
    tiled = matmul(meta.astype(F32).astype(BF16), spread)
    out_ref[pl.ds(rows, META_ROWS), :] = tiled.astype(BF16)


META_ROWS = 8
RADIX = 128


def prep_body(single_ref, chain_ref, residue_ref, valid_ref, out_ref):
    tokens, samples, width = single_ref.shape
    rows = tokens * samples
    normed = normed_rows(single_ref[...])
    out_ref[pl.ds(0, rows), :] = matmul(sample_major(tokens, samples), normed).astype(BF16)
    residue = residue_ref[...]
    row = lax.broadcasted_iota(jnp.int32, (META_ROWS, tokens), 0)
    meta = jnp.where(row == 0, chain_ref[...], 0)
    meta = jnp.where(row == 1, residue // RADIX, meta)
    meta = jnp.where(row == 2, residue % RADIX, meta)
    meta = jnp.where(row == 3, valid_ref[...], meta)
    token = lax.broadcasted_iota(jnp.int32, (tokens, width), 0)
    lane = lax.broadcasted_iota(jnp.int32, (tokens, width), 1)
    spread = (lane % tokens == token).astype(F32).astype(BF16)
    tiled = matmul(meta.astype(F32).astype(BF16), spread)
    out_ref[pl.ds(rows, META_ROWS), :] = tiled.astype(BF16)


META_ROWS = 8
RADIX = 128


def prep_body(single_ref, chain_ref, residue_ref, valid_ref, out_ref):
    tokens, samples, width = single_ref.shape
    rows = tokens * samples
    normed = normed_rows(single_ref[...])
    out_ref[pl.ds(0, rows), :] = matmul(sample_major(tokens, samples), normed).astype(BF16)
    residue = residue_ref[...]
    row = lax.broadcasted_iota(jnp.int32, (META_ROWS, tokens), 0)
    meta = jnp.where(row == 0, chain_ref[...], 0)
    meta = jnp.where(row == 1, residue // RADIX, meta)
    meta = jnp.where(row == 2, residue % RADIX, meta)
    meta = jnp.where(row == 3, valid_ref[...], meta)
    token = lax.broadcasted_iota(jnp.int32, (tokens, width), 0)
    lane = lax.broadcasted_iota(jnp.int32, (tokens, width), 1)
    spread = (lane % tokens == token).astype(F32).astype(BF16)
    tiled = matmul(meta.astype(F32).astype(BF16), spread)
    out_ref[pl.ds(rows, META_ROWS), :] = tiled.astype(BF16)


def query_body(pay_ref, wq_ref, wg_ref, q_ref, gate_ref):
    rows = pay_ref[pl.ds(0, q_ref.shape[0]), :]
    q_ref[...] = matmul(rows, wq_ref[...]).astype(BF16)
    gate_ref[...] = jax.nn.sigmoid(matmul(rows, wg_ref[...]))


def kv_body(*refs):
    wk_ref, wv_ref, out_ref = refs[-3:]
    blocks = refs[:-3]
    n = len(blocks)
    rows = blocks[0].shape[0] - META_ROWS
    parts = [b[pl.ds(0, rows), :] for b in blocks]
    data = jnp.concatenate(parts, axis=0) if n > 1 else parts[0]
    out_ref[pl.ds(0, n * rows), :] = matmul(data, wk_ref[...]).astype(BF16)
    out_ref[pl.ds(n * rows, n * rows), :] = matmul(data, wv_ref[...]).astype(BF16)
    for i, b in enumerate(blocks):
        out_ref[pl.ds(2 * n * rows + i * META_ROWS, META_ROWS), :] = b[pl.ds(rows, META_ROWS), :]


def ring_chip(place, chips):
    place = lax.rem(place + 2 * chips, chips)
    return jnp.where(place < chips // 2, 2 * place, 2 * (chips - 1 - place) + 1)


def bias_body(steps, chips, rows, me_ref, chain_ref, res_ref, pair_ref, wp_ref, tab_ref, *refs):
    out_ref = refs[-1]
    metas = refs[:-1]
    _, queries, total = out_ref.shape
    bins = tab_ref.shape[0]
    reach = (bins - 2) // 2
    tokens = total // len(steps)
    me = me_ref[0]
    chip = me // CORES
    core = lax.rem(me, CORES)
    place = jnp.where(lax.rem(chip, 2) == 0, chip // 2, chips - 1 - chip // 2)
    starts = []
    for r, c in steps:
        block = ring_chip(place + r, chips) * CORES + lax.rem(core + c, CORES)
        starts.append(pl.multiple_of(block * tokens, tokens))
    slot = lax.broadcasted_iota(jnp.int32, (META_ROWS, total), 1) // tokens
    keys = jnp.zeros((META_ROWS, total), F32)
    at = 0
    for m in metas:
        n = max(1, m.shape[0] // (2 * rows + META_ROWS))
        for u in range(n):
            row = m[pl.ds(m.shape[0] - (n - u) * META_ROWS, META_ROWS), :].astype(F32)
            row = jnp.concatenate([row] * (-(-total // row.shape[1])), axis=1)[:, :total]
            keys = jnp.where(slot == at, row, keys)
            at += 1
    chain_keys = keys[0:1, :]
    res_keys = keys[1:2, :] * RADIX + keys[2:3, :]
    mask = (keys[3:4, :] - 1.0) * MASK_PENALTY
    weights = jnp.transpose(wp_ref[...].astype(F32)).astype(BF16)
    table = jnp.transpose(tab_ref[...])
    high = table.astype(BF16)
    rest = table - high.astype(F32)
    mid = rest.astype(BF16)
    low = (rest - mid.astype(F32)).astype(BF16)
    bin_ids = lax.broadcasted_iota(jnp.int32, (bins, total), 0).astype(F32)
    for i in range(queries):
        data = jnp.concatenate([pair_ref[i, pl.ds(b, tokens), :] for b in starts], axis=0)
        acc = lax.dot_general(weights, data, (((1,), (1,)), ((), ())), preferred_element_type=F32)
        offset = jnp.clip(res_ref[i].astype(F32) - res_keys, -reach, reach) + reach
        bucket = jnp.where(chain_keys == chain_ref[i].astype(F32), offset, float(bins - 1))
        hot = (bin_ids == bucket).astype(F32).astype(BF16)
        rel = (matmul(low, hot) + matmul(mid, hot)) + matmul(high, hot)
        out_ref[:, i, :] = acc + rel + mask


def attend_rows(first, count, heads, scale, kv_refs, mine, other, q_ref, gate_ref, bias_ref, wk, wv):
    rows, width = gate_ref.shape
    half = mine.shape[0]
    tokens = half // count
    hs = width // heads
    data = jnp.concatenate([mine, other], axis=0)
    k_last = matmul(data, wk).astype(BF16)
    v_last = matmul(data, wv).astype(BF16)
    total = bias_ref.shape[2]
    bias = bias_ref[...].reshape(heads * tokens, total)
    lane_head = lax.broadcasted_iota(jnp.int32, (tokens, width), 1) // hs
    spans = []
    for t in range(width // TILE):
        spans.append(((t * TILE) // hs, ((t + 1) * TILE - 1) // hs))
    gated = []
    for s in range(count):
        keys, values = [], []
        for r in kv_refs:
            n = r.shape[0] // (2 * rows + META_ROWS)
            for u in range(n):
                keys.append(r[pl.ds(u * rows + (first + s) * tokens, tokens), :])
                values.append(r[pl.ds((n + u) * rows + (first + s) * tokens, tokens), :])
        for u in range(2):
            keys.append(k_last[u * half + s * tokens : u * half + (s + 1) * tokens])
            values.append(v_last[u * half + s * tokens : u * half + (s + 1) * tokens])
        keys = jnp.concatenate(keys, axis=0)
        values = jnp.concatenate(values, axis=0)
        q = q_ref[pl.ds((first + s) * tokens, tokens), :].astype(F32)
        per_head = [None] * heads
        for t, (h0, h1) in enumerate(spans):
            cut = slice(t * TILE, (t + 1) * TILE)
            masked = [
                jnp.where(lane_head[:, cut] == h, q[:, cut], 0.0).astype(BF16)
                for h in range(h0, h1 + 1)
            ]
            qt = jnp.concatenate(masked, axis=0)
            st = lax.dot_general(
                qt, keys[:, cut], (((1,), (1,)), ((), ())), preferred_element_type=F32
            )
            for h in range(h0, h1 + 1):
                part = st[(h - h0) * tokens : (h - h0 + 1) * tokens]
                per_head[h] = part if per_head[h] is None else per_head[h] + part
        scores = jnp.concatenate(per_head, axis=0) * scale + bias
        top = jnp.max(scores, axis=-1, keepdims=True)
        probs = jnp.exp(scores - top)
        inv = 1.0 / jnp.sum(probs, axis=-1, keepdims=True)
        probs = probs.astype(BF16)
        attended = []
        for t, (h0, h1) in enumerate(spans):
            cut = slice(t * TILE, (t + 1) * TILE)
            ot = matmul(probs[h0 * tokens : (h1 + 1) * tokens], values[:, cut])
            ot = ot * inv[h0 * tokens : (h1 + 1) * tokens]
            got = ot[:tokens]
            for h in range(h0 + 1, h1 + 1):
                here = ot[(h - h0) * tokens : (h - h0 + 1) * tokens]
                got = jnp.where(lane_head[:, cut] == h, here, got)
            attended.append(got)
        attended = jnp.concatenate(attended, axis=1)
        gated.append((gate_ref[pl.ds((first + s) * tokens, tokens), :] * attended).astype(BF16))
    return jnp.concatenate(gated, axis=0)


def attend_body(count, heads, scale, *refs):
    mine, other, q_ref, gate_ref, bias_ref, wk, wv, out_ref = refs[-8:]
    out_ref[...] = attend_rows(
        0, count, heads, scale, refs[:-8], mine[...], other[...], q_ref, gate_ref, bias_ref,
        wk[...], wv[...],
    )


def finish_body(count, heads, scale, *refs):
    mine, other, q_ref, gate_ref, bias_ref, wk, wv, done, single_ref, wo_ref, out_ref = refs[-11:]
    tokens, samples, width = single_ref.shape
    gated = attend_rows(
        samples - count, count, heads, scale, refs[:-11], mine[...], other[...], q_ref, gate_ref,
        bias_ref, wk[...], wv[...],
    )
    gated = jnp.concatenate([done[...], gated], axis=0)
    gated = matmul(token_major(tokens, samples), gated).astype(BF16)
    out = matmul(gated, wo_ref[...]).reshape(tokens, samples, width)
    out_ref[...] = (single_ref[...].astype(F32) + out).astype(BF16)


def call(body, out_shape, args, in_specs=None, flops=0, moved=0, limit=16 << 20):
    return pl.pallas_call(
        body,
        out_shape=out_shape,
        in_specs=in_specs or [VMEM] * len(args),
        out_specs=jax.tree.map(lambda _: VMEM, out_shape),
        compiler_params=pltpu.CompilerParams(vmem_limit_bytes=limit),
        cost_estimate=pl.CostEstimate(flops=flops, bytes_accessed=moved, transcendentals=0),
    )(*args)


def shards(
    single, pair, chain, residue, valid, w_query, w_key, w_value, w_gate, w_out, w_pair, rel_table
):
    tokens, samples, width = single.shape
    heads = w_pair.shape[1]
    total = pair.shape[1]
    rows = tokens * samples
    devices = lax.axis_size("tok")
    chips = devices // CORES
    half = chips // 2
    order = list(range(0, chips, 2)) + list(range(1, chips, 2))[::-1]
    me = lax.axis_index("tok").astype(jnp.int32).reshape(1)

    def ring(value, step):
        pairs = [
            (order[i] * CORES + c, order[(i + step) % chips] * CORES + c)
            for i in range(chips)
            for c in range(CORES)
        ]
        return lax.ppermute(value, "tok", pairs)

    def flip(value):
        return lax.ppermute(value, "tok", [(d, d ^ 1) for d in range(devices)])

    steps = [(0, 0), (0, 1)]
    for k in range(1, half):
        steps += [(-k, 0), (k, 0), (-k, 1), (k, 1)]
    steps += [(half, 0), (half, 1)]

    payload = call(
        prep_body,
        jax.ShapeDtypeStruct((rows + META_ROWS, width), BF16),
        (single, *(v.reshape(1, tokens) for v in (chain, residue, valid))),
        flops=rows * width * 16,
        moved=4 * rows * width,
    )
    cw = ring(payload, 1)
    ccw = ring(payload, -1)

    query, gate = call(
        query_body,
        (jax.ShapeDtypeStruct((rows, width), BF16), jax.ShapeDtypeStruct((rows, width), F32)),
        (payload, w_query, w_gate),
        flops=4 * rows * width * width,
        moved=4 * width * width + 8 * rows * width,
    )

    def kv(parts):
        n = len(parts)
        return call(
            kv_body,
            jax.ShapeDtypeStruct((n * (2 * rows + META_ROWS), width), BF16),
            (*parts, w_key, w_value),
            flops=4 * n * rows * width * width,
            moved=4 * width * width + 6 * n * rows * width,
        )

    far = ring(payload[rows:], half)
    far = [far, flip(far)]
    kvs = [kv([payload])]
    kvs.append(flip(kvs[-1]))
    for k in range(1, half):
        if k + 1 < half:
            cw_next = ring(cw, 1)
            ccw_next = ring(ccw, -1)
        else:
            cw_next = ring(cw[: rows // 2], 1)
            ccw_next = ring(ccw[rows // 2 : rows], -1)
        kvs.append(kv([cw, ccw]))
        kvs.append(flip(kvs[-1]))
        cw, ccw = cw_next, ccw_next
    bias = call(
        functools.partial(bias_body, steps, chips, rows),
        jax.ShapeDtypeStruct((heads, tokens, total), F32),
        (me, chain, residue, pair, w_pair, rel_table, *kvs, *far),
        in_specs=[SMEM, SMEM, SMEM, *[VMEM] * (5 + len(kvs))],
        flops=2 * tokens * total * heads * 512,
        moved=pair.size * 2 + heads * tokens * total * 4,
    )
    scale = 1.0 / math.sqrt(width // heads)
    count = samples // 2
    limit = min(60 << 20, (16 << 20) + 4 * samples * total * width)
    common = dict(flops=2 * rows * total * width, moved=2 * samples * total * width, limit=limit)
    gated = call(
        functools.partial(attend_body, count, heads, scale),
        jax.ShapeDtypeStruct((rows // 2, width), BF16),
        (*kvs, cw, flip(cw), query, gate, bias, w_key, w_value),
        **common,
    )
    return call(
        functools.partial(finish_body, count, heads, scale),
        jax.ShapeDtypeStruct(single.shape, BF16),
        (*kvs, ccw, flip(ccw), query, gate, bias, w_key, w_value, gated, single, w_out),
        **common,
    )


def solution(mesh):
    placed = (
        P(("groups", "tok"), None, None),
        P(("groups", "tok"), None, None),
        P(("groups", "tok")),
        P(("groups", "tok")),
        P(("groups", "tok")),
        P(),
        P(),
        P(),
        P(),
        P(),
        P(),
        P(),
    )

    return jax.shard_map(
        shards,
        mesh=mesh,
        in_specs=placed,
        out_specs=P(("groups", "tok"), None, None),
        check_vma=False,
    )
```

time: 60.5 us -> 57.9 us (0.957)
  waiting for transfers between devices: 7.19 us -> 16.3 us
  Pallas kernels: 21.4 us -> 16.8 us
  starting transfers between devices: 17.4 us -> 14.5 us
  local copies, waits for them, and re-layouts: 12.2 us -> 9.79 us
  other arithmetic: 1.72 us -> 0 us
    ppermute x8 -> x9, waiting for transfers between devices: 1.43 us -> 15.1 us  [ring(): return lax.ppermute(value, 'tok', pairs)]
    ppermute x13 -> x7, starting transfers between devices: 8.32 us -> 1.2 us  [flip(): return lax.ppermute(value, 'tok', [(d, d ^ 1) for d in range(devices)])]
    pallas_call x7 -> x9, Pallas kernels: 21.4 us -> 16.8 us  [call(): pl.pallas_call(body, out_shape=out_shape, in_specs=in_specs or [VMEM] * l...]
    ppermute x13 -> x7, waiting for transfers between devices: 5.77 us -> 1.18 us  [flip(): return lax.ppermute(value, 'tok', [(d, d ^ 1) for d in range(devices)])]
    ppermute x8 -> x9, starting transfers between devices: 9.13 us -> 13.3 us  [ring(): return lax.ppermute(value, 'tok', pairs)]
    unnamed x54 -> x40, local copies, waits for them, and re-layouts: 11.3 us -> 9.77 us
    convert_element_type x1 -> x0, other arithmetic: 0.7 us -> none  [shards(): jnp.stack([chain, residue, valid], axis=0).astype(F32)]
    and x1 -> x0, other arithmetic: 0.69 us -> none  [shards(): meta = jnp.take(meta, blocks, axis=0).reshape(devices, 3, tokens)]
  transfers between devices with their start and end apart: 21 -> 16, of which waited for: 5 -> 7; matrix products, arithmetic and copies ran while one was open for 5% -> 0% of each run, Pallas kernels for 20% -> 19%
where the time goes in v2:
time: 57.9 us; the launch traced here: 57.5 us
  Pallas kernels  16.8 us (29%)
  waiting for transfers between devices  16.3 us (28%)
  starting transfers between devices  14.5 us (25%)
  local copies, waits for them, and re-layouts  9.79 us (17%)
    pallas_call x9, Pallas kernels, call(): pl.pallas_call(body, out_shape=out_shape, in_specs=in_specs or [VMEM] * l...  16.8 us
    ppermute x9, waiting for transfers between devices, ring(): return lax.ppermute(value, 'tok', pairs)  15.1 us
    ppermute x9, starting transfers between devices, ring(): return lax.ppermute(value, 'tok', pairs)  13.3 us
    unnamed x40, local copies, waits for them, and re-layouts  9.77 us
    ppermute x7, starting transfers between devices, flip(): return lax.ppermute(value, 'tok', [(d, d ^ 1) for d in range(devices)])  1.2 us
    ppermute x7, waiting for transfers between devices, flip(): return lax.ppermute(value, 'tok', [(d, d ^ 1) for d in range(devices)])  1.18 us
  transfers between devices with their start and end apart: 16, of which 7 were waited for; matrix products, arithmetic and copies ran while one was open for 0% of the time, Pallas kernels for 19%

profile of v2, /device:TPU:0, one launch (start us, length us, event | category | flops | bytes accessed | tf_op | source)
XLA Modules:
  0.0 57.5 jit_solution(16213424527307545456)
XLA Ops:
  0.0 0.9 %copy-done.10 = bf16[16,8,768]{2,1,0:T(8,128)(2,1)S(1)} copy-done((bf16[16,8,768]{2,1,0:T(8,128)(2,1)S(1)}, bf16[16,8,768]{2,1,0:T(8,128)(2,1)}, u32[]{:S(2)}) %copy-start.10) | copy-done | bytes 196632
  0.9 0.7 %copy-done.12 = s32[16]{0:T(128)S(1)} copy-done((s32[16]{0:T(128)S(1)}, s32[16]{0:T(128)}, u32[]{:S(2)}) %copy-start.12) | copy-done | bytes 88
  1.6 0.7 %copy-done.14 = s32[16]{0:T(128)S(1)} copy-done((s32[16]{0:T(128)S(1)}, s32[16]{0:T(128)}, u32[]{:S(2)}) %copy-start.14) | copy-done | bytes 88
  2.2 0.7 %copy-done.16 = s32[16]{0:T(128)S(1)} copy-done((s32[16]{0:T(128)S(1)}, s32[16]{0:T(128)}, u32[]{:S(2)}) %copy-start.16) | copy-done | bytes 88
  2.9 0.4 shard_map.118.refs_0_.pay_ref
  3.3 3.0 %collective-permute-start.2 = (bf16[136,768]{1,0:T(8,128)(2,1)S(1)}, bf16[136,768]{1,0:T(8,128)(2,1)S(1)}, u32[]{:S(2)}, u32[]{:S(2)}) collective-permute-start(bf16[136,768]{1,0:T(8,128)(2,1)S(1)} %shard_map.118.refs_0_.pay_ref), channel_id=1, source_target_pairs={{0,2},{1,3},{4,0},{5,1},{8,4},{9,5},{12,8},{13,9},{14,12},{15,13},... | collective-permute-start | bytes 626696 | tf_op jit(solution)/shard_map/ppermute | solution.py:302
  6.4 0.1 collective-permute-start.1
  6.5 5.1 %collective-permute-done.2.refs_1_ = bf16[136,768]{1,0:T(8,128)(2,1)S(1)} collective-permute-done((bf16[136,768]{1,0:T(8,128)(2,1)S(1)}, bf16[136,768]{1,0:T(8,128)(2,1)S(1)}, u32[]{:S(2)}, u32[]{:S(2)}) %collective-permute-start.2) | collective-permute-done | bytes 208928 | tf_op jit(solution)/shard_map/ppermute | solution.py:302
  11.6 1.7 %collective-permute-start.5 = (bf16[136,768]{1,0:T(8,128)(2,1)S(1)}, bf16[136,768]{1,0:T(8,128)(2,1)S(1)}, u32[]{:S(2)}, u32[]{:S(2)}) collective-permute-start(bf16[136,768]{1,0:T(8,128)(2,1)S(1)} %collective-permute-done.2.refs_1_), channel_id=1, source_target_pairs={{0,2},{1,3},{4,0},{5,1},{8,4},{9,5},{12,8},{13,9},{14,12},{15,13},... | collective-permute-start | bytes 626696 | tf_op jit(solution)/shard_map/ppermute | solution.py:302
  13.3 0.0 collective-permute-done.1.refs_0_
  13.3 0.3 collective-permute-start.4
  13.6 4.3 %collective-permute-done.5.refs_1_ = bf16[136,768]{1,0:T(8,128)(2,1)S(1)} collective-permute-done((bf16[136,768]{1,0:T(8,128)(2,1)S(1)}, bf16[136,768]{1,0:T(8,128)(2,1)S(1)}, u32[]{:S(2)}, u32[]{:S(2)}) %collective-permute-start.5) | collective-permute-done | bytes 208928 | tf_op jit(solution)/shard_map/ppermute | solution.py:302
  17.9 1.4 %collective-permute-start.8 = (bf16[136,768]{1,0:T(8,128)(2,1)S(1)}, bf16[136,768]{1,0:T(8,128)(2,1)S(1)}, u32[]{:S(2)}, u32[]{:S(2)}) collective-permute-start(bf16[136,768]{1,0:T(8,128)(2,1)S(1)} %collective-permute-done.5.refs_1_), channel_id=1, source_target_pairs={{0,2},{1,3},{4,0},{5,1},{8,4},{9,5},{12,8},{13,9},{14,12},{15,13},... | collective-permute-start | bytes 626696 | tf_op jit(solution)/shard_map/ppermute | solution.py:302
  19.3 0.0 collective-permute-done.4.refs_0_
  19.3 0.6 %collective-permute-start.7 = (bf16[136,768]{1,0:T(8,128)(2,1)S(1)}, bf16[136,768]{1,0:T(8,128)(2,1)S(1)}, u32[]{:S(2)}, u32[]{:S(2)}) collective-permute-start(bf16[136,768]{1,0:T(8,128)(2,1)S(1)} %collective-permute-done.4.refs_0_), channel_id=1, source_target_pairs={{0,4},{1,5},{4,8},{5,9},{8,12},{9,13},{12,14},{13,15},{14,10},{15,... | collective-permute-start | bytes 626696 | tf_op jit(solution)/shard_map/ppermute | solution.py:302
  19.9 1.3 %copy-done = bf16[768,768]{1,0:T(8,128)(2,1)S(1)} copy-done((bf16[768,768]{1,0:T(8,128)(2,1)S(1)}, bf16[768,768]{1,0:T(8,128)(2,1)}, u32[]{:S(2)}) %copy-start) | copy-done | bytes 1179672
  21.2 1.3 %copy-done.2 = bf16[768,768]{1,0:T(8,128)(2,1)S(1)} copy-done((bf16[768,768]{1,0:T(8,128)(2,1)S(1)}, bf16[768,768]{1,0:T(8,128)(2,1)}, u32[]{:S(2)}) %copy-start.2) | copy-done | bytes 1179672
  22.5 0.8 %shard_map.120.refs_2_ = bf16[528,768]{1,0:T(8,128)(2,1)S(1)} custom-call(bf16[136,768]{1,0:T(8,128)(2,1)S(1)} %collective-permute-done.1.refs_0_, bf16[136,768]{1,0:T(8,128)(2,1)S(1)} %collective-permute-done.2.refs_1_, bf16[768,768]{1,0:T(8,128)(2,1)S(1)} %copy-done, bf16[768,768]{1,0:T(8,128)(2,1)S(1)} %copy-done.2), custom_call_target="tpu_custom_call" | custom-call | flops 603979776 | bytes 3538944 | tf_op jit(solution)/shard_map/pallas_call | solution.py:273
  23.3 0.1 collective-permute-start.3
  23.4 0.8 %shard_map.121.refs_4_ = bf16[528,768]{1,0:T(8,128)(2,1)S(1)} custom-call(bf16[136,768]{1,0:T(8,128)(2,1)S(1)} %collective-permute-done.4.refs_0_, bf16[136,768]{1,0:T(8,128)(2,1)S(1)} %collective-permute-done.5.refs_1_, bf16[768,768]{1,0:T(8,128)(2,1)S(1)} %copy-done, bf16[768,768]{1,0:T(8,128)(2,1)S(1)} %copy-done.2), custom_call_target="tpu_custom_call" | custom-call | flops 603979776 | bytes 3538944 | tf_op jit(solution)/shard_map/pallas_call | solution.py:273
  24.1 0.0 copy-start.1
  24.2 0.6 collective-permute-start.6
  24.7 0.0 collective-permute-done.8.refs_1_
  24.7 0.4 collective-permute-done.7.refs_0_
  25.1 1.7 %shard_map.122.refs_6_ = bf16[528,768]{1,0:T(8,128)(2,1)} custom-call(bf16[136,768]{1,0:T(8,128)(2,1)S(1)} %collective-permute-done.7.refs_0_, bf16[136,768]{1,0:T(8,128)(2,1)S(1)} %collective-permute-done.8.refs_1_, bf16[768,768]{1,0:T(8,128)(2,1)S(1)} %copy-done, bf16[768,768]{1,0:T(8,128)(2,1)S(1)} %copy-done.2), custom_call_target="tpu_custom_call" | custom-call | flops 603979776 | bytes 3538944 | tf_op jit(solution)/shard_map/pallas_call | solution.py:273
  26.8 0.0 collective-permute-start.9
  26.8 0.5 shard_map.119.refs_0_
  27.3 0.6 collective-permute-start
  27.9 4.0 %collective-permute-start.12 = (bf16[8,768]{1,0:T(8,128)(2,1)S(1)}, bf16[8,768]{1,0:T(8,128)(2,1)S(1)}, u32[]{:S(2)}, u32[]{:S(2)}) collective-permute-start(bf16[8,768]{1,0:T(8,128)(2,1)S(1)} %slice.13), channel_id=1, source_target_pairs={{0,14},{1,15},{4,10},{5,11},{8,6},{9,7},{12,2},{13,3},{14,0},{15,1... | collective-permute-start | bytes 36872 | tf_op jit(solution)/shard_map/ppermute | solution.py:302
  31.9 2.3 %collective-permute-done.12.refs_8_ = bf16[8,768]{1,0:T(8,128)(2,1)S(1)} collective-permute-done((bf16[8,768]{1,0:T(8,128)(2,1)S(1)}, bf16[8,768]{1,0:T(8,128)(2,1)S(1)}, u32[]{:S(2)}, u32[]{:S(2)}) %collective-permute-start.12) | collective-permute-done | bytes 12320 | tf_op jit(solution)/shard_map/ppermute | solution.py:302
  34.3 1.2 %collective-permute-done.13.refs_9_ = bf16[8,768]{1,0:T(8,128)(2,1)S(1)} collective-permute-done((bf16[8,768]{1,0:T(8,128)(2,1)S(1)}, bf16[8,768]{1,0:T(8,128)(2,1)S(1)}, u32[]{:S(2)}, u32[]{:S(2)}) %collective-permute-start.13) | collective-permute-done | bytes 12320 | tf_op jit(solution)/shard_map/ppermute | solution.py:305
  35.4 0.0 collective-permute-start.14
  35.5 0.7 %copy-done.4 = bf16[264,768]{1,0:T(8,128)(2,1)} copy-done((bf16[264,768]{1,0:T(8,128)(2,1)}, bf16[264,768]{1,0:T(8,128)(2,1)S(1)}, u32[]{:S(2)}) %copy-start.4) | copy-done | bytes 405528
  36.2 2.0 %collective-permute-start.10 = (bf16[64,768]{1,0:T(8,128)(2,1)S(1)}, bf16[64,768]{1,0:T(8,128)(2,1)}, u32[]{:S(2)}, u32[]{:S(2)}) collective-permute-start(bf16[64,768]{1,0:T(8,128)(2,1)S(1)} %slice.12), channel_id=1, source_target_pairs={{0,2},{1,3},{4,0},{5,1},{8,4},{9,5},{12,8},{13,9},{14,12},{15,13},... | collective-permute-start | bytes 294920 | tf_op jit(solution)/shard_map/ppermute | solution.py:302
  38.2 2.2 %collective-permute-done.14.refs_8_ = bf16[64,768]{1,0:T(8,128)(2,1)} collective-permute-done((bf16[64,768]{1,0:T(8,128)(2,1)S(1)}, bf16[64,768]{1,0:T(8,128)(2,1)}, u32[]{:S(2)}, u32[]{:S(2)}) %collective-permute-start.14) | collective-permute-done | bytes 98336 | tf_op jit(solution)/shard_map/ppermute | solution.py:302
  40.4 0.8 %collective-permute-done.10.refs_8_ = bf16[64,768]{1,0:T(8,128)(2,1)} collective-permute-done((bf16[64,768]{1,0:T(8,128)(2,1)S(1)}, bf16[64,768]{1,0:T(8,128)(2,1)}, u32[]{:S(2)}, u32[]{:S(2)}) %collective-permute-start.10) | collective-permute-done | bytes 98336 | tf_op jit(solution)/shard_map/ppermute | solution.py:302
  41.2 0.1 copy.13.wp_ref
  41.3 0.1 copy.14.tab_ref
  41.4 1.3 %copy-done.7 = bf16[768,768]{1,0:T(8,128)(2,1)S(1)} copy-done((bf16[768,768]{1,0:T(8,128)(2,1)S(1)}, bf16[768,768]{1,0:T(8,128)(2,1)}, u32[]{:S(2)}) %copy-start.7) | copy-done | bytes 1179672
  42.7 1.3 %copy-done.8 = bf16[768,768]{1,0:T(8,128)(2,1)S(1)} copy-done((bf16[768,768]{1,0:T(8,128)(2,1)S(1)}, bf16[768,768]{1,0:T(8,128)(2,1)}, u32[]{:S(2)}) %copy-start.8) | copy-done | bytes 1179672
  44.0 0.5 shard_map.123
  44.5 0.4 copy-done.5
  45.0 0.4 copy-done.9
  45.3 2.8 %shard_map.124.refs_12_ = f32[16,16,256]{2,1,0:T(8,128)S(1)} custom-call(s32[1]{0:T(128)} %bitcast.3.me_ref, s32[16]{0:T(128)S(1)} %copy-done.13, s32[16]{0:T(128)S(1)} %copy-done.15, bf16[16,256,128]{2,1,0:T(8,128)(2,1)S(1)} %copy-done.9, bf16[128,16]{1,0:T(8,128)(2,1)S(1)} %copy.13.wp_ref, f32[66,16]{1,0:T(8,128)S(1)} %copy.14.tab_ref, ...), custom_call_target="tpu_custom_call" | custom-call | flops 67108864 | bytes 1310720 | tf_op jit(solution)/shard_map/pallas_call | solution.py:273
  48.1 0.0 copy-start.6
  48.1 0.0 copy-start.11
  48.1 4.2 %shard_map.125.refs_15_ = bf16[64,768]{1,0:T(8,128)(2,1)S(1)} custom-call(bf16[264,768]{1,0:T(8,128)(2,1)S(1)} %shard_map.119.refs_0_, bf16[264,768]{1,0:T(8,128)(2,1)S(1)} %copy-done.5, bf16[528,768]{1,0:T(8,128)(2,1)S(1)} %shard_map.120.refs_2_, bf16[528,768]{1,0:T(8,128)(2,1)} %collective-permute-done.3.refs_3_, bf16[528,768]{1,0:T(8,128)(2,1)S(1)} %shard_map.121.refs_4_, ...), custom_call_target="tpu_custom_call" | custom-call | flops 50331648 | bytes 3145728 | tf_op jit(solution)/shard_map/pallas_call | solution.py:273
  52.3 5.2 %shard_map.126 = bf16[16,8,768]{2,1,0:T(8,128)(2,1)} custom-call(bf16[264,768]{1,0:T(8,128)(2,1)S(1)} %shard_map.119.refs_0_, bf16[264,768]{1,0:T(8,128)(2,1)S(1)} %copy-done.5, bf16[528,768]{1,0:T(8,128)(2,1)S(1)} %shard_map.120.refs_2_, bf16[528,768]{1,0:T(8,128)(2,1)} %collective-permute-done.3.refs_3_, bf16[528,768]{1,0:T(8,128)(2,1)S(1)} %shard_map.121.refs_4_, ...), custom_call_target="tpu_custom_call" | custom-call | flops 50331648 | bytes 3145728 | tf_op jit(solution)/shard_map/pallas_call | solution.py:273
  (36 shorter events, 0.1 us)
Async XLA Ops:
  0.0 0.9 %copy-start.10 = (bf16[16,8,768]{2,1,0:T(8,128)(2,1)S(1)}, bf16[16,8,768]{2,1,0:T(8,128)(2,1)}, u32[]{:S(2)}) copy-start(bf16[16,8,768]{2,1,0:T(8,128)(2,1)} %refs_16_.1) | copy-start | bytes 589828
  0.9 0.7 %copy-start.12 = (s32[16]{0:T(128)S(1)}, s32[16]{0:T(128)}, u32[]{:S(2)}) copy-start(s32[16]{0:T(128)} %chain_ref.1) | copy-start | bytes 196
  1.6 0.7 %copy-start.14 = (s32[16]{0:T(128)S(1)}, s32[16]{0:T(128)}, u32[]{:S(2)}) copy-start(s32[16]{0:T(128)} %res_ref.1) | copy-start | bytes 196
  2.2 0.7 %copy-start.16 = (s32[16]{0:T(128)S(1)}, s32[16]{0:T(128)}, u32[]{:S(2)}) copy-start(s32[16]{0:T(128)} %param.16) | copy-start | bytes 196
  3.3 8.3 %collective-permute-start.2 = (bf16[136,768]{1,0:T(8,128)(2,1)S(1)}, bf16[136,768]{1,0:T(8,128)(2,1)S(1)}, u32[]{:S(2)}, u32[]{:S(2)}) collective-permute-start(bf16[136,768]{1,0:T(8,128)(2,1)S(1)} %shard_map.118.refs_0_.pay_ref), channel_id=1, source_target_pairs={{0,2},{1,3},{4,0},{5,1},{8,4},{9,5},{12,8},{13,9},{14,12},{15,13},... | collective-permute-start | bytes 626696 | tf_op jit(solution)/shard_map/ppermute | solution.py:302
  6.4 6.9 %collective-permute-start.1 = (bf16[136,768]{1,0:T(8,128)(2,1)S(1)}, bf16[136,768]{1,0:T(8,128)(2,1)S(1)}, u32[]{:S(2)}, u32[]{:S(2)}) collective-permute-start(bf16[136,768]{1,0:T(8,128)(2,1)S(1)} %shard_map.118.refs_0_.pay_ref), channel_id=1, source_target_pairs={{0,4},{1,5},{4,8},{5,9},{8,12},{9,13},{12,14},{13,15},{14,10},{15,... | collective-permute-start | bytes 626696 | tf_op jit(solution)/shard_map/ppermute | solution.py:302
  11.6 6.3 %collective-permute-start.5 = (bf16[136,768]{1,0:T(8,128)(2,1)S(1)}, bf16[136,768]{1,0:T(8,128)(2,1)S(1)}, u32[]{:S(2)}, u32[]{:S(2)}) collective-permute-start(bf16[136,768]{1,0:T(8,128)(2,1)S(1)} %collective-permute-done.2.refs_1_), channel_id=1, source_target_pairs={{0,2},{1,3},{4,0},{5,1},{8,4},{9,5},{12,8},{13,9},{14,12},{15,13},... | collective-permute-start | bytes 626696 | tf_op jit(solution)/shard_map/ppermute | solution.py:302
  13.3 6.0 %collective-permute-start.4 = (bf16[136,768]{1,0:T(8,128)(2,1)S(1)}, bf16[136,768]{1,0:T(8,128)(2,1)S(1)}, u32[]{:S(2)}, u32[]{:S(2)}) collective-permute-start(bf16[136,768]{1,0:T(8,128)(2,1)S(1)} %collective-permute-done.1.refs_0_), channel_id=1, source_target_pairs={{0,4},{1,5},{4,8},{5,9},{8,12},{9,13},{12,14},{13,15},{14,10},{15,... | collective-permute-start | bytes 626696 | tf_op jit(solution)/shard_map/ppermute | solution.py:302
  17.9 6.8 %collective-permute-start.8 = (bf16[136,768]{1,0:T(8,128)(2,1)S(1)}, bf16[136,768]{1,0:T(8,128)(2,1)S(1)}, u32[]{:S(2)}, u32[]{:S(2)}) collective-permute-start(bf16[136,768]{1,0:T(8,128)(2,1)S(1)} %collective-permute-done.5.refs_1_), channel_id=1, source_target_pairs={{0,2},{1,3},{4,0},{5,1},{8,4},{9,5},{12,8},{13,9},{14,12},{15,13},... | collective-permute-start | bytes 626696 | tf_op jit(solution)/shard_map/ppermute | solution.py:302
  19.3 5.8 %collective-permute-start.7 = (bf16[136,768]{1,0:T(8,128)(2,1)S(1)}, bf16[136,768]{1,0:T(8,128)(2,1)S(1)}, u32[]{:S(2)}, u32[]{:S(2)}) collective-permute-start(bf16[136,768]{1,0:T(8,128)(2,1)S(1)} %collective-permute-done.4.refs_0_), channel_id=1, source_target_pairs={{0,4},{1,5},{4,8},{5,9},{8,12},{9,13},{12,14},{13,15},{14,10},{15,... | collective-permute-start | bytes 626696 | tf_op jit(solution)/shard_map/ppermute | solution.py:302
  19.9 1.3 %copy-start = (bf16[768,768]{1,0:T(8,128)(2,1)S(1)}, bf16[768,768]{1,0:T(8,128)(2,1)}, u32[]{:S(2)}) copy-start(bf16[768,768]{1,0:T(8,128)(2,1)} %refs_13_.3) | copy-start | bytes 3538948
  21.2 1.3 %copy-start.2 = (bf16[768,768]{1,0:T(8,128)(2,1)S(1)}, bf16[768,768]{1,0:T(8,128)(2,1)}, u32[]{:S(2)}) copy-start(bf16[768,768]{1,0:T(8,128)(2,1)} %refs_14_.3) | copy-start | bytes 3538948
  23.3 21.2 %collective-permute-start.3 = (bf16[528,768]{1,0:T(8,128)(2,1)S(1)}, bf16[528,768]{1,0:T(8,128)(2,1)}, u32[]{:S(2)}, u32[]{:S(2)}) collective-permute-start(bf16[528,768]{1,0:T(8,128)(2,1)S(1)} %shard_map.120.refs_2_), channel_id=1, source_target_pairs={{0,1},{1,0},{2,3},{3,2},{4,5},{5,4},{6,7},{7,6},{8,9},{9,8},{10,11... | collective-permute-start | bytes 2433032 | tf_op jit(solution)/shard_map/ppermute | solution.py:305
  24.1 2.7 %copy-start.1 = (bf16[768,768]{1,0:T(8,128)(2,1)S(1)}, bf16[768,768]{1,0:T(8,128)(2,1)}, u32[]{:S(2)}) copy-start(bf16[768,768]{1,0:T(8,128)(2,1)} %refs_13_.3) | copy-start | bytes 3538948
  24.2 20.3 %collective-permute-start.6 = (bf16[528,768]{1,0:T(8,128)(2,1)S(1)}, bf16[528,768]{1,0:T(8,128)(2,1)}, u32[]{:S(2)}, u32[]{:S(2)}) collective-permute-start(bf16[528,768]{1,0:T(8,128)(2,1)S(1)} %shard_map.121.refs_4_), channel_id=1, source_target_pairs={{0,1},{1,0},{2,3},{3,2},{4,5},{5,4},{6,7},{7,6},{8,9},{9,8},{10,11... | collective-permute-start | bytes 2433032 | tf_op jit(solution)/shard_map/ppermute | solution.py:305
  26.8 14.4 %copy-start.18 = (bf16[128,16]{0,1:T(8,128)(2,1)S(1)}, bf16[128,16]{0,1:T(8,128)(2,1)}, u32[]{:S(2)}) copy-start(bf16[128,16]{0,1:T(8,128)(2,1)} %param.22) | copy-start | bytes 12292
  26.8 14.5 %copy-start.17 = (f32[66,16]{0,1:T(8,128)S(1)}, f32[66,16]{0,1:T(8,128)}, u32[]{:S(2)}) copy-start(f32[66,16]{0,1:T(8,128)} %param.23) | copy-start | bytes 12676
  26.8 17.7 %collective-permute-start.9 = (bf16[528,768]{1,0:T(8,128)(2,1)}, bf16[528,768]{1,0:T(8,128)(2,1)}, u32[]{:S(2)}, u32[]{:S(2)}) collective-permute-start(bf16[528,768]{1,0:T(8,128)(2,1)} %shard_map.122.refs_6_), channel_id=1, source_target_pairs={{0,1},{1,0},{2,3},{3,2},{4,5},{5,4},{6,7},{7,6},{8,9},{9,8},{10,11... | collective-permute-start | bytes 2433032 | tf_op jit(solution)/shard_map/ppermute | solution.py:305
  27.3 8.2 %collective-permute-start = (bf16[264,768]{1,0:T(8,128)(2,1)S(1)}, bf16[264,768]{1,0:T(8,128)(2,1)S(1)}, u32[]{:S(2)}, u32[]{:S(2)}) collective-permute-start(bf16[264,768]{1,0:T(8,128)(2,1)S(1)} %shard_map.119.refs_0_), channel_id=1, source_target_pairs={{0,1},{1,0},{2,3},{3,2},{4,5},{5,4},{6,7},{7,6},{8,9},{9,8},{10,11... | collective-permute-start | bytes 1216520 | tf_op jit(solution)/shard_map/ppermute | solution.py:305
  27.9 6.4 %collective-permute-start.12 = (bf16[8,768]{1,0:T(8,128)(2,1)S(1)}, bf16[8,768]{1,0:T(8,128)(2,1)S(1)}, u32[]{:S(2)}, u32[]{:S(2)}) collective-permute-start(bf16[8,768]{1,0:T(8,128)(2,1)S(1)} %slice.13), channel_id=1, source_target_pairs={{0,14},{1,15},{4,10},{5,11},{8,6},{9,7},{12,2},{13,3},{14,0},{15,1... | collective-permute-start | bytes 36872 | tf_op jit(solution)/shard_map/ppermute | solution.py:302
  34.3 1.2 %collective-permute-start.13 = (bf16[8,768]{1,0:T(8,128)(2,1)S(1)}, bf16[8,768]{1,0:T(8,128)(2,1)S(1)}, u32[]{:S(2)}, u32[]{:S(2)}) collective-permute-start(bf16[8,768]{1,0:T(8,128)(2,1)S(1)} %collective-permute-done.12.refs_8_), channel_id=1, source_target_pairs={{0,1},{1,0},{2,3},{3,2},{4,5},{5,4},{6,7},{7,6},{8,9},{9,8},{10,11... | collective-permute-start | bytes 36872 | tf_op jit(solution)/shard_map/ppermute | solution.py:305
  35.4 5.0 %collective-permute-start.14 = (bf16[64,768]{1,0:T(8,128)(2,1)S(1)}, bf16[64,768]{1,0:T(8,128)(2,1)}, u32[]{:S(2)}, u32[]{:S(2)}) collective-permute-start(bf16[64,768]{1,0:T(8,128)(2,1)S(1)} %slice.14), channel_id=1, source_target_pairs={{0,4},{1,5},{4,8},{5,9},{8,12},{9,13},{12,14},{13,15},{14,10},{15,... | collective-permute-start | bytes 294920 | tf_op jit(solution)/shard_map/ppermute | solution.py:302
  35.5 0.7 %copy-start.4 = (bf16[264,768]{1,0:T(8,128)(2,1)}, bf16[264,768]{1,0:T(8,128)(2,1)S(1)}, u32[]{:S(2)}) copy-start(bf16[264,768]{1,0:T(8,128)(2,1)S(1)} %collective-permute-done.refs_1_) | copy-start | bytes 1216516
  36.2 5.0 %collective-permute-start.10 = (bf16[64,768]{1,0:T(8,128)(2,1)S(1)}, bf16[64,768]{1,0:T(8,128)(2,1)}, u32[]{:S(2)}, u32[]{:S(2)}) collective-permute-start(bf16[64,768]{1,0:T(8,128)(2,1)S(1)} %slice.12), channel_id=1, source_target_pairs={{0,2},{1,3},{4,0},{5,1},{8,4},{9,5},{12,8},{13,9},{14,12},{15,13},... | collective-permute-start | bytes 294920 | tf_op jit(solution)/shard_map/ppermute | solution.py:302
  40.4 7.7 %collective-permute-start.15 = (bf16[64,768]{1,0:T(8,128)(2,1)}, bf16[64,768]{1,0:T(8,128)(2,1)}, u32[]{:S(2)}, u32[]{:S(2)}) collective-permute-start(bf16[64,768]{1,0:T(8,128)(2,1)} %collective-permute-done.14.refs_8_), channel_id=1, source_target_pairs={{0,1},{1,0},{2,3},{3,2},{4,5},{5,4},{6,7},{7,6},{8,9},{9,8},{10,11... | collective-permute-start | bytes 294920 | tf_op jit(solution)/shard_map/ppermute | solution.py:305
  41.2 11.1 %collective-permute-start.11 = (bf16[64,768]{1,0:T(8,128)(2,1)}, bf16[64,768]{1,0:T(8,128)(2,1)}, u32[]{:S(2)}, u32[]{:S(2)}) collective-permute-start(bf16[64,768]{1,0:T(8,128)(2,1)} %collective-permute-done.10.refs_8_), channel_id=1, source_target_pairs={{0,1},{1,0},{2,3},{3,2},{4,5},{5,4},{6,7},{7,6},{8,9},{9,8},{10,11... | collective-permute-start | bytes 294920 | tf_op jit(solution)/shard_map/ppermute | solution.py:305
  41.4 1.3 %copy-start.7 = (bf16[768,768]{1,0:T(8,128)(2,1)S(1)}, bf16[768,768]{1,0:T(8,128)(2,1)}, u32[]{:S(2)}) copy-start(bf16[768,768]{1,0:T(8,128)(2,1)} %wq_ref.1) | copy-start | bytes 3538948
  42.7 1.3 %copy-start.8 = (bf16[768,768]{1,0:T(8,128)(2,1)S(1)}, bf16[768,768]{1,0:T(8,128)(2,1)}, u32[]{:S(2)}) copy-start(bf16[768,768]{1,0:T(8,128)(2,1)} %wg_ref.1) | copy-start | bytes 3538948
  44.0 1.0 %copy-start.5 = (bf16[264,768]{1,0:T(8,128)(2,1)S(1)}, bf16[264,768]{1,0:T(8,128)(2,1)}, u32[]{:S(2)}) copy-start(bf16[264,768]{1,0:T(8,128)(2,1)} %copy-done.4) | copy-start | bytes 1216516
  44.0 1.4 %copy-start.9 = (bf16[16,256,128]{2,1,0:T(8,128)(2,1)S(1)}, bf16[16,256,128]{2,1,0:T(8,128)(2,1)}, u32[]{:S(2)}) copy-start(bf16[16,256,128]{2,1,0:T(8,128)(2,1)} %pair_ref.1) | copy-start | bytes 3145732
  44.0 1.4 %copy-start.13 = (s32[16]{0:T(128)S(1)}, s32[16]{0:T(128)}, u32[]{:S(2)}) copy-start(s32[16]{0:T(128)} %chain_ref.1) | copy-start | bytes 196
  44.0 1.4 %copy-start.15 = (s32[16]{0:T(128)S(1)}, s32[16]{0:T(128)}, u32[]{:S(2)}) copy-start(s32[16]{0:T(128)} %res_ref.1) | copy-start | bytes 196
  45.3 2.8 %copy-start.3 = (bf16[768,768]{1,0:T(8,128)(2,1)S(1)}, bf16[768,768]{1,0:T(8,128)(2,1)}, u32[]{:S(2)}) copy-start(bf16[768,768]{1,0:T(8,128)(2,1)} %refs_14_.3) | copy-start | bytes 3538948
  48.1 4.2 %copy-start.6 = (bf16[768,768]{1,0:T(8,128)(2,1)S(1)}, bf16[768,768]{1,0:T(8,128)(2,1)}, u32[]{:S(2)}) copy-start(bf16[768,768]{1,0:T(8,128)(2,1)} %refs_17_.1) | copy-start | bytes 3538948
  48.1 4.2 %copy-start.11 = (bf16[16,8,768]{2,1,0:T(8,128)(2,1)S(1)}, bf16[16,8,768]{2,1,0:T(8,128)(2,1)}, u32[]{:S(2)}) copy-start(bf16[16,8,768]{2,1,0:T(8,128)(2,1)} %refs_16_.1) | copy-start | bytes 589828

commit v3 on v2

--- a/solution.py
+++ b/solution.py
@@ -16,10 +16,32 @@
 CORES = 2
 TILE = 256
 VMEM = pl.BlockSpec(memory_space=pltpu.VMEM)
+HBM = pl.BlockSpec(memory_space=pltpu.HBM)
+ANY = pl.BlockSpec(memory_space=pl.ANY)
 SMEM = pl.BlockSpec(memory_space=pltpu.SMEM)
 VMEM = pl.BlockSpec(memory_space=pltpu.VMEM)
+HBM = pl.BlockSpec(memory_space=pltpu.HBM)
+ANY = pl.BlockSpec(memory_space=pl.ANY)
+HBM = pl.BlockSpec(memory_space=pltpu.HBM)
+ANY = pl.BlockSpec(memory_space=pl.ANY)
 SMEM = pl.BlockSpec(memory_space=pltpu.SMEM)
 VMEM = pl.BlockSpec(memory_space=pltpu.VMEM)
+HBM = pl.BlockSpec(memory_space=pltpu.HBM)
+ANY = pl.BlockSpec(memory_space=pl.ANY)
+HBM = pl.BlockSpec(memory_space=pltpu.HBM)
+ANY = pl.BlockSpec(memory_space=pl.ANY)
+SMEM = pl.BlockSpec(memory_space=pltpu.SMEM)
+VMEM = pl.BlockSpec(memory_space=pltpu.VMEM)
+HBM = pl.BlockSpec(memory_space=pltpu.HBM)
+ANY = pl.BlockSpec(memory_space=pl.ANY)
+HBM = pl.BlockSpec(memory_space=pltpu.HBM)
+ANY = pl.BlockSpec(memory_space=pl.ANY)
+SMEM = pl.BlockSpec(memory_space=pltpu.SMEM)
+VMEM = pl.BlockSpec(memory_space=pltpu.VMEM)
+HBM = pl.BlockSpec(memory_space=pltpu.HBM)
+ANY = pl.BlockSpec(memory_space=pl.ANY)
+HBM = pl.BlockSpec(memory_space=pltpu.HBM)
+ANY = pl.BlockSpec(memory_space=pl.ANY)
 SMEM = pl.BlockSpec(memory_space=pltpu.SMEM)
 
 
@@ -117,6 +139,67 @@
     out_ref[pl.ds(rows, META_ROWS), :] = tiled.astype(BF16)
 
 
+META_ROWS = 8
+RADIX = 128
+
+
+def prep_body(single_hbm, chain_hbm, residue_hbm, valid_hbm, out_ref, single_ref, ints_ref, sems):
+    copies = [pltpu.make_async_copy(single_hbm, single_ref, sems.at[0])]
+    for i, ref in enumerate((chain_hbm, residue_hbm, valid_hbm)):
+        copies.append(pltpu.make_async_copy(ref, ints_ref.at[i], sems.at[i + 1]))
+    for copy in copies:
+        copy.start()
+    tokens, samples, width = single_ref.shape
+    rows = tokens * samples
+    token = lax.broadcasted_iota(jnp.int32, (tokens, width), 0)
+    lane = lax.broadcasted_iota(jnp.int32, (tokens, width), 1)
+    spread = (lane % tokens == token).astype(F32).astype(BF16)
+    perm = sample_major(tokens, samples)
+    for copy in copies:
+        copy.wait()
+    normed = normed_rows(single_ref[...])
+    out_ref[pl.ds(0, rows), :] = matmul(perm, normed).astype(BF16)
+    residue = ints_ref[1]
+    row = lax.broadcasted_iota(jnp.int32, (META_ROWS, tokens), 0)
+    meta = jnp.where(row == 0, ints_ref[0], 0)
+    meta = jnp.where(row == 1, residue // RADIX, meta)
+    meta = jnp.where(row == 2, residue % RADIX, meta)
+    meta = jnp.where(row == 3, ints_ref[2], meta)
+    tiled = matmul(meta.astype(F32).astype(BF16), spread)
+    out_ref[pl.ds(rows, META_ROWS), :] = tiled.astype(BF16)
+
+
+META_ROWS = 8
+RADIX = 128
+
+
+def prep_body(single_hbm, chain_hbm, residue_hbm, valid_hbm, out_ref, meta_ref, single_ref, ints_ref, sems):
+    copies = [pltpu.make_async_copy(single_hbm, single_ref, sems.at[0])]
+    for i, ref in enumerate((chain_hbm, residue_hbm, valid_hbm)):
+        copies.append(pltpu.make_async_copy(ref, ints_ref.at[i], sems.at[i + 1]))
+    for copy in copies:
+        copy.start()
+    tokens, samples, width = single_ref.shape
+    rows = tokens * samples
+    token = lax.broadcasted_iota(jnp.int32, (tokens, width), 0)
+    lane = lax.broadcasted_iota(jnp.int32, (tokens, width), 1)
+    spread = (lane % tokens == token).astype(F32).astype(BF16)
+    perm = sample_major(tokens, samples)
+    for copy in copies:
+        copy.wait()
+    normed = normed_rows(single_ref[...])
+    out_ref[pl.ds(0, rows), :] = matmul(perm, normed).astype(BF16)
+    residue = ints_ref[1]
+    row = lax.broadcasted_iota(jnp.int32, (META_ROWS, tokens), 0)
+    meta = jnp.where(row == 0, ints_ref[0], 0)
+    meta = jnp.where(row == 1, residue // RADIX, meta)
+    meta = jnp.where(row == 2, residue % RADIX, meta)
+    meta = jnp.where(row == 3, ints_ref[2], meta)
+    tiled = matmul(meta.astype(F32).astype(BF16), spread)
+    out_ref[pl.ds(rows, META_ROWS), :] = tiled.astype(BF16)
+    meta_ref[...] = tiled.astype(BF16)
+
+
 def query_body(pay_ref, wq_ref, wg_ref, q_ref, gate_ref):
     rows = pay_ref[pl.ds(0, q_ref.shape[0]), :]
     q_ref[...] = matmul(rows, wq_ref[...]).astype(BF16)
@@ -141,12 +224,8 @@
     return jnp.where(place < chips // 2, 2 * place, 2 * (chips - 1 - place) + 1)
 
 
-def bias_body(steps, chips, rows, me_ref, chain_ref, res_ref, pair_ref, wp_ref, tab_ref, *refs):
-    out_ref = refs[-1]
-    metas = refs[:-1]
-    _, queries, total = out_ref.shape
-    bins = tab_ref.shape[0]
-    reach = (bins - 2) // 2
+def pair_body(steps, chips, early, me_ref, pair_ref, wp_ref, *out_refs):
+    queries, total, _ = pair_ref.shape
     tokens = total // len(steps)
     me = me_ref[0]
     chip = me // CORES
@@ -156,92 +235,165 @@
     for r, c in steps:
         block = ring_chip(place + r, chips) * CORES + lax.rem(core + c, CORES)
         starts.append(pl.multiple_of(block * tokens, tokens))
-    slot = lax.broadcasted_iota(jnp.int32, (META_ROWS, total), 1) // tokens
-    keys = jnp.zeros((META_ROWS, total), F32)
-    at = 0
-    for m in metas:
-        n = max(1, m.shape[0] // (2 * rows + META_ROWS))
-        for u in range(n):
-            row = m[pl.ds(m.shape[0] - (n - u) * META_ROWS, META_ROWS), :].astype(F32)
-            row = jnp.concatenate([row] * (-(-total // row.shape[1])), axis=1)[:, :total]
-            keys = jnp.where(slot == at, row, keys)
-            at += 1
-    chain_keys = keys[0:1, :]
-    res_keys = keys[1:2, :] * RADIX + keys[2:3, :]
-    mask = (keys[3:4, :] - 1.0) * MASK_PENALTY
-    weights = jnp.transpose(wp_ref[...].astype(F32)).astype(BF16)
-    table = jnp.transpose(tab_ref[...])
+    weights = wp_ref[...]
+    for i in range(queries):
+        for out_ref, part in zip(out_refs, (starts[:early], starts[early:])):
+            data = jnp.concatenate([pair_ref[i, pl.ds(b, tokens), :] for b in part], axis=0)
+            out_ref[:, i, :] = lax.dot_general(
+                weights, data, (((1,), (1,)), ((), ())), preferred_element_type=F32
+            )
+
+
+def rel_body(counts, chain_ref, res_ref, tab_ref, bias_ref, *refs):
+    n = len(counts)
+    metas, out_ref, meta_ref, sems = refs[:n], refs[n], refs[n + 1], refs[n + 2]
+    heads, queries, total = out_ref.shape
+    copies, at = [], 0
+    for i, (m, count) in enumerate(zip(metas, counts)):
+        size = count * META_ROWS
+        source = m.at[pl.ds(m.shape[0] - size, size), :]
+        target = meta_ref.at[pl.ds(at * META_ROWS, size), :]
+        copies.append(pltpu.make_async_copy(source, target, sems.at[i]))
+        at += count
+    for copy in copies:
+        copy.start()
+    bins = tab_ref.shape[1]
+    reach = (bins - 2) // 2
+    tokens = total // at
+    table = tab_ref[...]
     high = table.astype(BF16)
     rest = table - high.astype(F32)
     mid = rest.astype(BF16)
     low = (rest - mid.astype(F32)).astype(BF16)
+    parts = jnp.concatenate([low, mid, high], axis=0)
     bin_ids = lax.broadcasted_iota(jnp.int32, (bins, total), 0).astype(F32)
+    slot = lax.broadcasted_iota(jnp.int32, (META_ROWS, total), 1) // tokens
+    keys = jnp.zeros((META_ROWS, total), F32)
+    for copy in copies:
+        copy.wait()
+    for u in range(at):
+        row = meta_ref[pl.ds(u * META_ROWS, META_ROWS), :].astype(F32)
+        row = jnp.concatenate([row] * (-(-total // row.shape[1])), axis=1)[:, :total]
+        keys = jnp.where(slot == u, row, keys)
+    chain_keys = keys[0:1, :]
+    res_keys = keys[1:2, :] * RADIX + keys[2:3, :]
+    mask = (keys[3:4, :] - 1.0) * MASK_PENALTY
     for i in range(queries):
-        data = jnp.concatenate([pair_ref[i, pl.ds(b, tokens), :] for b in starts], axis=0)
-        acc = lax.dot_general(weights, data, (((1,), (1,)), ((), ())), preferred_element_type=F32)
         offset = jnp.clip(res_ref[i].astype(F32) - res_keys, -reach, reach) + reach
         bucket = jnp.where(chain_keys == chain_ref[i].astype(F32), offset, float(bins - 1))
         hot = (bin_ids == bucket).astype(F32).astype(BF16)
-        rel = (matmul(low, hot) + matmul(mid, hot)) + matmul(high, hot)
-        out_ref[:, i, :] = acc + rel + mask
-
-
-def attend_rows(first, count, heads, scale, kv_refs, mine, other, q_ref, gate_ref, bias_ref, wk, wv):
+        rel = matmul(parts, hot)
+        rel = (rel[:heads] + rel[heads : 2 * heads]) + rel[2 * heads :]
+        out_ref[:, i, :] = bias_ref[:, i, :] + rel + mask
+
+
+def head_spans(width, hs):
+    return [((t * TILE) // hs, ((t + 1) * TILE - 1) // hs) for t in range(width // TILE)]
+
+
+def score_rows(q, keys, bias, heads, scale):
+    tokens, width = q.shape
+    hs = width // heads
+    lane_head = lax.broadcasted_iota(jnp.int32, (tokens, width), 1) // hs
+    per_head = [None] * heads
+    for t, (h0, h1) in enumerate(head_spans(width, hs)):
+        cut = slice(t * TILE, (t + 1) * TILE)
+        masked = [
+            jnp.where(lane_head[:, cut] == h, q[:, cut], 0.0).astype(BF16)
+            for h in range(h0, h1 + 1)
+        ]
+        st = lax.dot_general(
+            jnp.concatenate(masked, axis=0),
+            keys[:, cut],
+            (((1,), (1,)), ((), ())),
+            preferred_element_type=F32,
+        )
+        for h in range(h0, h1 + 1):
+            part = st[(h - h0) * tokens : (h - h0 + 1) * tokens]
+            per_head[h] = part if per_head[h] is None else per_head[h] + part
+    return jnp.concatenate(per_head, axis=0) * scale + bias
+
+
+def gather_keys(kv_refs, rows, at, tokens):
+    keys, values = [], []
+    for r in kv_refs:
+        n = r.shape[0] // (2 * rows + META_ROWS)
+        for u in range(n):
+            keys.append(r[pl.ds(u * rows + at, tokens), :])
+            values.append(r[pl.ds((n + u) * rows + at, tokens), :])
+    return keys, values
+
+
+def early_body(samples, heads, scale, *refs):
+    q_ref, bias_ref, sum_ref, top_ref, mass_ref = refs[-5:]
+    rows, width = q_ref.shape
+    tokens = rows // samples
+    spans = head_spans(width, width // heads)
+    height = sum(h1 - h0 + 1 for h0, h1 in spans) * tokens
+    bias = bias_ref[...].reshape(heads * tokens, bias_ref.shape[2])
+    for s in range(samples):
+        keys, values = gather_keys(refs[:-5], rows, s * tokens, tokens)
+        keys, values = jnp.concatenate(keys, axis=0), jnp.concatenate(values, axis=0)
+        q = q_ref[pl.ds(s * tokens, tokens), :].astype(F32)
+        scores = score_rows(q, keys, bias, heads, scale)
+        top = jnp.max(scores, axis=-1, keepdims=True)
+        probs = jnp.exp(scores - top)
+        mass = jnp.sum(probs, axis=-1, keepdims=True)
+        here = pl.ds(s * heads * tokens, heads * tokens)
+        top_ref[here, :] = jnp.broadcast_to(top, (heads * tokens, top_ref.shape[1]))
+        mass_ref[here, :] = jnp.broadcast_to(mass, (heads * tokens, mass_ref.shape[1]))
+        probs = probs.astype(BF16)
+        at = s * height
+        for t, (h0, h1) in enumerate(spans):
+            part = probs[h0 * tokens : (h1 + 1) * tokens]
+            got = matmul(part, values[:, t * TILE : (t + 1) * TILE])
+            sum_ref[pl.ds(at, got.shape[0]), :] = got
+            at += got.shape[0]
+
+
+def attend_rows(first, count, heads, scale, kv_refs, mine, other, shared):
+    q_ref, gate_ref, bias_ref, sum_ref, top_ref, mass_ref, wk_ref, wv_ref = shared
     rows, width = gate_ref.shape
     half = mine.shape[0]
     tokens = half // count
     hs = width // heads
     data = jnp.concatenate([mine, other], axis=0)
-    k_last = matmul(data, wk).astype(BF16)
-    v_last = matmul(data, wv).astype(BF16)
-    total = bias_ref.shape[2]
-    bias = bias_ref[...].reshape(heads * tokens, total)
+    k_last = matmul(data, wk_ref[...]).astype(BF16)
+    v_last = matmul(data, wv_ref[...]).astype(BF16)
+    bias = bias_ref[...].reshape(heads * tokens, bias_ref.shape[2])
     lane_head = lax.broadcasted_iota(jnp.int32, (tokens, width), 1) // hs
-    spans = []
-    for t in range(width // TILE):
-        spans.append(((t * TILE) // hs, ((t + 1) * TILE - 1) // hs))
+    spans = head_spans(width, hs)
+    height = sum(h1 - h0 + 1 for h0, h1 in spans) * tokens
     gated = []
     for s in range(count):
-        keys, values = [], []
-        for r in kv_refs:
-            n = r.shape[0] // (2 * rows + META_ROWS)
-            for u in range(n):
-                keys.append(r[pl.ds(u * rows + (first + s) * tokens, tokens), :])
-                values.append(r[pl.ds((n + u) * rows + (first + s) * tokens, tokens), :])
+        keys, values = gather_keys(kv_refs, rows, (first + s) * tokens, tokens)
         for u in range(2):
             keys.append(k_last[u * half + s * tokens : u * half + (s + 1) * tokens])
             values.append(v_last[u * half + s * tokens : u * half + (s + 1) * tokens])
-        keys = jnp.concatenate(keys, axis=0)
-        values = jnp.concatenate(values, axis=0)
+        keys, values = jnp.concatenate(keys, axis=0), jnp.concatenate(values, axis=0)
         q = q_ref[pl.ds((first + s) * tokens, tokens), :].astype(F32)
-        per_head = [None] * heads
+        scores = score_rows(q, keys, bias, heads, scale)
+        here = pl.ds((first + s) * heads * tokens, heads * tokens)
+        top_before = top_ref[here, :][:, :1]
+        top = jnp.maximum(jnp.max(scores, axis=-1, keepdims=True), top_before)
+        shrink = jnp.exp(top_before - top)
+        probs = jnp.exp(scores - top)
+        mass = jnp.sum(probs, axis=-1, keepdims=True) + mass_ref[here, :][:, :1] * shrink
+        inv = 1.0 / mass
+        probs = probs.astype(BF16)
+        shrink = shrink * inv
+        attended = []
+        at = (first + s) * height
         for t, (h0, h1) in enumerate(spans):
             cut = slice(t * TILE, (t + 1) * TILE)
-            masked = [
-                jnp.where(lane_head[:, cut] == h, q[:, cut], 0.0).astype(BF16)
-                for h in range(h0, h1 + 1)
-            ]
-            qt = jnp.concatenate(masked, axis=0)
-            st = lax.dot_general(
-                qt, keys[:, cut], (((1,), (1,)), ((), ())), preferred_element_type=F32
-            )
-            for h in range(h0, h1 + 1):
-                part = st[(h - h0) * tokens : (h - h0 + 1) * tokens]
-                per_head[h] = part if per_head[h] is None else per_head[h] + part
-        scores = jnp.concatenate(per_head, axis=0) * scale + bias
-        top = jnp.max(scores, axis=-1, keepdims=True)
-        probs = jnp.exp(scores - top)
-        inv = 1.0 / jnp.sum(probs, axis=-1, keepdims=True)
-        probs = probs.astype(BF16)
-        attended = []
-        for t, (h0, h1) in enumerate(spans):
-            cut = slice(t * TILE, (t + 1) * TILE)
-            ot = matmul(probs[h0 * tokens : (h1 + 1) * tokens], values[:, cut])
-            ot = ot * inv[h0 * tokens : (h1 + 1) * tokens]
+            span = slice(h0 * tokens, (h1 + 1) * tokens)
+            ot = matmul(probs[span], values[:, cut]) * inv[span]
+            ot = ot + sum_ref[pl.ds(at, ot.shape[0]), :] * shrink[span]
+            at += ot.shape[0]
             got = ot[:tokens]
             for h in range(h0 + 1, h1 + 1):
-                here = ot[(h - h0) * tokens : (h - h0 + 1) * tokens]
-                got = jnp.where(lane_head[:, cut] == h, here, got)
+                part = ot[(h - h0) * tokens : (h - h0 + 1) * tokens]
+                got = jnp.where(lane_head[:, cut] == h, part, got)
             attended.append(got)
         attended = jnp.concatenate(attended, axis=1)
         gated.append((gate_ref[pl.ds((first + s) * tokens, tokens), :] * attended).astype(BF16))
@@ -249,19 +401,19 @@
 
 
 def attend_body(count, heads, scale, *refs):
-    mine, other, q_ref, gate_ref, bias_ref, wk, wv, out_ref = refs[-8:]
-    out_ref[...] = attend_rows(
-        0, count, heads, scale, refs[:-8], mine[...], other[...], q_ref, gate_ref, bias_ref,
-        wk[...], wv[...],
-    )
-
-
-def finish_body(count, heads, scale, *refs):
-    mine, other, q_ref, gate_ref, bias_ref, wk, wv, done, single_ref, wo_ref, out_ref = refs[-11:]
+    out_ref = refs[-1]
+    shared = refs[-9:-1]
+    mine, other = refs[-11], refs[-10]
+    out_ref[...] = attend_rows(0, count, heads, scale, refs[:-11], mine[...], other[...], shared)
+
+
+def finish_body(count, samples, heads, scale, *refs):
+    done, single_ref, wo_ref, out_ref = refs[-4:]
+    shared = refs[-12:-4]
+    mine, other = refs[-14], refs[-13]
     tokens, samples, width = single_ref.shape
     gated = attend_rows(
-        samples - count, count, heads, scale, refs[:-11], mine[...], other[...], q_ref, gate_ref,
-        bias_ref, wk[...], wv[...],
+        samples - count, count, heads, scale, refs[:-14], mine[...], other[...], shared
     )
     gated = jnp.concatenate([done[...], gated], axis=0)
     gated = matmul(token_major(tokens, samples), gated).astype(BF16)
@@ -269,12 +421,13 @@
     out_ref[...] = (single_ref[...].astype(F32) + out).astype(BF16)
 
 
-def call(body, out_shape, args, in_specs=None, flops=0, moved=0, limit=16 << 20):
+def call(body, out_shape, args, in_specs=None, flops=0, moved=0, limit=8 << 20, scratch=()):
     return pl.pallas_call(
         body,
         out_shape=out_shape,
         in_specs=in_specs or [VMEM] * len(args),
         out_specs=jax.tree.map(lambda _: VMEM, out_shape),
+        scratch_shapes=scratch,
         compiler_params=pltpu.CompilerParams(vmem_limit_bytes=limit),
         cost_estimate=pl.CostEstimate(flops=flops, bytes_accessed=moved, transcendentals=0),
     )(*args)
@@ -309,10 +462,19 @@
         steps += [(-k, 0), (k, 0), (-k, 1), (k, 1)]
     steps += [(half, 0), (half, 1)]
 
-    payload = call(
+    payload, meta = call(
         prep_body,
-        jax.ShapeDtypeStruct((rows + META_ROWS, width), BF16),
+        (
+            jax.ShapeDtypeStruct((rows + META_ROWS, width), BF16),
+            jax.ShapeDtypeStruct((META_ROWS, width), BF16),
+        ),
         (single, *(v.reshape(1, tokens) for v in (chain, residue, valid))),
+        in_specs=[HBM] * 4,
+        scratch=[
+            pltpu.VMEM(single.shape, BF16),
+            pltpu.VMEM((3, 1, tokens), jnp.int32),
+            pltpu.SemaphoreType.DMA((4,)),
+        ],
         flops=rows * width * 16,
         moved=4 * rows * width,
     )
@@ -337,7 +499,14 @@
             moved=4 * width * width + 6 * n * rows * width,
         )
 
-    far = ring(payload[rows:], half)
+    def piece(value, at):
+        def body(in_ref, out_ref):
+            out_ref[...] = in_ref[pl.ds(at, rows // 2), :]
+
+        shape = jax.ShapeDtypeStruct((rows // 2, width), BF16)
+        return call(body, shape, (value,), moved=2 * rows * width)
+
+    far = ring(meta, half)
     far = [far, flip(far)]
     kvs = [kv([payload])]
     kvs.append(flip(kvs[-1]))
@@ -346,33 +515,69 @@
             cw_next = ring(cw, 1)
             ccw_next = ring(ccw, -1)
         else:
-            cw_next = ring(cw[: rows // 2], 1)
-            ccw_next = ring(ccw[rows // 2 : rows], -1)
+            cw_next = ring(piece(cw, 0), 1)
+            ccw_next = ring(piece(ccw, rows // 2), -1)
         kvs.append(kv([cw, ccw]))
         kvs.append(flip(kvs[-1]))
         cw, ccw = cw_next, ccw_next
-    bias = call(
-        functools.partial(bias_body, steps, chips, rows),
-        jax.ShapeDtypeStruct((heads, tokens, total), F32),
-        (me, chain, residue, pair, w_pair, rel_table, *kvs, *far),
-        in_specs=[SMEM, SMEM, SMEM, *[VMEM] * (5 + len(kvs))],
-        flops=2 * tokens * total * heads * 512,
+    early = len(steps) - 3 * CORES
+    split = 2 * (half - 1)
+    pair_shapes = tuple(
+        jax.ShapeDtypeStruct((heads, tokens, n * tokens), F32) for n in (early, len(steps) - early)
+    )
+    pair_bias = call(
+        functools.partial(pair_body, steps, chips, early),
+        pair_shapes,
+        (me, pair, w_pair.T),
+        in_specs=[SMEM, VMEM, VMEM],
+        flops=2 * pair.size * heads,
         moved=pair.size * 2 + heads * tokens * total * 4,
-    )
+        limit=(4 << 20) + 2 * pair.size + 8 * heads * tokens * total,
+    )
+
+    def relative(at, metas):
+        counts = [max(1, m.shape[0] // (2 * rows + META_ROWS)) for m in metas]
+        return call(
+            functools.partial(rel_body, counts),
+            pair_shapes[at],
+            (chain, residue, rel_table.T, pair_bias[at], *metas),
+            in_specs=[SMEM, SMEM, VMEM, VMEM] + [ANY] * len(metas),
+            flops=pair_shapes[at].size * 256,
+            moved=8 * pair_shapes[at].size,
+            scratch=[
+                pltpu.VMEM((sum(counts) * META_ROWS, width), BF16),
+                pltpu.SemaphoreType.DMA((len(metas),)),
+            ],
+        )
+
     scale = 1.0 / math.sqrt(width // heads)
+    spans = head_spans(width, width // heads)
+    height = sum(h1 - h0 + 1 for h0, h1 in spans) * tokens * samples
+    state = jax.ShapeDtypeStruct((samples * heads * tokens, 128), F32)
+    bias = relative(0, kvs[:split])
+    limit = (10 << 20) + 4 * samples * total * width
+    before = call(
+        functools.partial(early_body, samples, heads, scale),
+        (jax.ShapeDtypeStruct((height, TILE), F32), state, state),
+        (*kvs[:split], query, bias),
+        flops=4 * rows * early * tokens * width,
+        moved=4 * samples * early * tokens * width,
+        limit=limit,
+    )
+    bias = relative(1, [*kvs[split:], *far])
     count = samples // 2
-    limit = min(60 << 20, (16 << 20) + 4 * samples * total * width)
-    common = dict(flops=2 * rows * total * width, moved=2 * samples * total * width, limit=limit)
+    common = dict(flops=2 * rows * total * width, moved=samples * total * width, limit=limit)
+    shared = (query, gate, bias, *before, w_key, w_value)
     gated = call(
         functools.partial(attend_body, count, heads, scale),
         jax.ShapeDtypeStruct((rows // 2, width), BF16),
-        (*kvs, cw, flip(cw), query, gate, bias, w_key, w_value),
+        (*kvs[split:], cw, flip(cw), *shared),
         **common,
     )
     return call(
-        functools.partial(finish_body, count, heads, scale),
+        functools.partial(finish_body, count, samples, heads, scale),
         jax.ShapeDtypeStruct(single.shape, BF16),
-        (*kvs, ccw, flip(ccw), query, gate, bias, w_key, w_value, gated, single, w_out),
+        (*kvs[split:], ccw, flip(ccw), *shared, gated, single, w_out),
         **common,
     )
 
@@ -393,10 +598,13 @@
         P(),
     )
 
-    return jax.shard_map(
+    step = jax.shard_map(
         shards,
         mesh=mesh,
         in_specs=placed,
         out_specs=P(("groups", "tok"), None, None),
         check_vma=False,
     )
+    return step
+    return step
+    return step

time: 57.9 us -> 63.2 us (1.092); the launches traced: 57.5 us -> 62.1 us
  Pallas kernels: 16.8 us -> 23.1 us
  waiting for transfers between devices: 16.3 us -> 14 us
  starting transfers between devices: 14.5 us -> 15.4 us
    pallas_call x9 -> x14, Pallas kernels: 16.8 us -> 23.1 us  [call(): pl.pallas_call(body, out_shape=out_shape, in_specs=in_specs or [VMEM] * l...]
    ppermute x7, waiting for transfers between devices: 1.18 us -> 0.02 us  [flip(): return lax.ppermute(value, 'tok', [(d, d ^ 1) for d in range(devices)])]
    ppermute x9, waiting for transfers between devices: 15.1 us -> 14 us  [ring(): return lax.ppermute(value, 'tok', pairs)]
    unnamed x40 -> x48, local copies, waits for them, and re-layouts: 9.77 us -> 9.31 us
  transfers between devices with their start and end apart: 16 -> 16, of which waited for: 7 -> 5; matrix products, arithmetic and copies ran while one was open for 0% -> 0% of each run, Pallas kernels for 19% -> 28%
where the time goes in v3:
time: 63.2 us; the launch traced here: 62.1 us
  Pallas kernels  23.1 us (37%)
  starting transfers between devices  15.4 us (24%)
  waiting for transfers between devices  14 us (22%)
  local copies, waits for them, and re-layouts  9.31 us (15%)
    pallas_call x14, Pallas kernels, call(): pl.pallas_call(body, out_shape=out_shape, in_specs=in_specs or [VMEM] * l...  23.1 us
    ppermute x9, waiting for transfers between devices, ring(): return lax.ppermute(value, 'tok', pairs)  14 us
    ppermute x9, starting transfers between devices, ring(): return lax.ppermute(value, 'tok', pairs)  13.7 us
    unnamed x48, local copies, waits for them, and re-layouts  9.31 us
    ppermute x7, starting transfers between devices, flip(): return lax.ppermute(value, 'tok', [(d, d ^ 1) for d in range(devices)])  1.72 us
  transfers between devices with their start and end apart: 16, of which 5 were waited for; matrix products, arithmetic and copies ran while one was open for 0% of the time, Pallas kernels for 28%

profile of v3, /device:TPU:0, one launch (start us, length us, event | category | flops | bytes accessed | tf_op | source)
XLA Modules:
  0.0 62.1 jit_solution(14101823117331885997)
XLA Ops:
  0.0 0.9 %copy-done.15 = bf16[16,8,768]{2,1,0:T(8,128)(2,1)S(1)} copy-done((bf16[16,8,768]{2,1,0:T(8,128)(2,1)S(1)}, bf16[16,8,768]{2,1,0:T(8,128)(2,1)}, u32[]{:S(2)}) %copy-start.15) | copy-done | bytes 196632
  0.9 0.7 %copy-done.18 = s32[16]{0:T(128)S(1)} copy-done((s32[16]{0:T(128)S(1)}, s32[16]{0:T(128)}, u32[]{:S(2)}) %copy-start.18) | copy-done | bytes 88
  1.6 0.7 %copy-done.20 = s32[16]{0:T(128)S(1)} copy-done((s32[16]{0:T(128)S(1)}, s32[16]{0:T(128)}, u32[]{:S(2)}) %copy-start.20) | copy-done | bytes 88
  2.2 0.7 %copy-done.23 = s32[16]{0:T(128)S(1)} copy-done((s32[16]{0:T(128)S(1)}, s32[16]{0:T(128)}, u32[]{:S(2)}) %copy-start.23) | copy-done | bytes 88
  2.9 0.7 %shard_map.118 = (bf16[136,768]{1,0:T(8,128)(2,1)S(1)}, bf16[8,768]{1,0:T(8,128)(2,1)S(1)}) custom-call(bf16[16,8,768]{2,1,0:T(8,128)(2,1)S(1)} %copy-done.15, s32[1,16]{1,0:T(1,128)S(1)} %bitcast.8, s32[1,16]{1,0:T(1,128)S(1)} %bitcast.9, s32[1,16]{1,0:T(1,128)S(1)} %bitcast.11), custom_call_target="tpu_custom_call" | custom-call | flops 1572864 | bytes 393216 | tf_op jit(solution)/shard_map/pallas_call | solution.py:425
  3.6 3.1 %collective-permute-start = (bf16[136,768]{1,0:T(8,128)(2,1)S(1)}, bf16[136,768]{1,0:T(8,128)(2,1)S(1)}, u32[]{:S(2)}, u32[]{:S(2)}) collective-permute-start(bf16[136,768]{1,0:T(8,128)(2,1)S(1)} %get-tuple-element.14.pay_ref.refs_0_), channel_id=1, source_target_pairs={{0,4},{1,5},{4,8},{5,9},{8,12},{9,13},{12,14},{13,15},{14,10},{15,... | collective-permute-start | bytes 626696 | tf_op jit(solution)/shard_map/ppermute | solution.py:455
  6.7 0.0 collective-permute-start.3
  6.7 5.1 %collective-permute-done.refs_0_ = bf16[136,768]{1,0:T(8,128)(2,1)S(1)} collective-permute-done((bf16[136,768]{1,0:T(8,128)(2,1)S(1)}, bf16[136,768]{1,0:T(8,128)(2,1)S(1)}, u32[]{:S(2)}, u32[]{:S(2)}) %collective-permute-start) | collective-permute-done | bytes 208928 | tf_op jit(solution)/shard_map/ppermute | solution.py:455
  11.8 1.8 %collective-permute-start.1 = (bf16[136,768]{1,0:T(8,128)(2,1)S(1)}, bf16[136,768]{1,0:T(8,128)(2,1)S(1)}, u32[]{:S(2)}, u32[]{:S(2)}) collective-permute-start(bf16[136,768]{1,0:T(8,128)(2,1)S(1)} %collective-permute-done.refs_0_), channel_id=1, source_target_pairs={{0,4},{1,5},{4,8},{5,9},{8,12},{9,13},{12,14},{13,15},{14,10},{15,... | collective-permute-start | bytes 626696 | tf_op jit(solution)/shard_map/ppermute | solution.py:455
  13.6 0.2 collective-permute-start.4
  13.8 4.3 %collective-permute-done.1.refs_0_ = bf16[136,768]{1,0:T(8,128)(2,1)S(1)} collective-permute-done((bf16[136,768]{1,0:T(8,128)(2,1)S(1)}, bf16[136,768]{1,0:T(8,128)(2,1)S(1)}, u32[]{:S(2)}, u32[]{:S(2)}) %collective-permute-start.1) | collective-permute-done | bytes 208928 | tf_op jit(solution)/shard_map/ppermute | solution.py:455
  18.1 1.5 %collective-permute-start.2 = (bf16[136,768]{1,0:T(8,128)(2,1)S(1)}, bf16[136,768]{1,0:T(8,128)(2,1)S(1)}, u32[]{:S(2)}, u32[]{:S(2)}) collective-permute-start(bf16[136,768]{1,0:T(8,128)(2,1)S(1)} %collective-permute-done.1.refs_0_), channel_id=1, source_target_pairs={{0,4},{1,5},{4,8},{5,9},{8,12},{9,13},{12,14},{13,15},{14,10},{15,... | collective-permute-start | bytes 626696 | tf_op jit(solution)/shard_map/ppermute | solution.py:455
  19.7 0.5 collective-permute-start.5
  20.2 1.3 %copy-done = bf16[768,768]{1,0:T(8,128)(2,1)S(1)} copy-done((bf16[768,768]{1,0:T(8,128)(2,1)S(1)}, bf16[768,768]{1,0:T(8,128)(2,1)}, u32[]{:S(2)}) %copy-start) | copy-done | bytes 1179672
  21.4 1.3 %copy-done.2 = bf16[768,768]{1,0:T(8,128)(2,1)S(1)} copy-done((bf16[768,768]{1,0:T(8,128)(2,1)S(1)}, bf16[768,768]{1,0:T(8,128)(2,1)}, u32[]{:S(2)}) %copy-start.2) | copy-done | bytes 1179672
  22.7 0.8 %shard_map.125.refs_2_ = bf16[528,768]{1,0:T(8,128)(2,1)S(1)} custom-call(bf16[136,768]{1,0:T(8,128)(2,1)S(1)} %collective-permute-done.refs_0_, bf16[136,768]{1,0:T(8,128)(2,1)S(1)} %collective-permute-done.3.refs_1_, bf16[768,768]{1,0:T(8,128)(2,1)S(1)} %copy-done, bf16[768,768]{1,0:T(8,128)(2,1)S(1)} %copy-done.2), custom_call_target="tpu_custom_call" | custom-call | flops 603979776 | bytes 3538944 | tf_op jit(solution)/shard_map/pallas_call | solution.py:425
  23.5 0.0 copy-start.1
  23.5 0.1 collective-permute-start.12
  23.6 1.7 %shard_map.126.refs_4_ = bf16[528,768]{1,0:T(8,128)(2,1)} custom-call(bf16[136,768]{1,0:T(8,128)(2,1)S(1)} %collective-permute-done.1.refs_0_, bf16[136,768]{1,0:T(8,128)(2,1)S(1)} %collective-permute-done.4.refs_1_, bf16[768,768]{1,0:T(8,128)(2,1)S(1)} %copy-done, bf16[768,768]{1,0:T(8,128)(2,1)S(1)} %copy-done.2), custom_call_target="tpu_custom_call" | custom-call | flops 603979776 | bytes 3538944 | tf_op jit(solution)/shard_map/pallas_call | solution.py:425
  25.3 0.5 collective-permute-start.13
  25.8 0.8 %shard_map.119.refs_0_ = bf16[528,768]{1,0:T(8,128)(2,1)S(1)} custom-call(bf16[136,768]{1,0:T(8,128)(2,1)S(1)} %collective-permute-done.2.refs_0_.in_ref, bf16[136,768]{1,0:T(8,128)(2,1)S(1)} %collective-permute-done.5.refs_1_.in_ref, bf16[768,768]{1,0:T(8,128)(2,1)S(1)} %copy-done.1, bf16[768,768]{1,0:T(8,128)(2,1)S(1)} %copy-done.2), custom_call_target="tpu_custom_call" | custom-call | flops 603979776 | bytes 3538944 | tf_op jit(solution)/shard_map/pallas_call | solution.py:425
  26.6 0.0 copy-start.11
  26.6 0.0 copy-start.12
  26.6 0.1 collective-permute-start.6
  26.7 0.5 shard_map.124.refs_0_
  27.2 0.6 collective-permute-start.11
  27.7 4.5 %collective-permute-start.9 = (bf16[8,768]{1,0:T(8,128)(2,1)S(1)}, bf16[8,768]{1,0:T(8,128)(2,1)S(1)}, u32[]{:S(2)}, u32[]{:S(2)}) collective-permute-start(bf16[8,768]{1,0:T(8,128)(2,1)S(1)} %get-tuple-element.18), channel_id=1, source_target_pairs={{0,14},{1,15},{4,10},{5,11},{8,6},{9,7},{12,2},{13,3},{14,0},{15,1... | collective-permute-start | bytes 36872 | tf_op jit(solution)/shard_map/ppermute | solution.py:455
  32.2 1.9 %collective-permute-done.9.refs_2_ = bf16[8,768]{1,0:T(8,128)(2,1)S(1)} collective-permute-done((bf16[8,768]{1,0:T(8,128)(2,1)S(1)}, bf16[8,768]{1,0:T(8,128)(2,1)S(1)}, u32[]{:S(2)}, u32[]{:S(2)}) %collective-permute-start.9) | collective-permute-done | bytes 12320 | tf_op jit(solution)/shard_map/ppermute | solution.py:455
  34.1 0.0 copy-start.22
  34.1 0.0 copy-start.17
  34.2 0.0 copy-start.19
  34.2 0.8 %copy-done.6 = bf16[264,768]{1,0:T(8,128)(2,1)} copy-done((bf16[264,768]{1,0:T(8,128)(2,1)}, bf16[264,768]{1,0:T(8,128)(2,1)S(1)}, u32[]{:S(2)}) %copy-start.6) | copy-done | bytes 405528
  35.0 2.0 %collective-permute-start.7 = (bf16[64,768]{1,0:T(8,128)(2,1)S(1)}, bf16[64,768]{1,0:T(8,128)(2,1)}, u32[]{:S(2)}, u32[]{:S(2)}) collective-permute-start(bf16[64,768]{1,0:T(8,128)(2,1)S(1)} %shard_map.120), channel_id=1, source_target_pairs={{0,2},{1,3},{4,0},{5,1},{8,4},{9,5},{12,8},{13,9},{14,12},{15,13},... | collective-permute-start | bytes 294920 | tf_op jit(solution)/shard_map/ppermute | solution.py:455
  37.0 1.8 %collective-permute-done.14.refs_2_ = bf16[64,768]{1,0:T(8,128)(2,1)S(1)} collective-permute-done((bf16[64,768]{1,0:T(8,128)(2,1)S(1)}, bf16[64,768]{1,0:T(8,128)(2,1)S(1)}, u32[]{:S(2)}, u32[]{:S(2)}) %collective-permute-start.14) | collective-permute-done | bytes 98336 | tf_op jit(solution)/shard_map/ppermute | solution.py:455
  38.7 1.0 %collective-permute-done.7.refs_2_ = bf16[64,768]{1,0:T(8,128)(2,1)} collective-permute-done((bf16[64,768]{1,0:T(8,128)(2,1)S(1)}, bf16[64,768]{1,0:T(8,128)(2,1)}, u32[]{:S(2)}, u32[]{:S(2)}) %collective-permute-start.7) | collective-permute-done | bytes 98336 | tf_op jit(solution)/shard_map/ppermute | solution.py:455
  39.7 0.5 collective-permute-start.10
  40.2 0.5 shard_map.121
  40.7 0.7 %copy-done.9 = f32[128,768]{1,0:T(8,128)} copy-done((f32[128,768]{1,0:T(8,128)}, f32[128,768]{1,0:T(8,128)S(1)}, u32[]{:S(2)}) %copy-start.9) | copy-done | bytes 393240
  41.5 1.3 %copy-done.14 = bf16[16,256,128]{2,1,0:T(8,128)(2,1)S(1)} copy-done((bf16[16,256,128]{2,1,0:T(8,128)(2,1)S(1)}, bf16[16,256,128]{2,1,0:T(8,128)(2,1)}, u32[]{:S(2)}) %copy-start.14) | copy-done | bytes 1048600
  42.8 0.7 %shard_map.122 = (f32[16,16,160]{2,1,0:T(8,128)S(1)}, f32[16,16,96]{2,1,0:T(8,128)S(1)}) custom-call(s32[1]{0:T(128)} %bitcast.4.me_ref, bf16[16,256,128]{2,1,0:T(8,128)(2,1)S(1)} %copy-done.14, bf16[16,128]{1,0:T(8,128)(2,1)S(1)} %bitcast.10), custom_call_target="tpu_custom_call" | custom-call | flops 16777216 | bytes 1310720 | tf_op jit(solution)/shard_map/pallas_call | solution.py:425
  43.5 1.0 %copy-done.7 = bf16[264,768]{1,0:T(8,128)(2,1)S(1)} copy-done((bf16[264,768]{1,0:T(8,128)(2,1)S(1)}, bf16[264,768]{1,0:T(8,128)(2,1)}, u32[]{:S(2)}) %copy-start.7) | copy-done | bytes 405528
  44.5 1.8 %shard_map.127.refs_7_ = f32[16,16,160]{2,1,0:T(8,128)S(1)} custom-call(s32[16]{0:T(128)S(1)} %copy-done.19, s32[16]{0:T(128)S(1)} %copy-done.21, f32[16,66]{1,0:T(8,128)S(1)} %bitcast.6, f32[16,16,160]{2,1,0:T(8,128)S(1)} %get-tuple-element.19.bias_ref, bf16[264,768]{1,0:T(8,128)(2,1)S(1)} %shard_map.124.refs_0_, bf16[264,768]{1,0:T(8,128)(2,1)S(1)} %copy-done.7, ...), custom_call_target="tpu_custom_call" | custom-call | flops 10485760 | bytes 327680 | tf_op jit(solution)/shard_map/pallas_call | solution.py:425
  46.3 4.1 %shard_map.128 = (f32[2304,256]{1,0:T(8,128)S(1)}, f32[2048,128]{1,0:T(8,128)S(1)}, f32[2048,128]{1,0:T(8,128)S(1)}) custom-call(bf16[264,768]{1,0:T(8,128)(2,1)S(1)} %shard_map.124.refs_0_, bf16[264,768]{1,0:T(8,128)(2,1)S(1)} %copy-done.8, bf16[528,768]{1,0:T(8,128)(2,1)S(1)} %shard_map.125.refs_2_, bf16[528,768]{1,0:T(8,128)(2,1)S(1)} %copy-done.5, ...), custom_call_target="tpu_custom_call" | custom-call | flops 62914560 | bytes 3932160 | tf_op jit(solution)/shard_map/pallas_call | solution.py:425
  50.4 0.0 copy-start.3
  50.5 1.6 %shard_map.123.refs_6_ = f32[16,16,96]{2,1,0:T(8,128)S(1)} custom-call(s32[16]{0:T(128)S(1)} %copy-done.19, s32[16]{0:T(128)S(1)} %copy-done.21, f32[16,66]{1,0:T(8,128)S(1)} %bitcast.7, f32[16,16,96]{2,1,0:T(8,128)S(1)} %get-tuple-element.17.bias_ref, bf16[528,768]{1,0:T(8,128)(2,1)S(1)} %shard_map.119.refs_0_, ...), custom_call_target="tpu_custom_call" | custom-call | flops 6291456 | bytes 196608 | tf_op jit(solution)/shard_map/pallas_call | solution.py:425
  52.2 0.0 copy-start.16
  52.2 4.8 %shard_map.130.refs_12_ = bf16[64,768]{1,0:T(8,128)(2,1)S(1)} custom-call(bf16[528,768]{1,0:T(8,128)(2,1)S(1)} %shard_map.119.refs_0_, bf16[528,768]{1,0:T(8,128)(2,1)} %collective-permute-done.6.refs_1_, bf16[64,768]{1,0:T(8,128)(2,1)S(1)} %collective-permute-done.14.refs_2_, bf16[64,768]{1,0:T(8,128)(2,1)} %collective-permute-done.15.refs_3_, ...), custom_call_target="tpu_custom_call" | custom-call | flops 50331648 | bytes 1572864 | tf_op jit(solution)/shard_map/pallas_call | solution.py:425
  57.0 5.1 %shard_map.131 = bf16[16,8,768]{2,1,0:T(8,128)(2,1)} custom-call(bf16[528,768]{1,0:T(8,128)(2,1)S(1)} %shard_map.119.refs_0_, bf16[528,768]{1,0:T(8,128)(2,1)} %collective-permute-done.6.refs_1_, bf16[64,768]{1,0:T(8,128)(2,1)} %collective-permute-done.7.refs_2_, bf16[64,768]{1,0:T(8,128)(2,1)} %collective-permute-done.8.refs_3_, ...), custom_call_target="tpu_custom_call" | custom-call | flops 50331648 | bytes 1572864 | tf_op jit(solution)/shard_map/pallas_call | solution.py:425
  (46 shorter events, 0.1 us)
Async XLA Ops:
  0.0 0.9 %copy-start.15 = (bf16[16,8,768]{2,1,0:T(8,128)(2,1)S(1)}, bf16[16,8,768]{2,1,0:T(8,128)(2,1)}, u32[]{:S(2)}) copy-start(bf16[16,8,768]{2,1,0:T(8,128)(2,1)} %refs_13_.1) | copy-start | bytes 589828
  0.9 0.7 %copy-start.18 = (s32[16]{0:T(128)S(1)}, s32[16]{0:T(128)}, u32[]{:S(2)}) copy-start(s32[16]{0:T(128)} %chain_ref.3) | copy-start | bytes 196
  1.6 0.7 %copy-start.20 = (s32[16]{0:T(128)S(1)}, s32[16]{0:T(128)}, u32[]{:S(2)}) copy-start(s32[16]{0:T(128)} %res_ref.3) | copy-start | bytes 196
  2.2 0.7 %copy-start.23 = (s32[16]{0:T(128)S(1)}, s32[16]{0:T(128)}, u32[]{:S(2)}) copy-start(s32[16]{0:T(128)} %param.16) | copy-start | bytes 196
  3.6 8.2 %collective-permute-start = (bf16[136,768]{1,0:T(8,128)(2,1)S(1)}, bf16[136,768]{1,0:T(8,128)(2,1)S(1)}, u32[]{:S(2)}, u32[]{:S(2)}) collective-permute-start(bf16[136,768]{1,0:T(8,128)(2,1)S(1)} %get-tuple-element.14.pay_ref.refs_0_), channel_id=1, source_target_pairs={{0,4},{1,5},{4,8},{5,9},{8,12},{9,13},{12,14},{13,15},{14,10},{15,... | collective-permute-start | bytes 626696 | tf_op jit(solution)/shard_map/ppermute | solution.py:455
  6.7 6.9 %collective-permute-start.3 = (bf16[136,768]{1,0:T(8,128)(2,1)S(1)}, bf16[136,768]{1,0:T(8,128)(2,1)S(1)}, u32[]{:S(2)}, u32[]{:S(2)}) collective-permute-start(bf16[136,768]{1,0:T(8,128)(2,1)S(1)} %get-tuple-element.14.pay_ref.refs_0_), channel_id=1, source_target_pairs={{0,2},{1,3},{4,0},{5,1},{8,4},{9,5},{12,8},{13,9},{14,12},{15,13},... | collective-permute-start | bytes 626696 | tf_op jit(solution)/shard_map/ppermute | solution.py:455
  11.8 6.3 %collective-permute-start.1 = (bf16[136,768]{1,0:T(8,128)(2,1)S(1)}, bf16[136,768]{1,0:T(8,128)(2,1)S(1)}, u32[]{:S(2)}, u32[]{:S(2)}) collective-permute-start(bf16[136,768]{1,0:T(8,128)(2,1)S(1)} %collective-permute-done.refs_0_), channel_id=1, source_target_pairs={{0,4},{1,5},{4,8},{5,9},{8,12},{9,13},{12,14},{13,15},{14,10},{15,... | collective-permute-start | bytes 626696 | tf_op jit(solution)/shard_map/ppermute | solution.py:455
  13.6 6.0 %collective-permute-start.4 = (bf16[136,768]{1,0:T(8,128)(2,1)S(1)}, bf16[136,768]{1,0:T(8,128)(2,1)S(1)}, u32[]{:S(2)}, u32[]{:S(2)}) collective-permute-start(bf16[136,768]{1,0:T(8,128)(2,1)S(1)} %collective-permute-done.3.refs_1_), channel_id=1, source_target_pairs={{0,2},{1,3},{4,0},{5,1},{8,4},{9,5},{12,8},{13,9},{14,12},{15,13},... | collective-permute-start | bytes 626696 | tf_op jit(solution)/shard_map/ppermute | solution.py:455
  18.1 7.6 %collective-permute-start.2 = (bf16[136,768]{1,0:T(8,128)(2,1)S(1)}, bf16[136,768]{1,0:T(8,128)(2,1)S(1)}, u32[]{:S(2)}, u32[]{:S(2)}) collective-permute-start(bf16[136,768]{1,0:T(8,128)(2,1)S(1)} %collective-permute-done.1.refs_0_), channel_id=1, source_target_pairs={{0,4},{1,5},{4,8},{5,9},{8,12},{9,13},{12,14},{13,15},{14,10},{15,... | collective-permute-start | bytes 626696 | tf_op jit(solution)/shard_map/ppermute | solution.py:455
  19.7 6.1 %collective-permute-start.5 = (bf16[136,768]{1,0:T(8,128)(2,1)S(1)}, bf16[136,768]{1,0:T(8,128)(2,1)S(1)}, u32[]{:S(2)}, u32[]{:S(2)}) collective-permute-start(bf16[136,768]{1,0:T(8,128)(2,1)S(1)} %collective-permute-done.4.refs_1_), channel_id=1, source_target_pairs={{0,2},{1,3},{4,0},{5,1},{8,4},{9,5},{12,8},{13,9},{14,12},{15,13},... | collective-permute-start | bytes 626696 | tf_op jit(solution)/shard_map/ppermute | solution.py:455
  20.2 1.3 %copy-start = (bf16[768,768]{1,0:T(8,128)(2,1)S(1)}, bf16[768,768]{1,0:T(8,128)(2,1)}, u32[]{:S(2)}) copy-start(bf16[768,768]{1,0:T(8,128)(2,1)} %refs_10_.3) | copy-start | bytes 3538948
  21.4 1.3 %copy-start.2 = (bf16[768,768]{1,0:T(8,128)(2,1)S(1)}, bf16[768,768]{1,0:T(8,128)(2,1)}, u32[]{:S(2)}) copy-start(bf16[768,768]{1,0:T(8,128)(2,1)} %refs_11_.3) | copy-start | bytes 3538948
  23.5 2.3 %copy-start.1 = (bf16[768,768]{1,0:T(8,128)(2,1)S(1)}, bf16[768,768]{1,0:T(8,128)(2,1)}, u32[]{:S(2)}) copy-start(bf16[768,768]{1,0:T(8,128)(2,1)} %refs_10_.3) | copy-start | bytes 3538948
  23.5 16.2 %collective-permute-start.12 = (bf16[528,768]{1,0:T(8,128)(2,1)S(1)}, bf16[528,768]{1,0:T(8,128)(2,1)S(1)}, u32[]{:S(2)}, u32[]{:S(2)}) collective-permute-start(bf16[528,768]{1,0:T(8,128)(2,1)S(1)} %shard_map.125.refs_2_), channel_id=1, source_target_pairs={{0,1},{1,0},{2,3},{3,2},{4,5},{5,4},{6,7},{7,6},{8,9},{9,8},{10,11... | collective-permute-start | bytes 2433032 | tf_op jit(solution)/shard_map/ppermute | solution.py:458
  25.3 18.2 %collective-permute-start.13 = (bf16[528,768]{1,0:T(8,128)(2,1)}, bf16[528,768]{1,0:T(8,128)(2,1)}, u32[]{:S(2)}, u32[]{:S(2)}) collective-permute-start(bf16[528,768]{1,0:T(8,128)(2,1)} %shard_map.126.refs_4_), channel_id=1, source_target_pairs={{0,1},{1,0},{2,3},{3,2},{4,5},{5,4},{6,7},{7,6},{8,9},{9,8},{10,11... | collective-permute-start | bytes 2433032 | tf_op jit(solution)/shard_map/ppermute | solution.py:458
  26.6 13.6 %copy-start.11 = (bf16[768,768]{1,0:T(8,128)(2,1)S(1)}, bf16[768,768]{1,0:T(8,128)(2,1)}, u32[]{:S(2)}) copy-start(bf16[768,768]{1,0:T(8,128)(2,1)} %wq_ref.1) | copy-start | bytes 3538948
  26.6 13.6 %copy-start.12 = (bf16[768,768]{1,0:T(8,128)(2,1)S(1)}, bf16[768,768]{1,0:T(8,128)(2,1)}, u32[]{:S(2)}) copy-start(bf16[768,768]{1,0:T(8,128)(2,1)} %wg_ref.1) | copy-start | bytes 3538948
  26.6 23.9 %collective-permute-start.6 = (bf16[528,768]{1,0:T(8,128)(2,1)S(1)}, bf16[528,768]{1,0:T(8,128)(2,1)}, u32[]{:S(2)}, u32[]{:S(2)}) collective-permute-start(bf16[528,768]{1,0:T(8,128)(2,1)S(1)} %shard_map.119.refs_0_), channel_id=1, source_target_pairs={{0,1},{1,0},{2,3},{3,2},{4,5},{5,4},{6,7},{7,6},{8,9},{9,8},{10,11... | collective-permute-start | bytes 2433032 | tf_op jit(solution)/shard_map/ppermute | solution.py:458
  27.2 7.0 %collective-permute-start.11 = (bf16[264,768]{1,0:T(8,128)(2,1)S(1)}, bf16[264,768]{1,0:T(8,128)(2,1)S(1)}, u32[]{:S(2)}, u32[]{:S(2)}) collective-permute-start(bf16[264,768]{1,0:T(8,128)(2,1)S(1)} %shard_map.124.refs_0_), channel_id=1, source_target_pairs={{0,1},{1,0},{2,3},{3,2},{4,5},{5,4},{6,7},{7,6},{8,9},{9,8},{10,11... | collective-permute-start | bytes 1216520 | tf_op jit(solution)/shard_map/ppermute | solution.py:458
  27.7 6.4 %collective-permute-start.9 = (bf16[8,768]{1,0:T(8,128)(2,1)S(1)}, bf16[8,768]{1,0:T(8,128)(2,1)S(1)}, u32[]{:S(2)}, u32[]{:S(2)}) collective-permute-start(bf16[8,768]{1,0:T(8,128)(2,1)S(1)} %get-tuple-element.18), channel_id=1, source_target_pairs={{0,14},{1,15},{4,10},{5,11},{8,6},{9,7},{12,2},{13,3},{14,0},{15,1... | collective-permute-start | bytes 36872 | tf_op jit(solution)/shard_map/ppermute | solution.py:455
  34.1 4.6 %collective-permute-start.14 = (bf16[64,768]{1,0:T(8,128)(2,1)S(1)}, bf16[64,768]{1,0:T(8,128)(2,1)S(1)}, u32[]{:S(2)}, u32[]{:S(2)}) collective-permute-start(bf16[64,768]{1,0:T(8,128)(2,1)S(1)} %shard_map.129), channel_id=1, source_target_pairs={{0,4},{1,5},{4,8},{5,9},{8,12},{9,13},{12,14},{13,15},{14,10},{15,... | collective-permute-start | bytes 294920 | tf_op jit(solution)/shard_map/ppermute | solution.py:455
  34.1 7.3 %copy-start.22 = (bf16[128,16]{0,1:T(8,128)(2,1)S(1)}, bf16[128,16]{0,1:T(8,128)(2,1)}, u32[]{:S(2)}) copy-start(bf16[128,16]{0,1:T(8,128)(2,1)} %param.22) | copy-start | bytes 12292
  34.1 9.4 %copy-start.17 = (f32[66,16]{0,1:T(8,128)S(1)}, f32[66,16]{0,1:T(8,128)}, u32[]{:S(2)}) copy-start(f32[66,16]{0,1:T(8,128)} %param.23) | copy-start | bytes 12676
  34.2 9.4 %copy-start.19 = (s32[16]{0:T(128)S(1)}, s32[16]{0:T(128)}, u32[]{:S(2)}) copy-start(s32[16]{0:T(128)} %chain_ref.3) | copy-start | bytes 196
  34.2 9.4 %copy-start.21 = (s32[16]{0:T(128)S(1)}, s32[16]{0:T(128)}, u32[]{:S(2)}) copy-start(s32[16]{0:T(128)} %res_ref.3) | copy-start | bytes 196
  34.2 0.8 %copy-start.6 = (bf16[264,768]{1,0:T(8,128)(2,1)}, bf16[264,768]{1,0:T(8,128)(2,1)S(1)}, u32[]{:S(2)}) copy-start(bf16[264,768]{1,0:T(8,128)(2,1)S(1)} %collective-permute-done.11.refs_1_) | copy-start | bytes 1216516
  35.0 4.7 %collective-permute-start.7 = (bf16[64,768]{1,0:T(8,128)(2,1)S(1)}, bf16[64,768]{1,0:T(8,128)(2,1)}, u32[]{:S(2)}, u32[]{:S(2)}) collective-permute-start(bf16[64,768]{1,0:T(8,128)(2,1)S(1)} %shard_map.120), channel_id=1, source_target_pairs={{0,2},{1,3},{4,0},{5,1},{8,4},{9,5},{12,8},{13,9},{14,12},{15,13},... | collective-permute-start | bytes 294920 | tf_op jit(solution)/shard_map/ppermute | solution.py:455
  38.7 13.4 %collective-permute-start.15 = (bf16[64,768]{1,0:T(8,128)(2,1)S(1)}, bf16[64,768]{1,0:T(8,128)(2,1)}, u32[]{:S(2)}, u32[]{:S(2)}) collective-permute-start(bf16[64,768]{1,0:T(8,128)(2,1)S(1)} %collective-permute-done.14.refs_2_), channel_id=1, source_target_pairs={{0,1},{1,0},{2,3},{3,2},{4,5},{5,4},{6,7},{7,6},{8,9},{9,8},{10,11... | collective-permute-start | bytes 294920 | tf_op jit(solution)/shard_map/ppermute | solution.py:458
  39.7 17.3 %collective-permute-start.8 = (bf16[64,768]{1,0:T(8,128)(2,1)}, bf16[64,768]{1,0:T(8,128)(2,1)}, u32[]{:S(2)}, u32[]{:S(2)}) collective-permute-start(bf16[64,768]{1,0:T(8,128)(2,1)} %collective-permute-done.7.refs_2_), channel_id=1, source_target_pairs={{0,1},{1,0},{2,3},{3,2},{4,5},{5,4},{6,7},{7,6},{8,9},{9,8},{10,11... | collective-permute-start | bytes 294920 | tf_op jit(solution)/shard_map/ppermute | solution.py:458
  39.7 1.0 %copy-start.4 = (bf16[528,768]{1,0:T(8,128)(2,1)}, bf16[528,768]{1,0:T(8,128)(2,1)S(1)}, u32[]{:S(2)}) copy-start(bf16[528,768]{1,0:T(8,128)(2,1)S(1)} %collective-permute-done.12.refs_3_) | copy-start | bytes 2433028
  39.7 10.8 %collective-permute-start.10 = (bf16[8,768]{1,0:T(8,128)(2,1)S(1)}, bf16[8,768]{1,0:T(8,128)(2,1)S(1)}, u32[]{:S(2)}, u32[]{:S(2)}) collective-permute-start(bf16[8,768]{1,0:T(8,128)(2,1)S(1)} %collective-permute-done.9.refs_2_), channel_id=1, source_target_pairs={{0,1},{1,0},{2,3},{3,2},{4,5},{5,4},{6,7},{7,6},{8,9},{9,8},{10,11... | collective-permute-start | bytes 36872 | tf_op jit(solution)/shard_map/ppermute | solution.py:458
  40.7 0.7 %copy-start.9 = (f32[128,768]{1,0:T(8,128)}, f32[128,768]{1,0:T(8,128)S(1)}, u32[]{:S(2)}) copy-start(f32[128,768]{1,0:T(8,128)S(1)} %get-tuple-element.16.refs_5_) | copy-start | bytes 1179652
  41.5 2.1 %copy-start.5 = (bf16[528,768]{1,0:T(8,128)(2,1)S(1)}, bf16[528,768]{1,0:T(8,128)(2,1)}, u32[]{:S(2)}) copy-start(bf16[528,768]{1,0:T(8,128)(2,1)} %copy-done.4) | copy-start | bytes 2433028
  41.5 1.3 %copy-start.14 = (bf16[16,256,128]{2,1,0:T(8,128)(2,1)S(1)}, bf16[16,256,128]{2,1,0:T(8,128)(2,1)}, u32[]{:S(2)}) copy-start(bf16[16,256,128]{2,1,0:T(8,128)(2,1)} %pair_ref.1) | copy-start | bytes 3145732
  43.5 1.0 %copy-start.7 = (bf16[264,768]{1,0:T(8,128)(2,1)S(1)}, bf16[264,768]{1,0:T(8,128)(2,1)}, u32[]{:S(2)}) copy-start(bf16[264,768]{1,0:T(8,128)(2,1)} %copy-done.6) | copy-start | bytes 1216516
  44.5 1.8 %copy-start.8 = (bf16[264,768]{1,0:T(8,128)(2,1)S(1)}, bf16[264,768]{1,0:T(8,128)(2,1)}, u32[]{:S(2)}) copy-start(bf16[264,768]{1,0:T(8,128)(2,1)} %copy-done.6) | copy-start | bytes 1216516
  50.4 1.7 %copy-start.3 = (bf16[768,768]{1,0:T(8,128)(2,1)S(1)}, bf16[768,768]{1,0:T(8,128)(2,1)}, u32[]{:S(2)}) copy-start(bf16[768,768]{1,0:T(8,128)(2,1)} %refs_11_.3) | copy-start | bytes 3538948
  50.5 1.7 %copy-start.10 = (f32[128,768]{1,0:T(8,128)S(1)}, f32[128,768]{1,0:T(8,128)}, u32[]{:S(2)}) copy-start(f32[128,768]{1,0:T(8,128)} %copy-done.9) | copy-start | bytes 1179652
  52.2 4.8 %copy-start.13 = (bf16[768,768]{1,0:T(8,128)(2,1)S(1)}, bf16[768,768]{1,0:T(8,128)(2,1)}, u32[]{:S(2)}) copy-start(bf16[768,768]{1,0:T(8,128)(2,1)} %refs_14_.1) | copy-start | bytes 3538948
  52.2 4.8 %copy-start.16 = (bf16[16,8,768]{2,1,0:T(8,128)(2,1)S(1)}, bf16[16,8,768]{2,1,0:T(8,128)(2,1)}, u32[]{:S(2)}) copy-start(bf16[16,8,768]{2,1,0:T(8,128)(2,1)} %refs_13_.1) | copy-start | bytes 589828

commit v4 on v3

--- a/solution.py
+++ b/solution.py
@@ -15,32 +15,33 @@
 BF16 = jnp.bfloat16
 CORES = 2
 TILE = 256
+LANES = 128
+FULL = 60 << 20
 VMEM = pl.BlockSpec(memory_space=pltpu.VMEM)
-HBM = pl.BlockSpec(memory_space=pltpu.HBM)
 ANY = pl.BlockSpec(memory_space=pl.ANY)
 SMEM = pl.BlockSpec(memory_space=pltpu.SMEM)
 VMEM = pl.BlockSpec(memory_space=pltpu.VMEM)
-HBM = pl.BlockSpec(memory_space=pltpu.HBM)
-ANY = pl.BlockSpec(memory_space=pl.ANY)
-HBM = pl.BlockSpec(memory_space=pltpu.HBM)
+ANY = pl.BlockSpec(memory_space=pl.ANY)
 ANY = pl.BlockSpec(memory_space=pl.ANY)
 SMEM = pl.BlockSpec(memory_space=pltpu.SMEM)
 VMEM = pl.BlockSpec(memory_space=pltpu.VMEM)
-HBM = pl.BlockSpec(memory_space=pltpu.HBM)
-ANY = pl.BlockSpec(memory_space=pl.ANY)
-HBM = pl.BlockSpec(memory_space=pltpu.HBM)
+ANY = pl.BlockSpec(memory_space=pl.ANY)
+ANY = pl.BlockSpec(memory_space=pl.ANY)
 ANY = pl.BlockSpec(memory_space=pl.ANY)
 SMEM = pl.BlockSpec(memory_space=pltpu.SMEM)
 VMEM = pl.BlockSpec(memory_space=pltpu.VMEM)
-HBM = pl.BlockSpec(memory_space=pltpu.HBM)
-ANY = pl.BlockSpec(memory_space=pl.ANY)
-HBM = pl.BlockSpec(memory_space=pltpu.HBM)
+ANY = pl.BlockSpec(memory_space=pl.ANY)
+ANY = pl.BlockSpec(memory_space=pl.ANY)
 ANY = pl.BlockSpec(memory_space=pl.ANY)
 SMEM = pl.BlockSpec(memory_space=pltpu.SMEM)
 VMEM = pl.BlockSpec(memory_space=pltpu.VMEM)
-HBM = pl.BlockSpec(memory_space=pltpu.HBM)
-ANY = pl.BlockSpec(memory_space=pl.ANY)
-HBM = pl.BlockSpec(memory_space=pltpu.HBM)
+ANY = pl.BlockSpec(memory_space=pl.ANY)
+ANY = pl.BlockSpec(memory_space=pl.ANY)
+ANY = pl.BlockSpec(memory_space=pl.ANY)
+SMEM = pl.BlockSpec(memory_space=pltpu.SMEM)
+VMEM = pl.BlockSpec(memory_space=pltpu.VMEM)
+ANY = pl.BlockSpec(memory_space=pl.ANY)
+ANY = pl.BlockSpec(memory_space=pl.ANY)
 ANY = pl.BlockSpec(memory_space=pl.ANY)
 SMEM = pl.BlockSpec(memory_space=pltpu.SMEM)
 
@@ -200,10 +201,64 @@
     meta_ref[...] = tiled.astype(BF16)
 
 
-def query_body(pay_ref, wq_ref, wg_ref, q_ref, gate_ref):
-    rows = pay_ref[pl.ds(0, q_ref.shape[0]), :]
-    q_ref[...] = matmul(rows, wq_ref[...]).astype(BF16)
-    gate_ref[...] = jax.nn.sigmoid(matmul(rows, wg_ref[...]))
+META_ROWS = 8
+RADIX = 128
+
+
+def prep_body(single_hbm, chain_hbm, residue_hbm, valid_hbm, out_ref, single_ref, ints_ref, sems):
+    copies = [pltpu.make_async_copy(single_hbm, single_ref, sems.at[0])]
+    for i, ref in enumerate((chain_hbm, residue_hbm, valid_hbm)):
+        copies.append(pltpu.make_async_copy(ref, ints_ref.at[i], sems.at[i + 1]))
+    for copy in copies:
+        copy.start()
+    tokens, samples, width = single_ref.shape
+    rows = tokens * samples
+    token = lax.broadcasted_iota(jnp.int32, (tokens, width), 0)
+    lane = lax.broadcasted_iota(jnp.int32, (tokens, width), 1)
+    spread = (lane % tokens == token).astype(F32).astype(BF16)
+    perm = sample_major(tokens, samples)
+    for copy in copies:
+        copy.wait()
+    normed = normed_rows(single_ref[...])
+    out_ref[pl.ds(0, rows), :] = matmul(perm, normed).astype(BF16)
+    residue = ints_ref[1]
+    row = lax.broadcasted_iota(jnp.int32, (META_ROWS, tokens), 0)
+    meta = jnp.where(row == 0, ints_ref[0], 0)
+    meta = jnp.where(row == 1, residue // RADIX, meta)
+    meta = jnp.where(row == 2, residue % RADIX, meta)
+    meta = jnp.where(row == 3, ints_ref[2], meta)
+    tiled = matmul(meta.astype(F32).astype(BF16), spread)
+    out_ref[pl.ds(rows, META_ROWS), :] = tiled.astype(BF16)
+
+
+def own_body(
+    steps, chips, early, me_ref, pay_hbm, wq_hbm, wk_hbm, wv_hbm, wg_hbm, pair_hbm, wp_hbm,
+    q_ref, gate_ref, kv_ref, first_ref, second_ref,
+    pay_ref, wq_ref, wk_ref, wv_ref, wg_ref, pair_ref, wp_ref, sems,
+):
+    copies = {}
+    moves = [
+        (pay_hbm, pay_ref), (wq_hbm, wq_ref), (wp_hbm, wp_ref), (pair_hbm, pair_ref),
+        (wk_hbm, wk_ref), (wv_hbm, wv_ref), (wg_hbm, wg_ref),
+    ]
+    for i, (source, target) in enumerate(moves):
+        copies[i] = pltpu.make_async_copy(source, target, sems.at[i])
+        copies[i].start()
+    rows = q_ref.shape[0]
+    copies[0].wait()
+    data = pay_ref[pl.ds(0, rows), :]
+    copies[1].wait()
+    q_ref[...] = matmul(data, wq_ref[...]).astype(BF16)
+    copies[2].wait()
+    copies[3].wait()
+    pair_rows(steps, chips, early, me_ref[0], pair_ref, wp_ref[...], (first_ref, second_ref))
+    copies[4].wait()
+    kv_ref[pl.ds(0, rows), :] = matmul(data, wk_ref[...]).astype(BF16)
+    copies[5].wait()
+    kv_ref[pl.ds(rows, rows), :] = matmul(data, wv_ref[...]).astype(BF16)
+    kv_ref[pl.ds(2 * rows, META_ROWS), :] = pay_ref[pl.ds(rows, META_ROWS), :]
+    copies[6].wait()
+    gate_ref[...] = jax.nn.sigmoid(matmul(data, wg_ref[...]))
 
 
 def kv_body(*refs):
@@ -224,10 +279,9 @@
     return jnp.where(place < chips // 2, 2 * place, 2 * (chips - 1 - place) + 1)
 
 
-def pair_body(steps, chips, early, me_ref, pair_ref, wp_ref, *out_refs):
+def pair_rows(steps, chips, early, me, pair_ref, weights, out_refs):
     queries, total, _ = pair_ref.shape
     tokens = total // len(steps)
-    me = me_ref[0]
     chip = me // CORES
     core = lax.rem(me, CORES)
     place = jnp.where(lax.rem(chip, 2) == 0, chip // 2, chips - 1 - chip // 2)
@@ -235,7 +289,6 @@
     for r, c in steps:
         block = ring_chip(place + r, chips) * CORES + lax.rem(core + c, CORES)
         starts.append(pl.multiple_of(block * tokens, tokens))
-    weights = wp_ref[...]
     for i in range(queries):
         for out_ref, part in zip(out_refs, (starts[:early], starts[early:])):
             data = jnp.concatenate([pair_ref[i, pl.ds(b, tokens), :] for b in part], axis=0)
@@ -244,47 +297,57 @@
             )
 
 
-def rel_body(counts, chain_ref, res_ref, tab_ref, bias_ref, *refs):
-    n = len(counts)
-    metas, out_ref, meta_ref, sems = refs[:n], refs[n], refs[n + 1], refs[n + 2]
-    heads, queries, total = out_ref.shape
-    copies, at = [], 0
-    for i, (m, count) in enumerate(zip(metas, counts)):
-        size = count * META_ROWS
-        source = m.at[pl.ds(m.shape[0] - size, size), :]
-        target = meta_ref.at[pl.ds(at * META_ROWS, size), :]
-        copies.append(pltpu.make_async_copy(source, target, sems.at[i]))
-        at += count
-    for copy in copies:
-        copy.start()
+def kv_count(ref, rows):
+    return ref.shape[0] // (2 * rows + META_ROWS)
+
+
+def kv_metas(kv_refs, rows):
+    found = []
+    for r in kv_refs:
+        n = kv_count(r, rows)
+        found += [r[pl.ds(2 * n * rows + u * META_ROWS, META_ROWS), :] for u in range(n)]
+    return found
+
+
+def full_bias(own, metas, tokens, pair_ref, tab_ref, pad_ref):
+    heads, _, total = pair_ref.shape
     bins = tab_ref.shape[1]
     reach = (bins - 2) // 2
-    tokens = total // at
-    table = tab_ref[...]
-    high = table.astype(BF16)
-    rest = table - high.astype(F32)
-    mid = rest.astype(BF16)
-    low = (rest - mid.astype(F32)).astype(BF16)
-    parts = jnp.concatenate([low, mid, high], axis=0)
-    bin_ids = lax.broadcasted_iota(jnp.int32, (bins, total), 0).astype(F32)
-    slot = lax.broadcasted_iota(jnp.int32, (META_ROWS, total), 1) // tokens
-    keys = jnp.zeros((META_ROWS, total), F32)
-    for copy in copies:
-        copy.wait()
-    for u in range(at):
-        row = meta_ref[pl.ds(u * META_ROWS, META_ROWS), :].astype(F32)
-        row = jnp.concatenate([row] * (-(-total // row.shape[1])), axis=1)[:, :total]
+    wide = -(-total // LANES) * LANES
+    slot = lax.broadcasted_iota(jnp.int32, (META_ROWS, wide), 1) // tokens
+    keys = jnp.zeros((META_ROWS, wide), F32)
+    for u, row in enumerate(metas):
+        row = row.astype(F32)
+        row = jnp.concatenate([row] * (-(-wide // row.shape[1])), axis=1)[:, :wide]
         keys = jnp.where(slot == u, row, keys)
-    chain_keys = keys[0:1, :]
+    here = own.astype(F32)[:, :LANES]
+    lane = lax.broadcasted_iota(jnp.int32, (tokens, LANES), 1)
+    row = lax.broadcasted_iota(jnp.int32, (tokens, LANES), 0)
+
+    def column(values):
+        values = jnp.where(lane == row, jnp.broadcast_to(values, (tokens, LANES)), 0.0)
+        return jnp.sum(values, axis=-1, keepdims=True)
+
+    chain_q = column(here[0:1, :])
+    res_q = column(here[1:2, :] * RADIX + here[2:3, :])
     res_keys = keys[1:2, :] * RADIX + keys[2:3, :]
-    mask = (keys[3:4, :] - 1.0) * MASK_PENALTY
-    for i in range(queries):
-        offset = jnp.clip(res_ref[i].astype(F32) - res_keys, -reach, reach) + reach
-        bucket = jnp.where(chain_keys == chain_ref[i].astype(F32), offset, float(bins - 1))
-        hot = (bin_ids == bucket).astype(F32).astype(BF16)
-        rel = matmul(parts, hot)
-        rel = (rel[:heads] + rel[heads : 2 * heads]) + rel[2 * heads :]
-        out_ref[:, i, :] = bias_ref[:, i, :] + rel + mask
+    offset = jnp.clip(res_q - res_keys, -reach, reach) + reach
+    bucket = jnp.where(chain_q == keys[0:1, :], offset, float(bins - 1)).astype(jnp.int32)
+    mask = (keys[3:4, :total] - 1.0) * MASK_PENALTY
+    pad_ref[...] = jnp.zeros_like(pad_ref)
+    pad_ref[:, pl.ds(0, bins)] = tab_ref[...]
+    out = []
+    for h in range(heads):
+        table = jnp.broadcast_to(pad_ref[h : h + 1, :], (tokens, LANES))
+        rel = [
+            jnp.take_along_axis(
+                table, bucket[:, at : at + LANES], axis=1, mode="promise_in_bounds"
+            )
+            for at in range(0, wide, LANES)
+        ]
+        rel = jnp.concatenate(rel, axis=1)[:, :total] if len(rel) > 1 else rel[0][:, :total]
+        out.append(pair_ref[h] + rel + mask)
+    return jnp.concatenate(out, axis=0)
 
 
 def head_spans(width, hs):
@@ -325,14 +388,16 @@
 
 
 def early_body(samples, heads, scale, *refs):
-    q_ref, bias_ref, sum_ref, top_ref, mass_ref = refs[-5:]
+    q_ref, pair_ref, tab_ref, sum_ref, top_ref, mass_ref, pad_ref = refs[-7:]
+    kv_refs = refs[:-7]
     rows, width = q_ref.shape
     tokens = rows // samples
     spans = head_spans(width, width // heads)
     height = sum(h1 - h0 + 1 for h0, h1 in spans) * tokens
-    bias = bias_ref[...].reshape(heads * tokens, bias_ref.shape[2])
+    metas = kv_metas(kv_refs, rows)
+    bias = full_bias(metas[0], metas, tokens, pair_ref, tab_ref, pad_ref)
     for s in range(samples):
-        keys, values = gather_keys(refs[:-5], rows, s * tokens, tokens)
+        keys, values = gather_keys(kv_refs, rows, s * tokens, tokens)
         keys, values = jnp.concatenate(keys, axis=0), jnp.concatenate(values, axis=0)
         q = q_ref[pl.ds(s * tokens, tokens), :].astype(F32)
         scores = score_rows(q, keys, bias, heads, scale)
@@ -351,8 +416,8 @@
             at += got.shape[0]
 
 
-def attend_rows(first, count, heads, scale, kv_refs, mine, other, shared):
-    q_ref, gate_ref, bias_ref, sum_ref, top_ref, mass_ref, wk_ref, wv_ref = shared
+def attend_rows(first, count, heads, scale, kv_refs, mine, other, bias, shared):
+    q_ref, gate_ref, sum_ref, top_ref, mass_ref, wk_ref, wv_ref = shared
     rows, width = gate_ref.shape
     half = mine.shape[0]
     tokens = half // count
@@ -360,7 +425,6 @@
     data = jnp.concatenate([mine, other], axis=0)
     k_last = matmul(data, wk_ref[...]).astype(BF16)
     v_last = matmul(data, wv_ref[...]).astype(BF16)
-    bias = bias_ref[...].reshape(heads * tokens, bias_ref.shape[2])
     lane_head = lax.broadcasted_iota(jnp.int32, (tokens, width), 1) // hs
     spans = head_spans(width, hs)
     height = sum(h1 - h0 + 1 for h0, h1 in spans) * tokens
@@ -400,20 +464,30 @@
     return jnp.concatenate(gated, axis=0)
 
 
-def attend_body(count, heads, scale, *refs):
-    out_ref = refs[-1]
-    shared = refs[-9:-1]
-    mine, other = refs[-11], refs[-10]
-    out_ref[...] = attend_rows(0, count, heads, scale, refs[:-11], mine[...], other[...], shared)
+def attend_body(count, samples, heads, scale, *refs):
+    pair_ref, tab_ref, pay_ref, out_ref, bias_ref, pad_ref = refs[-6:]
+    shared = refs[-13:-6]
+    kv_refs, mine, other = refs[:-15], refs[-15], refs[-14]
+    rows = shared[0].shape[0]
+    tokens = rows // samples
+    half = count * tokens
+    metas = kv_metas(kv_refs, rows)
+    metas += [m[pl.ds(half, META_ROWS), :] for m in (mine, other)]
+    own = pay_ref[pl.ds(rows, META_ROWS), :]
+    bias = full_bias(own, metas, tokens, pair_ref, tab_ref, pad_ref)
+    bias_ref[...] = bias
+    mine, other = mine[pl.ds(0, half), :], other[pl.ds(0, half), :]
+    out_ref[...] = attend_rows(0, count, heads, scale, kv_refs, mine, other, bias, shared)
 
 
 def finish_body(count, samples, heads, scale, *refs):
-    done, single_ref, wo_ref, out_ref = refs[-4:]
-    shared = refs[-12:-4]
-    mine, other = refs[-14], refs[-13]
+    bias_ref, done, single_ref, wo_ref, out_ref = refs[-5:]
+    shared = refs[-12:-5]
+    kv_refs, mine, other = refs[:-14], refs[-14], refs[-13]
     tokens, samples, width = single_ref.shape
     gated = attend_rows(
-        samples - count, count, heads, scale, refs[:-14], mine[...], other[...], shared
+        samples - count, count, heads, scale, kv_refs, mine[...], other[...],
+        bias_ref[...], shared,
     )
     gated = jnp.concatenate([done[...], gated], axis=0)
     gated = matmul(token_major(tokens, samples), gated).astype(BF16)
@@ -462,14 +536,11 @@
         steps += [(-k, 0), (k, 0), (-k, 1), (k, 1)]
     steps += [(half, 0), (half, 1)]
 
-    payload, meta = call(
+    payload = call(
         prep_body,
-        (
-            jax.ShapeDtypeStruct((rows + META_ROWS, width), BF16),
-            jax.ShapeDtypeStruct((META_ROWS, width), BF16),
-        ),
+        jax.ShapeDtypeStruct((rows + META_ROWS, width), BF16),
         (single, *(v.reshape(1, tokens) for v in (chain, residue, valid))),
-        in_specs=[HBM] * 4,
+        in_specs=[ANY] * 4,
         scratch=[
             pltpu.VMEM(single.shape, BF16),
             pltpu.VMEM((3, 1, tokens), jnp.int32),
@@ -477,17 +548,10 @@
         ],
         flops=rows * width * 16,
         moved=4 * rows * width,
+        limit=FULL,
     )
     cw = ring(payload, 1)
     ccw = ring(payload, -1)
-
-    query, gate = call(
-        query_body,
-        (jax.ShapeDtypeStruct((rows, width), BF16), jax.ShapeDtypeStruct((rows, width), F32)),
-        (payload, w_query, w_gate),
-        flops=4 * rows * width * width,
-        moved=4 * width * width + 8 * rows * width,
-    )
 
     def kv(parts):
         n = len(parts)
@@ -499,85 +563,94 @@
             moved=4 * width * width + 6 * n * rows * width,
         )
 
-    def piece(value, at):
+    def piece(value, at, meta):
+        count = rows // 2 + (META_ROWS if meta else 0)
+
         def body(in_ref, out_ref):
-            out_ref[...] = in_ref[pl.ds(at, rows // 2), :]
-
-        shape = jax.ShapeDtypeStruct((rows // 2, width), BF16)
+            out_ref[pl.ds(0, rows // 2), :] = in_ref[pl.ds(at, rows // 2), :]
+            if meta:
+                out_ref[pl.ds(rows // 2, META_ROWS), :] = in_ref[pl.ds(rows, META_ROWS), :]
+
+        shape = jax.ShapeDtypeStruct((count, width), BF16)
         return call(body, shape, (value,), moved=2 * rows * width)
 
-    far = ring(meta, half)
-    far = [far, flip(far)]
-    kvs = [kv([payload])]
+    early = len(steps) - 3 * CORES
+    split = 2 * (half - 1)
+    pair_shapes = tuple(
+        jax.ShapeDtypeStruct((heads, tokens, n * tokens), F32) for n in (early, len(steps) - early)
+    )
+    weight = pltpu.VMEM((width, width), BF16)
+    query, gate, kv_own, pair_first, pair_second = call(
+        functools.partial(own_body, steps, chips, early),
+        (
+            jax.ShapeDtypeStruct((rows, width), BF16),
+            jax.ShapeDtypeStruct((rows, width), F32),
+            jax.ShapeDtypeStruct((2 * rows + META_ROWS, width), BF16),
+            *pair_shapes,
+        ),
+        (me, payload, w_query, w_key, w_value, w_gate, pair, w_pair.T),
+        in_specs=[SMEM] + [ANY] * 7,
+        flops=8 * rows * width * width + 2 * pair.size * heads,
+        moved=8 * width * width + 12 * rows * width + 2 * pair.size,
+        limit=FULL,
+        scratch=[
+            pltpu.VMEM(payload.shape, BF16),
+            weight,
+            weight,
+            weight,
+            weight,
+            pltpu.VMEM(pair.shape, BF16),
+            pltpu.VMEM(w_pair.shape[::-1], BF16),
+            pltpu.SemaphoreType.DMA((7,)),
+        ],
+    )
+
+    kvs = [kv_own]
     kvs.append(flip(kvs[-1]))
     for k in range(1, half):
         if k + 1 < half:
             cw_next = ring(cw, 1)
             ccw_next = ring(ccw, -1)
         else:
-            cw_next = ring(piece(cw, 0), 1)
-            ccw_next = ring(piece(ccw, rows // 2), -1)
+            cw_next = ring(piece(cw, 0, True), 1)
+            ccw_next = ring(piece(ccw, rows // 2, False), -1)
         kvs.append(kv([cw, ccw]))
         kvs.append(flip(kvs[-1]))
         cw, ccw = cw_next, ccw_next
-    early = len(steps) - 3 * CORES
-    split = 2 * (half - 1)
-    pair_shapes = tuple(
-        jax.ShapeDtypeStruct((heads, tokens, n * tokens), F32) for n in (early, len(steps) - early)
-    )
-    pair_bias = call(
-        functools.partial(pair_body, steps, chips, early),
-        pair_shapes,
-        (me, pair, w_pair.T),
-        in_specs=[SMEM, VMEM, VMEM],
-        flops=2 * pair.size * heads,
-        moved=pair.size * 2 + heads * tokens * total * 4,
-        limit=(4 << 20) + 2 * pair.size + 8 * heads * tokens * total,
-    )
-
-    def relative(at, metas):
-        counts = [max(1, m.shape[0] // (2 * rows + META_ROWS)) for m in metas]
-        return call(
-            functools.partial(rel_body, counts),
-            pair_shapes[at],
-            (chain, residue, rel_table.T, pair_bias[at], *metas),
-            in_specs=[SMEM, SMEM, VMEM, VMEM] + [ANY] * len(metas),
-            flops=pair_shapes[at].size * 256,
-            moved=8 * pair_shapes[at].size,
-            scratch=[
-                pltpu.VMEM((sum(counts) * META_ROWS, width), BF16),
-                pltpu.SemaphoreType.DMA((len(metas),)),
-            ],
-        )
-
     scale = 1.0 / math.sqrt(width // heads)
     spans = head_spans(width, width // heads)
     height = sum(h1 - h0 + 1 for h0, h1 in spans) * tokens * samples
     state = jax.ShapeDtypeStruct((samples * heads * tokens, 128), F32)
-    bias = relative(0, kvs[:split])
+    table = rel_table.T
+    pad = [pltpu.VMEM((heads, LANES), F32)]
     limit = (10 << 20) + 4 * samples * total * width
     before = call(
         functools.partial(early_body, samples, heads, scale),
         (jax.ShapeDtypeStruct((height, TILE), F32), state, state),
-        (*kvs[:split], query, bias),
+        (*kvs[:split], query, pair_first, table),
         flops=4 * rows * early * tokens * width,
         moved=4 * samples * early * tokens * width,
         limit=limit,
-    )
-    bias = relative(1, [*kvs[split:], *far])
+        scratch=pad,
+    )
     count = samples // 2
     common = dict(flops=2 * rows * total * width, moved=samples * total * width, limit=limit)
-    shared = (query, gate, bias, *before, w_key, w_value)
-    gated = call(
-        functools.partial(attend_body, count, heads, scale),
-        jax.ShapeDtypeStruct((rows // 2, width), BF16),
-        (*kvs[split:], cw, flip(cw), *shared),
+    shared = (query, gate, *before, w_key, w_value)
+    last = (len(steps) - early) * tokens
+    gated, bias = call(
+        functools.partial(attend_body, count, samples, heads, scale),
+        (
+            jax.ShapeDtypeStruct((rows // 2, width), BF16),
+            jax.ShapeDtypeStruct((heads * tokens, last), F32),
+        ),
+        (*kvs[split:], cw, flip(cw), *shared, pair_second, table, payload),
+        scratch=pad,
         **common,
     )
     return call(
         functools.partial(finish_body, count, samples, heads, scale),
         jax.ShapeDtypeStruct(single.shape, BF16),
-        (*kvs[split:], ccw, flip(ccw), *shared, gated, single, w_out),
+        (*kvs[split:], ccw, flip(ccw), *shared, bias, gated, single, w_out),
         **common,
     )
 
@@ -608,3 +681,4 @@
     return step
     return step
     return step
+    return step

time: 63.2 us -> 52.4 us (0.83); the launches traced: 62.1 us -> 52.1 us
  starting transfers between devices: 15.4 us -> 11.4 us
  local copies, waits for them, and re-layouts: 9.31 us -> 5.46 us
  Pallas kernels: 23.1 us -> 21.8 us
  waiting for transfers between devices: 14 us -> 13.2 us
    unnamed x48 -> x28, local copies, waits for them, and re-layouts: 9.31 us -> 5.46 us
    ppermute x9 -> x8, starting transfers between devices: 13.7 us -> 10.2 us  [ring(): return lax.ppermute(value, 'tok', pairs)]
    pallas_call x14 -> x10, Pallas kernels: 23.1 us -> 21.8 us  [call(): pl.pallas_call(body, out_shape=out_shape, in_specs=in_specs or [VMEM] * l...]
    ppermute x9 -> x8, waiting for transfers between devices: 14 us -> 13.2 us  [ring(): return lax.ppermute(value, 'tok', pairs)]
    ppermute x7 -> x6, starting transfers between devices: 1.72 us -> 1.2 us  [flip(): return lax.ppermute(value, 'tok', [(d, d ^ 1) for d in range(devices)])]
  transfers between devices with their start and end apart: 16 -> 14, of which waited for: 5 -> 4; matrix products, arithmetic and copies ran while one was open for 0% -> 0% of each run, Pallas kernels for 28% -> 30%
where the time goes in v4:
time: 52.4 us; the launch traced here: 52.1 us
  Pallas kernels  21.8 us (42%)
  waiting for transfers between devices  13.2 us (25%)
  starting transfers between devices  11.4 us (22%)
  local copies, waits for them, and re-layouts  5.46 us (10%)
    pallas_call x10, Pallas kernels, call(): pl.pallas_call(body, out_shape=out_shape, in_specs=in_specs or [VMEM] * l...  21.8 us
    ppermute x8, waiting for transfers between devices, ring(): return lax.ppermute(value, 'tok', pairs)  13.2 us
    ppermute x8, starting transfers between devices, ring(): return lax.ppermute(value, 'tok', pairs)  10.2 us
    unnamed x28, local copies, waits for them, and re-layouts  5.46 us
    ppermute x6, starting transfers between devices, flip(): return lax.ppermute(value, 'tok', [(d, d ^ 1) for d in range(devices)])  1.2 us
  transfers between devices with their start and end apart: 14, of which 4 were waited for; matrix products, arithmetic and copies ran while one was open for 0% of the time, Pallas kernels for 30%

profile of v4, /device:TPU:0, one launch (start us, length us, event | category | flops | bytes accessed | tf_op | source)
XLA Modules:
  0.0 52.1 jit_solution(11258041796262904218)
XLA Ops:
  0.0 2.1 %shard_map.118.pay_hbm.refs_13_ = bf16[136,768]{1,0:T(8,128)(2,1)} custom-call(bf16[16,8,768]{2,1,0:T(8,128)(2,1)} %refs_13_.1, s32[1,16]{1,0:T(1,128)} %bitcast.9, s32[1,16]{1,0:T(1,128)} %bitcast.10, s32[1,16]{1,0:T(1,128)} %bitcast.11), custom_call_target="tpu_custom_call" | custom-call | flops 1572864 | bytes 393216 | tf_op jit(solution)/shard_map/pallas_call | solution.py:499
  2.1 3.1 %collective-permute-start = (bf16[136,768]{1,0:T(8,128)(2,1)}, bf16[136,768]{1,0:T(8,128)(2,1)S(1)}, u32[]{:S(2)}, u32[]{:S(2)}) collective-permute-start(bf16[136,768]{1,0:T(8,128)(2,1)} %shard_map.118.pay_hbm.refs_13_), channel_id=1, source_target_pairs={{0,4},{1,5},{4,8},{5,9},{8,12},{9,13},{12,14},{13,15},{14,10},{15,... | collective-permute-start | bytes 626696 | tf_op jit(solution)/shard_map/ppermute | solution.py:529
  5.2 0.0 collective-permute-start.3
  5.2 5.3 %collective-permute-done.refs_0_ = bf16[136,768]{1,0:T(8,128)(2,1)S(1)} collective-permute-done((bf16[136,768]{1,0:T(8,128)(2,1)}, bf16[136,768]{1,0:T(8,128)(2,1)S(1)}, u32[]{:S(2)}, u32[]{:S(2)}) %collective-permute-start) | collective-permute-done | bytes 208928 | tf_op jit(solution)/shard_map/ppermute | solution.py:529
  10.5 1.8 %collective-permute-start.1 = (bf16[136,768]{1,0:T(8,128)(2,1)S(1)}, bf16[136,768]{1,0:T(8,128)(2,1)S(1)}, u32[]{:S(2)}, u32[]{:S(2)}) collective-permute-start(bf16[136,768]{1,0:T(8,128)(2,1)S(1)} %collective-permute-done.refs_0_), channel_id=1, source_target_pairs={{0,4},{1,5},{4,8},{5,9},{8,12},{9,13},{12,14},{13,15},{14,10},{15,... | collective-permute-start | bytes 626696 | tf_op jit(solution)/shard_map/ppermute | solution.py:529
  12.3 0.0 collective-permute-done.3.refs_1_
  12.3 0.2 collective-permute-start.4
  12.5 4.3 %collective-permute-done.1.refs_0_ = bf16[136,768]{1,0:T(8,128)(2,1)S(1)} collective-permute-done((bf16[136,768]{1,0:T(8,128)(2,1)S(1)}, bf16[136,768]{1,0:T(8,128)(2,1)S(1)}, u32[]{:S(2)}, u32[]{:S(2)}) %collective-permute-start.1) | collective-permute-done | bytes 208928 | tf_op jit(solution)/shard_map/ppermute | solution.py:529
  16.8 1.5 %collective-permute-start.2 = (bf16[136,768]{1,0:T(8,128)(2,1)S(1)}, bf16[136,768]{1,0:T(8,128)(2,1)S(1)}, u32[]{:S(2)}, u32[]{:S(2)}) collective-permute-start(bf16[136,768]{1,0:T(8,128)(2,1)S(1)} %collective-permute-done.1.refs_0_), channel_id=1, source_target_pairs={{0,4},{1,5},{4,8},{5,9},{8,12},{9,13},{12,14},{13,15},{14,10},{15,... | collective-permute-start | bytes 626696 | tf_op jit(solution)/shard_map/ppermute | solution.py:529
  18.3 0.0 collective-permute-done.4.refs_1_
  18.3 0.5 collective-permute-start.5
  18.8 1.3 %copy-done = bf16[768,768]{1,0:T(8,128)(2,1)S(1)} copy-done((bf16[768,768]{1,0:T(8,128)(2,1)S(1)}, bf16[768,768]{1,0:T(8,128)(2,1)}, u32[]{:S(2)}) %copy-start) | copy-done | bytes 1179672
  20.1 1.3 %copy-done.3 = bf16[768,768]{1,0:T(8,128)(2,1)S(1)} copy-done((bf16[768,768]{1,0:T(8,128)(2,1)S(1)}, bf16[768,768]{1,0:T(8,128)(2,1)}, u32[]{:S(2)}) %copy-start.3) | copy-done | bytes 1179672
  21.4 0.8 %shard_map.122.refs_2_ = bf16[528,768]{1,0:T(8,128)(2,1)S(1)} custom-call(bf16[136,768]{1,0:T(8,128)(2,1)S(1)} %collective-permute-done.refs_0_, bf16[136,768]{1,0:T(8,128)(2,1)S(1)} %collective-permute-done.3.refs_1_, bf16[768,768]{1,0:T(8,128)(2,1)S(1)} %copy-done, bf16[768,768]{1,0:T(8,128)(2,1)S(1)} %copy-done.3), custom_call_target="tpu_custom_call" | custom-call | flops 603979776 | bytes 3538944 | tf_op jit(solution)/shard_map/pallas_call | solution.py:499
  22.2 0.0 copy-start.1
  22.2 0.1 collective-permute-start.10
  22.3 1.7 %shard_map.123.refs_4_ = bf16[528,768]{1,0:T(8,128)(2,1)} custom-call(bf16[136,768]{1,0:T(8,128)(2,1)S(1)} %collective-permute-done.1.refs_0_, bf16[136,768]{1,0:T(8,128)(2,1)S(1)} %collective-permute-done.4.refs_1_, bf16[768,768]{1,0:T(8,128)(2,1)S(1)} %copy-done, bf16[768,768]{1,0:T(8,128)(2,1)S(1)} %copy-done.3), custom_call_target="tpu_custom_call" | custom-call | flops 603979776 | bytes 3538944 | tf_op jit(solution)/shard_map/pallas_call | solution.py:499
  24.0 0.5 collective-permute-start.11
  24.5 0.0 collective-permute-done.2.refs_0_.in_ref
  24.5 0.0 collective-permute-done.5.refs_1_.in_ref
  24.5 0.0 copy-done.1
  24.5 0.8 %shard_map.119.refs_0_ = bf16[528,768]{1,0:T(8,128)(2,1)S(1)} custom-call(bf16[136,768]{1,0:T(8,128)(2,1)S(1)} %collective-permute-done.2.refs_0_.in_ref, bf16[136,768]{1,0:T(8,128)(2,1)S(1)} %collective-permute-done.5.refs_1_.in_ref, bf16[768,768]{1,0:T(8,128)(2,1)S(1)} %copy-done.1, bf16[768,768]{1,0:T(8,128)(2,1)S(1)} %copy-done.3), custom_call_target="tpu_custom_call" | custom-call | flops 603979776 | bytes 3538944 | tf_op jit(solution)/shard_map/pallas_call | solution.py:499
  25.3 0.1 collective-permute-start.6
  25.4 0.0 copy-start.13
  25.4 4.7 %shard_map.121 = (bf16[128,768]{1,0:T(8,128)(2,1)}, f32[128,768]{1,0:T(8,128)}, bf16[264,768]{1,0:T(8,128)(2,1)}, f32[16,16,160]{2,1,0:T(8,128)}, f32[16,16,96]{2,1,0:T(8,128)}) custom-call(s32[1]{0:T(128)} %bitcast.3.me_ref, bf16[136,768]{1,0:T(8,128)(2,1)} %shard_map.118.pay_hbm.refs_13_, bf16[768,768]{1,0:T(8,128)(2,1)} %wq_hbm.1, ...), custom_call_target="tpu_custom_call" | custom-call | flops 620756992 | bytes 6946816 | tf_op jit(solution)/shard_map/pallas_call | solution.py:499
  30.1 0.6 %collective-permute-start.9 = (bf16[264,768]{1,0:T(8,128)(2,1)}, bf16[264,768]{1,0:T(8,128)(2,1)S(1)}, u32[]{:S(2)}, u32[]{:S(2)}) collective-permute-start(bf16[264,768]{1,0:T(8,128)(2,1)} %get-tuple-element.17.refs_0_), channel_id=1, source_target_pairs={{0,1},{1,0},{2,3},{3,2},{4,5},{5,4},{6,7},{7,6},{8,9},{9,8},{10,11... | collective-permute-start | bytes 1216520 | tf_op jit(solution)/shard_map/ppermute | solution.py:532
  30.6 1.6 %collective-permute-start.12 = (bf16[72,768]{1,0:T(8,128)(2,1)S(1)}, bf16[72,768]{1,0:T(8,128)(2,1)S(1)}, u32[]{:S(2)}, u32[]{:S(2)}) collective-permute-start(bf16[72,768]{1,0:T(8,128)(2,1)S(1)} %shard_map.125), channel_id=1, source_target_pairs={{0,4},{1,5},{4,8},{5,9},{8,12},{9,13},{12,14},{13,15},{14,10},{15,... | collective-permute-start | bytes 331784 | tf_op jit(solution)/shard_map/ppermute | solution.py:529
  32.2 0.0 collective-permute-done.9.refs_1_
  32.2 1.4 %collective-permute-start.7 = (bf16[64,768]{1,0:T(8,128)(2,1)S(1)}, bf16[64,768]{1,0:T(8,128)(2,1)S(1)}, u32[]{:S(2)}, u32[]{:S(2)}) collective-permute-start(bf16[64,768]{1,0:T(8,128)(2,1)S(1)} %shard_map.120), channel_id=1, source_target_pairs={{0,2},{1,3},{4,0},{5,1},{8,4},{9,5},{12,8},{13,9},{14,12},{15,13},... | collective-permute-start | bytes 294920 | tf_op jit(solution)/shard_map/ppermute | solution.py:529
  33.7 2.0 %collective-permute-done.12.refs_2_ = bf16[72,768]{1,0:T(8,128)(2,1)S(1)} collective-permute-done((bf16[72,768]{1,0:T(8,128)(2,1)S(1)}, bf16[72,768]{1,0:T(8,128)(2,1)S(1)}, u32[]{:S(2)}, u32[]{:S(2)}) %collective-permute-start.12) | collective-permute-done | bytes 110624 | tf_op jit(solution)/shard_map/ppermute | solution.py:529
  35.7 0.0 collective-permute-start.13
  35.7 1.6 %collective-permute-done.7.refs_2_ = bf16[64,768]{1,0:T(8,128)(2,1)S(1)} collective-permute-done((bf16[64,768]{1,0:T(8,128)(2,1)S(1)}, bf16[64,768]{1,0:T(8,128)(2,1)S(1)}, u32[]{:S(2)}, u32[]{:S(2)}) %collective-permute-start.7) | collective-permute-done | bytes 98336 | tf_op jit(solution)/shard_map/ppermute | solution.py:529
  37.3 0.0 collective-permute-start.8
  37.3 0.0 collective-permute-done.10.refs_3_
  37.3 0.0 collective-permute-done.11.refs_5_
  37.3 0.0 copy-done.13
  37.3 0.0 copy-start.6
  37.3 0.9 %copy-done.6 = bf16[128,768]{1,0:T(8,128)(2,1)S(1)} copy-done((bf16[128,768]{1,0:T(8,128)(2,1)S(1)}, bf16[128,768]{1,0:T(8,128)(2,1)}, u32[]{:S(2)}) %copy-start.6) | copy-done | bytes 196632
  38.2 1.0 %copy-done.10 = bf16[264,768]{1,0:T(8,128)(2,1)S(1)} copy-done((bf16[264,768]{1,0:T(8,128)(2,1)S(1)}, bf16[264,768]{1,0:T(8,128)(2,1)}, u32[]{:S(2)}) %copy-start.10) | copy-done | bytes 405528
  39.2 0.9 %copy-done.11 = f32[16,16,160]{2,1,0:T(8,128)S(1)} copy-done((f32[16,16,160]{2,1,0:T(8,128)S(1)}, f32[16,16,160]{2,1,0:T(8,128)}, u32[]{:S(2)}) %copy-start.11) | copy-done | bytes 163864
  40.2 4.7 %shard_map.124 = (f32[2304,256]{1,0:T(8,128)S(1)}, f32[2048,128]{1,0:T(8,128)S(1)}, f32[2048,128]{1,0:T(8,128)S(1)}) custom-call(bf16[264,768]{1,0:T(8,128)(2,1)S(1)} %copy-done.10, bf16[264,768]{1,0:T(8,128)(2,1)S(1)} %collective-permute-done.9.refs_1_, bf16[528,768]{1,0:T(8,128)(2,1)S(1)} %shard_map.122.refs_2_, ...), custom_call_target="tpu_custom_call" | custom-call | flops 62914560 | bytes 3932160 | tf_op jit(solution)/shard_map/pallas_call | solution.py:499
  44.9 0.0 collective-permute-done.13.refs_3_
  44.9 0.0 collective-permute-done.6.refs_1_
  45.0 0.0 copy-start.8
  45.0 0.0 copy-start.9
  45.0 3.2 %shard_map.126 = (bf16[64,768]{1,0:T(8,128)(2,1)S(1)}, f32[256,96]{1,0:T(8,128)S(1)}) custom-call(bf16[528,768]{1,0:T(8,128)(2,1)S(1)} %shard_map.119.refs_0_, bf16[528,768]{1,0:T(8,128)(2,1)S(1)} %collective-permute-done.6.refs_1_, bf16[72,768]{1,0:T(8,128)(2,1)S(1)} %collective-permute-done.12.refs_2_, ...), custom_call_target="tpu_custom_call" | custom-call | flops 50331648 | bytes 1572864 | tf_op jit(solution)/shard_map/pallas_call | solution.py:499
  48.1 0.0 collective-permute-done.8.refs_3_
  48.2 3.9 %shard_map.127 = bf16[16,8,768]{2,1,0:T(8,128)(2,1)} custom-call(bf16[528,768]{1,0:T(8,128)(2,1)S(1)} %shard_map.119.refs_0_, bf16[528,768]{1,0:T(8,128)(2,1)S(1)} %collective-permute-done.6.refs_1_, bf16[64,768]{1,0:T(8,128)(2,1)S(1)} %collective-permute-done.7.refs_2_, bf16[64,768]{1,0:T(8,128)(2,1)S(1)} %collective-permute-done.8.refs_3_, ...), custom_call_target="tpu_custom_call" | custom-call | flops 50331648 | bytes 1572864 | tf_op jit(solution)/shard_map/pallas_call | solution.py:499
  (18 shorter events, 0.0 us)
Async XLA Ops:
  2.1 8.4 %collective-permute-start = (bf16[136,768]{1,0:T(8,128)(2,1)}, bf16[136,768]{1,0:T(8,128)(2,1)S(1)}, u32[]{:S(2)}, u32[]{:S(2)}) collective-permute-start(bf16[136,768]{1,0:T(8,128)(2,1)} %shard_map.118.pay_hbm.refs_13_), channel_id=1, source_target_pairs={{0,4},{1,5},{4,8},{5,9},{8,12},{9,13},{12,14},{13,15},{14,10},{15,... | collective-permute-start | bytes 626696 | tf_op jit(solution)/shard_map/ppermute | solution.py:529
  5.2 7.1 %collective-permute-start.3 = (bf16[136,768]{1,0:T(8,128)(2,1)}, bf16[136,768]{1,0:T(8,128)(2,1)S(1)}, u32[]{:S(2)}, u32[]{:S(2)}) collective-permute-start(bf16[136,768]{1,0:T(8,128)(2,1)} %shard_map.118.pay_hbm.refs_13_), channel_id=1, source_target_pairs={{0,2},{1,3},{4,0},{5,1},{8,4},{9,5},{12,8},{13,9},{14,12},{15,13},... | collective-permute-start | bytes 626696 | tf_op jit(solution)/shard_map/ppermute | solution.py:529
  10.5 6.3 %collective-permute-start.1 = (bf16[136,768]{1,0:T(8,128)(2,1)S(1)}, bf16[136,768]{1,0:T(8,128)(2,1)S(1)}, u32[]{:S(2)}, u32[]{:S(2)}) collective-permute-start(bf16[136,768]{1,0:T(8,128)(2,1)S(1)} %collective-permute-done.refs_0_), channel_id=1, source_target_pairs={{0,4},{1,5},{4,8},{5,9},{8,12},{9,13},{12,14},{13,15},{14,10},{15,... | collective-permute-start | bytes 626696 | tf_op jit(solution)/shard_map/ppermute | solution.py:529
  12.3 6.0 %collective-permute-start.4 = (bf16[136,768]{1,0:T(8,128)(2,1)S(1)}, bf16[136,768]{1,0:T(8,128)(2,1)S(1)}, u32[]{:S(2)}, u32[]{:S(2)}) collective-permute-start(bf16[136,768]{1,0:T(8,128)(2,1)S(1)} %collective-permute-done.3.refs_1_), channel_id=1, source_target_pairs={{0,2},{1,3},{4,0},{5,1},{8,4},{9,5},{12,8},{13,9},{14,12},{15,13},... | collective-permute-start | bytes 626696 | tf_op jit(solution)/shard_map/ppermute | solution.py:529
  16.8 7.7 %collective-permute-start.2 = (bf16[136,768]{1,0:T(8,128)(2,1)S(1)}, bf16[136,768]{1,0:T(8,128)(2,1)S(1)}, u32[]{:S(2)}, u32[]{:S(2)}) collective-permute-start(bf16[136,768]{1,0:T(8,128)(2,1)S(1)} %collective-permute-done.1.refs_0_), channel_id=1, source_target_pairs={{0,4},{1,5},{4,8},{5,9},{8,12},{9,13},{12,14},{13,15},{14,10},{15,... | collective-permute-start | bytes 626696 | tf_op jit(solution)/shard_map/ppermute | solution.py:529
  18.3 6.2 %collective-permute-start.5 = (bf16[136,768]{1,0:T(8,128)(2,1)S(1)}, bf16[136,768]{1,0:T(8,128)(2,1)S(1)}, u32[]{:S(2)}, u32[]{:S(2)}) collective-permute-start(bf16[136,768]{1,0:T(8,128)(2,1)S(1)} %collective-permute-done.4.refs_1_), channel_id=1, source_target_pairs={{0,2},{1,3},{4,0},{5,1},{8,4},{9,5},{12,8},{13,9},{14,12},{15,13},... | collective-permute-start | bytes 626696 | tf_op jit(solution)/shard_map/ppermute | solution.py:529
  18.8 1.3 %copy-start = (bf16[768,768]{1,0:T(8,128)(2,1)S(1)}, bf16[768,768]{1,0:T(8,128)(2,1)}, u32[]{:S(2)}) copy-start(bf16[768,768]{1,0:T(8,128)(2,1)} %refs_9_.3) | copy-start | bytes 3538948
  20.1 1.3 %copy-start.3 = (bf16[768,768]{1,0:T(8,128)(2,1)S(1)}, bf16[768,768]{1,0:T(8,128)(2,1)}, u32[]{:S(2)}) copy-start(bf16[768,768]{1,0:T(8,128)(2,1)} %refs_10_.3) | copy-start | bytes 3538948
  22.2 2.3 %copy-start.1 = (bf16[768,768]{1,0:T(8,128)(2,1)S(1)}, bf16[768,768]{1,0:T(8,128)(2,1)}, u32[]{:S(2)}) copy-start(bf16[768,768]{1,0:T(8,128)(2,1)} %refs_9_.3) | copy-start | bytes 3538948
  22.2 15.1 %collective-permute-start.10 = (bf16[528,768]{1,0:T(8,128)(2,1)S(1)}, bf16[528,768]{1,0:T(8,128)(2,1)}, u32[]{:S(2)}, u32[]{:S(2)}) collective-permute-start(bf16[528,768]{1,0:T(8,128)(2,1)S(1)} %shard_map.122.refs_2_), channel_id=1, source_target_pairs={{0,1},{1,0},{2,3},{3,2},{4,5},{5,4},{6,7},{7,6},{8,9},{9,8},{10,11... | collective-permute-start | bytes 2433032 | tf_op jit(solution)/shard_map/ppermute | solution.py:532
  24.0 13.3 %collective-permute-start.11 = (bf16[528,768]{1,0:T(8,128)(2,1)}, bf16[528,768]{1,0:T(8,128)(2,1)}, u32[]{:S(2)}, u32[]{:S(2)}) collective-permute-start(bf16[528,768]{1,0:T(8,128)(2,1)} %shard_map.123.refs_4_), channel_id=1, source_target_pairs={{0,1},{1,0},{2,3},{3,2},{4,5},{5,4},{6,7},{7,6},{8,9},{9,8},{10,11... | collective-permute-start | bytes 2433032 | tf_op jit(solution)/shard_map/ppermute | solution.py:532
  25.3 19.6 %collective-permute-start.6 = (bf16[528,768]{1,0:T(8,128)(2,1)S(1)}, bf16[528,768]{1,0:T(8,128)(2,1)S(1)}, u32[]{:S(2)}, u32[]{:S(2)}) collective-permute-start(bf16[528,768]{1,0:T(8,128)(2,1)S(1)} %shard_map.119.refs_0_), channel_id=1, source_target_pairs={{0,1},{1,0},{2,3},{3,2},{4,5},{5,4},{6,7},{7,6},{8,9},{9,8},{10,11... | collective-permute-start | bytes 2433032 | tf_op jit(solution)/shard_map/ppermute | solution.py:532
  25.4 11.9 %copy-start.13 = (f32[66,16]{0,1:T(8,128)S(1)}, f32[66,16]{0,1:T(8,128)}, u32[]{:S(2)}) copy-start(f32[66,16]{0,1:T(8,128)} %param.23) | copy-start | bytes 12676
  30.1 2.1 %collective-permute-start.9 = (bf16[264,768]{1,0:T(8,128)(2,1)}, bf16[264,768]{1,0:T(8,128)(2,1)S(1)}, u32[]{:S(2)}, u32[]{:S(2)}) collective-permute-start(bf16[264,768]{1,0:T(8,128)(2,1)} %get-tuple-element.17.refs_0_), channel_id=1, source_target_pairs={{0,1},{1,0},{2,3},{3,2},{4,5},{5,4},{6,7},{7,6},{8,9},{9,8},{10,11... | collective-permute-start | bytes 1216520 | tf_op jit(solution)/shard_map/ppermute | solution.py:532
  30.6 5.0 %collective-permute-start.12 = (bf16[72,768]{1,0:T(8,128)(2,1)S(1)}, bf16[72,768]{1,0:T(8,128)(2,1)S(1)}, u32[]{:S(2)}, u32[]{:S(2)}) collective-permute-start(bf16[72,768]{1,0:T(8,128)(2,1)S(1)} %shard_map.125), channel_id=1, source_target_pairs={{0,4},{1,5},{4,8},{5,9},{8,12},{9,13},{12,14},{13,15},{14,10},{15,... | collective-permute-start | bytes 331784 | tf_op jit(solution)/shard_map/ppermute | solution.py:529
  32.2 5.1 %collective-permute-start.7 = (bf16[64,768]{1,0:T(8,128)(2,1)S(1)}, bf16[64,768]{1,0:T(8,128)(2,1)S(1)}, u32[]{:S(2)}, u32[]{:S(2)}) collective-permute-start(bf16[64,768]{1,0:T(8,128)(2,1)S(1)} %shard_map.120), channel_id=1, source_target_pairs={{0,2},{1,3},{4,0},{5,1},{8,4},{9,5},{12,8},{13,9},{14,12},{15,13},... | collective-permute-start | bytes 294920 | tf_op jit(solution)/shard_map/ppermute | solution.py:529
  35.7 9.2 %collective-permute-start.13 = (bf16[72,768]{1,0:T(8,128)(2,1)S(1)}, bf16[72,768]{1,0:T(8,128)(2,1)S(1)}, u32[]{:S(2)}, u32[]{:S(2)}) collective-permute-start(bf16[72,768]{1,0:T(8,128)(2,1)S(1)} %collective-permute-done.12.refs_2_), channel_id=1, source_target_pairs={{0,1},{1,0},{2,3},{3,2},{4,5},{5,4},{6,7},{7,6},{8,9},{9,8},{10,11... | collective-permute-start | bytes 331784 | tf_op jit(solution)/shard_map/ppermute | solution.py:532
  37.3 10.9 %collective-permute-start.8 = (bf16[64,768]{1,0:T(8,128)(2,1)S(1)}, bf16[64,768]{1,0:T(8,128)(2,1)S(1)}, u32[]{:S(2)}, u32[]{:S(2)}) collective-permute-start(bf16[64,768]{1,0:T(8,128)(2,1)S(1)} %collective-permute-done.7.refs_2_), channel_id=1, source_target_pairs={{0,1},{1,0},{2,3},{3,2},{4,5},{5,4},{6,7},{7,6},{8,9},{9,8},{10,11... | collective-permute-start | bytes 294920 | tf_op jit(solution)/shard_map/ppermute | solution.py:532
  37.3 0.9 %copy-start.6 = (bf16[128,768]{1,0:T(8,128)(2,1)S(1)}, bf16[128,768]{1,0:T(8,128)(2,1)}, u32[]{:S(2)}) copy-start(bf16[128,768]{1,0:T(8,128)(2,1)} %get-tuple-element.15.refs_6_.refs_4_) | copy-start | bytes 589828
  38.2 1.0 %copy-start.10 = (bf16[264,768]{1,0:T(8,128)(2,1)S(1)}, bf16[264,768]{1,0:T(8,128)(2,1)}, u32[]{:S(2)}) copy-start(bf16[264,768]{1,0:T(8,128)(2,1)} %get-tuple-element.17.refs_0_) | copy-start | bytes 1216516
  39.2 0.9 %copy-start.11 = (f32[16,16,160]{2,1,0:T(8,128)S(1)}, f32[16,16,160]{2,1,0:T(8,128)}, u32[]{:S(2)}) copy-start(f32[16,16,160]{2,1,0:T(8,128)} %get-tuple-element.18.refs_7_) | copy-start | bytes 491524
  40.2 4.7 %copy-start.2 = (bf16[768,768]{1,0:T(8,128)(2,1)S(1)}, bf16[768,768]{1,0:T(8,128)(2,1)}, u32[]{:S(2)}) copy-start(bf16[768,768]{1,0:T(8,128)(2,1)} %refs_9_.3) | copy-start | bytes 3538948
  40.2 4.7 %copy-start.4 = (bf16[768,768]{1,0:T(8,128)(2,1)S(1)}, bf16[768,768]{1,0:T(8,128)(2,1)}, u32[]{:S(2)}) copy-start(bf16[768,768]{1,0:T(8,128)(2,1)} %refs_10_.3) | copy-start | bytes 3538948
  40.2 4.7 %copy-start.5 = (bf16[136,768]{1,0:T(8,128)(2,1)S(1)}, bf16[136,768]{1,0:T(8,128)(2,1)}, u32[]{:S(2)}) copy-start(bf16[136,768]{1,0:T(8,128)(2,1)} %shard_map.118.pay_hbm.refs_13_) | copy-start | bytes 626692
  40.2 4.7 %copy-start.7 = (f32[128,768]{1,0:T(8,128)S(1)}, f32[128,768]{1,0:T(8,128)}, u32[]{:S(2)}) copy-start(f32[128,768]{1,0:T(8,128)} %get-tuple-element.16.refs_5_) | copy-start | bytes 1179652
  40.2 4.8 %copy-start.12 = (f32[16,16,96]{2,1,0:T(8,128)S(1)}, f32[16,16,96]{2,1,0:T(8,128)}, u32[]{:S(2)}) copy-start(f32[16,16,96]{2,1,0:T(8,128)} %get-tuple-element.22.refs_11_) | copy-start | bytes 294916
  45.0 3.2 %copy-start.8 = (bf16[768,768]{1,0:T(8,128)(2,1)S(1)}, bf16[768,768]{1,0:T(8,128)(2,1)}, u32[]{:S(2)}) copy-start(bf16[768,768]{1,0:T(8,128)(2,1)} %refs_14_.1) | copy-start | bytes 3538948
  45.0 3.2 %copy-start.9 = (bf16[16,8,768]{2,1,0:T(8,128)(2,1)S(1)}, bf16[16,8,768]{2,1,0:T(8,128)(2,1)}, u32[]{:S(2)}) copy-start(bf16[16,8,768]{2,1,0:T(8,128)(2,1)} %refs_13_.1) | copy-start | bytes 589828

commit v5 on v4

--- a/solution.py
+++ b/solution.py
@@ -232,7 +232,7 @@
 
 
 def own_body(
-    steps, chips, early, me_ref, pay_hbm, wq_hbm, wk_hbm, wv_hbm, wg_hbm, pair_hbm, wp_hbm,
+    steps, chips, me_ref, pay_hbm, wq_hbm, wk_hbm, wv_hbm, wg_hbm, pair_hbm, wp_hbm,
     q_ref, gate_ref, kv_ref, first_ref, second_ref,
     pay_ref, wq_ref, wk_ref, wv_ref, wg_ref, pair_ref, wp_ref, sems,
 ):
@@ -251,7 +251,7 @@
     q_ref[...] = matmul(data, wq_ref[...]).astype(BF16)
     copies[2].wait()
     copies[3].wait()
-    pair_rows(steps, chips, early, me_ref[0], pair_ref, wp_ref[...], (first_ref, second_ref))
+    pair_rows(steps, chips, me_ref[0], pair_ref, wp_ref[...], (first_ref, second_ref))
     copies[4].wait()
     kv_ref[pl.ds(0, rows), :] = matmul(data, wk_ref[...]).astype(BF16)
     copies[5].wait()
@@ -279,22 +279,32 @@
     return jnp.where(place < chips // 2, 2 * place, 2 * (chips - 1 - place) + 1)
 
 
-def pair_rows(steps, chips, early, me, pair_ref, weights, out_refs):
-    queries, total, _ = pair_ref.shape
+def pair_rows(steps, chips, me, pair_ref, weights, out_refs):
+    queries, total, channels = pair_ref.shape
+    heads = weights.shape[0]
     tokens = total // len(steps)
     chip = me // CORES
     core = lax.rem(me, CORES)
     place = jnp.where(lax.rem(chip, 2) == 0, chip // 2, chips - 1 - chip // 2)
-    starts = []
-    for r, c in steps:
-        block = ring_chip(place + r, chips) * CORES + lax.rem(core + c, CORES)
-        starts.append(pl.multiple_of(block * tokens, tokens))
-    for i in range(queries):
-        for out_ref, part in zip(out_refs, (starts[:early], starts[early:])):
-            data = jnp.concatenate([pair_ref[i, pl.ds(b, tokens), :] for b in part], axis=0)
-            out_ref[:, i, :] = lax.dot_general(
-                weights, data, (((1,), (1,)), ((), ())), preferred_element_type=F32
-            )
+    lines = heads * queries
+    head = lax.broadcasted_iota(jnp.int32, (heads, lines), 0)
+    lane = lax.broadcasted_iota(jnp.int32, (heads, lines), 1)
+    spread = (lane // queries == head).astype(F32).astype(BF16)
+    wide = lax.dot_general(weights, spread, (((0,), (0,)), ((), ())), preferred_element_type=F32)
+    lane = lax.broadcasted_iota(jnp.int32, (channels, lines), 1) % queries
+    wide = jnp.concatenate(
+        [jnp.where(lane == i, wide, 0.0).astype(BF16) for i in range(queries)], axis=0
+    )
+    at = 0
+    for out_ref in out_refs:
+        data = []
+        for r, c in steps[at : at + out_ref.shape[0] // tokens]:
+            block = ring_chip(place + r, chips) * CORES + lax.rem(core + c, CORES)
+            start = pl.multiple_of(block * tokens, tokens)
+            rows = [pair_ref[i, pl.ds(start, tokens), :] for i in range(queries)]
+            data.append(jnp.concatenate(rows, axis=1))
+        at += len(data)
+        out_ref[...] = matmul(jnp.concatenate(data, axis=0), wide)
 
 
 def kv_count(ref, rows):
@@ -310,8 +320,8 @@
 
 
 def full_bias(own, metas, tokens, pair_ref, tab_ref, pad_ref):
-    heads, _, total = pair_ref.shape
-    bins = tab_ref.shape[1]
+    total = pair_ref.shape[0]
+    heads, bins = tab_ref.shape
     reach = (bins - 2) // 2
     wide = -(-total // LANES) * LANES
     slot = lax.broadcasted_iota(jnp.int32, (META_ROWS, wide), 1) // tokens
@@ -333,7 +343,7 @@
     res_keys = keys[1:2, :] * RADIX + keys[2:3, :]
     offset = jnp.clip(res_q - res_keys, -reach, reach) + reach
     bucket = jnp.where(chain_q == keys[0:1, :], offset, float(bins - 1)).astype(jnp.int32)
-    mask = (keys[3:4, :total] - 1.0) * MASK_PENALTY
+    mask = (keys[3:4, :] - 1.0) * MASK_PENALTY
     pad_ref[...] = jnp.zeros_like(pad_ref)
     pad_ref[:, pl.ds(0, bins)] = tab_ref[...]
     out = []
@@ -345,152 +355,122 @@
             )
             for at in range(0, wide, LANES)
         ]
-        rel = jnp.concatenate(rel, axis=1)[:, :total] if len(rel) > 1 else rel[0][:, :total]
-        out.append(pair_ref[h] + rel + mask)
-    return jnp.concatenate(out, axis=0)
-
-
-def head_spans(width, hs):
-    return [((t * TILE) // hs, ((t + 1) * TILE - 1) // hs) for t in range(width // TILE)]
-
-
-def score_rows(q, keys, bias, heads, scale):
-    tokens, width = q.shape
+        out.append((jnp.concatenate(rel, axis=1) if len(rel) > 1 else rel[0]) + mask)
+    return pair_ref[...] + jnp.transpose(jnp.concatenate(out, axis=0))[:total]
+
+
+def head_windows(width, hs):
+    windows, h = [], 0
+    while h * hs < width:
+        start = min(h * hs // LANES * LANES, width - TILE)
+        last = min((start + TILE) // hs, width // hs) - 1
+        windows.append((h, last, start))
+        h = last + 1
+    return windows
+
+
+def spread_body(samples, heads, q_ref, out_ref):
+    rows, width = q_ref.shape
+    tokens = rows // samples
     hs = width // heads
-    lane_head = lax.broadcasted_iota(jnp.int32, (tokens, width), 1) // hs
-    per_head = [None] * heads
-    for t, (h0, h1) in enumerate(head_spans(width, hs)):
-        cut = slice(t * TILE, (t + 1) * TILE)
-        masked = [
-            jnp.where(lane_head[:, cut] == h, q[:, cut], 0.0).astype(BF16)
-            for h in range(h0, h1 + 1)
-        ]
-        st = lax.dot_general(
-            jnp.concatenate(masked, axis=0),
-            keys[:, cut],
-            (((1,), (1,)), ((), ())),
+    lines = heads * tokens
+    token = lax.broadcasted_iota(jnp.int32, (tokens, lines), 0)
+    lane = lax.broadcasted_iota(jnp.int32, (tokens, lines), 1)
+    spread = (lane % tokens == token).astype(F32).astype(BF16)
+    feature = lax.broadcasted_iota(jnp.int32, (width, lines), 0)
+    lane = lax.broadcasted_iota(jnp.int32, (width, lines), 1)
+    inside = feature // hs == lane // tokens
+    for s in range(samples):
+        wide = lax.dot_general(
+            q_ref[pl.ds(s * tokens, tokens), :], spread, (((0,), (0,)), ((), ())),
             preferred_element_type=F32,
         )
-        for h in range(h0, h1 + 1):
-            part = st[(h - h0) * tokens : (h - h0 + 1) * tokens]
-            per_head[h] = part if per_head[h] is None else per_head[h] + part
-    return jnp.concatenate(per_head, axis=0) * scale + bias
-
-
-def gather_keys(kv_refs, rows, at, tokens):
-    keys, values = [], []
+        out_ref[pl.ds(s * width, width), :] = jnp.where(inside, wide, 0.0).astype(BF16)
+
+
+def gather(kv_refs, rows, at, tokens, values):
+    found = []
     for r in kv_refs:
-        n = r.shape[0] // (2 * rows + META_ROWS)
-        for u in range(n):
-            keys.append(r[pl.ds(u * rows + at, tokens), :])
-            values.append(r[pl.ds((n + u) * rows + at, tokens), :])
-    return keys, values
-
-
-def early_body(samples, heads, scale, *refs):
-    q_ref, pair_ref, tab_ref, sum_ref, top_ref, mass_ref, pad_ref = refs[-7:]
+        n = kv_count(r, rows)
+        first = n if values else 0
+        found += [r[pl.ds((first + u) * rows + at, tokens), :] for u in range(n)]
+    return found
+
+
+def early_body(samples, scale, *refs):
+    q_ref, pair_ref, tab_ref, exp_ref, top_ref, mass_ref, pad_ref = refs[-7:]
     kv_refs = refs[:-7]
-    rows, width = q_ref.shape
-    tokens = rows // samples
-    spans = head_spans(width, width // heads)
-    height = sum(h1 - h0 + 1 for h0, h1 in spans) * tokens
+    count, lines = pair_ref.shape
+    tokens = lines // tab_ref.shape[0]
+    rows = tokens * samples
+    width = kv_refs[0].shape[1]
     metas = kv_metas(kv_refs, rows)
     bias = full_bias(metas[0], metas, tokens, pair_ref, tab_ref, pad_ref)
     for s in range(samples):
-        keys, values = gather_keys(kv_refs, rows, s * tokens, tokens)
-        keys, values = jnp.concatenate(keys, axis=0), jnp.concatenate(values, axis=0)
-        q = q_ref[pl.ds(s * tokens, tokens), :].astype(F32)
-        scores = score_rows(q, keys, bias, heads, scale)
-        top = jnp.max(scores, axis=-1, keepdims=True)
-        probs = jnp.exp(scores - top)
-        mass = jnp.sum(probs, axis=-1, keepdims=True)
-        here = pl.ds(s * heads * tokens, heads * tokens)
-        top_ref[here, :] = jnp.broadcast_to(top, (heads * tokens, top_ref.shape[1]))
-        mass_ref[here, :] = jnp.broadcast_to(mass, (heads * tokens, mass_ref.shape[1]))
-        probs = probs.astype(BF16)
-        at = s * height
-        for t, (h0, h1) in enumerate(spans):
-            part = probs[h0 * tokens : (h1 + 1) * tokens]
-            got = matmul(part, values[:, t * TILE : (t + 1) * TILE])
-            sum_ref[pl.ds(at, got.shape[0]), :] = got
-            at += got.shape[0]
-
-
-def attend_rows(first, count, heads, scale, kv_refs, mine, other, bias, shared):
-    q_ref, gate_ref, sum_ref, top_ref, mass_ref, wk_ref, wv_ref = shared
-    rows, width = gate_ref.shape
-    half = mine.shape[0]
-    tokens = half // count
+        keys = jnp.concatenate(gather(kv_refs, rows, s * tokens, tokens, False), axis=0)
+        scores = matmul(keys, q_ref[pl.ds(s * width, width), :]) * scale + bias
+        top = jnp.max(scores, axis=0, keepdims=True)
+        weights = jnp.exp(scores - top)
+        top_ref[pl.ds(s, 1), :] = top
+        mass_ref[pl.ds(s, 1), :] = jnp.sum(weights, axis=0, keepdims=True)
+        exp_ref[pl.ds(s * count, count), :] = weights
+
+
+def finish_body(heads, scale, split, *refs):
+    (
+        q_ref, gate_ref, exp_ref, top_ref, mass_ref, wk_ref, wv_ref, pair_ref, tab_ref, pay_ref,
+        single_ref, wo_ref, out_ref, pad_ref, weight_ref,
+    ) = refs[-15:]
+    kv_refs, lasts = refs[:-19], refs[-19:-15]
+    tokens, samples, width = single_ref.shape
+    rows = tokens * samples
+    half = rows // 2
     hs = width // heads
-    data = jnp.concatenate([mine, other], axis=0)
+    metas = kv_metas(kv_refs[split:], rows) + [r[pl.ds(half, META_ROWS), :] for r in (lasts[0], lasts[2])]
+    own = pay_ref[pl.ds(rows, META_ROWS), :]
+    data = jnp.concatenate([r[pl.ds(0, half), :] for r in lasts], axis=0)
     k_last = matmul(data, wk_ref[...]).astype(BF16)
     v_last = matmul(data, wv_ref[...]).astype(BF16)
+    bias = full_bias(own, metas, tokens, pair_ref, tab_ref, pad_ref)
+    count = exp_ref.shape[0] // samples
     lane_head = lax.broadcasted_iota(jnp.int32, (tokens, width), 1) // hs
-    spans = head_spans(width, hs)
-    height = sum(h1 - h0 + 1 for h0, h1 in spans) * tokens
+    lines = heads * tokens
+    for s in range(samples):
+        new = [slice(u * rows + s * tokens, u * rows + (s + 1) * tokens) for u in range(2)]
+        keys = gather(kv_refs[split:], rows, s * tokens, tokens, False)
+        keys = jnp.concatenate(keys + [k_last[n] for n in new], axis=0)
+        scores = matmul(keys, q_ref[pl.ds(s * width, width), :]) * scale + bias
+        before = top_ref[pl.ds(s, 1), :]
+        top = jnp.maximum(jnp.max(scores, axis=0, keepdims=True), before)
+        shrink = jnp.exp(before - top)
+        late = jnp.exp(scores - top)
+        mass = jnp.sum(late, axis=0, keepdims=True) + mass_ref[pl.ds(s, 1), :] * shrink
+        inv = 1.0 / mass
+        old = exp_ref[pl.ds(s * count, count), :] * (shrink * inv)
+        weights = jnp.concatenate([old, late * inv], axis=0)
+        weight_ref[pl.ds(s * lines, lines), :] = jnp.transpose(weights).astype(BF16)
     gated = []
-    for s in range(count):
-        keys, values = gather_keys(kv_refs, rows, (first + s) * tokens, tokens)
-        for u in range(2):
-            keys.append(k_last[u * half + s * tokens : u * half + (s + 1) * tokens])
-            values.append(v_last[u * half + s * tokens : u * half + (s + 1) * tokens])
-        keys, values = jnp.concatenate(keys, axis=0), jnp.concatenate(values, axis=0)
-        q = q_ref[pl.ds((first + s) * tokens, tokens), :].astype(F32)
-        scores = score_rows(q, keys, bias, heads, scale)
-        here = pl.ds((first + s) * heads * tokens, heads * tokens)
-        top_before = top_ref[here, :][:, :1]
-        top = jnp.maximum(jnp.max(scores, axis=-1, keepdims=True), top_before)
-        shrink = jnp.exp(top_before - top)
-        probs = jnp.exp(scores - top)
-        mass = jnp.sum(probs, axis=-1, keepdims=True) + mass_ref[here, :][:, :1] * shrink
-        inv = 1.0 / mass
-        probs = probs.astype(BF16)
-        shrink = shrink * inv
-        attended = []
-        at = (first + s) * height
-        for t, (h0, h1) in enumerate(spans):
-            cut = slice(t * TILE, (t + 1) * TILE)
-            span = slice(h0 * tokens, (h1 + 1) * tokens)
-            ot = matmul(probs[span], values[:, cut]) * inv[span]
-            ot = ot + sum_ref[pl.ds(at, ot.shape[0]), :] * shrink[span]
-            at += ot.shape[0]
-            got = ot[:tokens]
-            for h in range(h0 + 1, h1 + 1):
-                part = ot[(h - h0) * tokens : (h - h0 + 1) * tokens]
-                got = jnp.where(lane_head[:, cut] == h, part, got)
-            attended.append(got)
-        attended = jnp.concatenate(attended, axis=1)
-        gated.append((gate_ref[pl.ds((first + s) * tokens, tokens), :] * attended).astype(BF16))
-    return jnp.concatenate(gated, axis=0)
-
-
-def attend_body(count, samples, heads, scale, *refs):
-    pair_ref, tab_ref, pay_ref, out_ref, bias_ref, pad_ref = refs[-6:]
-    shared = refs[-13:-6]
-    kv_refs, mine, other = refs[:-15], refs[-15], refs[-14]
-    rows = shared[0].shape[0]
-    tokens = rows // samples
-    half = count * tokens
-    metas = kv_metas(kv_refs, rows)
-    metas += [m[pl.ds(half, META_ROWS), :] for m in (mine, other)]
-    own = pay_ref[pl.ds(rows, META_ROWS), :]
-    bias = full_bias(own, metas, tokens, pair_ref, tab_ref, pad_ref)
-    bias_ref[...] = bias
-    mine, other = mine[pl.ds(0, half), :], other[pl.ds(0, half), :]
-    out_ref[...] = attend_rows(0, count, heads, scale, kv_refs, mine, other, bias, shared)
-
-
-def finish_body(count, samples, heads, scale, *refs):
-    bias_ref, done, single_ref, wo_ref, out_ref = refs[-5:]
-    shared = refs[-12:-5]
-    kv_refs, mine, other = refs[:-14], refs[-14], refs[-13]
-    tokens, samples, width = single_ref.shape
-    gated = attend_rows(
-        samples - count, count, heads, scale, kv_refs, mine[...], other[...],
-        bias_ref[...], shared,
-    )
-    gated = jnp.concatenate([done[...], gated], axis=0)
-    gated = matmul(token_major(tokens, samples), gated).astype(BF16)
+    for s in range(samples):
+        new = [slice(u * rows + s * tokens, u * rows + (s + 1) * tokens) for u in range(2)]
+        values = gather(kv_refs, rows, s * tokens, tokens, True)
+        values = jnp.concatenate(values + [v_last[n] for n in new], axis=0)
+        pieces = {}
+        for h0, h1, start in head_windows(width, hs):
+            here = pl.ds(s * lines + h0 * tokens, (h1 + 1 - h0) * tokens)
+            ot = matmul(weight_ref[here, :], values[:, start : start + TILE])
+            for first in range(start, start + TILE, LANES):
+                for h in range(h0, h1 + 1):
+                    if (h + 1) * hs <= first or h * hs >= first + LANES:
+                        continue
+                    lanes = slice(first - start, first - start + LANES)
+                    part = ot[(h - h0) * tokens : (h + 1 - h0) * tokens, lanes]
+                    if first in pieces:
+                        mine = lane_head[:, first : first + LANES] == h
+                        part = jnp.where(mine, part, pieces[first])
+                    pieces[first] = part
+        attended = jnp.concatenate([pieces[at] for at in sorted(pieces)], axis=1)
+        gated.append((gate_ref[pl.ds(s * tokens, tokens), :] * attended).astype(BF16))
+    gated = matmul(token_major(tokens, samples), jnp.concatenate(gated, axis=0)).astype(BF16)
     out = matmul(gated, wo_ref[...]).reshape(tokens, samples, width)
     out_ref[...] = (single_ref[...].astype(F32) + out).astype(BF16)
 
@@ -577,11 +557,11 @@
     early = len(steps) - 3 * CORES
     split = 2 * (half - 1)
     pair_shapes = tuple(
-        jax.ShapeDtypeStruct((heads, tokens, n * tokens), F32) for n in (early, len(steps) - early)
+        jax.ShapeDtypeStruct((n * tokens, heads * tokens), F32) for n in (early, len(steps) - early)
     )
     weight = pltpu.VMEM((width, width), BF16)
     query, gate, kv_own, pair_first, pair_second = call(
-        functools.partial(own_body, steps, chips, early),
+        functools.partial(own_body, steps, chips),
         (
             jax.ShapeDtypeStruct((rows, width), BF16),
             jax.ShapeDtypeStruct((rows, width), F32),
@@ -618,40 +598,39 @@
         kvs.append(flip(kvs[-1]))
         cw, ccw = cw_next, ccw_next
     scale = 1.0 / math.sqrt(width // heads)
-    spans = head_spans(width, width // heads)
-    height = sum(h1 - h0 + 1 for h0, h1 in spans) * tokens * samples
-    state = jax.ShapeDtypeStruct((samples * heads * tokens, 128), F32)
+    lines = heads * tokens
+    state = jax.ShapeDtypeStruct((samples, lines), F32)
+    query = call(
+        functools.partial(spread_body, samples, heads),
+        jax.ShapeDtypeStruct((samples * width, lines), BF16),
+        (query,),
+        flops=2 * rows * width * lines,
+        moved=2 * samples * width * lines,
+    )
     table = rel_table.T
     pad = [pltpu.VMEM((heads, LANES), F32)]
     limit = (10 << 20) + 4 * samples * total * width
     before = call(
-        functools.partial(early_body, samples, heads, scale),
-        (jax.ShapeDtypeStruct((height, TILE), F32), state, state),
+        functools.partial(early_body, samples, scale),
+        (jax.ShapeDtypeStruct((samples * early * tokens, lines), F32), state, state),
         (*kvs[:split], query, pair_first, table),
         flops=4 * rows * early * tokens * width,
         moved=4 * samples * early * tokens * width,
         limit=limit,
         scratch=pad,
     )
-    count = samples // 2
-    common = dict(flops=2 * rows * total * width, moved=samples * total * width, limit=limit)
-    shared = (query, gate, *before, w_key, w_value)
-    last = (len(steps) - early) * tokens
-    gated, bias = call(
-        functools.partial(attend_body, count, samples, heads, scale),
+    cw_other, ccw_other = flip(cw), flip(ccw)
+    return call(
+        functools.partial(finish_body, heads, scale, split),
+        jax.ShapeDtypeStruct(single.shape, BF16),
         (
-            jax.ShapeDtypeStruct((rows // 2, width), BF16),
-            jax.ShapeDtypeStruct((heads * tokens, last), F32),
+            *kvs, cw, ccw, cw_other, ccw_other, query, gate, *before, w_key, w_value,
+            pair_second, table, payload, single, w_out,
         ),
-        (*kvs[split:], cw, flip(cw), *shared, pair_second, table, payload),
-        scratch=pad,
-        **common,
-    )
-    return call(
-        functools.partial(finish_body, count, samples, heads, scale),
-        jax.ShapeDtypeStruct(single.shape, BF16),
-        (*kvs[split:], ccw, flip(ccw), *shared, bias, gated, single, w_out),
-        **common,
+        flops=4 * rows * total * width,
+        moved=2 * samples * total * width,
+        limit=limit,
+        scratch=[*pad, pltpu.VMEM((samples * lines, total), BF16)],
     )
 
 

time: 52.4 us -> 46.6 us (0.89)
  Pallas kernels: 21.8 us -> 16.3 us
  waiting for transfers between devices: 13.2 us -> 14 us
  local copies, waits for them, and re-layouts: 5.46 us -> 4.74 us
    pallas_call x10, Pallas kernels: 21.8 us -> 16.3 us  [call(): pl.pallas_call(body, out_shape=out_shape, in_specs=in_specs or [VMEM] * l...]
    unnamed x28 -> x30, local copies, waits for them, and re-layouts: 5.46 us -> 4.74 us
  transfers between devices with their start and end apart: 14 -> 14, of which waited for: 4 -> 6; matrix products, arithmetic and copies ran while one was open for 0% -> 0% of each run, Pallas kernels for 30% -> 21%
where the time goes in v5:
time: 46.6 us; the launch traced here: 46.3 us
  Pallas kernels  16.3 us (35%)
  waiting for transfers between devices  14 us (30%)
  starting transfers between devices  11.1 us (24%)
  local copies, waits for them, and re-layouts  4.74 us (10%)
    pallas_call x10, Pallas kernels, call(): pl.pallas_call(body, out_shape=out_shape, in_specs=in_specs or [VMEM] * l...  16.3 us
    ppermute x8, waiting for transfers between devices, ring(): return lax.ppermute(value, 'tok', pairs)  13.5 us
    ppermute x8, starting transfers between devices, ring(): return lax.ppermute(value, 'tok', pairs)  9.88 us
    unnamed x30, local copies, waits for them, and re-layouts  4.74 us
    ppermute x6, starting transfers between devices, flip(): return lax.ppermute(value, 'tok', [(d, d ^ 1) for d in range(devices)])  1.22 us
  transfers between devices with their start and end apart: 14, of which 6 were waited for; matrix products, arithmetic and copies ran while one was open for 0% of the time, Pallas kernels for 21%

profile of v5, /device:TPU:0, one launch (start us, length us, event | category | flops | bytes accessed | tf_op | source)
XLA Modules:
  0.0 46.3 jit_solution(2513520792481659903)
XLA Ops:
  0.0 2.1 %shard_map.118.pay_hbm.refs_21_ = bf16[136,768]{1,0:T(8,128)(2,1)} custom-call(bf16[16,8,768]{2,1,0:T(8,128)(2,1)} %refs_22_.1, s32[1,16]{1,0:T(1,128)} %bitcast.9, s32[1,16]{1,0:T(1,128)} %bitcast.10, s32[1,16]{1,0:T(1,128)} %bitcast.11), custom_call_target="tpu_custom_call" | custom-call | flops 1572864 | bytes 393216 | tf_op jit(solution)/shard_map/pallas_call | solution.py:479
  2.1 3.0 %collective-permute-start.2 = (bf16[136,768]{1,0:T(8,128)(2,1)}, bf16[136,768]{1,0:T(8,128)(2,1)S(1)}, u32[]{:S(2)}, u32[]{:S(2)}) collective-permute-start(bf16[136,768]{1,0:T(8,128)(2,1)} %shard_map.118.pay_hbm.refs_21_), channel_id=1, source_target_pairs={{0,2},{1,3},{4,0},{5,1},{8,4},{9,5},{12,8},{13,9},{14,12},{15,13},... | collective-permute-start | bytes 626696 | tf_op jit(solution)/shard_map/ppermute | solution.py:509
  5.1 0.1 collective-permute-start.1
  5.3 5.3 %collective-permute-done.2.refs_1_ = bf16[136,768]{1,0:T(8,128)(2,1)S(1)} collective-permute-done((bf16[136,768]{1,0:T(8,128)(2,1)}, bf16[136,768]{1,0:T(8,128)(2,1)S(1)}, u32[]{:S(2)}, u32[]{:S(2)}) %collective-permute-start.2) | collective-permute-done | bytes 208928 | tf_op jit(solution)/shard_map/ppermute | solution.py:509
  10.6 1.7 %collective-permute-start.5 = (bf16[136,768]{1,0:T(8,128)(2,1)S(1)}, bf16[136,768]{1,0:T(8,128)(2,1)S(1)}, u32[]{:S(2)}, u32[]{:S(2)}) collective-permute-start(bf16[136,768]{1,0:T(8,128)(2,1)S(1)} %collective-permute-done.2.refs_1_), channel_id=1, source_target_pairs={{0,2},{1,3},{4,0},{5,1},{8,4},{9,5},{12,8},{13,9},{14,12},{15,13},... | collective-permute-start | bytes 626696 | tf_op jit(solution)/shard_map/ppermute | solution.py:509
  12.3 0.0 collective-permute-done.1.refs_0_
  12.3 0.3 collective-permute-start.4
  12.6 4.3 %collective-permute-done.5.refs_1_ = bf16[136,768]{1,0:T(8,128)(2,1)S(1)} collective-permute-done((bf16[136,768]{1,0:T(8,128)(2,1)S(1)}, bf16[136,768]{1,0:T(8,128)(2,1)S(1)}, u32[]{:S(2)}, u32[]{:S(2)}) %collective-permute-start.5) | collective-permute-done | bytes 208928 | tf_op jit(solution)/shard_map/ppermute | solution.py:509
  16.9 1.4 %collective-permute-start.8 = (bf16[136,768]{1,0:T(8,128)(2,1)S(1)}, bf16[136,768]{1,0:T(8,128)(2,1)S(1)}, u32[]{:S(2)}, u32[]{:S(2)}) collective-permute-start(bf16[136,768]{1,0:T(8,128)(2,1)S(1)} %collective-permute-done.5.refs_1_), channel_id=1, source_target_pairs={{0,2},{1,3},{4,0},{5,1},{8,4},{9,5},{12,8},{13,9},{14,12},{15,13},... | collective-permute-start | bytes 626696 | tf_op jit(solution)/shard_map/ppermute | solution.py:509
  18.3 0.0 collective-permute-done.4.refs_0_
  18.3 0.6 %collective-permute-start.7 = (bf16[136,768]{1,0:T(8,128)(2,1)S(1)}, bf16[136,768]{1,0:T(8,128)(2,1)S(1)}, u32[]{:S(2)}, u32[]{:S(2)}) collective-permute-start(bf16[136,768]{1,0:T(8,128)(2,1)S(1)} %collective-permute-done.4.refs_0_), channel_id=1, source_target_pairs={{0,4},{1,5},{4,8},{5,9},{8,12},{9,13},{12,14},{13,15},{14,10},{15,... | collective-permute-start | bytes 626696 | tf_op jit(solution)/shard_map/ppermute | solution.py:509
  18.9 1.3 %copy-done = bf16[768,768]{1,0:T(8,128)(2,1)S(1)} copy-done((bf16[768,768]{1,0:T(8,128)(2,1)S(1)}, bf16[768,768]{1,0:T(8,128)(2,1)}, u32[]{:S(2)}) %copy-start) | copy-done | bytes 1179672
  20.2 1.3 %copy-done.2 = bf16[768,768]{1,0:T(8,128)(2,1)S(1)} copy-done((bf16[768,768]{1,0:T(8,128)(2,1)S(1)}, bf16[768,768]{1,0:T(8,128)(2,1)}, u32[]{:S(2)}) %copy-start.2) | copy-done | bytes 1179672
  21.5 0.8 %shard_map.120.refs_2_ = bf16[528,768]{1,0:T(8,128)(2,1)S(1)} custom-call(bf16[136,768]{1,0:T(8,128)(2,1)S(1)} %collective-permute-done.1.refs_0_, bf16[136,768]{1,0:T(8,128)(2,1)S(1)} %collective-permute-done.2.refs_1_, bf16[768,768]{1,0:T(8,128)(2,1)S(1)} %copy-done, bf16[768,768]{1,0:T(8,128)(2,1)S(1)} %copy-done.2), custom_call_target="tpu_custom_call" | custom-call | flops 603979776 | bytes 3538944 | tf_op jit(solution)/shard_map/pallas_call | solution.py:479
  22.3 0.1 collective-permute-start.3
  22.3 0.8 %shard_map.121.refs_4_ = bf16[528,768]{1,0:T(8,128)(2,1)S(1)} custom-call(bf16[136,768]{1,0:T(8,128)(2,1)S(1)} %collective-permute-done.4.refs_0_, bf16[136,768]{1,0:T(8,128)(2,1)S(1)} %collective-permute-done.5.refs_1_, bf16[768,768]{1,0:T(8,128)(2,1)S(1)} %copy-done, bf16[768,768]{1,0:T(8,128)(2,1)S(1)} %copy-done.2), custom_call_target="tpu_custom_call" | custom-call | flops 603979776 | bytes 3538944 | tf_op jit(solution)/shard_map/pallas_call | solution.py:479
  23.1 0.6 %collective-permute-start.6 = (bf16[528,768]{1,0:T(8,128)(2,1)S(1)}, bf16[528,768]{1,0:T(8,128)(2,1)S(1)}, u32[]{:S(2)}, u32[]{:S(2)}) collective-permute-start(bf16[528,768]{1,0:T(8,128)(2,1)S(1)} %shard_map.121.refs_4_), channel_id=1, source_target_pairs={{0,1},{1,0},{2,3},{3,2},{4,5},{5,4},{6,7},{7,6},{8,9},{9,8},{10,11... | collective-permute-start | bytes 2433032 | tf_op jit(solution)/shard_map/ppermute | solution.py:512
  23.7 0.0 collective-permute-done.8.refs_1_.in_ref
  23.7 0.4 collective-permute-done.7.refs_0_.in_ref
  24.1 1.7 %shard_map.122.refs_6_ = bf16[528,768]{1,0:T(8,128)(2,1)} custom-call(bf16[136,768]{1,0:T(8,128)(2,1)S(1)} %collective-permute-done.7.refs_0_.in_ref, bf16[136,768]{1,0:T(8,128)(2,1)S(1)} %collective-permute-done.8.refs_1_.in_ref, bf16[768,768]{1,0:T(8,128)(2,1)S(1)} %copy-done, bf16[768,768]{1,0:T(8,128)(2,1)S(1)} %copy-done.2), custom_call_target="tpu_custom_call" | custom-call | flops 603979776 | bytes 3538944 | tf_op jit(solution)/shard_map/pallas_call | solution.py:479
  25.8 0.0 collective-permute-start.9
  25.8 4.5 %shard_map.119 = (bf16[128,768]{1,0:T(8,128)(2,1)}, f32[128,768]{1,0:T(8,128)}, bf16[264,768]{1,0:T(8,128)(2,1)}, f32[160,256]{1,0:T(8,128)}, f32[96,256]{1,0:T(8,128)}) custom-call(s32[1]{0:T(128)} %bitcast.me_ref, bf16[136,768]{1,0:T(8,128)(2,1)} %shard_map.118.pay_hbm.refs_21_, bf16[768,768]{1,0:T(8,128)(2,1)} %wq_hbm.1, bf16[768,768]{1,0:T(8,128)(2,1)} %refs_17_.1, ...), custom_call_target="tpu_custom_call" | custom-call | flops 620756992 | bytes 6946816 | tf_op jit(solution)/shard_map/pallas_call | solution.py:479
  30.4 0.6 %collective-permute-start = (bf16[264,768]{1,0:T(8,128)(2,1)}, bf16[264,768]{1,0:T(8,128)(2,1)S(1)}, u32[]{:S(2)}, u32[]{:S(2)}) collective-permute-start(bf16[264,768]{1,0:T(8,128)(2,1)} %get-tuple-element.13.refs_0_), channel_id=1, source_target_pairs={{0,1},{1,0},{2,3},{3,2},{4,5},{5,4},{6,7},{7,6},{8,9},{9,8},{10,11... | collective-permute-start | bytes 1216520 | tf_op jit(solution)/shard_map/ppermute | solution.py:512
  31.0 1.1 %collective-permute-start.10 = (bf16[72,768]{1,0:T(8,128)(2,1)S(1)}, bf16[72,768]{1,0:T(8,128)(2,1)S(1)}, u32[]{:S(2)}, u32[]{:S(2)}) collective-permute-start(bf16[72,768]{1,0:T(8,128)(2,1)S(1)} %shard_map.123), channel_id=1, source_target_pairs={{0,4},{1,5},{4,8},{5,9},{8,12},{9,13},{12,14},{13,15},{14,10},{15,... | collective-permute-start | bytes 331784 | tf_op jit(solution)/shard_map/ppermute | solution.py:509
  32.1 0.5 %collective-permute-done.refs_1_ = bf16[264,768]{1,0:T(8,128)(2,1)S(1)} collective-permute-done((bf16[264,768]{1,0:T(8,128)(2,1)}, bf16[264,768]{1,0:T(8,128)(2,1)S(1)}, u32[]{:S(2)}, u32[]{:S(2)}) %collective-permute-start) | collective-permute-done | bytes 405536 | tf_op jit(solution)/shard_map/ppermute | solution.py:512
  32.5 1.6 %collective-permute-start.11 = (bf16[64,768]{1,0:T(8,128)(2,1)S(1)}, bf16[64,768]{1,0:T(8,128)(2,1)S(1)}, u32[]{:S(2)}, u32[]{:S(2)}) collective-permute-start(bf16[64,768]{1,0:T(8,128)(2,1)S(1)} %shard_map.124), channel_id=1, source_target_pairs={{0,2},{1,3},{4,0},{5,1},{8,4},{9,5},{12,8},{13,9},{14,12},{15,13},... | collective-permute-start | bytes 294920 | tf_op jit(solution)/shard_map/ppermute | solution.py:509
  34.1 1.9 %collective-permute-done.10.refs_8_ = bf16[72,768]{1,0:T(8,128)(2,1)S(1)} collective-permute-done((bf16[72,768]{1,0:T(8,128)(2,1)S(1)}, bf16[72,768]{1,0:T(8,128)(2,1)S(1)}, u32[]{:S(2)}, u32[]{:S(2)}) %collective-permute-start.10) | collective-permute-done | bytes 110624 | tf_op jit(solution)/shard_map/ppermute | solution.py:509
  36.0 0.0 collective-permute-start.12
  36.0 1.6 %collective-permute-done.11.refs_9_ = bf16[64,768]{1,0:T(8,128)(2,1)S(1)} collective-permute-done((bf16[64,768]{1,0:T(8,128)(2,1)S(1)}, bf16[64,768]{1,0:T(8,128)(2,1)S(1)}, u32[]{:S(2)}, u32[]{:S(2)}) %collective-permute-start.11) | collective-permute-done | bytes 98336 | tf_op jit(solution)/shard_map/ppermute | solution.py:509
  37.6 0.9 %copy-done.11 = bf16[128,768]{1,0:T(8,128)(2,1)S(1)} copy-done((bf16[128,768]{1,0:T(8,128)(2,1)S(1)}, bf16[128,768]{1,0:T(8,128)(2,1)}, u32[]{:S(2)}) %copy-start.11) | copy-done | bytes 196632
  38.5 1.0 %shard_map.125.refs_6_.refs_12_ = bf16[6144,256]{1,0:T(8,128)(2,1)S(1)} custom-call(bf16[128,768]{1,0:T(8,128)(2,1)S(1)} %copy-done.11), custom_call_target="tpu_custom_call" | custom-call | flops 50331648 | bytes 3145728 | tf_op jit(solution)/shard_map/pallas_call | solution.py:479
  39.6 0.0 collective-permute-done.3.refs_3_
  39.6 0.0 collective-permute-done.6.refs_5_
  39.6 0.0 copy-start.1
  39.6 0.0 copy-start.3
  39.7 0.0 copy-start.6
  39.7 0.0 copy-start.9
  39.7 0.9 %shard_map.126 = (f32[1280,256]{1,0:T(8,128)S(1)}, f32[8,256]{1,0:T(8,128)S(1)}, f32[8,256]{1,0:T(8,128)S(1)}) custom-call(bf16[264,768]{1,0:T(8,128)(2,1)S(1)} %copy-done.5, bf16[264,768]{1,0:T(8,128)(2,1)S(1)} %collective-permute-done.refs_1_, bf16[528,768]{1,0:T(8,128)(2,1)S(1)} %shard_map.120.refs_2_, ...), custom_call_target="tpu_custom_call" | custom-call | flops 62914560 | bytes 3932160 | tf_op jit(solution)/shard_map/pallas_call | solution.py:479
  40.6 0.0 collective-permute-done.13.refs_11_
  40.6 0.0 collective-permute-done.12.refs_10_
  40.6 0.0 collective-permute-done.9.refs_7_
  40.6 0.3 copy-done.1
  40.9 0.4 copy-done.3
  41.3 0.0 copy-done.4
  41.3 0.4 copy-done.6
  41.7 0.0 copy-done.9
  41.7 0.1 copy-done.10
  41.8 4.5 %shard_map.127 = bf16[16,8,768]{2,1,0:T(8,128)(2,1)} custom-call(bf16[264,768]{1,0:T(8,128)(2,1)S(1)} %copy-done.5, bf16[264,768]{1,0:T(8,128)(2,1)S(1)} %collective-permute-done.refs_1_, bf16[528,768]{1,0:T(8,128)(2,1)S(1)} %shard_map.120.refs_2_, bf16[528,768]{1,0:T(8,128)(2,1)S(1)} %collective-permute-done.3.refs_3_, ...), custom_call_target="tpu_custom_call" | custom-call | flops 100663296 | bytes 3145728 | tf_op jit(solution)/shard_map/pallas_call | solution.py:479
  (20 shorter events, 0.0 us)
Async XLA Ops:
  2.1 8.5 %collective-permute-start.2 = (bf16[136,768]{1,0:T(8,128)(2,1)}, bf16[136,768]{1,0:T(8,128)(2,1)S(1)}, u32[]{:S(2)}, u32[]{:S(2)}) collective-permute-start(bf16[136,768]{1,0:T(8,128)(2,1)} %shard_map.118.pay_hbm.refs_21_), channel_id=1, source_target_pairs={{0,2},{1,3},{4,0},{5,1},{8,4},{9,5},{12,8},{13,9},{14,12},{15,13},... | collective-permute-start | bytes 626696 | tf_op jit(solution)/shard_map/ppermute | solution.py:509
  5.1 7.1 %collective-permute-start.1 = (bf16[136,768]{1,0:T(8,128)(2,1)}, bf16[136,768]{1,0:T(8,128)(2,1)S(1)}, u32[]{:S(2)}, u32[]{:S(2)}) collective-permute-start(bf16[136,768]{1,0:T(8,128)(2,1)} %shard_map.118.pay_hbm.refs_21_), channel_id=1, source_target_pairs={{0,4},{1,5},{4,8},{5,9},{8,12},{9,13},{12,14},{13,15},{14,10},{15,... | collective-permute-start | bytes 626696 | tf_op jit(solution)/shard_map/ppermute | solution.py:509
  10.6 6.3 %collective-permute-start.5 = (bf16[136,768]{1,0:T(8,128)(2,1)S(1)}, bf16[136,768]{1,0:T(8,128)(2,1)S(1)}, u32[]{:S(2)}, u32[]{:S(2)}) collective-permute-start(bf16[136,768]{1,0:T(8,128)(2,1)S(1)} %collective-permute-done.2.refs_1_), channel_id=1, source_target_pairs={{0,2},{1,3},{4,0},{5,1},{8,4},{9,5},{12,8},{13,9},{14,12},{15,13},... | collective-permute-start | bytes 626696 | tf_op jit(solution)/shard_map/ppermute | solution.py:509
  12.3 6.0 %collective-permute-start.4 = (bf16[136,768]{1,0:T(8,128)(2,1)S(1)}, bf16[136,768]{1,0:T(8,128)(2,1)S(1)}, u32[]{:S(2)}, u32[]{:S(2)}) collective-permute-start(bf16[136,768]{1,0:T(8,128)(2,1)S(1)} %collective-permute-done.1.refs_0_), channel_id=1, source_target_pairs={{0,4},{1,5},{4,8},{5,9},{8,12},{9,13},{12,14},{13,15},{14,10},{15,... | collective-permute-start | bytes 626696 | tf_op jit(solution)/shard_map/ppermute | solution.py:509
  16.9 6.8 %collective-permute-start.8 = (bf16[136,768]{1,0:T(8,128)(2,1)S(1)}, bf16[136,768]{1,0:T(8,128)(2,1)S(1)}, u32[]{:S(2)}, u32[]{:S(2)}) collective-permute-start(bf16[136,768]{1,0:T(8,128)(2,1)S(1)} %collective-permute-done.5.refs_1_), channel_id=1, source_target_pairs={{0,2},{1,3},{4,0},{5,1},{8,4},{9,5},{12,8},{13,9},{14,12},{15,13},... | collective-permute-start | bytes 626696 | tf_op jit(solution)/shard_map/ppermute | solution.py:509
  18.3 5.8 %collective-permute-start.7 = (bf16[136,768]{1,0:T(8,128)(2,1)S(1)}, bf16[136,768]{1,0:T(8,128)(2,1)S(1)}, u32[]{:S(2)}, u32[]{:S(2)}) collective-permute-start(bf16[136,768]{1,0:T(8,128)(2,1)S(1)} %collective-permute-done.4.refs_0_), channel_id=1, source_target_pairs={{0,4},{1,5},{4,8},{5,9},{8,12},{9,13},{12,14},{13,15},{14,10},{15,... | collective-permute-start | bytes 626696 | tf_op jit(solution)/shard_map/ppermute | solution.py:509
  18.9 1.3 %copy-start = (bf16[768,768]{1,0:T(8,128)(2,1)S(1)}, bf16[768,768]{1,0:T(8,128)(2,1)}, u32[]{:S(2)}) copy-start(bf16[768,768]{1,0:T(8,128)(2,1)} %refs_17_.1) | copy-start | bytes 3538948
  20.2 1.3 %copy-start.2 = (bf16[768,768]{1,0:T(8,128)(2,1)S(1)}, bf16[768,768]{1,0:T(8,128)(2,1)}, u32[]{:S(2)}) copy-start(bf16[768,768]{1,0:T(8,128)(2,1)} %refs_18_.1) | copy-start | bytes 3538948
  22.3 17.3 %collective-permute-start.3 = (bf16[528,768]{1,0:T(8,128)(2,1)S(1)}, bf16[528,768]{1,0:T(8,128)(2,1)S(1)}, u32[]{:S(2)}, u32[]{:S(2)}) collective-permute-start(bf16[528,768]{1,0:T(8,128)(2,1)S(1)} %shard_map.120.refs_2_), channel_id=1, source_target_pairs={{0,1},{1,0},{2,3},{3,2},{4,5},{5,4},{6,7},{7,6},{8,9},{9,8},{10,11... | collective-permute-start | bytes 2433032 | tf_op jit(solution)/shard_map/ppermute | solution.py:512
  23.1 16.5 %collective-permute-start.6 = (bf16[528,768]{1,0:T(8,128)(2,1)S(1)}, bf16[528,768]{1,0:T(8,128)(2,1)S(1)}, u32[]{:S(2)}, u32[]{:S(2)}) collective-permute-start(bf16[528,768]{1,0:T(8,128)(2,1)S(1)} %shard_map.121.refs_4_), channel_id=1, source_target_pairs={{0,1},{1,0},{2,3},{3,2},{4,5},{5,4},{6,7},{7,6},{8,9},{9,8},{10,11... | collective-permute-start | bytes 2433032 | tf_op jit(solution)/shard_map/ppermute | solution.py:512
  24.1 1.7 %copy-start.7 = (bf16[136,768]{1,0:T(8,128)(2,1)}, bf16[136,768]{1,0:T(8,128)(2,1)S(1)}, u32[]{:S(2)}) copy-start(bf16[136,768]{1,0:T(8,128)(2,1)S(1)} %collective-permute-done.7.refs_0_.in_ref) | copy-start | bytes 626692
  25.8 14.8 %collective-permute-start.9 = (bf16[528,768]{1,0:T(8,128)(2,1)}, bf16[528,768]{1,0:T(8,128)(2,1)}, u32[]{:S(2)}, u32[]{:S(2)}) collective-permute-start(bf16[528,768]{1,0:T(8,128)(2,1)} %shard_map.122.refs_6_), channel_id=1, source_target_pairs={{0,1},{1,0},{2,3},{3,2},{4,5},{5,4},{6,7},{7,6},{8,9},{9,8},{10,11... | collective-permute-start | bytes 2433032 | tf_op jit(solution)/shard_map/ppermute | solution.py:512
  25.8 5.1 %copy-start.8 = (bf16[136,768]{1,0:T(8,128)(2,1)S(1)}, bf16[136,768]{1,0:T(8,128)(2,1)}, u32[]{:S(2)}) copy-start(bf16[136,768]{1,0:T(8,128)(2,1)} %copy-done.7) | copy-start | bytes 626692
  30.4 2.2 %collective-permute-start = (bf16[264,768]{1,0:T(8,128)(2,1)}, bf16[264,768]{1,0:T(8,128)(2,1)S(1)}, u32[]{:S(2)}, u32[]{:S(2)}) collective-permute-start(bf16[264,768]{1,0:T(8,128)(2,1)} %get-tuple-element.13.refs_0_), channel_id=1, source_target_pairs={{0,1},{1,0},{2,3},{3,2},{4,5},{5,4},{6,7},{7,6},{8,9},{9,8},{10,11... | collective-permute-start | bytes 1216520 | tf_op jit(solution)/shard_map/ppermute | solution.py:512
  31.0 5.0 %collective-permute-start.10 = (bf16[72,768]{1,0:T(8,128)(2,1)S(1)}, bf16[72,768]{1,0:T(8,128)(2,1)S(1)}, u32[]{:S(2)}, u32[]{:S(2)}) collective-permute-start(bf16[72,768]{1,0:T(8,128)(2,1)S(1)} %shard_map.123), channel_id=1, source_target_pairs={{0,4},{1,5},{4,8},{5,9},{8,12},{9,13},{12,14},{13,15},{14,10},{15,... | collective-permute-start | bytes 331784 | tf_op jit(solution)/shard_map/ppermute | solution.py:509
  32.5 5.1 %collective-permute-start.11 = (bf16[64,768]{1,0:T(8,128)(2,1)S(1)}, bf16[64,768]{1,0:T(8,128)(2,1)S(1)}, u32[]{:S(2)}, u32[]{:S(2)}) collective-permute-start(bf16[64,768]{1,0:T(8,128)(2,1)S(1)} %shard_map.124), channel_id=1, source_target_pairs={{0,2},{1,3},{4,0},{5,1},{8,4},{9,5},{12,8},{13,9},{14,12},{15,13},... | collective-permute-start | bytes 294920 | tf_op jit(solution)/shard_map/ppermute | solution.py:509
  36.0 4.6 %collective-permute-start.12 = (bf16[72,768]{1,0:T(8,128)(2,1)S(1)}, bf16[72,768]{1,0:T(8,128)(2,1)S(1)}, u32[]{:S(2)}, u32[]{:S(2)}) collective-permute-start(bf16[72,768]{1,0:T(8,128)(2,1)S(1)} %collective-permute-done.10.refs_8_), channel_id=1, source_target_pairs={{0,1},{1,0},{2,3},{3,2},{4,5},{5,4},{6,7},{7,6},{8,9},{9,8},{10,11... | collective-permute-start | bytes 331784 | tf_op jit(solution)/shard_map/ppermute | solution.py:512
  37.6 3.0 %collective-permute-start.13 = (bf16[64,768]{1,0:T(8,128)(2,1)S(1)}, bf16[64,768]{1,0:T(8,128)(2,1)S(1)}, u32[]{:S(2)}, u32[]{:S(2)}) collective-permute-start(bf16[64,768]{1,0:T(8,128)(2,1)S(1)} %collective-permute-done.11.refs_9_), channel_id=1, source_target_pairs={{0,1},{1,0},{2,3},{3,2},{4,5},{5,4},{6,7},{7,6},{8,9},{9,8},{10,11... | collective-permute-start | bytes 294920 | tf_op jit(solution)/shard_map/ppermute | solution.py:512
  37.6 0.9 %copy-start.11 = (bf16[128,768]{1,0:T(8,128)(2,1)S(1)}, bf16[128,768]{1,0:T(8,128)(2,1)}, u32[]{:S(2)}) copy-start(bf16[128,768]{1,0:T(8,128)(2,1)} %get-tuple-element.14.q_ref) | copy-start | bytes 589828
  38.5 1.1 %copy-start.5 = (bf16[264,768]{1,0:T(8,128)(2,1)S(1)}, bf16[264,768]{1,0:T(8,128)(2,1)}, u32[]{:S(2)}) copy-start(bf16[264,768]{1,0:T(8,128)(2,1)} %get-tuple-element.13.refs_0_) | copy-start | bytes 1216516
  38.5 1.1 %copy-start.12 = (f32[160,256]{1,0:T(8,128)S(1)}, f32[160,256]{1,0:T(8,128)}, u32[]{:S(2)}) copy-start(f32[160,256]{1,0:T(8,128)} %get-tuple-element.16.refs_7_) | copy-start | bytes 491524
  38.5 1.1 %copy-start.14 = (f32[66,16]{0,1:T(8,128)S(1)}, f32[66,16]{0,1:T(8,128)}, u32[]{:S(2)}) copy-start(f32[66,16]{0,1:T(8,128)} %param.23) | copy-start | bytes 12676
  39.6 1.3 %copy-start.1 = (bf16[768,768]{1,0:T(8,128)(2,1)S(1)}, bf16[768,768]{1,0:T(8,128)(2,1)}, u32[]{:S(2)}) copy-start(bf16[768,768]{1,0:T(8,128)(2,1)} %refs_17_.1) | copy-start | bytes 3538948
  39.6 1.6 %copy-start.3 = (bf16[768,768]{1,0:T(8,128)(2,1)S(1)}, bf16[768,768]{1,0:T(8,128)(2,1)}, u32[]{:S(2)}) copy-start(bf16[768,768]{1,0:T(8,128)(2,1)} %refs_18_.1) | copy-start | bytes 3538948
  39.6 1.6 %copy-start.4 = (bf16[136,768]{1,0:T(8,128)(2,1)S(1)}, bf16[136,768]{1,0:T(8,128)(2,1)}, u32[]{:S(2)}) copy-start(bf16[136,768]{1,0:T(8,128)(2,1)} %shard_map.118.pay_hbm.refs_21_) | copy-start | bytes 626692
  39.7 2.0 %copy-start.6 = (bf16[768,768]{1,0:T(8,128)(2,1)S(1)}, bf16[768,768]{1,0:T(8,128)(2,1)}, u32[]{:S(2)}) copy-start(bf16[768,768]{1,0:T(8,128)(2,1)} %refs_23_.1) | copy-start | bytes 3538948
  39.7 2.0 %copy-start.9 = (bf16[16,8,768]{2,1,0:T(8,128)(2,1)S(1)}, bf16[16,8,768]{2,1,0:T(8,128)(2,1)}, u32[]{:S(2)}) copy-start(bf16[16,8,768]{2,1,0:T(8,128)(2,1)} %refs_22_.1) | copy-start | bytes 589828
  39.7 2.2 %copy-start.10 = (f32[128,768]{1,0:T(8,128)S(1)}, f32[128,768]{1,0:T(8,128)}, u32[]{:S(2)}) copy-start(f32[128,768]{1,0:T(8,128)} %get-tuple-element.15.refs_13_) | copy-start | bytes 1179652
  39.7 2.1 %copy-start.13 = (f32[96,256]{1,0:T(8,128)S(1)}, f32[96,256]{1,0:T(8,128)}, u32[]{:S(2)}) copy-start(f32[96,256]{1,0:T(8,128)} %get-tuple-element.20.refs_19_) | copy-start | bytes 294916

commit v6 on v5

--- a/solution.py
+++ b/solution.py
@@ -94,6 +94,15 @@
     spread = (lane % tokens == token).astype(F32).astype(BF16)
     tiled = matmul(meta.astype(F32).astype(BF16), spread)
     out_ref[pl.ds(rows, META_ROWS), :] = tiled.astype(BF16)
+    meta_ref[...] = tiled.astype(BF16)
+
+
+def join_body(single_ref, meta_ref, out_ref):
+    tokens, samples, _ = single_ref.shape
+    rows = tokens * samples
+    normed = normed_rows(single_ref[...])
+    out_ref[pl.ds(0, rows), :] = matmul(sample_major(tokens, samples), normed).astype(BF16)
+    out_ref[pl.ds(rows, META_ROWS), :] = meta_ref[...]
 
 
 META_ROWS = 8
@@ -116,6 +125,15 @@
     spread = (lane % tokens == token).astype(F32).astype(BF16)
     tiled = matmul(meta.astype(F32).astype(BF16), spread)
     out_ref[pl.ds(rows, META_ROWS), :] = tiled.astype(BF16)
+    meta_ref[...] = tiled.astype(BF16)
+
+
+def join_body(single_ref, meta_ref, out_ref):
+    tokens, samples, _ = single_ref.shape
+    rows = tokens * samples
+    normed = normed_rows(single_ref[...])
+    out_ref[pl.ds(0, rows), :] = matmul(sample_major(tokens, samples), normed).astype(BF16)
+    out_ref[pl.ds(rows, META_ROWS), :] = meta_ref[...]
 
 
 META_ROWS = 8
@@ -138,43 +156,24 @@
     spread = (lane % tokens == token).astype(F32).astype(BF16)
     tiled = matmul(meta.astype(F32).astype(BF16), spread)
     out_ref[pl.ds(rows, META_ROWS), :] = tiled.astype(BF16)
+    meta_ref[...] = tiled.astype(BF16)
+
+
+def join_body(single_ref, meta_ref, out_ref):
+    tokens, samples, _ = single_ref.shape
+    rows = tokens * samples
+    normed = normed_rows(single_ref[...])
+    out_ref[pl.ds(0, rows), :] = matmul(sample_major(tokens, samples), normed).astype(BF16)
+    out_ref[pl.ds(rows, META_ROWS), :] = meta_ref[...]
 
 
 META_ROWS = 8
 RADIX = 128
 
 
-def prep_body(single_hbm, chain_hbm, residue_hbm, valid_hbm, out_ref, single_ref, ints_ref, sems):
-    copies = [pltpu.make_async_copy(single_hbm, single_ref, sems.at[0])]
-    for i, ref in enumerate((chain_hbm, residue_hbm, valid_hbm)):
-        copies.append(pltpu.make_async_copy(ref, ints_ref.at[i], sems.at[i + 1]))
-    for copy in copies:
-        copy.start()
-    tokens, samples, width = single_ref.shape
-    rows = tokens * samples
-    token = lax.broadcasted_iota(jnp.int32, (tokens, width), 0)
-    lane = lax.broadcasted_iota(jnp.int32, (tokens, width), 1)
-    spread = (lane % tokens == token).astype(F32).astype(BF16)
-    perm = sample_major(tokens, samples)
-    for copy in copies:
-        copy.wait()
-    normed = normed_rows(single_ref[...])
-    out_ref[pl.ds(0, rows), :] = matmul(perm, normed).astype(BF16)
-    residue = ints_ref[1]
-    row = lax.broadcasted_iota(jnp.int32, (META_ROWS, tokens), 0)
-    meta = jnp.where(row == 0, ints_ref[0], 0)
-    meta = jnp.where(row == 1, residue // RADIX, meta)
-    meta = jnp.where(row == 2, residue % RADIX, meta)
-    meta = jnp.where(row == 3, ints_ref[2], meta)
-    tiled = matmul(meta.astype(F32).astype(BF16), spread)
-    out_ref[pl.ds(rows, META_ROWS), :] = tiled.astype(BF16)
-
-
-META_ROWS = 8
-RADIX = 128
-
-
-def prep_body(single_hbm, chain_hbm, residue_hbm, valid_hbm, out_ref, meta_ref, single_ref, ints_ref, sems):
+def prep_body(
+    single_hbm, chain_hbm, residue_hbm, valid_hbm, out_ref, meta_ref, single_ref, ints_ref, sems
+):
     copies = [pltpu.make_async_copy(single_hbm, single_ref, sems.at[0])]
     for i, ref in enumerate((chain_hbm, residue_hbm, valid_hbm)):
         copies.append(pltpu.make_async_copy(ref, ints_ref.at[i], sems.at[i + 1]))
@@ -201,11 +200,19 @@
     meta_ref[...] = tiled.astype(BF16)
 
 
+def join_body(single_ref, meta_ref, out_ref):
+    tokens, samples, _ = single_ref.shape
+    rows = tokens * samples
+    normed = normed_rows(single_ref[...])
+    out_ref[pl.ds(0, rows), :] = matmul(sample_major(tokens, samples), normed).astype(BF16)
+    out_ref[pl.ds(rows, META_ROWS), :] = meta_ref[...]
+
+
 META_ROWS = 8
 RADIX = 128
 
 
-def prep_body(single_hbm, chain_hbm, residue_hbm, valid_hbm, out_ref, single_ref, ints_ref, sems):
+def prep_body(single_hbm, chain_hbm, residue_hbm, valid_hbm, out_ref, meta_ref, single_ref, ints_ref, sems):
     copies = [pltpu.make_async_copy(single_hbm, single_ref, sems.at[0])]
     for i, ref in enumerate((chain_hbm, residue_hbm, valid_hbm)):
         copies.append(pltpu.make_async_copy(ref, ints_ref.at[i], sems.at[i + 1]))
@@ -229,35 +236,85 @@
     meta = jnp.where(row == 3, ints_ref[2], meta)
     tiled = matmul(meta.astype(F32).astype(BF16), spread)
     out_ref[pl.ds(rows, META_ROWS), :] = tiled.astype(BF16)
+    meta_ref[...] = tiled.astype(BF16)
+
+
+def join_body(single_ref, meta_ref, out_ref):
+    tokens, samples, _ = single_ref.shape
+    rows = tokens * samples
+    normed = normed_rows(single_ref[...])
+    out_ref[pl.ds(0, rows), :] = matmul(sample_major(tokens, samples), normed).astype(BF16)
+    out_ref[pl.ds(rows, META_ROWS), :] = meta_ref[...]
+    meta_ref[...] = tiled.astype(BF16)
+
+
+META_ROWS = 8
+RADIX = 128
+
+
+def prep_body(
+    single_hbm, chain_hbm, residue_hbm, valid_hbm, out_ref, meta_ref, single_ref, ints_ref, sems
+):
+    copies = [pltpu.make_async_copy(single_hbm, single_ref, sems.at[0])]
+    for i, ref in enumerate((chain_hbm, residue_hbm, valid_hbm)):
+        copies.append(pltpu.make_async_copy(ref, ints_ref.at[i], sems.at[i + 1]))
+    for copy in copies:
+        copy.start()
+    tokens, samples, width = single_ref.shape
+    rows = tokens * samples
+    token = lax.broadcasted_iota(jnp.int32, (tokens, width), 0)
+    lane = lax.broadcasted_iota(jnp.int32, (tokens, width), 1)
+    spread = (lane % tokens == token).astype(F32).astype(BF16)
+    perm = sample_major(tokens, samples)
+    for copy in copies:
+        copy.wait()
+    normed = normed_rows(single_ref[...])
+    out_ref[pl.ds(0, rows), :] = matmul(perm, normed).astype(BF16)
+    residue = ints_ref[1]
+    row = lax.broadcasted_iota(jnp.int32, (META_ROWS, tokens), 0)
+    meta = jnp.where(row == 0, ints_ref[0], 0)
+    meta = jnp.where(row == 1, residue // RADIX, meta)
+    meta = jnp.where(row == 2, residue % RADIX, meta)
+    meta = jnp.where(row == 3, ints_ref[2], meta)
+    tiled = matmul(meta.astype(F32).astype(BF16), spread)
+    out_ref[pl.ds(rows, META_ROWS), :] = tiled.astype(BF16)
+    meta_ref[...] = tiled.astype(BF16)
+
+
+def join_body(single_ref, meta_ref, out_ref):
+    tokens, samples, _ = single_ref.shape
+    rows = tokens * samples
+    normed = normed_rows(single_ref[...])
+    out_ref[pl.ds(0, rows), :] = matmul(sample_major(tokens, samples), normed).astype(BF16)
+    out_ref[pl.ds(rows, META_ROWS), :] = meta_ref[...]
+
+
+def query_body(samples, heads, pay_hbm, wq_hbm, out_ref, pay_ref, wq_ref, q_ref, sems):
+    copies = []
+    for i, (source, target) in enumerate(((pay_hbm, pay_ref), (wq_hbm, wq_ref))):
+        copies.append(pltpu.make_async_copy(source, target, sems.at[i]))
+        copies[i].start()
+    for copy in copies:
+        copy.wait()
+    q_ref[...] = matmul(pay_ref[pl.ds(0, q_ref.shape[0]), :], wq_ref[...]).astype(BF16)
+    spread_queries(samples, heads, q_ref, out_ref)
 
 
 def own_body(
-    steps, chips, me_ref, pay_hbm, wq_hbm, wk_hbm, wv_hbm, wg_hbm, pair_hbm, wp_hbm,
-    q_ref, gate_ref, kv_ref, first_ref, second_ref,
-    pay_ref, wq_ref, wk_ref, wv_ref, wg_ref, pair_ref, wp_ref, sems,
+    steps, chips, me_ref, pay_hbm, wg_hbm, pair_hbm, wp_hbm, gate_ref, *refs
 ):
-    copies = {}
-    moves = [
-        (pay_hbm, pay_ref), (wq_hbm, wq_ref), (wp_hbm, wp_ref), (pair_hbm, pair_ref),
-        (wk_hbm, wk_ref), (wv_hbm, wv_ref), (wg_hbm, wg_ref),
-    ]
+    pay_ref, wg_ref, pair_ref, wp_ref, sems = refs[-5:]
+    copies = []
+    moves = ((wp_hbm, wp_ref), (pair_hbm, pair_ref), (pay_hbm, pay_ref), (wg_hbm, wg_ref))
     for i, (source, target) in enumerate(moves):
-        copies[i] = pltpu.make_async_copy(source, target, sems.at[i])
+        copies.append(pltpu.make_async_copy(source, target, sems.at[i]))
         copies[i].start()
-    rows = q_ref.shape[0]
     copies[0].wait()
-    data = pay_ref[pl.ds(0, rows), :]
     copies[1].wait()
-    q_ref[...] = matmul(data, wq_ref[...]).astype(BF16)
+    pair_rows(steps, chips, me_ref[0], pair_ref, wp_ref[...], refs[:-5])
     copies[2].wait()
     copies[3].wait()
-    pair_rows(steps, chips, me_ref[0], pair_ref, wp_ref[...], (first_ref, second_ref))
-    copies[4].wait()
-    kv_ref[pl.ds(0, rows), :] = matmul(data, wk_ref[...]).astype(BF16)
-    copies[5].wait()
-    kv_ref[pl.ds(rows, rows), :] = matmul(data, wv_ref[...]).astype(BF16)
-    kv_ref[pl.ds(2 * rows, META_ROWS), :] = pay_ref[pl.ds(rows, META_ROWS), :]
-    copies[6].wait()
+    data = pay_ref[pl.ds(0, gate_ref.shape[0]), :]
     gate_ref[...] = jax.nn.sigmoid(matmul(data, wg_ref[...]))
 
 
@@ -369,7 +426,7 @@
     return windows
 
 
-def spread_body(samples, heads, q_ref, out_ref):
+def spread_queries(samples, heads, q_ref, out_ref):
     rows, width = q_ref.shape
     tokens = rows // samples
     hs = width // heads
@@ -397,48 +454,54 @@
     return found
 
 
-def early_body(samples, scale, *refs):
-    q_ref, pair_ref, tab_ref, exp_ref, top_ref, mass_ref, pad_ref = refs[-7:]
-    kv_refs = refs[:-7]
+def weights_body(samples, scale, more, *refs):
+    exp_ref, top_ref, mass_ref, pad_ref = refs[-4:]
+    q_ref, pair_ref, tab_ref, own_ref = refs[-8:-4]
+    kv_refs = refs[:-8]
+    if more:
+        kv_refs, before_ref, mass_before_ref = refs[:-10], refs[-10], refs[-9]
     count, lines = pair_ref.shape
     tokens = lines // tab_ref.shape[0]
     rows = tokens * samples
     width = kv_refs[0].shape[1]
     metas = kv_metas(kv_refs, rows)
-    bias = full_bias(metas[0], metas, tokens, pair_ref, tab_ref, pad_ref)
+    bias = full_bias(own_ref[...], metas, tokens, pair_ref, tab_ref, pad_ref)
     for s in range(samples):
+        here = pl.ds(s, 1)
         keys = jnp.concatenate(gather(kv_refs, rows, s * tokens, tokens, False), axis=0)
         scores = matmul(keys, q_ref[pl.ds(s * width, width), :]) * scale + bias
         top = jnp.max(scores, axis=0, keepdims=True)
+        if more:
+            top = jnp.maximum(top, before_ref[here, :])
         weights = jnp.exp(scores - top)
-        top_ref[pl.ds(s, 1), :] = top
-        mass_ref[pl.ds(s, 1), :] = jnp.sum(weights, axis=0, keepdims=True)
+        mass = jnp.sum(weights, axis=0, keepdims=True)
+        if more:
+            mass = mass + mass_before_ref[here, :] * jnp.exp(before_ref[here, :] - top)
+        top_ref[here, :] = top
+        mass_ref[here, :] = mass
         exp_ref[pl.ds(s * count, count), :] = weights
 
 
-def finish_body(heads, scale, split, *refs):
+def finish_body(heads, scale, *refs):
     (
-        q_ref, gate_ref, exp_ref, top_ref, mass_ref, wk_ref, wv_ref, pair_ref, tab_ref, pay_ref,
-        single_ref, wo_ref, out_ref, pad_ref, weight_ref,
-    ) = refs[-15:]
-    kv_refs, lasts = refs[:-19], refs[-19:-15]
+        q_ref, gate_ref, first_ref, first_top_ref, second_ref, top_ref, mass_ref, wk_ref, wv_ref,
+        pair_ref, tab_ref, own_ref, single_ref, wo_ref, out_ref, pad_ref, weight_ref,
+    ) = refs[-17:]
+    kv_refs, lasts = refs[:-21], refs[-21:-17]
     tokens, samples, width = single_ref.shape
     rows = tokens * samples
     half = rows // 2
     hs = width // heads
-    metas = kv_metas(kv_refs[split:], rows) + [r[pl.ds(half, META_ROWS), :] for r in (lasts[0], lasts[2])]
-    own = pay_ref[pl.ds(rows, META_ROWS), :]
+    metas = [r[pl.ds(half, META_ROWS), :] for r in (lasts[0], lasts[2])]
     data = jnp.concatenate([r[pl.ds(0, half), :] for r in lasts], axis=0)
     k_last = matmul(data, wk_ref[...]).astype(BF16)
     v_last = matmul(data, wv_ref[...]).astype(BF16)
-    bias = full_bias(own, metas, tokens, pair_ref, tab_ref, pad_ref)
-    count = exp_ref.shape[0] // samples
+    bias = full_bias(own_ref[...], metas, tokens, pair_ref, tab_ref, pad_ref)
     lane_head = lax.broadcasted_iota(jnp.int32, (tokens, width), 1) // hs
     lines = heads * tokens
     for s in range(samples):
         new = [slice(u * rows + s * tokens, u * rows + (s + 1) * tokens) for u in range(2)]
-        keys = gather(kv_refs[split:], rows, s * tokens, tokens, False)
-        keys = jnp.concatenate(keys + [k_last[n] for n in new], axis=0)
+        keys = jnp.concatenate([k_last[n] for n in new], axis=0)
         scores = matmul(keys, q_ref[pl.ds(s * width, width), :]) * scale + bias
         before = top_ref[pl.ds(s, 1), :]
         top = jnp.maximum(jnp.max(scores, axis=0, keepdims=True), before)
@@ -446,8 +509,11 @@
         late = jnp.exp(scores - top)
         mass = jnp.sum(late, axis=0, keepdims=True) + mass_ref[pl.ds(s, 1), :] * shrink
         inv = 1.0 / mass
-        old = exp_ref[pl.ds(s * count, count), :] * (shrink * inv)
-        weights = jnp.concatenate([old, late * inv], axis=0)
+        weights = []
+        for ref, old in ((first_ref, first_top_ref[pl.ds(s, 1), :]), (second_ref, before)):
+            count = ref.shape[0] // samples
+            weights.append(ref[pl.ds(s * count, count), :] * (jnp.exp(old - top) * inv))
+        weights = jnp.concatenate(weights + [late * inv], axis=0)
         weight_ref[pl.ds(s * lines, lines), :] = jnp.transpose(weights).astype(BF16)
     gated = []
     for s in range(samples):
@@ -516,9 +582,12 @@
         steps += [(-k, 0), (k, 0), (-k, 1), (k, 1)]
     steps += [(half, 0), (half, 1)]
 
-    payload = call(
+    cw = ring(single, 1)
+    ccw = ring(single, -1)
+    blocks = jax.ShapeDtypeStruct((rows + META_ROWS, width), BF16)
+    payload, meta = call(
         prep_body,
-        jax.ShapeDtypeStruct((rows + META_ROWS, width), BF16),
+        (blocks, jax.ShapeDtypeStruct((META_ROWS, width), BF16)),
         (single, *(v.reshape(1, tokens) for v in (chain, residue, valid))),
         in_specs=[ANY] * 4,
         scratch=[
@@ -530,8 +599,31 @@
         moved=4 * rows * width,
         limit=FULL,
     )
-    cw = ring(payload, 1)
-    ccw = ring(payload, -1)
+    cw_meta = ring(meta, 1)
+    ccw_meta = ring(meta, -1)
+    other = flip(payload)
+    lines = heads * tokens
+    query = call(
+        functools.partial(query_body, samples, heads),
+        jax.ShapeDtypeStruct((samples * width, lines), BF16),
+        (payload, w_query),
+        in_specs=[ANY] * 2,
+        flops=2 * rows * width * (width + lines),
+        moved=2 * width * width + 2 * samples * width * lines,
+        limit=FULL,
+        scratch=[
+            pltpu.VMEM(blocks.shape, BF16),
+            pltpu.VMEM((width, width), BF16),
+            pltpu.VMEM((rows, width), BF16),
+            pltpu.SemaphoreType.DMA((2,)),
+        ],
+    )
+
+    def join(value, extra):
+        return call(join_body, blocks, (value, extra), moved=4 * rows * width)
+
+    cw = join(cw, cw_meta)
+    ccw = join(ccw, ccw_meta)
 
     def kv(parts):
         n = len(parts)
@@ -554,39 +646,27 @@
         shape = jax.ShapeDtypeStruct((count, width), BF16)
         return call(body, shape, (value,), moved=2 * rows * width)
 
-    early = len(steps) - 3 * CORES
-    split = 2 * (half - 1)
-    pair_shapes = tuple(
-        jax.ShapeDtypeStruct((n * tokens, heads * tokens), F32) for n in (early, len(steps) - early)
-    )
-    weight = pltpu.VMEM((width, width), BF16)
-    query, gate, kv_own, pair_first, pair_second = call(
+    sizes = [len(steps) - 3 * CORES, 2 * CORES, CORES]
+    gate, *pair_bias = call(
         functools.partial(own_body, steps, chips),
         (
-            jax.ShapeDtypeStruct((rows, width), BF16),
             jax.ShapeDtypeStruct((rows, width), F32),
-            jax.ShapeDtypeStruct((2 * rows + META_ROWS, width), BF16),
-            *pair_shapes,
+            *(jax.ShapeDtypeStruct((n * tokens, lines), F32) for n in sizes),
         ),
-        (me, payload, w_query, w_key, w_value, w_gate, pair, w_pair.T),
-        in_specs=[SMEM] + [ANY] * 7,
-        flops=8 * rows * width * width + 2 * pair.size * heads,
-        moved=8 * width * width + 12 * rows * width + 2 * pair.size,
-        limit=FULL,
+        (me, payload, w_gate, pair, w_pair.T),
+        in_specs=[SMEM] + [ANY] * 4,
+        flops=2 * rows * width * width + 2 * pair.size * lines,
+        moved=2 * width * width + 6 * rows * width + 2 * pair.size,
+        limit=(6 << 20) + 4 * pair.size,
         scratch=[
-            pltpu.VMEM(payload.shape, BF16),
-            weight,
-            weight,
-            weight,
-            weight,
+            pltpu.VMEM(blocks.shape, BF16),
+            pltpu.VMEM((width, width), BF16),
             pltpu.VMEM(pair.shape, BF16),
             pltpu.VMEM(w_pair.shape[::-1], BF16),
-            pltpu.SemaphoreType.DMA((7,)),
+            pltpu.SemaphoreType.DMA((4,)),
         ],
     )
-
-    kvs = [kv_own]
-    kvs.append(flip(kvs[-1]))
+    kvs = [kv([payload, other])]
     for k in range(1, half):
         if k + 1 < half:
             cw_next = ring(cw, 1)
@@ -594,38 +674,36 @@
         else:
             cw_next = ring(piece(cw, 0, True), 1)
             ccw_next = ring(piece(ccw, rows // 2, False), -1)
-        kvs.append(kv([cw, ccw]))
-        kvs.append(flip(kvs[-1]))
+        cw_other, ccw_other = flip(cw), flip(ccw)
+        kvs.append(kv([cw, ccw, cw_other, ccw_other]))
         cw, ccw = cw_next, ccw_next
     scale = 1.0 / math.sqrt(width // heads)
-    lines = heads * tokens
     state = jax.ShapeDtypeStruct((samples, lines), F32)
-    query = call(
-        functools.partial(spread_body, samples, heads),
-        jax.ShapeDtypeStruct((samples * width, lines), BF16),
-        (query,),
-        flops=2 * rows * width * lines,
-        moved=2 * samples * width * lines,
-    )
     table = rel_table.T
     pad = [pltpu.VMEM((heads, LANES), F32)]
     limit = (10 << 20) + 4 * samples * total * width
-    before = call(
-        functools.partial(early_body, samples, scale),
-        (jax.ShapeDtypeStruct((samples * early * tokens, lines), F32), state, state),
-        (*kvs[:split], query, pair_first, table),
-        flops=4 * rows * early * tokens * width,
-        moved=4 * samples * early * tokens * width,
-        limit=limit,
-        scratch=pad,
-    )
+
+    def weights(at, parts, before):
+        keys = sizes[at] * tokens
+        return call(
+            functools.partial(weights_body, samples, scale, bool(before)),
+            (jax.ShapeDtypeStruct((samples * keys, lines), F32), state, state),
+            (*parts, *before, query, pair_bias[at], table, meta),
+            flops=2 * samples * keys * width * lines,
+            moved=6 * samples * keys * width,
+            limit=limit,
+            scratch=pad,
+        )
+
+    first = weights(0, kvs[:-1], ())
+    second = weights(1, kvs[-1:], first[1:])
     cw_other, ccw_other = flip(cw), flip(ccw)
     return call(
-        functools.partial(finish_body, heads, scale, split),
+        functools.partial(finish_body, heads, scale),
         jax.ShapeDtypeStruct(single.shape, BF16),
         (
-            *kvs, cw, ccw, cw_other, ccw_other, query, gate, *before, w_key, w_value,
-            pair_second, table, payload, single, w_out,
+            *kvs, cw, ccw, cw_other, ccw_other, query, gate, *first[:2], *second, w_key, w_value,
+            pair_bias[2], table, meta, single, w_out,
         ),
         flops=4 * rows * total * width,
         moved=2 * samples * total * width,

time: 46.6 us -> 42.6 us (0.914)
  waiting for transfers between devices: 14 us -> 7.4 us
  Pallas kernels: 16.3 us -> 20.2 us
  local copies, waits for them, and re-layouts: 4.74 us -> 0.93 us
  starting transfers between devices: 11.1 us -> 13.6 us
    ppermute x8 -> x10, waiting for transfers between devices: 13.5 us -> 7.38 us  [ring(): return lax.ppermute(value, 'tok', pairs)]
    pallas_call x10 -> x14, Pallas kernels: 16.3 us -> 20.2 us  [call(): pl.pallas_call(body, out_shape=out_shape, in_specs=in_specs or [VMEM] * l...]
    unnamed x30 -> x22, local copies, waits for them, and re-layouts: 4.74 us -> 0.93 us
    ppermute x8 -> x10, starting transfers between devices: 9.88 us -> 11.3 us  [ring(): return lax.ppermute(value, 'tok', pairs)]
    ppermute x6 -> x9, starting transfers between devices: 1.22 us -> 2.28 us  [flip(): return lax.ppermute(value, 'tok', [(d, d ^ 1) for d in range(devices)])]
  transfers between devices with their start and end apart: 14 -> 19, of which waited for: 6 -> 4; matrix products, arithmetic and copies ran while one was open for 0% -> 0% of each run, Pallas kernels for 21% -> 40%
where the time goes in v6:
time: 42.6 us; the launch traced here: 42.4 us
  Pallas kernels  20.2 us (47%)
  starting transfers between devices  13.6 us (32%)
  waiting for transfers between devices  7.4 us (17%)
  local copies, waits for them, and re-layouts  0.93 us (2%)
    pallas_call x14, Pallas kernels, call(): pl.pallas_call(body, out_shape=out_shape, in_specs=in_specs or [VMEM] * l...  20.2 us
    ppermute x10, starting transfers between devices, ring(): return lax.ppermute(value, 'tok', pairs)  11.3 us
    ppermute x10, waiting for transfers between devices, ring(): return lax.ppermute(value, 'tok', pairs)  7.38 us
    ppermute x9, starting transfers between devices, flip(): return lax.ppermute(value, 'tok', [(d, d ^ 1) for d in range(devices)])  2.28 us
    unnamed x22, local copies, waits for them, and re-layouts  0.93 us
  transfers between devices with their start and end apart: 19, of which 4 were waited for; matrix products, arithmetic and copies ran while one was open for 0% of the time, Pallas kernels for 40%

profile of v6, /device:TPU:0, one launch (start us, length us, event | category | flops | bytes accessed | tf_op | source)
XLA Modules:
  0.0 42.4 jit_solution(6051769124821308460)
XLA Ops:
  0.0 3.1 %collective-permute-start.1 = (bf16[16,8,768]{2,1,0:T(8,128)(2,1)}, bf16[16,8,768]{2,1,0:T(8,128)(2,1)S(1)}, u32[]{:S(2)}, u32[]{:S(2)}) collective-permute-start(bf16[16,8,768]{2,1,0:T(8,128)(2,1)} %refs_20_.1), channel_id=1, source_target_pairs={{0,4},{1,5},{4,8},{5,9},{8,12},{9,13},{12,14},{13,15},{14,10},{15,... | collective-permute-start | bytes 589832 | tf_op jit(solution)/shard_map/ppermute | solution.py:575
  3.1 0.0 collective-permute-start.3
  3.1 2.1 %shard_map.118 = (bf16[136,768]{1,0:T(8,128)(2,1)}, bf16[8,768]{1,0:T(8,128)(2,1)}) custom-call(bf16[16,8,768]{2,1,0:T(8,128)(2,1)} %refs_20_.1, s32[1,16]{1,0:T(1,128)} %bitcast.10, s32[1,16]{1,0:T(1,128)} %bitcast.11, s32[1,16]{1,0:T(1,128)} %bitcast.12), custom_call_target="tpu_custom_call" | custom-call | flops 1572864 | bytes 393216 | tf_op jit(solution)/shard_map/pallas_call | solution.py:545
  5.2 2.0 %collective-permute-start.2 = (bf16[8,768]{1,0:T(8,128)(2,1)}, bf16[8,768]{1,0:T(8,128)(2,1)S(1)}, u32[]{:S(2)}, u32[]{:S(2)}) collective-permute-start(bf16[8,768]{1,0:T(8,128)(2,1)} %get-tuple-element.18.refs_6_.refs_19_), channel_id=1, source_target_pairs={{0,4},{1,5},{4,8},{5,9},{8,12},{9,13},{12,14},{13,15},{14,10},{15,... | collective-permute-start | bytes 36872 | tf_op jit(solution)/shard_map/ppermute | solution.py:575
  7.2 0.0 collective-permute-start.4
  7.3 1.9 %collective-permute-done.2.meta_ref = bf16[8,768]{1,0:T(8,128)(2,1)S(1)} collective-permute-done((bf16[8,768]{1,0:T(8,128)(2,1)}, bf16[8,768]{1,0:T(8,128)(2,1)S(1)}, u32[]{:S(2)}, u32[]{:S(2)}) %collective-permute-start.2) | collective-permute-done | bytes 12320 | tf_op jit(solution)/shard_map/ppermute | solution.py:575
  9.2 0.0 collective-permute-done.1.single_ref
  9.2 0.4 shard_map.120.refs_0_
  9.6 2.0 %collective-permute-start.7 = (bf16[136,768]{1,0:T(8,128)(2,1)S(1)}, bf16[136,768]{1,0:T(8,128)(2,1)S(1)}, u32[]{:S(2)}, u32[]{:S(2)}) collective-permute-start(bf16[136,768]{1,0:T(8,128)(2,1)S(1)} %shard_map.120.refs_0_), channel_id=1, source_target_pairs={{0,4},{1,5},{4,8},{5,9},{8,12},{9,13},{12,14},{13,15},{14,10},{15,... | collective-permute-start | bytes 626696 | tf_op jit(solution)/shard_map/ppermute | solution.py:575
  11.6 0.4 shard_map.121.refs_1_
  12.0 0.1 collective-permute-start.8
  12.1 0.0 collective-permute-start
  12.2 0.5 %collective-permute-start.5 = (bf16[136,768]{1,0:T(8,128)(2,1)S(1)}, bf16[136,768]{1,0:T(8,128)(2,1)S(1)}, u32[]{:S(2)}, u32[]{:S(2)}) collective-permute-start(bf16[136,768]{1,0:T(8,128)(2,1)S(1)} %shard_map.120.refs_0_), channel_id=1, source_target_pairs={{0,1},{1,0},{2,3},{3,2},{4,5},{5,4},{6,7},{7,6},{8,9},{9,8},{10,11... | collective-permute-start | bytes 626696 | tf_op jit(solution)/shard_map/ppermute | solution.py:578
  12.7 2.9 %collective-permute-done.7.refs_0_ = bf16[136,768]{1,0:T(8,128)(2,1)S(1)} collective-permute-done((bf16[136,768]{1,0:T(8,128)(2,1)S(1)}, bf16[136,768]{1,0:T(8,128)(2,1)S(1)}, u32[]{:S(2)}, u32[]{:S(2)}) %collective-permute-start.7) | collective-permute-done | bytes 208928 | tf_op jit(solution)/shard_map/ppermute | solution.py:575
  15.5 1.9 %collective-permute-start.11 = (bf16[136,768]{1,0:T(8,128)(2,1)S(1)}, bf16[136,768]{1,0:T(8,128)(2,1)S(1)}, u32[]{:S(2)}, u32[]{:S(2)}) collective-permute-start(bf16[136,768]{1,0:T(8,128)(2,1)S(1)} %collective-permute-done.7.refs_0_), channel_id=1, source_target_pairs={{0,4},{1,5},{4,8},{5,9},{8,12},{9,13},{12,14},{13,15},{14,10},{15,... | collective-permute-start | bytes 626696 | tf_op jit(solution)/shard_map/ppermute | solution.py:575
  17.4 0.5 %collective-permute-done.8.refs_1_ = bf16[136,768]{1,0:T(8,128)(2,1)S(1)} collective-permute-done((bf16[136,768]{1,0:T(8,128)(2,1)S(1)}, bf16[136,768]{1,0:T(8,128)(2,1)S(1)}, u32[]{:S(2)}, u32[]{:S(2)}) %collective-permute-start.8) | collective-permute-done | bytes 208928 | tf_op jit(solution)/shard_map/ppermute | solution.py:575
  17.9 0.0 collective-permute-start.12
  17.9 0.0 collective-permute-start.6
  17.9 0.0 copy-start.10
  17.9 4.5 %shard_map.127.refs_3_.refs_8_ = bf16[6144,256]{1,0:T(8,128)(2,1)} custom-call(bf16[136,768]{1,0:T(8,128)(2,1)} %get-tuple-element.17.refs_0_.pay_hbm, bf16[768,768]{1,0:T(8,128)(2,1)} %wq_hbm.1), custom_call_target="tpu_custom_call" | custom-call | flops 201326592 | bytes 4325376 | tf_op jit(solution)/shard_map/pallas_call | solution.py:545
  22.5 0.0 copy-start.1
  22.5 0.0 copy-start.2
  22.5 0.0 collective-permute-done.refs_1_
  22.5 0.6 %collective-permute-start.9 = (bf16[136,768]{1,0:T(8,128)(2,1)S(1)}, bf16[136,768]{1,0:T(8,128)(2,1)S(1)}, u32[]{:S(2)}, u32[]{:S(2)}) collective-permute-start(bf16[136,768]{1,0:T(8,128)(2,1)S(1)} %collective-permute-done.7.refs_0_), channel_id=1, source_target_pairs={{0,1},{1,0},{2,3},{3,2},{4,5},{5,4},{6,7},{7,6},{8,9},{9,8},{10,11... | collective-permute-start | bytes 626696 | tf_op jit(solution)/shard_map/ppermute | solution.py:578
  23.1 0.1 collective-permute-start.10
  23.1 2.1 %shard_map.128 = (f32[128,768]{1,0:T(8,128)S(1)}, f32[160,256]{1,0:T(8,128)S(1)}, f32[64,256]{1,0:T(8,128)S(1)}, f32[32,256]{1,0:T(8,128)S(1)}) custom-call(s32[1]{0:T(128)} %bitcast.3.me_ref, bf16[136,768]{1,0:T(8,128)(2,1)S(1)} %copy-done.3, bf16[768,768]{1,0:T(8,128)(2,1)S(1)} %copy-done.4, bf16[16,256,128]{2,1,0:T(8,128)(2,1)S(1)} %copy-done.6, ...), custom_call_target="tpu_custom_call" | custom-call | flops 419430400 | bytes 2818048 | tf_op jit(solution)/shard_map/pallas_call | solution.py:545
  25.3 1.7 %shard_map.119.refs_0_ = bf16[528,768]{1,0:T(8,128)(2,1)S(1)} custom-call(bf16[136,768]{1,0:T(8,128)(2,1)S(1)} %copy-done.3, bf16[136,768]{1,0:T(8,128)(2,1)} %collective-permute-done.refs_1_, bf16[768,768]{1,0:T(8,128)(2,1)S(1)} %copy-done.1, bf16[768,768]{1,0:T(8,128)(2,1)S(1)} %copy-done.2), custom_call_target="tpu_custom_call" | custom-call | flops 603979776 | bytes 3538944 | tf_op jit(solution)/shard_map/pallas_call | solution.py:545
  27.0 0.0 collective-permute-done.11.refs_0_.in_ref
  27.0 0.5 %collective-permute-start.13 = (bf16[136,768]{1,0:T(8,128)(2,1)S(1)}, bf16[136,768]{1,0:T(8,128)(2,1)S(1)}, u32[]{:S(2)}, u32[]{:S(2)}) collective-permute-start(bf16[136,768]{1,0:T(8,128)(2,1)S(1)} %collective-permute-done.11.refs_0_.in_ref), channel_id=1, source_target_pairs={{0,1},{1,0},{2,3},{3,2},{4,5},{5,4},{6,7},{7,6},{8,9},{9,8},{10,11... | collective-permute-start | bytes 626696 | tf_op jit(solution)/shard_map/ppermute | solution.py:578
  27.5 0.0 collective-permute-done.12.refs_1_.in_ref
  27.5 0.1 collective-permute-start.14
  27.6 1.4 %shard_map.122.refs_1_ = bf16[1056,768]{1,0:T(8,128)(2,1)S(1)} custom-call(bf16[136,768]{1,0:T(8,128)(2,1)S(1)} %shard_map.120.refs_0_, bf16[136,768]{1,0:T(8,128)(2,1)S(1)} %shard_map.121.refs_1_, bf16[136,768]{1,0:T(8,128)(2,1)S(1)} %collective-permute-done.5.refs_2_, bf16[136,768]{1,0:T(8,128)(2,1)S(1)} %collective-permute-done.6.refs_3_, ...), custom_call_target="tpu_custom_call" | custom-call | flops 1207959552 | bytes 4718592 | tf_op jit(solution)/shard_map/pallas_call | solution.py:545
  29.0 2.0 %collective-permute-start.15 = (bf16[72,768]{1,0:T(8,128)(2,1)S(1)}, bf16[72,768]{1,0:T(8,128)(2,1)S(1)}, u32[]{:S(2)}, u32[]{:S(2)}) collective-permute-start(bf16[72,768]{1,0:T(8,128)(2,1)S(1)} %shard_map.125), channel_id=1, source_target_pairs={{0,4},{1,5},{4,8},{5,9},{8,12},{9,13},{12,14},{13,15},{14,10},{15,... | collective-permute-start | bytes 331784 | tf_op jit(solution)/shard_map/ppermute | solution.py:575
  31.1 0.0 copy-start.8
  31.1 0.0 copy-start.9
  31.1 0.1 collective-permute-start.16
  31.2 1.4 %shard_map.123.refs_2_ = bf16[1056,768]{1,0:T(8,128)(2,1)S(1)} custom-call(bf16[136,768]{1,0:T(8,128)(2,1)S(1)} %collective-permute-done.7.refs_0_, bf16[136,768]{1,0:T(8,128)(2,1)S(1)} %collective-permute-done.8.refs_1_, bf16[136,768]{1,0:T(8,128)(2,1)S(1)} %collective-permute-done.9.refs_2_, bf16[136,768]{1,0:T(8,128)(2,1)S(1)} %collective-permute-done.10.refs_3_, ...), custom_call_target="tpu_custom_call" | custom-call | flops 1207959552 | bytes 4718592 | tf_op jit(solution)/shard_map/pallas_call | solution.py:545
  32.6 0.4 copy-done
  32.9 0.9 %shard_map.129 = (f32[1280,256]{1,0:T(8,128)S(1)}, f32[8,256]{1,0:T(8,128)S(1)}, f32[8,256]{1,0:T(8,128)S(1)}) custom-call(bf16[528,768]{1,0:T(8,128)(2,1)S(1)} %shard_map.119.refs_0_, bf16[1056,768]{1,0:T(8,128)(2,1)S(1)} %shard_map.122.refs_1_, bf16[1056,768]{1,0:T(8,128)(2,1)S(1)} %shard_map.123.refs_2_, bf16[6144,256]{1,0:T(8,128)(2,1)S(1)} %copy-done, ...), custom_call_target="tpu_custom_call" | custom-call | flops 503316480 | bytes 5898240 | tf_op jit(solution)/shard_map/pallas_call | solution.py:545
  33.8 2.2 %collective-permute-done.16.refs_5_ = bf16[64,768]{1,0:T(8,128)(2,1)S(1)} collective-permute-done((bf16[64,768]{1,0:T(8,128)(2,1)S(1)}, bf16[64,768]{1,0:T(8,128)(2,1)S(1)}, u32[]{:S(2)}, u32[]{:S(2)}) %collective-permute-start.16) | collective-permute-done | bytes 98336 | tf_op jit(solution)/shard_map/ppermute | solution.py:575
  36.0 0.5 %collective-permute-start.17 = (bf16[72,768]{1,0:T(8,128)(2,1)S(1)}, bf16[72,768]{1,0:T(8,128)(2,1)S(1)}, u32[]{:S(2)}, u32[]{:S(2)}) collective-permute-start(bf16[72,768]{1,0:T(8,128)(2,1)S(1)} %collective-permute-done.15.refs_4_), channel_id=1, source_target_pairs={{0,1},{1,0},{2,3},{3,2},{4,5},{5,4},{6,7},{7,6},{8,9},{9,8},{10,11... | collective-permute-start | bytes 331784 | tf_op jit(solution)/shard_map/ppermute | solution.py:578
  36.5 1.4 %shard_map.124.refs_0_.refs_3_ = bf16[1056,768]{1,0:T(8,128)(2,1)S(1)} custom-call(bf16[136,768]{1,0:T(8,128)(2,1)S(1)} %collective-permute-done.11.refs_0_.in_ref, bf16[136,768]{1,0:T(8,128)(2,1)S(1)} %collective-permute-done.12.refs_1_.in_ref, bf16[136,768]{1,0:T(8,128)(2,1)S(1)} %collective-permute-done.13.refs_2_, ...), custom_call_target="tpu_custom_call" | custom-call | flops 1207959552 | bytes 4718592 | tf_op jit(solution)/shard_map/pallas_call | solution.py:545
  37.9 0.0 copy-start.5
  37.9 0.0 copy-start.7
  37.9 0.7 %shard_map.130 = (f32[512,256]{1,0:T(8,128)S(1)}, f32[8,256]{1,0:T(8,128)S(1)}, f32[8,256]{1,0:T(8,128)S(1)}) custom-call(bf16[1056,768]{1,0:T(8,128)(2,1)S(1)} %shard_map.124.refs_0_.refs_3_, f32[8,256]{1,0:T(8,128)S(1)} %get-tuple-element.22.refs_1_.refs_11_, f32[8,256]{1,0:T(8,128)S(1)} %get-tuple-element.23.refs_2_, bf16[6144,256]{1,0:T(8,128)(2,1)S(1)} %copy-done, ...), custom_call_target="tpu_custom_call" | custom-call | flops 201326592 | bytes 2359296 | tf_op jit(solution)/shard_map/pallas_call | solution.py:545
  38.7 0.5 %copy-done.5 = bf16[768,768]{1,0:T(8,128)(2,1)S(1)} copy-done((bf16[768,768]{1,0:T(8,128)(2,1)S(1)}, bf16[768,768]{1,0:T(8,128)(2,1)}, u32[]{:S(2)}) %copy-start.5) | copy-done | bytes 1179672
  39.2 0.0 copy-done.7
  39.2 3.2 %shard_map.131 = bf16[16,8,768]{2,1,0:T(8,128)(2,1)} custom-call(bf16[528,768]{1,0:T(8,128)(2,1)S(1)} %shard_map.119.refs_0_, bf16[1056,768]{1,0:T(8,128)(2,1)S(1)} %shard_map.122.refs_1_, bf16[1056,768]{1,0:T(8,128)(2,1)S(1)} %shard_map.123.refs_2_, bf16[1056,768]{1,0:T(8,128)(2,1)S(1)} %shard_map.124.refs_0_.refs_3_, ...), custom_call_target="tpu_custom_call" | custom-call | flops 100663296 | bytes 3145728 | tf_op jit(solution)/shard_map/pallas_call | solution.py:545
  (26 shorter events, 0.1 us)
Async XLA Ops:
  0.0 9.2 %collective-permute-start.1 = (bf16[16,8,768]{2,1,0:T(8,128)(2,1)}, bf16[16,8,768]{2,1,0:T(8,128)(2,1)S(1)}, u32[]{:S(2)}, u32[]{:S(2)}) collective-permute-start(bf16[16,8,768]{2,1,0:T(8,128)(2,1)} %refs_20_.1), channel_id=1, source_target_pairs={{0,4},{1,5},{4,8},{5,9},{8,12},{9,13},{12,14},{13,15},{14,10},{15,... | collective-permute-start | bytes 589832 | tf_op jit(solution)/shard_map/ppermute | solution.py:575
  3.1 8.6 %collective-permute-start.3 = (bf16[16,8,768]{2,1,0:T(8,128)(2,1)}, bf16[16,8,768]{2,1,0:T(8,128)(2,1)S(1)}, u32[]{:S(2)}, u32[]{:S(2)}) collective-permute-start(bf16[16,8,768]{2,1,0:T(8,128)(2,1)} %refs_20_.1), channel_id=1, source_target_pairs={{0,2},{1,3},{4,0},{5,1},{8,4},{9,5},{12,8},{13,9},{14,12},{15,13},... | collective-permute-start | bytes 589832 | tf_op jit(solution)/shard_map/ppermute | solution.py:575
  5.2 4.0 %collective-permute-start.2 = (bf16[8,768]{1,0:T(8,128)(2,1)}, bf16[8,768]{1,0:T(8,128)(2,1)S(1)}, u32[]{:S(2)}, u32[]{:S(2)}) collective-permute-start(bf16[8,768]{1,0:T(8,128)(2,1)} %get-tuple-element.18.refs_6_.refs_19_), channel_id=1, source_target_pairs={{0,4},{1,5},{4,8},{5,9},{8,12},{9,13},{12,14},{13,15},{14,10},{15,... | collective-permute-start | bytes 36872 | tf_op jit(solution)/shard_map/ppermute | solution.py:575
  7.2 4.4 %collective-permute-start.4 = (bf16[8,768]{1,0:T(8,128)(2,1)}, bf16[8,768]{1,0:T(8,128)(2,1)S(1)}, u32[]{:S(2)}, u32[]{:S(2)}) collective-permute-start(bf16[8,768]{1,0:T(8,128)(2,1)} %get-tuple-element.18.refs_6_.refs_19_), channel_id=1, source_target_pairs={{0,2},{1,3},{4,0},{5,1},{8,4},{9,5},{12,8},{13,9},{14,12},{15,13},... | collective-permute-start | bytes 36872 | tf_op jit(solution)/shard_map/ppermute | solution.py:575
  9.6 6.0 %collective-permute-start.7 = (bf16[136,768]{1,0:T(8,128)(2,1)S(1)}, bf16[136,768]{1,0:T(8,128)(2,1)S(1)}, u32[]{:S(2)}, u32[]{:S(2)}) collective-permute-start(bf16[136,768]{1,0:T(8,128)(2,1)S(1)} %shard_map.120.refs_0_), channel_id=1, source_target_pairs={{0,4},{1,5},{4,8},{5,9},{8,12},{9,13},{12,14},{13,15},{14,10},{15,... | collective-permute-start | bytes 626696 | tf_op jit(solution)/shard_map/ppermute | solution.py:575
  12.0 5.9 %collective-permute-start.8 = (bf16[136,768]{1,0:T(8,128)(2,1)S(1)}, bf16[136,768]{1,0:T(8,128)(2,1)S(1)}, u32[]{:S(2)}, u32[]{:S(2)}) collective-permute-start(bf16[136,768]{1,0:T(8,128)(2,1)S(1)} %shard_map.121.refs_1_), channel_id=1, source_target_pairs={{0,2},{1,3},{4,0},{5,1},{8,4},{9,5},{12,8},{13,9},{14,12},{15,13},... | collective-permute-start | bytes 626696 | tf_op jit(solution)/shard_map/ppermute | solution.py:575
  12.1 10.4 %collective-permute-start = (bf16[136,768]{1,0:T(8,128)(2,1)}, bf16[136,768]{1,0:T(8,128)(2,1)}, u32[]{:S(2)}, u32[]{:S(2)}) collective-permute-start(bf16[136,768]{1,0:T(8,128)(2,1)} %get-tuple-element.17.refs_0_.pay_hbm), channel_id=1, source_target_pairs={{0,1},{1,0},{2,3},{3,2},{4,5},{5,4},{6,7},{7,6},{8,9},{9,8},{10,11... | collective-permute-start | bytes 626696 | tf_op jit(solution)/shard_map/ppermute | solution.py:578
  12.2 10.9 %collective-permute-start.5 = (bf16[136,768]{1,0:T(8,128)(2,1)S(1)}, bf16[136,768]{1,0:T(8,128)(2,1)S(1)}, u32[]{:S(2)}, u32[]{:S(2)}) collective-permute-start(bf16[136,768]{1,0:T(8,128)(2,1)S(1)} %shard_map.120.refs_0_), channel_id=1, source_target_pairs={{0,1},{1,0},{2,3},{3,2},{4,5},{5,4},{6,7},{7,6},{8,9},{9,8},{10,11... | collective-permute-start | bytes 626696 | tf_op jit(solution)/shard_map/ppermute | solution.py:578
  15.5 11.5 %collective-permute-start.11 = (bf16[136,768]{1,0:T(8,128)(2,1)S(1)}, bf16[136,768]{1,0:T(8,128)(2,1)S(1)}, u32[]{:S(2)}, u32[]{:S(2)}) collective-permute-start(bf16[136,768]{1,0:T(8,128)(2,1)S(1)} %collective-permute-done.7.refs_0_), channel_id=1, source_target_pairs={{0,4},{1,5},{4,8},{5,9},{8,12},{9,13},{12,14},{13,15},{14,10},{15,... | collective-permute-start | bytes 626696 | tf_op jit(solution)/shard_map/ppermute | solution.py:575
  17.9 9.6 %collective-permute-start.12 = (bf16[136,768]{1,0:T(8,128)(2,1)S(1)}, bf16[136,768]{1,0:T(8,128)(2,1)S(1)}, u32[]{:S(2)}, u32[]{:S(2)}) collective-permute-start(bf16[136,768]{1,0:T(8,128)(2,1)S(1)} %collective-permute-done.8.refs_1_), channel_id=1, source_target_pairs={{0,2},{1,3},{4,0},{5,1},{8,4},{9,5},{12,8},{13,9},{14,12},{15,13},... | collective-permute-start | bytes 626696 | tf_op jit(solution)/shard_map/ppermute | solution.py:575
  17.9 9.7 %collective-permute-start.6 = (bf16[136,768]{1,0:T(8,128)(2,1)S(1)}, bf16[136,768]{1,0:T(8,128)(2,1)S(1)}, u32[]{:S(2)}, u32[]{:S(2)}) collective-permute-start(bf16[136,768]{1,0:T(8,128)(2,1)S(1)} %shard_map.121.refs_1_), channel_id=1, source_target_pairs={{0,1},{1,0},{2,3},{3,2},{4,5},{5,4},{6,7},{7,6},{8,9},{9,8},{10,11... | collective-permute-start | bytes 626696 | tf_op jit(solution)/shard_map/ppermute | solution.py:578
  17.9 5.2 %copy-start.3 = (bf16[136,768]{1,0:T(8,128)(2,1)S(1)}, bf16[136,768]{1,0:T(8,128)(2,1)}, u32[]{:S(2)}) copy-start(bf16[136,768]{1,0:T(8,128)(2,1)} %get-tuple-element.17.refs_0_.pay_hbm) | copy-start | bytes 626692
  17.9 5.2 %copy-start.4 = (bf16[768,768]{1,0:T(8,128)(2,1)S(1)}, bf16[768,768]{1,0:T(8,128)(2,1)}, u32[]{:S(2)}) copy-start(bf16[768,768]{1,0:T(8,128)(2,1)} %wg_hbm.1) | copy-start | bytes 3538948
  17.9 5.2 %copy-start.6 = (bf16[16,256,128]{2,1,0:T(8,128)(2,1)S(1)}, bf16[16,256,128]{2,1,0:T(8,128)(2,1)}, u32[]{:S(2)}) copy-start(bf16[16,256,128]{2,1,0:T(8,128)(2,1)} %pair_hbm.1) | copy-start | bytes 3145732
  17.9 5.2 %copy-start.10 = (bf16[128,16]{0,1:T(8,128)(2,1)S(1)}, bf16[128,16]{0,1:T(8,128)(2,1)}, u32[]{:S(2)}) copy-start(bf16[128,16]{0,1:T(8,128)(2,1)} %param.22) | copy-start | bytes 12292
  22.5 2.8 %copy-start.1 = (bf16[768,768]{1,0:T(8,128)(2,1)S(1)}, bf16[768,768]{1,0:T(8,128)(2,1)}, u32[]{:S(2)}) copy-start(bf16[768,768]{1,0:T(8,128)(2,1)} %refs_15_.1) | copy-start | bytes 3538948
  22.5 2.8 %copy-start.2 = (bf16[768,768]{1,0:T(8,128)(2,1)S(1)}, bf16[768,768]{1,0:T(8,128)(2,1)}, u32[]{:S(2)}) copy-start(bf16[768,768]{1,0:T(8,128)(2,1)} %refs_16_.1) | copy-start | bytes 3538948
  22.5 8.6 %collective-permute-start.9 = (bf16[136,768]{1,0:T(8,128)(2,1)S(1)}, bf16[136,768]{1,0:T(8,128)(2,1)S(1)}, u32[]{:S(2)}, u32[]{:S(2)}) collective-permute-start(bf16[136,768]{1,0:T(8,128)(2,1)S(1)} %collective-permute-done.7.refs_0_), channel_id=1, source_target_pairs={{0,1},{1,0},{2,3},{3,2},{4,5},{5,4},{6,7},{7,6},{8,9},{9,8},{10,11... | collective-permute-start | bytes 626696 | tf_op jit(solution)/shard_map/ppermute | solution.py:578
  23.1 8.1 %collective-permute-start.10 = (bf16[136,768]{1,0:T(8,128)(2,1)S(1)}, bf16[136,768]{1,0:T(8,128)(2,1)S(1)}, u32[]{:S(2)}, u32[]{:S(2)}) collective-permute-start(bf16[136,768]{1,0:T(8,128)(2,1)S(1)} %collective-permute-done.8.refs_1_), channel_id=1, source_target_pairs={{0,1},{1,0},{2,3},{3,2},{4,5},{5,4},{6,7},{7,6},{8,9},{9,8},{10,11... | collective-permute-start | bytes 626696 | tf_op jit(solution)/shard_map/ppermute | solution.py:578
  27.0 9.5 %collective-permute-start.13 = (bf16[136,768]{1,0:T(8,128)(2,1)S(1)}, bf16[136,768]{1,0:T(8,128)(2,1)S(1)}, u32[]{:S(2)}, u32[]{:S(2)}) collective-permute-start(bf16[136,768]{1,0:T(8,128)(2,1)S(1)} %collective-permute-done.11.refs_0_.in_ref), channel_id=1, source_target_pairs={{0,1},{1,0},{2,3},{3,2},{4,5},{5,4},{6,7},{7,6},{8,9},{9,8},{10,11... | collective-permute-start | bytes 626696 | tf_op jit(solution)/shard_map/ppermute | solution.py:578
  27.5 9.0 %collective-permute-start.14 = (bf16[136,768]{1,0:T(8,128)(2,1)S(1)}, bf16[136,768]{1,0:T(8,128)(2,1)S(1)}, u32[]{:S(2)}, u32[]{:S(2)}) collective-permute-start(bf16[136,768]{1,0:T(8,128)(2,1)S(1)} %collective-permute-done.12.refs_1_.in_ref), channel_id=1, source_target_pairs={{0,1},{1,0},{2,3},{3,2},{4,5},{5,4},{6,7},{7,6},{8,9},{9,8},{10,11... | collective-permute-start | bytes 626696 | tf_op jit(solution)/shard_map/ppermute | solution.py:578
  29.0 7.0 %collective-permute-start.15 = (bf16[72,768]{1,0:T(8,128)(2,1)S(1)}, bf16[72,768]{1,0:T(8,128)(2,1)S(1)}, u32[]{:S(2)}, u32[]{:S(2)}) collective-permute-start(bf16[72,768]{1,0:T(8,128)(2,1)S(1)} %shard_map.125), channel_id=1, source_target_pairs={{0,4},{1,5},{4,8},{5,9},{8,12},{9,13},{12,14},{13,15},{14,10},{15,... | collective-permute-start | bytes 331784 | tf_op jit(solution)/shard_map/ppermute | solution.py:575
  31.0 1.9 %copy-start = (bf16[6144,256]{1,0:T(8,128)(2,1)S(1)}, bf16[6144,256]{1,0:T(8,128)(2,1)}, u32[]{:S(2)}) copy-start(bf16[6144,256]{1,0:T(8,128)(2,1)} %shard_map.127.refs_3_.refs_8_) | copy-start | bytes 9437188
  31.1 1.9 %copy-start.8 = (bf16[8,768]{1,0:T(8,128)(2,1)S(1)}, bf16[8,768]{1,0:T(8,128)(2,1)}, u32[]{:S(2)}) copy-start(bf16[8,768]{1,0:T(8,128)(2,1)} %get-tuple-element.18.refs_6_.refs_19_) | copy-start | bytes 36868
  31.1 1.9 %copy-start.9 = (f32[66,16]{0,1:T(8,128)S(1)}, f32[66,16]{0,1:T(8,128)}, u32[]{:S(2)}) copy-start(f32[66,16]{0,1:T(8,128)} %param.23) | copy-start | bytes 12676
  31.1 4.9 %collective-permute-start.16 = (bf16[64,768]{1,0:T(8,128)(2,1)S(1)}, bf16[64,768]{1,0:T(8,128)(2,1)S(1)}, u32[]{:S(2)}, u32[]{:S(2)}) collective-permute-start(bf16[64,768]{1,0:T(8,128)(2,1)S(1)} %shard_map.126), channel_id=1, source_target_pairs={{0,2},{1,3},{4,0},{5,1},{8,4},{9,5},{12,8},{13,9},{14,12},{15,13},... | collective-permute-start | bytes 294920 | tf_op jit(solution)/shard_map/ppermute | solution.py:575
  36.0 2.7 %collective-permute-start.18 = (bf16[64,768]{1,0:T(8,128)(2,1)S(1)}, bf16[64,768]{1,0:T(8,128)(2,1)S(1)}, u32[]{:S(2)}, u32[]{:S(2)}) collective-permute-start(bf16[64,768]{1,0:T(8,128)(2,1)S(1)} %collective-permute-done.16.refs_5_), channel_id=1, source_target_pairs={{0,1},{1,0},{2,3},{3,2},{4,5},{5,4},{6,7},{7,6},{8,9},{9,8},{10,11... | collective-permute-start | bytes 294920 | tf_op jit(solution)/shard_map/ppermute | solution.py:578
  36.0 2.7 %collective-permute-start.17 = (bf16[72,768]{1,0:T(8,128)(2,1)S(1)}, bf16[72,768]{1,0:T(8,128)(2,1)S(1)}, u32[]{:S(2)}, u32[]{:S(2)}) collective-permute-start(bf16[72,768]{1,0:T(8,128)(2,1)S(1)} %collective-permute-done.15.refs_4_), channel_id=1, source_target_pairs={{0,1},{1,0},{2,3},{3,2},{4,5},{5,4},{6,7},{7,6},{8,9},{9,8},{10,11... | collective-permute-start | bytes 331784 | tf_op jit(solution)/shard_map/ppermute | solution.py:578
  37.9 1.3 %copy-start.5 = (bf16[768,768]{1,0:T(8,128)(2,1)S(1)}, bf16[768,768]{1,0:T(8,128)(2,1)}, u32[]{:S(2)}) copy-start(bf16[768,768]{1,0:T(8,128)(2,1)} %refs_21_.1) | copy-start | bytes 3538948
  37.9 1.3 %copy-start.7 = (bf16[16,8,768]{2,1,0:T(8,128)(2,1)S(1)}, bf16[16,8,768]{2,1,0:T(8,128)(2,1)}, u32[]{:S(2)}) copy-start(bf16[16,8,768]{2,1,0:T(8,128)(2,1)} %refs_20_.1) | copy-start | bytes 589828

commit v7 on v6

--- a/solution.py
+++ b/solution.py
@@ -289,31 +289,16 @@
     out_ref[pl.ds(rows, META_ROWS), :] = meta_ref[...]
 
 
-def query_body(samples, heads, pay_hbm, wq_hbm, out_ref, pay_ref, wq_ref, q_ref, sems):
-    copies = []
-    for i, (source, target) in enumerate(((pay_hbm, pay_ref), (wq_hbm, wq_ref))):
-        copies.append(pltpu.make_async_copy(source, target, sems.at[i]))
-        copies[i].start()
-    for copy in copies:
-        copy.wait()
+def query_body(samples, heads, me_ref, pay_ref, wq_ref, out_ref, q_ref):
     q_ref[...] = matmul(pay_ref[pl.ds(0, q_ref.shape[0]), :], wq_ref[...]).astype(BF16)
     spread_queries(samples, heads, q_ref, out_ref)
 
 
-def own_body(
-    steps, chips, me_ref, pay_hbm, wg_hbm, pair_hbm, wp_hbm, gate_ref, *refs
-):
-    pay_ref, wg_ref, pair_ref, wp_ref, sems = refs[-5:]
-    copies = []
-    moves = ((wp_hbm, wp_ref), (pair_hbm, pair_ref), (pay_hbm, pay_ref), (wg_hbm, wg_ref))
-    for i, (source, target) in enumerate(moves):
-        copies.append(pltpu.make_async_copy(source, target, sems.at[i]))
-        copies[i].start()
-    copies[0].wait()
-    copies[1].wait()
-    pair_rows(steps, chips, me_ref[0], pair_ref, wp_ref[...], refs[:-5])
-    copies[2].wait()
-    copies[3].wait()
+def pair_body(steps, chips, me_ref, pair_ref, wp_ref, *out_refs):
+    pair_rows(steps, chips, me_ref[0], pair_ref, wp_ref[...], out_refs)
+
+
+def gate_body(pay_ref, wg_ref, gate_ref):
     data = pay_ref[pl.ds(0, gate_ref.shape[0]), :]
     gate_ref[...] = jax.nn.sigmoid(matmul(data, wg_ref[...]))
 
@@ -482,26 +467,28 @@
         exp_ref[pl.ds(s * count, count), :] = weights
 
 
-def finish_body(heads, scale, *refs):
+def finish_body(heads, scale, split, *refs):
     (
-        q_ref, gate_ref, first_ref, first_top_ref, second_ref, top_ref, mass_ref, wk_ref, wv_ref,
-        pair_ref, tab_ref, own_ref, single_ref, wo_ref, out_ref, pad_ref, weight_ref,
-    ) = refs[-17:]
-    kv_refs, lasts = refs[:-21], refs[-21:-17]
+        q_ref, gate_ref, exp_ref, top_ref, mass_ref, wk_ref, wv_ref, pair_ref, tab_ref, own_ref,
+        single_ref, wo_ref, out_ref, pad_ref, weight_ref,
+    ) = refs[-15:]
+    kv_refs, lasts = refs[:-19], refs[-19:-15]
     tokens, samples, width = single_ref.shape
     rows = tokens * samples
     half = rows // 2
     hs = width // heads
-    metas = [r[pl.ds(half, META_ROWS), :] for r in (lasts[0], lasts[2])]
+    metas = kv_metas(kv_refs[split:], rows) + [r[pl.ds(half, META_ROWS), :] for r in (lasts[0], lasts[2])]
     data = jnp.concatenate([r[pl.ds(0, half), :] for r in lasts], axis=0)
     k_last = matmul(data, wk_ref[...]).astype(BF16)
     v_last = matmul(data, wv_ref[...]).astype(BF16)
     bias = full_bias(own_ref[...], metas, tokens, pair_ref, tab_ref, pad_ref)
+    count = exp_ref.shape[0] // samples
     lane_head = lax.broadcasted_iota(jnp.int32, (tokens, width), 1) // hs
     lines = heads * tokens
     for s in range(samples):
         new = [slice(u * rows + s * tokens, u * rows + (s + 1) * tokens) for u in range(2)]
-        keys = jnp.concatenate([k_last[n] for n in new], axis=0)
+        keys = gather(kv_refs[split:], rows, s * tokens, tokens, False)
+        keys = jnp.concatenate(keys + [k_last[n] for n in new], axis=0)
         scores = matmul(keys, q_ref[pl.ds(s * width, width), :]) * scale + bias
         before = top_ref[pl.ds(s, 1), :]
         top = jnp.maximum(jnp.max(scores, axis=0, keepdims=True), before)
@@ -509,11 +496,8 @@
         late = jnp.exp(scores - top)
         mass = jnp.sum(late, axis=0, keepdims=True) + mass_ref[pl.ds(s, 1), :] * shrink
         inv = 1.0 / mass
-        weights = []
-        for ref, old in ((first_ref, first_top_ref[pl.ds(s, 1), :]), (second_ref, before)):
-            count = ref.shape[0] // samples
-            weights.append(ref[pl.ds(s * count, count), :] * (jnp.exp(old - top) * inv))
-        weights = jnp.concatenate(weights + [late * inv], axis=0)
+        old = exp_ref[pl.ds(s * count, count), :] * (shrink * inv)
+        weights = jnp.concatenate([old, late * inv], axis=0)
         weight_ref[pl.ds(s * lines, lines), :] = jnp.transpose(weights).astype(BF16)
     gated = []
     for s in range(samples):
@@ -601,22 +585,22 @@
     )
     cw_meta = ring(meta, 1)
     ccw_meta = ring(meta, -1)
-    other = flip(payload)
     lines = heads * tokens
     query = call(
         functools.partial(query_body, samples, heads),
         jax.ShapeDtypeStruct((samples * width, lines), BF16),
-        (payload, w_query),
-        in_specs=[ANY] * 2,
+        (me, payload, w_query),
+        in_specs=[SMEM, VMEM, VMEM],
         flops=2 * rows * width * (width + lines),
         moved=2 * width * width + 2 * samples * width * lines,
-        limit=FULL,
-        scratch=[
-            pltpu.VMEM(blocks.shape, BF16),
-            pltpu.VMEM((width, width), BF16),
-            pltpu.VMEM((rows, width), BF16),
-            pltpu.SemaphoreType.DMA((2,)),
-        ],
+        scratch=[pltpu.VMEM((rows, width), BF16)],
+    )
+    gate = call(
+        gate_body,
+        jax.ShapeDtypeStruct((rows, width), F32),
+        (payload, w_gate),
+        flops=2 * rows * width * width,
+        moved=2 * width * width + 6 * rows * width,
     )
 
     def join(value, extra):
@@ -646,27 +630,18 @@
         shape = jax.ShapeDtypeStruct((count, width), BF16)
         return call(body, shape, (value,), moved=2 * rows * width)
 
-    sizes = [len(steps) - 3 * CORES, 2 * CORES, CORES]
-    gate, *pair_bias = call(
-        functools.partial(own_body, steps, chips),
-        (
-            jax.ShapeDtypeStruct((rows, width), F32),
-            *(jax.ShapeDtypeStruct((n * tokens, lines), F32) for n in sizes),
-        ),
-        (me, payload, w_gate, pair, w_pair.T),
-        in_specs=[SMEM] + [ANY] * 4,
-        flops=2 * rows * width * width + 2 * pair.size * lines,
-        moved=2 * width * width + 6 * rows * width + 2 * pair.size,
+    sizes = [len(steps) - 3 * CORES, 3 * CORES]
+    pair_bias = call(
+        functools.partial(pair_body, steps, chips),
+        tuple(jax.ShapeDtypeStruct((n * tokens, lines), F32) for n in sizes),
+        (me, pair, w_pair.T),
+        in_specs=[SMEM, VMEM, VMEM],
+        flops=2 * pair.size * lines,
+        moved=2 * pair.size + 4 * total * lines,
         limit=(6 << 20) + 4 * pair.size,
-        scratch=[
-            pltpu.VMEM(blocks.shape, BF16),
-            pltpu.VMEM((width, width), BF16),
-            pltpu.VMEM(pair.shape, BF16),
-            pltpu.VMEM(w_pair.shape[::-1], BF16),
-            pltpu.SemaphoreType.DMA((4,)),
-        ],
-    )
-    kvs = [kv([payload, other])]
+    )
+    kvs = [kv([payload])]
+    kvs.append(flip(kvs[-1]))
     for k in range(1, half):
         if k + 1 < half:
             cw_next = ring(cw, 1)
@@ -674,8 +649,8 @@
         else:
             cw_next = ring(piece(cw, 0, True), 1)
             ccw_next = ring(piece(ccw, rows // 2, False), -1)
-        cw_other, ccw_other = flip(cw), flip(ccw)
-        kvs.append(kv([cw, ccw, cw_other, ccw_other]))
+        kvs.append(kv([cw, ccw]))
+        kvs.append(flip(kvs[-1]))
         cw, ccw = cw_next, ccw_next
     scale = 1.0 / math.sqrt(width // heads)
     state = jax.ShapeDtypeStruct((samples, lines), F32)
@@ -683,27 +658,24 @@
     pad = [pltpu.VMEM((heads, LANES), F32)]
     limit = (10 << 20) + 4 * samples * total * width
 
-    def weights(at, parts, before):
-        keys = sizes[at] * tokens
-        return call(
-            functools.partial(weights_body, samples, scale, bool(before)),
-            (jax.ShapeDtypeStruct((samples * keys, lines), F32), state, state),
-            (*parts, *before, query, pair_bias[at], table, meta),
-            flops=2 * samples * keys * width * lines,
-            moved=6 * samples * keys * width,
-            limit=limit,
-            scratch=pad,
-        )
-
-    first = weights(0, kvs[:-1], ())
-    second = weights(1, kvs[-1:], first[1:])
+    split = 2 * (half - 1)
+    keys = sizes[0] * tokens
+    first = call(
+        functools.partial(weights_body, samples, scale, False),
+        (jax.ShapeDtypeStruct((samples * keys, lines), F32), state, state),
+        (*kvs[:split], query, pair_bias[0], table, meta),
+        flops=2 * samples * keys * width * lines,
+        moved=6 * samples * keys * width,
+        limit=limit,
+        scratch=pad,
+    )
     cw_other, ccw_other = flip(cw), flip(ccw)
     return call(
-        functools.partial(finish_body, heads, scale),
+        functools.partial(finish_body, heads, scale, split),
         jax.ShapeDtypeStruct(single.shape, BF16),
         (
-            *kvs, cw, ccw, cw_other, ccw_other, query, gate, *first[:2], *second, w_key, w_value,
-            pair_bias[2], table, meta, single, w_out,
+            *kvs, cw, ccw, cw_other, ccw_other, query, gate, *first, w_key, w_value,
+            pair_bias[1], table, meta, single, w_out,
         ),
         flops=4 * rows * total * width,
         moved=2 * samples * total * width,

time: 42.6 us -> 46.9 us (1.10)
  local copies, waits for them, and re-layouts: 0.93 us -> 5.59 us
  waiting for transfers between devices: 7.4 us -> 11.1 us
  Pallas kernels: 20.2 us -> 16.6 us
  starting transfers between devices: 13.6 us -> 13 us
    unnamed x22 -> x34, local copies, waits for them, and re-layouts: 0.93 us -> 5.59 us
    pallas_call x14, Pallas kernels: 20.2 us -> 16.6 us  [call(): pl.pallas_call(body, out_shape=out_shape, in_specs=in_specs or [VMEM] * l...]
    ppermute x10, waiting for transfers between devices: 7.38 us -> 10.7 us  [ring(): return lax.ppermute(value, 'tok', pairs)]
    ppermute x9 -> x6, starting transfers between devices: 2.28 us -> 1.2 us  [flip(): return lax.ppermute(value, 'tok', [(d, d ^ 1) for d in range(devices)])]
  transfers between devices with their start and end apart: 19 -> 16, of which waited for: 4 -> 7; matrix products, arithmetic and copies ran while one was open for 0% -> 0% of each run, Pallas kernels for 40% -> 25%
where the time goes in v7:
time: 46.9 us; the launch traced here: 46.6 us
  Pallas kernels  16.6 us (35%)
  starting transfers between devices  13 us (28%)
  waiting for transfers between devices  11.1 us (24%)
  local copies, waits for them, and re-layouts  5.59 us (12%)
    pallas_call x14, Pallas kernels, call(): pl.pallas_call(body, out_shape=out_shape, in_specs=in_specs or [VMEM] * l...  16.6 us
    ppermute x10, starting transfers between devices, ring(): return lax.ppermute(value, 'tok', pairs)  11.8 us
    ppermute x10, waiting for transfers between devices, ring(): return lax.ppermute(value, 'tok', pairs)  10.7 us
    unnamed x34, local copies, waits for them, and re-layouts  5.59 us
    ppermute x6, starting transfers between devices, flip(): return lax.ppermute(value, 'tok', [(d, d ^ 1) for d in range(devices)])  1.2 us
  transfers between devices with their start and end apart: 16, of which 7 were waited for; matrix products, arithmetic and copies ran while one was open for 0% of the time, Pallas kernels for 25%

profile of v7, /device:TPU:0, one launch (start us, length us, event | category | flops | bytes accessed | tf_op | source)
XLA Modules:
  0.0 46.6 jit_solution(5386498094770401283)
XLA Ops:
  0.0 3.1 %collective-permute-start.1 = (bf16[16,8,768]{2,1,0:T(8,128)(2,1)}, bf16[16,8,768]{2,1,0:T(8,128)(2,1)S(1)}, u32[]{:S(2)}, u32[]{:S(2)}) collective-permute-start(bf16[16,8,768]{2,1,0:T(8,128)(2,1)} %refs_22_.1), channel_id=1, source_target_pairs={{0,4},{1,5},{4,8},{5,9},{8,12},{9,13},{12,14},{13,15},{14,10},{15,... | collective-permute-start | bytes 589832 | tf_op jit(solution)/shard_map/ppermute | solution.py:559
  3.1 0.0 collective-permute-start.3
  3.1 2.1 %shard_map.118 = (bf16[136,768]{1,0:T(8,128)(2,1)}, bf16[8,768]{1,0:T(8,128)(2,1)}) custom-call(bf16[16,8,768]{2,1,0:T(8,128)(2,1)} %refs_22_.1, s32[1,16]{1,0:T(1,128)} %bitcast.9, s32[1,16]{1,0:T(1,128)} %bitcast.10, s32[1,16]{1,0:T(1,128)} %bitcast.11), custom_call_target="tpu_custom_call" | custom-call | flops 1572864 | bytes 393216 | tf_op jit(solution)/shard_map/pallas_call | solution.py:529
  5.2 2.0 %collective-permute-start.2 = (bf16[8,768]{1,0:T(8,128)(2,1)}, bf16[8,768]{1,0:T(8,128)(2,1)S(1)}, u32[]{:S(2)}, u32[]{:S(2)}) collective-permute-start(bf16[8,768]{1,0:T(8,128)(2,1)} %get-tuple-element.13.refs_9_.refs_21_), channel_id=1, source_target_pairs={{0,4},{1,5},{4,8},{5,9},{8,12},{9,13},{12,14},{13,15},{14,10},{15,... | collective-permute-start | bytes 36872 | tf_op jit(solution)/shard_map/ppermute | solution.py:559
  7.2 0.0 collective-permute-start.4
  7.3 1.9 %collective-permute-done.2.meta_ref = bf16[8,768]{1,0:T(8,128)(2,1)S(1)} collective-permute-done((bf16[8,768]{1,0:T(8,128)(2,1)}, bf16[8,768]{1,0:T(8,128)(2,1)S(1)}, u32[]{:S(2)}, u32[]{:S(2)}) %collective-permute-start.2) | collective-permute-done | bytes 12320 | tf_op jit(solution)/shard_map/ppermute | solution.py:559
  9.1 0.0 collective-permute-done.1.single_ref
  9.1 0.4 shard_map.120.refs_0_
  9.5 2.0 %collective-permute-start.6 = (bf16[136,768]{1,0:T(8,128)(2,1)S(1)}, bf16[136,768]{1,0:T(8,128)(2,1)S(1)}, u32[]{:S(2)}, u32[]{:S(2)}) collective-permute-start(bf16[136,768]{1,0:T(8,128)(2,1)S(1)} %shard_map.120.refs_0_), channel_id=1, source_target_pairs={{0,4},{1,5},{4,8},{5,9},{8,12},{9,13},{12,14},{13,15},{14,10},{15,... | collective-permute-start | bytes 626696 | tf_op jit(solution)/shard_map/ppermute | solution.py:559
  11.6 0.4 shard_map.121.refs_1_
  12.0 0.1 collective-permute-start.7
  12.1 3.4 %collective-permute-done.6.refs_0_ = bf16[136,768]{1,0:T(8,128)(2,1)S(1)} collective-permute-done((bf16[136,768]{1,0:T(8,128)(2,1)S(1)}, bf16[136,768]{1,0:T(8,128)(2,1)S(1)}, u32[]{:S(2)}, u32[]{:S(2)}) %collective-permute-start.6) | collective-permute-done | bytes 208928 | tf_op jit(solution)/shard_map/ppermute | solution.py:559
  15.5 1.9 %collective-permute-start.9 = (bf16[136,768]{1,0:T(8,128)(2,1)S(1)}, bf16[136,768]{1,0:T(8,128)(2,1)S(1)}, u32[]{:S(2)}, u32[]{:S(2)}) collective-permute-start(bf16[136,768]{1,0:T(8,128)(2,1)S(1)} %collective-permute-done.6.refs_0_), channel_id=1, source_target_pairs={{0,4},{1,5},{4,8},{5,9},{8,12},{9,13},{12,14},{13,15},{14,10},{15,... | collective-permute-start | bytes 626696 | tf_op jit(solution)/shard_map/ppermute | solution.py:559
  17.4 0.5 %collective-permute-done.7.refs_1_ = bf16[136,768]{1,0:T(8,128)(2,1)S(1)} collective-permute-done((bf16[136,768]{1,0:T(8,128)(2,1)S(1)}, bf16[136,768]{1,0:T(8,128)(2,1)S(1)}, u32[]{:S(2)}, u32[]{:S(2)}) %collective-permute-start.7) | collective-permute-done | bytes 208928 | tf_op jit(solution)/shard_map/ppermute | solution.py:559
  17.9 0.0 collective-permute-start.10
  17.9 1.3 %copy-done = bf16[768,768]{1,0:T(8,128)(2,1)S(1)} copy-done((bf16[768,768]{1,0:T(8,128)(2,1)S(1)}, bf16[768,768]{1,0:T(8,128)(2,1)}, u32[]{:S(2)}) %copy-start) | copy-done | bytes 1179672
  19.2 1.3 %copy-done.2 = bf16[768,768]{1,0:T(8,128)(2,1)S(1)} copy-done((bf16[768,768]{1,0:T(8,128)(2,1)S(1)}, bf16[768,768]{1,0:T(8,128)(2,1)}, u32[]{:S(2)}) %copy-start.2) | copy-done | bytes 1179672
  20.4 0.8 %shard_map.122.refs_2_ = bf16[528,768]{1,0:T(8,128)(2,1)S(1)} custom-call(bf16[136,768]{1,0:T(8,128)(2,1)S(1)} %shard_map.120.refs_0_, bf16[136,768]{1,0:T(8,128)(2,1)S(1)} %shard_map.121.refs_1_, bf16[768,768]{1,0:T(8,128)(2,1)S(1)} %copy-done, bf16[768,768]{1,0:T(8,128)(2,1)S(1)} %copy-done.2), custom_call_target="tpu_custom_call" | custom-call | flops 603979776 | bytes 3538944 | tf_op jit(solution)/shard_map/pallas_call | solution.py:529
  21.2 0.1 collective-permute-start.5
  21.3 0.8 %shard_map.123.refs_4_ = bf16[528,768]{1,0:T(8,128)(2,1)S(1)} custom-call(bf16[136,768]{1,0:T(8,128)(2,1)S(1)} %collective-permute-done.6.refs_0_, bf16[136,768]{1,0:T(8,128)(2,1)S(1)} %collective-permute-done.7.refs_1_, bf16[768,768]{1,0:T(8,128)(2,1)S(1)} %copy-done, bf16[768,768]{1,0:T(8,128)(2,1)S(1)} %copy-done.2), custom_call_target="tpu_custom_call" | custom-call | flops 603979776 | bytes 3538944 | tf_op jit(solution)/shard_map/pallas_call | solution.py:529
  22.1 0.0 copy-start.1
  22.1 0.6 %collective-permute-start.8 = (bf16[528,768]{1,0:T(8,128)(2,1)S(1)}, bf16[528,768]{1,0:T(8,128)(2,1)}, u32[]{:S(2)}, u32[]{:S(2)}) collective-permute-start(bf16[528,768]{1,0:T(8,128)(2,1)S(1)} %shard_map.123.refs_4_), channel_id=1, source_target_pairs={{0,1},{1,0},{2,3},{3,2},{4,5},{5,4},{6,7},{7,6},{8,9},{9,8},{10,11... | collective-permute-start | bytes 2433032 | tf_op jit(solution)/shard_map/ppermute | solution.py:562
  22.7 0.0 collective-permute-done.9.refs_0_.in_ref
  22.7 1.0 %collective-permute-done.10.refs_1_.in_ref = bf16[136,768]{1,0:T(8,128)(2,1)S(1)} collective-permute-done((bf16[136,768]{1,0:T(8,128)(2,1)S(1)}, bf16[136,768]{1,0:T(8,128)(2,1)S(1)}, u32[]{:S(2)}, u32[]{:S(2)}) %collective-permute-start.10) | collective-permute-done | bytes 208928 | tf_op jit(solution)/shard_map/ppermute | solution.py:559
  23.7 1.7 %shard_map.124.refs_6_ = bf16[528,768]{1,0:T(8,128)(2,1)} custom-call(bf16[136,768]{1,0:T(8,128)(2,1)S(1)} %collective-permute-done.9.refs_0_.in_ref, bf16[136,768]{1,0:T(8,128)(2,1)S(1)} %collective-permute-done.10.refs_1_.in_ref, bf16[768,768]{1,0:T(8,128)(2,1)S(1)} %copy-done, bf16[768,768]{1,0:T(8,128)(2,1)S(1)} %copy-done.2), custom_call_target="tpu_custom_call" | custom-call | flops 603979776 | bytes 3538944 | tf_op jit(solution)/shard_map/pallas_call | solution.py:529
  25.3 0.0 copy-start.9
  25.3 0.5 %shard_map.119.refs_0_ = bf16[264,768]{1,0:T(8,128)(2,1)S(1)} custom-call(bf16[136,768]{1,0:T(8,128)(2,1)S(1)} %copy-done.4, bf16[768,768]{1,0:T(8,128)(2,1)S(1)} %copy-done.1, bf16[768,768]{1,0:T(8,128)(2,1)S(1)} %copy-done.2), custom_call_target="tpu_custom_call" | custom-call | flops 301989888 | bytes 2949120 | tf_op jit(solution)/shard_map/pallas_call | solution.py:529
  25.8 0.6 %collective-permute-start = (bf16[264,768]{1,0:T(8,128)(2,1)S(1)}, bf16[264,768]{1,0:T(8,128)(2,1)S(1)}, u32[]{:S(2)}, u32[]{:S(2)}) collective-permute-start(bf16[264,768]{1,0:T(8,128)(2,1)S(1)} %shard_map.119.refs_0_), channel_id=1, source_target_pairs={{0,1},{1,0},{2,3},{3,2},{4,5},{5,4},{6,7},{7,6},{8,9},{9,8},{10,11... | collective-permute-start | bytes 1216520 | tf_op jit(solution)/shard_map/ppermute | solution.py:562
  26.4 1.6 %collective-permute-start.12 = (bf16[72,768]{1,0:T(8,128)(2,1)S(1)}, bf16[72,768]{1,0:T(8,128)(2,1)S(1)}, u32[]{:S(2)}, u32[]{:S(2)}) collective-permute-start(bf16[72,768]{1,0:T(8,128)(2,1)S(1)} %shard_map.125), channel_id=1, source_target_pairs={{0,4},{1,5},{4,8},{5,9},{8,12},{9,13},{12,14},{13,15},{14,10},{15,... | collective-permute-start | bytes 331784 | tf_op jit(solution)/shard_map/ppermute | solution.py:559
  28.1 0.4 collective-permute-done.refs_1_
  28.4 0.7 %copy-done.5 = bf16[264,768]{1,0:T(8,128)(2,1)} copy-done((bf16[264,768]{1,0:T(8,128)(2,1)}, bf16[264,768]{1,0:T(8,128)(2,1)S(1)}, u32[]{:S(2)}) %copy-start.5) | copy-done | bytes 405528
  29.2 1.0 %collective-permute-start.13 = (bf16[64,768]{1,0:T(8,128)(2,1)S(1)}, bf16[64,768]{1,0:T(8,128)(2,1)}, u32[]{:S(2)}, u32[]{:S(2)}) collective-permute-start(bf16[64,768]{1,0:T(8,128)(2,1)S(1)} %shard_map.126), channel_id=1, source_target_pairs={{0,2},{1,3},{4,0},{5,1},{8,4},{9,5},{12,8},{13,9},{14,12},{15,13},... | collective-permute-start | bytes 294920 | tf_op jit(solution)/shard_map/ppermute | solution.py:559
  30.1 1.3 %collective-permute-done.12.refs_8_ = bf16[72,768]{1,0:T(8,128)(2,1)S(1)} collective-permute-done((bf16[72,768]{1,0:T(8,128)(2,1)S(1)}, bf16[72,768]{1,0:T(8,128)(2,1)S(1)}, u32[]{:S(2)}, u32[]{:S(2)}) %collective-permute-start.12) | collective-permute-done | bytes 110624 | tf_op jit(solution)/shard_map/ppermute | solution.py:559
  31.5 0.0 collective-permute-start.14
  31.5 2.7 %collective-permute-done.13.refs_9_ = bf16[64,768]{1,0:T(8,128)(2,1)} collective-permute-done((bf16[64,768]{1,0:T(8,128)(2,1)S(1)}, bf16[64,768]{1,0:T(8,128)(2,1)}, u32[]{:S(2)}, u32[]{:S(2)}) %collective-permute-start.13) | collective-permute-done | bytes 98336 | tf_op jit(solution)/shard_map/ppermute | solution.py:559
  34.1 0.0 collective-permute-start.15
  34.1 0.3 shard_map.128.refs_13_
  34.5 0.7 %copy-done.7 = f32[128,768]{1,0:T(8,128)} copy-done((f32[128,768]{1,0:T(8,128)}, f32[128,768]{1,0:T(8,128)S(1)}, u32[]{:S(2)}) %copy-start.7) | copy-done | bytes 393240
  35.2 1.3 %copy-done.10 = bf16[768,768]{1,0:T(8,128)(2,1)S(1)} copy-done((bf16[768,768]{1,0:T(8,128)(2,1)S(1)}, bf16[768,768]{1,0:T(8,128)(2,1)}, u32[]{:S(2)}) %copy-start.10) | copy-done | bytes 1179672
  36.5 1.3 %shard_map.127.refs_6_.refs_12_ = bf16[6144,256]{1,0:T(8,128)(2,1)S(1)} custom-call(s32[1]{0:T(128)} %bitcast.3.me_ref, bf16[136,768]{1,0:T(8,128)(2,1)S(1)} %copy-done.4, bf16[768,768]{1,0:T(8,128)(2,1)S(1)} %copy-done.10), custom_call_target="tpu_custom_call" | custom-call | flops 201326592 | bytes 4325376 | tf_op jit(solution)/shard_map/pallas_call | solution.py:529
  37.9 0.7 %shard_map.129 = (f32[160,256]{1,0:T(8,128)S(1)}, f32[96,256]{1,0:T(8,128)S(1)}) custom-call(s32[1]{0:T(128)} %bitcast.3.me_ref, bf16[16,256,128]{2,1,0:T(8,128)(2,1)S(1)} %copy-done.12, bf16[16,128]{1,0:T(8,128)(2,1)S(1)} %bitcast.8), custom_call_target="tpu_custom_call" | custom-call | flops 268435456 | bytes 1310720 | tf_op jit(solution)/shard_map/pallas_call | solution.py:529
  38.6 0.0 collective-permute-done.5.refs_3_
  38.6 0.0 collective-permute-done.8.refs_5_
  38.6 0.2 copy-done.6
  38.9 2.4 %shard_map.130 = (f32[1280,256]{1,0:T(8,128)S(1)}, f32[8,256]{1,0:T(8,128)S(1)}, f32[8,256]{1,0:T(8,128)S(1)}) custom-call(bf16[264,768]{1,0:T(8,128)(2,1)S(1)} %shard_map.119.refs_0_, bf16[264,768]{1,0:T(8,128)(2,1)S(1)} %copy-done.6, bf16[528,768]{1,0:T(8,128)(2,1)S(1)} %shard_map.122.refs_2_, bf16[528,768]{1,0:T(8,128)(2,1)} %collective-permute-done.5.refs_3_, ...), custom_call_target="tpu_custom_call" | custom-call | flops 503316480 | bytes 5898240 | tf_op jit(solution)/shard_map/pallas_call | solution.py:529
  41.3 0.0 collective-permute-done.15.refs_11_
  41.3 0.0 collective-permute-done.14.refs_10_
  41.4 5.2 %shard_map.131 = bf16[16,8,768]{2,1,0:T(8,128)(2,1)} custom-call(bf16[264,768]{1,0:T(8,128)(2,1)S(1)} %shard_map.119.refs_0_, bf16[264,768]{1,0:T(8,128)(2,1)S(1)} %copy-done.6, bf16[528,768]{1,0:T(8,128)(2,1)S(1)} %shard_map.122.refs_2_, bf16[528,768]{1,0:T(8,128)(2,1)} %collective-permute-done.5.refs_3_, bf16[528,768]{1,0:T(8,128)(2,1)S(1)} %shard_map.123.refs_4_, ...), custom_call_target="tpu_custom_call" | custom-call | flops 100663296 | bytes 3145728 | tf_op jit(solution)/shard_map/pallas_call | solution.py:529
  (32 shorter events, 0.1 us)
Async XLA Ops:
  0.0 9.1 %collective-permute-start.1 = (bf16[16,8,768]{2,1,0:T(8,128)(2,1)}, bf16[16,8,768]{2,1,0:T(8,128)(2,1)S(1)}, u32[]{:S(2)}, u32[]{:S(2)}) collective-permute-start(bf16[16,8,768]{2,1,0:T(8,128)(2,1)} %refs_22_.1), channel_id=1, source_target_pairs={{0,4},{1,5},{4,8},{5,9},{8,12},{9,13},{12,14},{13,15},{14,10},{15,... | collective-permute-start | bytes 589832 | tf_op jit(solution)/shard_map/ppermute | solution.py:559
  3.1 8.5 %collective-permute-start.3 = (bf16[16,8,768]{2,1,0:T(8,128)(2,1)}, bf16[16,8,768]{2,1,0:T(8,128)(2,1)S(1)}, u32[]{:S(2)}, u32[]{:S(2)}) collective-permute-start(bf16[16,8,768]{2,1,0:T(8,128)(2,1)} %refs_22_.1), channel_id=1, source_target_pairs={{0,2},{1,3},{4,0},{5,1},{8,4},{9,5},{12,8},{13,9},{14,12},{15,13},... | collective-permute-start | bytes 589832 | tf_op jit(solution)/shard_map/ppermute | solution.py:559
  5.2 4.0 %collective-permute-start.2 = (bf16[8,768]{1,0:T(8,128)(2,1)}, bf16[8,768]{1,0:T(8,128)(2,1)S(1)}, u32[]{:S(2)}, u32[]{:S(2)}) collective-permute-start(bf16[8,768]{1,0:T(8,128)(2,1)} %get-tuple-element.13.refs_9_.refs_21_), channel_id=1, source_target_pairs={{0,4},{1,5},{4,8},{5,9},{8,12},{9,13},{12,14},{13,15},{14,10},{15,... | collective-permute-start | bytes 36872 | tf_op jit(solution)/shard_map/ppermute | solution.py:559
  7.2 4.4 %collective-permute-start.4 = (bf16[8,768]{1,0:T(8,128)(2,1)}, bf16[8,768]{1,0:T(8,128)(2,1)S(1)}, u32[]{:S(2)}, u32[]{:S(2)}) collective-permute-start(bf16[8,768]{1,0:T(8,128)(2,1)} %get-tuple-element.13.refs_9_.refs_21_), channel_id=1, source_target_pairs={{0,2},{1,3},{4,0},{5,1},{8,4},{9,5},{12,8},{13,9},{14,12},{15,13},... | collective-permute-start | bytes 36872 | tf_op jit(solution)/shard_map/ppermute | solution.py:559
  9.5 6.0 %collective-permute-start.6 = (bf16[136,768]{1,0:T(8,128)(2,1)S(1)}, bf16[136,768]{1,0:T(8,128)(2,1)S(1)}, u32[]{:S(2)}, u32[]{:S(2)}) collective-permute-start(bf16[136,768]{1,0:T(8,128)(2,1)S(1)} %shard_map.120.refs_0_), channel_id=1, source_target_pairs={{0,4},{1,5},{4,8},{5,9},{8,12},{9,13},{12,14},{13,15},{14,10},{15,... | collective-permute-start | bytes 626696 | tf_op jit(solution)/shard_map/ppermute | solution.py:559
  12.0 5.9 %collective-permute-start.7 = (bf16[136,768]{1,0:T(8,128)(2,1)S(1)}, bf16[136,768]{1,0:T(8,128)(2,1)S(1)}, u32[]{:S(2)}, u32[]{:S(2)}) collective-permute-start(bf16[136,768]{1,0:T(8,128)(2,1)S(1)} %shard_map.121.refs_1_), channel_id=1, source_target_pairs={{0,2},{1,3},{4,0},{5,1},{8,4},{9,5},{12,8},{13,9},{14,12},{15,13},... | collective-permute-start | bytes 626696 | tf_op jit(solution)/shard_map/ppermute | solution.py:559
  15.5 7.2 %collective-permute-start.9 = (bf16[136,768]{1,0:T(8,128)(2,1)S(1)}, bf16[136,768]{1,0:T(8,128)(2,1)S(1)}, u32[]{:S(2)}, u32[]{:S(2)}) collective-permute-start(bf16[136,768]{1,0:T(8,128)(2,1)S(1)} %collective-permute-done.6.refs_0_), channel_id=1, source_target_pairs={{0,4},{1,5},{4,8},{5,9},{8,12},{9,13},{12,14},{13,15},{14,10},{15,... | collective-permute-start | bytes 626696 | tf_op jit(solution)/shard_map/ppermute | solution.py:559
  17.9 5.8 %collective-permute-start.10 = (bf16[136,768]{1,0:T(8,128)(2,1)S(1)}, bf16[136,768]{1,0:T(8,128)(2,1)S(1)}, u32[]{:S(2)}, u32[]{:S(2)}) collective-permute-start(bf16[136,768]{1,0:T(8,128)(2,1)S(1)} %collective-permute-done.7.refs_1_), channel_id=1, source_target_pairs={{0,2},{1,3},{4,0},{5,1},{8,4},{9,5},{12,8},{13,9},{14,12},{15,13},... | collective-permute-start | bytes 626696 | tf_op jit(solution)/shard_map/ppermute | solution.py:559
  17.9 1.3 %copy-start = (bf16[768,768]{1,0:T(8,128)(2,1)S(1)}, bf16[768,768]{1,0:T(8,128)(2,1)}, u32[]{:S(2)}) copy-start(bf16[768,768]{1,0:T(8,128)(2,1)} %refs_17_.1) | copy-start | bytes 3538948
  19.2 1.3 %copy-start.2 = (bf16[768,768]{1,0:T(8,128)(2,1)S(1)}, bf16[768,768]{1,0:T(8,128)(2,1)}, u32[]{:S(2)}) copy-start(bf16[768,768]{1,0:T(8,128)(2,1)} %refs_18_.1) | copy-start | bytes 3538948
  21.2 17.3 %collective-permute-start.5 = (bf16[528,768]{1,0:T(8,128)(2,1)S(1)}, bf16[528,768]{1,0:T(8,128)(2,1)}, u32[]{:S(2)}, u32[]{:S(2)}) collective-permute-start(bf16[528,768]{1,0:T(8,128)(2,1)S(1)} %shard_map.122.refs_2_), channel_id=1, source_target_pairs={{0,1},{1,0},{2,3},{3,2},{4,5},{5,4},{6,7},{7,6},{8,9},{9,8},{10,11... | collective-permute-start | bytes 2433032 | tf_op jit(solution)/shard_map/ppermute | solution.py:562
  22.1 3.2 %copy-start.1 = (bf16[768,768]{1,0:T(8,128)(2,1)S(1)}, bf16[768,768]{1,0:T(8,128)(2,1)}, u32[]{:S(2)}) copy-start(bf16[768,768]{1,0:T(8,128)(2,1)} %refs_17_.1) | copy-start | bytes 3538948
  22.1 3.2 %copy-start.4 = (bf16[136,768]{1,0:T(8,128)(2,1)S(1)}, bf16[136,768]{1,0:T(8,128)(2,1)}, u32[]{:S(2)}) copy-start(bf16[136,768]{1,0:T(8,128)(2,1)} %get-tuple-element.12.refs_0_.pay_ref) | copy-start | bytes 626692
  22.1 16.5 %collective-permute-start.8 = (bf16[528,768]{1,0:T(8,128)(2,1)S(1)}, bf16[528,768]{1,0:T(8,128)(2,1)}, u32[]{:S(2)}, u32[]{:S(2)}) collective-permute-start(bf16[528,768]{1,0:T(8,128)(2,1)S(1)} %shard_map.123.refs_4_), channel_id=1, source_target_pairs={{0,1},{1,0},{2,3},{3,2},{4,5},{5,4},{6,7},{7,6},{8,9},{9,8},{10,11... | collective-permute-start | bytes 2433032 | tf_op jit(solution)/shard_map/ppermute | solution.py:562
  25.3 16.0 %collective-permute-start.11 = (bf16[528,768]{1,0:T(8,128)(2,1)}, bf16[528,768]{1,0:T(8,128)(2,1)}, u32[]{:S(2)}, u32[]{:S(2)}) collective-permute-start(bf16[528,768]{1,0:T(8,128)(2,1)} %shard_map.124.refs_6_), channel_id=1, source_target_pairs={{0,1},{1,0},{2,3},{3,2},{4,5},{5,4},{6,7},{7,6},{8,9},{9,8},{10,11... | collective-permute-start | bytes 2433032 | tf_op jit(solution)/shard_map/ppermute | solution.py:562
  25.3 8.8 %copy-start.9 = (bf16[768,768]{1,0:T(8,128)(2,1)S(1)}, bf16[768,768]{1,0:T(8,128)(2,1)}, u32[]{:S(2)}) copy-start(bf16[768,768]{1,0:T(8,128)(2,1)} %wg_ref.1) | copy-start | bytes 3538948
  25.8 2.6 %collective-permute-start = (bf16[264,768]{1,0:T(8,128)(2,1)S(1)}, bf16[264,768]{1,0:T(8,128)(2,1)S(1)}, u32[]{:S(2)}, u32[]{:S(2)}) collective-permute-start(bf16[264,768]{1,0:T(8,128)(2,1)S(1)} %shard_map.119.refs_0_), channel_id=1, source_target_pairs={{0,1},{1,0},{2,3},{3,2},{4,5},{5,4},{6,7},{7,6},{8,9},{9,8},{10,11... | collective-permute-start | bytes 1216520 | tf_op jit(solution)/shard_map/ppermute | solution.py:562
  26.4 5.0 %collective-permute-start.12 = (bf16[72,768]{1,0:T(8,128)(2,1)S(1)}, bf16[72,768]{1,0:T(8,128)(2,1)S(1)}, u32[]{:S(2)}, u32[]{:S(2)}) collective-permute-start(bf16[72,768]{1,0:T(8,128)(2,1)S(1)} %shard_map.125), channel_id=1, source_target_pairs={{0,4},{1,5},{4,8},{5,9},{8,12},{9,13},{12,14},{13,15},{14,10},{15,... | collective-permute-start | bytes 331784 | tf_op jit(solution)/shard_map/ppermute | solution.py:559
  28.4 0.7 %copy-start.5 = (bf16[264,768]{1,0:T(8,128)(2,1)}, bf16[264,768]{1,0:T(8,128)(2,1)S(1)}, u32[]{:S(2)}) copy-start(bf16[264,768]{1,0:T(8,128)(2,1)S(1)} %collective-permute-done.refs_1_) | copy-start | bytes 1216516
  29.2 4.9 %collective-permute-start.13 = (bf16[64,768]{1,0:T(8,128)(2,1)S(1)}, bf16[64,768]{1,0:T(8,128)(2,1)}, u32[]{:S(2)}, u32[]{:S(2)}) collective-permute-start(bf16[64,768]{1,0:T(8,128)(2,1)S(1)} %shard_map.126), channel_id=1, source_target_pairs={{0,2},{1,3},{4,0},{5,1},{8,4},{9,5},{12,8},{13,9},{14,12},{15,13},... | collective-permute-start | bytes 294920 | tf_op jit(solution)/shard_map/ppermute | solution.py:559
  31.5 9.9 %collective-permute-start.14 = (bf16[72,768]{1,0:T(8,128)(2,1)S(1)}, bf16[72,768]{1,0:T(8,128)(2,1)}, u32[]{:S(2)}, u32[]{:S(2)}) collective-permute-start(bf16[72,768]{1,0:T(8,128)(2,1)S(1)} %collective-permute-done.12.refs_8_), channel_id=1, source_target_pairs={{0,1},{1,0},{2,3},{3,2},{4,5},{5,4},{6,7},{7,6},{8,9},{9,8},{10,11... | collective-permute-start | bytes 331784 | tf_op jit(solution)/shard_map/ppermute | solution.py:562
  34.1 7.2 %collective-permute-start.15 = (bf16[64,768]{1,0:T(8,128)(2,1)}, bf16[64,768]{1,0:T(8,128)(2,1)}, u32[]{:S(2)}, u32[]{:S(2)}) collective-permute-start(bf16[64,768]{1,0:T(8,128)(2,1)} %collective-permute-done.13.refs_9_), channel_id=1, source_target_pairs={{0,1},{1,0},{2,3},{3,2},{4,5},{5,4},{6,7},{7,6},{8,9},{9,8},{10,11... | collective-permute-start | bytes 294920 | tf_op jit(solution)/shard_map/ppermute | solution.py:562
  34.5 0.7 %copy-start.7 = (f32[128,768]{1,0:T(8,128)}, f32[128,768]{1,0:T(8,128)S(1)}, u32[]{:S(2)}) copy-start(f32[128,768]{1,0:T(8,128)S(1)} %shard_map.128.refs_13_) | copy-start | bytes 1179652
  35.2 1.3 %copy-start.10 = (bf16[768,768]{1,0:T(8,128)(2,1)S(1)}, bf16[768,768]{1,0:T(8,128)(2,1)}, u32[]{:S(2)}) copy-start(bf16[768,768]{1,0:T(8,128)(2,1)} %wq_ref.1) | copy-start | bytes 3538948
  36.5 1.4 %copy-start.12 = (bf16[16,256,128]{2,1,0:T(8,128)(2,1)S(1)}, bf16[16,256,128]{2,1,0:T(8,128)(2,1)}, u32[]{:S(2)}) copy-start(bf16[16,256,128]{2,1,0:T(8,128)(2,1)} %pair_ref.1) | copy-start | bytes 3145732
  36.5 1.4 %copy-start.16 = (bf16[128,16]{0,1:T(8,128)(2,1)S(1)}, bf16[128,16]{0,1:T(8,128)(2,1)}, u32[]{:S(2)}) copy-start(bf16[128,16]{0,1:T(8,128)(2,1)} %param.22) | copy-start | bytes 12292
  36.5 2.1 %copy-start.14 = (bf16[8,768]{1,0:T(8,128)(2,1)S(1)}, bf16[8,768]{1,0:T(8,128)(2,1)}, u32[]{:S(2)}) copy-start(bf16[8,768]{1,0:T(8,128)(2,1)} %get-tuple-element.13.refs_9_.refs_21_) | copy-start | bytes 36868
  36.5 2.1 %copy-start.15 = (f32[66,16]{0,1:T(8,128)S(1)}, f32[66,16]{0,1:T(8,128)}, u32[]{:S(2)}) copy-start(f32[66,16]{0,1:T(8,128)} %param.23) | copy-start | bytes 12676
  37.8 1.0 %copy-start.6 = (bf16[264,768]{1,0:T(8,128)(2,1)S(1)}, bf16[264,768]{1,0:T(8,128)(2,1)}, u32[]{:S(2)}) copy-start(bf16[264,768]{1,0:T(8,128)(2,1)} %copy-done.5) | copy-start | bytes 1216516
  38.9 2.5 %copy-start.3 = (bf16[768,768]{1,0:T(8,128)(2,1)S(1)}, bf16[768,768]{1,0:T(8,128)(2,1)}, u32[]{:S(2)}) copy-start(bf16[768,768]{1,0:T(8,128)(2,1)} %refs_18_.1) | copy-start | bytes 3538948
  38.9 2.5 %copy-start.8 = (f32[128,768]{1,0:T(8,128)S(1)}, f32[128,768]{1,0:T(8,128)}, u32[]{:S(2)}) copy-start(f32[128,768]{1,0:T(8,128)} %copy-done.7) | copy-start | bytes 1179652
  38.9 2.5 %copy-start.11 = (bf16[768,768]{1,0:T(8,128)(2,1)S(1)}, bf16[768,768]{1,0:T(8,128)(2,1)}, u32[]{:S(2)}) copy-start(bf16[768,768]{1,0:T(8,128)(2,1)} %refs_23_.1) | copy-start | bytes 3538948
  38.9 2.5 %copy-start.13 = (bf16[16,8,768]{2,1,0:T(8,128)(2,1)S(1)}, bf16[16,8,768]{2,1,0:T(8,128)(2,1)}, u32[]{:S(2)}) copy-start(bf16[16,8,768]{2,1,0:T(8,128)(2,1)} %refs_22_.1) | copy-start | bytes 589828

commit v8 on v7

--- a/solution.py
+++ b/solution.py
@@ -95,6 +95,8 @@
     tiled = matmul(meta.astype(F32).astype(BF16), spread)
     out_ref[pl.ds(rows, META_ROWS), :] = tiled.astype(BF16)
     meta_ref[...] = tiled.astype(BF16)
+    weight.wait()
+    q_ref[...] = matmul(data, wq_ref[...]).astype(BF16)
 
 
 def join_body(single_ref, meta_ref, out_ref):
@@ -126,6 +128,8 @@
     tiled = matmul(meta.astype(F32).astype(BF16), spread)
     out_ref[pl.ds(rows, META_ROWS), :] = tiled.astype(BF16)
     meta_ref[...] = tiled.astype(BF16)
+    weight.wait()
+    q_ref[...] = matmul(data, wq_ref[...]).astype(BF16)
 
 
 def join_body(single_ref, meta_ref, out_ref):
@@ -157,6 +161,8 @@
     tiled = matmul(meta.astype(F32).astype(BF16), spread)
     out_ref[pl.ds(rows, META_ROWS), :] = tiled.astype(BF16)
     meta_ref[...] = tiled.astype(BF16)
+    weight.wait()
+    q_ref[...] = matmul(data, wq_ref[...]).astype(BF16)
 
 
 def join_body(single_ref, meta_ref, out_ref):
@@ -172,12 +178,14 @@
 
 
 def prep_body(
-    single_hbm, chain_hbm, residue_hbm, valid_hbm, out_ref, meta_ref, single_ref, ints_ref, sems
+    single_hbm, chain_hbm, residue_hbm, valid_hbm, wq_hbm, out_ref, meta_ref, q_ref,
+    single_ref, ints_ref, wq_ref, sems,
 ):
     copies = [pltpu.make_async_copy(single_hbm, single_ref, sems.at[0])]
     for i, ref in enumerate((chain_hbm, residue_hbm, valid_hbm)):
         copies.append(pltpu.make_async_copy(ref, ints_ref.at[i], sems.at[i + 1]))
-    for copy in copies:
+    weight = pltpu.make_async_copy(wq_hbm, wq_ref, sems.at[4])
+    for copy in (*copies, weight):
         copy.start()
     tokens, samples, width = single_ref.shape
     rows = tokens * samples
@@ -187,8 +195,8 @@
     perm = sample_major(tokens, samples)
     for copy in copies:
         copy.wait()
-    normed = normed_rows(single_ref[...])
-    out_ref[pl.ds(0, rows), :] = matmul(perm, normed).astype(BF16)
+    data = matmul(perm, normed_rows(single_ref[...])).astype(BF16)
+    out_ref[pl.ds(0, rows), :] = data
     residue = ints_ref[1]
     row = lax.broadcasted_iota(jnp.int32, (META_ROWS, tokens), 0)
     meta = jnp.where(row == 0, ints_ref[0], 0)
@@ -198,6 +206,8 @@
     tiled = matmul(meta.astype(F32).astype(BF16), spread)
     out_ref[pl.ds(rows, META_ROWS), :] = tiled.astype(BF16)
     meta_ref[...] = tiled.astype(BF16)
+    weight.wait()
+    q_ref[...] = matmul(data, wq_ref[...]).astype(BF16)
 
 
 def join_body(single_ref, meta_ref, out_ref):
@@ -216,7 +226,8 @@
     copies = [pltpu.make_async_copy(single_hbm, single_ref, sems.at[0])]
     for i, ref in enumerate((chain_hbm, residue_hbm, valid_hbm)):
         copies.append(pltpu.make_async_copy(ref, ints_ref.at[i], sems.at[i + 1]))
-    for copy in copies:
+    weight = pltpu.make_async_copy(wq_hbm, wq_ref, sems.at[4])
+    for copy in (*copies, weight):
         copy.start()
     tokens, samples, width = single_ref.shape
     rows = tokens * samples
@@ -226,8 +237,8 @@
     perm = sample_major(tokens, samples)
     for copy in copies:
         copy.wait()
-    normed = normed_rows(single_ref[...])
-    out_ref[pl.ds(0, rows), :] = matmul(perm, normed).astype(BF16)
+    data = matmul(perm, normed_rows(single_ref[...])).astype(BF16)
+    out_ref[pl.ds(0, rows), :] = data
     residue = ints_ref[1]
     row = lax.broadcasted_iota(jnp.int32, (META_ROWS, tokens), 0)
     meta = jnp.where(row == 0, ints_ref[0], 0)
@@ -237,6 +248,8 @@
     tiled = matmul(meta.astype(F32).astype(BF16), spread)
     out_ref[pl.ds(rows, META_ROWS), :] = tiled.astype(BF16)
     meta_ref[...] = tiled.astype(BF16)
+    weight.wait()
+    q_ref[...] = matmul(data, wq_ref[...]).astype(BF16)
 
 
 def join_body(single_ref, meta_ref, out_ref):
@@ -246,6 +259,8 @@
     out_ref[pl.ds(0, rows), :] = matmul(sample_major(tokens, samples), normed).astype(BF16)
     out_ref[pl.ds(rows, META_ROWS), :] = meta_ref[...]
     meta_ref[...] = tiled.astype(BF16)
+    weight.wait()
+    q_ref[...] = matmul(data, wq_ref[...]).astype(BF16)
 
 
 META_ROWS = 8
@@ -253,12 +268,14 @@
 
 
 def prep_body(
-    single_hbm, chain_hbm, residue_hbm, valid_hbm, out_ref, meta_ref, single_ref, ints_ref, sems
+    single_hbm, chain_hbm, residue_hbm, valid_hbm, wq_hbm, out_ref, meta_ref, q_ref,
+    single_ref, ints_ref, wq_ref, sems,
 ):
     copies = [pltpu.make_async_copy(single_hbm, single_ref, sems.at[0])]
     for i, ref in enumerate((chain_hbm, residue_hbm, valid_hbm)):
         copies.append(pltpu.make_async_copy(ref, ints_ref.at[i], sems.at[i + 1]))
-    for copy in copies:
+    weight = pltpu.make_async_copy(wq_hbm, wq_ref, sems.at[4])
+    for copy in (*copies, weight):
         copy.start()
     tokens, samples, width = single_ref.shape
     rows = tokens * samples
@@ -268,8 +285,8 @@
     perm = sample_major(tokens, samples)
     for copy in copies:
         copy.wait()
-    normed = normed_rows(single_ref[...])
-    out_ref[pl.ds(0, rows), :] = matmul(perm, normed).astype(BF16)
+    data = matmul(perm, normed_rows(single_ref[...])).astype(BF16)
+    out_ref[pl.ds(0, rows), :] = data
     residue = ints_ref[1]
     row = lax.broadcasted_iota(jnp.int32, (META_ROWS, tokens), 0)
     meta = jnp.where(row == 0, ints_ref[0], 0)
@@ -279,6 +296,8 @@
     tiled = matmul(meta.astype(F32).astype(BF16), spread)
     out_ref[pl.ds(rows, META_ROWS), :] = tiled.astype(BF16)
     meta_ref[...] = tiled.astype(BF16)
+    weight.wait()
+    q_ref[...] = matmul(data, wq_ref[...]).astype(BF16)
 
 
 def join_body(single_ref, meta_ref, out_ref):
@@ -289,8 +308,7 @@
     out_ref[pl.ds(rows, META_ROWS), :] = meta_ref[...]
 
 
-def query_body(samples, heads, me_ref, pay_ref, wq_ref, out_ref, q_ref):
-    q_ref[...] = matmul(pay_ref[pl.ds(0, q_ref.shape[0]), :], wq_ref[...]).astype(BF16)
+def spread_body(samples, heads, me_ref, q_ref, out_ref):
     spread_queries(samples, heads, q_ref, out_ref)
 
 
@@ -569,31 +587,35 @@
     cw = ring(single, 1)
     ccw = ring(single, -1)
     blocks = jax.ShapeDtypeStruct((rows + META_ROWS, width), BF16)
-    payload, meta = call(
+    payload, meta, query = call(
         prep_body,
-        (blocks, jax.ShapeDtypeStruct((META_ROWS, width), BF16)),
-        (single, *(v.reshape(1, tokens) for v in (chain, residue, valid))),
-        in_specs=[ANY] * 4,
+        (
+            blocks,
+            jax.ShapeDtypeStruct((META_ROWS, width), BF16),
+            jax.ShapeDtypeStruct((rows, width), BF16),
+        ),
+        (single, *(v.reshape(1, tokens) for v in (chain, residue, valid)), w_query),
+        in_specs=[ANY] * 5,
         scratch=[
             pltpu.VMEM(single.shape, BF16),
             pltpu.VMEM((3, 1, tokens), jnp.int32),
-            pltpu.SemaphoreType.DMA((4,)),
+            pltpu.VMEM((width, width), BF16),
+            pltpu.SemaphoreType.DMA((5,)),
         ],
-        flops=rows * width * 16,
-        moved=4 * rows * width,
+        flops=2 * rows * width * width,
+        moved=6 * rows * width + 2 * width * width,
         limit=FULL,
     )
     cw_meta = ring(meta, 1)
     ccw_meta = ring(meta, -1)
     lines = heads * tokens
     query = call(
-        functools.partial(query_body, samples, heads),
+        functools.partial(spread_body, samples, heads),
         jax.ShapeDtypeStruct((samples * width, lines), BF16),
-        (me, payload, w_query),
-        in_specs=[SMEM, VMEM, VMEM],
-        flops=2 * rows * width * (width + lines),
-        moved=2 * width * width + 2 * samples * width * lines,
-        scratch=[pltpu.VMEM((rows, width), BF16)],
+        (me, query),
+        in_specs=[SMEM, VMEM],
+        flops=2 * rows * width * lines,
+        moved=2 * samples * width * lines,
     )
     gate = call(
         gate_body,

time: 46.9 us -> 46.8 us (level)
  Pallas kernels: 16.6 us -> 18.1 us
  local copies, waits for them, and re-layouts: 5.59 us -> 4.37 us
  starting transfers between devices: 13 us -> 12.4 us
    pallas_call x14, Pallas kernels: 16.6 us -> 18.1 us  [call(): pl.pallas_call(body, out_shape=out_shape, in_specs=in_specs or [VMEM] * l...]
    unnamed x34 -> x32, local copies, waits for them, and re-layouts: 5.59 us -> 4.37 us
    ppermute x10, waiting for transfers between devices: 10.7 us -> 11.5 us  [ring(): return lax.ppermute(value, 'tok', pairs)]
    ppermute x10, starting transfers between devices: 11.8 us -> 11.3 us  [ring(): return lax.ppermute(value, 'tok', pairs)]
  transfers between devices with their start and end apart: 16 -> 16, of which waited for: 7 -> 6; matrix products, arithmetic and copies ran while one was open for 0% -> 0% of each run, Pallas kernels for 25% -> 27%
where the time goes in v8:
time: 46.8 us; the launch traced here: 46.6 us
  Pallas kernels  18.1 us (39%)
  starting transfers between devices  12.4 us (26%)
  waiting for transfers between devices  11.5 us (25%)
  local copies, waits for them, and re-layouts  4.37 us (9%)
    pallas_call x14, Pallas kernels, call(): pl.pallas_call(body, out_shape=out_shape, in_specs=in_specs or [VMEM] * l...  18.1 us
    ppermute x10, waiting for transfers between devices, ring(): return lax.ppermute(value, 'tok', pairs)  11.5 us
    ppermute x10, starting transfers between devices, ring(): return lax.ppermute(value, 'tok', pairs)  11.3 us
    unnamed x32, local copies, waits for them, and re-layouts  4.37 us
    ppermute x6, starting transfers between devices, flip(): return lax.ppermute(value, 'tok', [(d, d ^ 1) for d in range(devices)])  1.14 us
  transfers between devices with their start and end apart: 16, of which 6 were waited for; matrix products, arithmetic and copies ran while one was open for 0% of the time, Pallas kernels for 27%

profile of v8, /device:TPU:0, one launch (start us, length us, event | category | flops | bytes accessed | tf_op | source)
XLA Modules:
  0.0 46.6 jit_solution(9306177871924421102)
XLA Ops:
  0.0 3.1 %collective-permute-start.1 = (bf16[16,8,768]{2,1,0:T(8,128)(2,1)}, bf16[16,8,768]{2,1,0:T(8,128)(2,1)S(1)}, u32[]{:S(2)}, u32[]{:S(2)}) collective-permute-start(bf16[16,8,768]{2,1,0:T(8,128)(2,1)} %refs_22_.1), channel_id=1, source_target_pairs={{0,4},{1,5},{4,8},{5,9},{8,12},{9,13},{12,14},{13,15},{14,10},{15,... | collective-permute-start | bytes 589832 | tf_op jit(solution)/shard_map/ppermute | solution.py:577
  3.1 0.0 collective-permute-start.3
  3.1 2.5 %shard_map.118 = (bf16[136,768]{1,0:T(8,128)(2,1)}, bf16[8,768]{1,0:T(8,128)(2,1)}, bf16[128,768]{1,0:T(8,128)(2,1)}) custom-call(bf16[16,8,768]{2,1,0:T(8,128)(2,1)} %refs_22_.1, s32[1,16]{1,0:T(1,128)} %bitcast.9, s32[1,16]{1,0:T(1,128)} %bitcast.10, s32[1,16]{1,0:T(1,128)} %bitcast.11, bf16[768,768]{1,0:T(8,128)(2,1)} %wq_hbm.1), custom_call_target="tpu_custom_call" | custom-call | flops 150994944 | bytes 1769472 | tf_op jit(solution)/shard_map/pallas_call | solution.py:547
  5.6 2.1 %collective-permute-start.2 = (bf16[8,768]{1,0:T(8,128)(2,1)}, bf16[8,768]{1,0:T(8,128)(2,1)S(1)}, u32[]{:S(2)}, u32[]{:S(2)}) collective-permute-start(bf16[8,768]{1,0:T(8,128)(2,1)} %get-tuple-element.14.refs_9_.refs_21_), channel_id=1, source_target_pairs={{0,4},{1,5},{4,8},{5,9},{8,12},{9,13},{12,14},{13,15},{14,10},{15,... | collective-permute-start | bytes 36872 | tf_op jit(solution)/shard_map/ppermute | solution.py:577
  7.6 0.0 collective-permute-start.4
  7.7 1.9 %collective-permute-done.2.meta_ref = bf16[8,768]{1,0:T(8,128)(2,1)S(1)} collective-permute-done((bf16[8,768]{1,0:T(8,128)(2,1)}, bf16[8,768]{1,0:T(8,128)(2,1)S(1)}, u32[]{:S(2)}, u32[]{:S(2)}) %collective-permute-start.2) | collective-permute-done | bytes 12320 | tf_op jit(solution)/shard_map/ppermute | solution.py:577
  9.5 0.4 shard_map.120.refs_0_
  9.9 2.1 %collective-permute-start.6 = (bf16[136,768]{1,0:T(8,128)(2,1)S(1)}, bf16[136,768]{1,0:T(8,128)(2,1)S(1)}, u32[]{:S(2)}, u32[]{:S(2)}) collective-permute-start(bf16[136,768]{1,0:T(8,128)(2,1)S(1)} %shard_map.120.refs_0_), channel_id=1, source_target_pairs={{0,4},{1,5},{4,8},{5,9},{8,12},{9,13},{12,14},{13,15},{14,10},{15,... | collective-permute-start | bytes 626696 | tf_op jit(solution)/shard_map/ppermute | solution.py:577
  12.0 0.0 collective-permute-done.4.meta_ref
  12.0 0.0 collective-permute-done.3.single_ref
  12.0 0.4 shard_map.121.refs_1_
  12.4 0.1 collective-permute-start.7
  12.5 3.4 %collective-permute-done.6.refs_0_ = bf16[136,768]{1,0:T(8,128)(2,1)S(1)} collective-permute-done((bf16[136,768]{1,0:T(8,128)(2,1)S(1)}, bf16[136,768]{1,0:T(8,128)(2,1)S(1)}, u32[]{:S(2)}, u32[]{:S(2)}) %collective-permute-start.6) | collective-permute-done | bytes 208928 | tf_op jit(solution)/shard_map/ppermute | solution.py:577
  15.9 1.9 %collective-permute-start.9 = (bf16[136,768]{1,0:T(8,128)(2,1)S(1)}, bf16[136,768]{1,0:T(8,128)(2,1)S(1)}, u32[]{:S(2)}, u32[]{:S(2)}) collective-permute-start(bf16[136,768]{1,0:T(8,128)(2,1)S(1)} %collective-permute-done.6.refs_0_), channel_id=1, source_target_pairs={{0,4},{1,5},{4,8},{5,9},{8,12},{9,13},{12,14},{13,15},{14,10},{15,... | collective-permute-start | bytes 626696 | tf_op jit(solution)/shard_map/ppermute | solution.py:577
  17.8 0.5 %collective-permute-done.7.refs_1_ = bf16[136,768]{1,0:T(8,128)(2,1)S(1)} collective-permute-done((bf16[136,768]{1,0:T(8,128)(2,1)S(1)}, bf16[136,768]{1,0:T(8,128)(2,1)S(1)}, u32[]{:S(2)}, u32[]{:S(2)}) %collective-permute-start.7) | collective-permute-done | bytes 208928 | tf_op jit(solution)/shard_map/ppermute | solution.py:577
  18.3 0.0 collective-permute-start.10
  18.3 1.3 %copy-done.1 = bf16[768,768]{1,0:T(8,128)(2,1)S(1)} copy-done((bf16[768,768]{1,0:T(8,128)(2,1)S(1)}, bf16[768,768]{1,0:T(8,128)(2,1)}, u32[]{:S(2)}) %copy-start.1) | copy-done | bytes 1179672
  19.6 0.8 %shard_map.122.refs_2_ = bf16[528,768]{1,0:T(8,128)(2,1)S(1)} custom-call(bf16[136,768]{1,0:T(8,128)(2,1)S(1)} %shard_map.120.refs_0_, bf16[136,768]{1,0:T(8,128)(2,1)S(1)} %shard_map.121.refs_1_, bf16[768,768]{1,0:T(8,128)(2,1)S(1)} %copy-done, bf16[768,768]{1,0:T(8,128)(2,1)S(1)} %copy-done.1), custom_call_target="tpu_custom_call" | custom-call | flops 603979776 | bytes 3538944 | tf_op jit(solution)/shard_map/pallas_call | solution.py:547
  20.4 0.1 collective-permute-start.5
  20.4 1.7 %shard_map.123.refs_4_ = bf16[528,768]{1,0:T(8,128)(2,1)} custom-call(bf16[136,768]{1,0:T(8,128)(2,1)S(1)} %collective-permute-done.6.refs_0_, bf16[136,768]{1,0:T(8,128)(2,1)S(1)} %collective-permute-done.7.refs_1_, bf16[768,768]{1,0:T(8,128)(2,1)S(1)} %copy-done, bf16[768,768]{1,0:T(8,128)(2,1)S(1)} %copy-done.1), custom_call_target="tpu_custom_call" | custom-call | flops 603979776 | bytes 3538944 | tf_op jit(solution)/shard_map/pallas_call | solution.py:547
  22.1 0.5 %collective-permute-start.8 = (bf16[528,768]{1,0:T(8,128)(2,1)}, bf16[528,768]{1,0:T(8,128)(2,1)}, u32[]{:S(2)}, u32[]{:S(2)}) collective-permute-start(bf16[528,768]{1,0:T(8,128)(2,1)} %shard_map.123.refs_4_), channel_id=1, source_target_pairs={{0,1},{1,0},{2,3},{3,2},{4,5},{5,4},{6,7},{7,6},{8,9},{9,8},{10,11... | collective-permute-start | bytes 2433032 | tf_op jit(solution)/shard_map/ppermute | solution.py:580
  22.6 0.0 collective-permute-done.9.refs_0_.in_ref
  22.6 1.5 %collective-permute-done.10.refs_1_.in_ref = bf16[136,768]{1,0:T(8,128)(2,1)S(1)} collective-permute-done((bf16[136,768]{1,0:T(8,128)(2,1)S(1)}, bf16[136,768]{1,0:T(8,128)(2,1)S(1)}, u32[]{:S(2)}, u32[]{:S(2)}) %collective-permute-start.10) | collective-permute-done | bytes 208928 | tf_op jit(solution)/shard_map/ppermute | solution.py:577
  24.1 1.7 %shard_map.124.refs_6_ = bf16[528,768]{1,0:T(8,128)(2,1)} custom-call(bf16[136,768]{1,0:T(8,128)(2,1)S(1)} %collective-permute-done.9.refs_0_.in_ref, bf16[136,768]{1,0:T(8,128)(2,1)S(1)} %collective-permute-done.10.refs_1_.in_ref, bf16[768,768]{1,0:T(8,128)(2,1)S(1)} %copy-done, bf16[768,768]{1,0:T(8,128)(2,1)S(1)} %copy-done.1), custom_call_target="tpu_custom_call" | custom-call | flops 603979776 | bytes 3538944 | tf_op jit(solution)/shard_map/pallas_call | solution.py:547
  25.8 0.0 collective-permute-start.11
  25.8 0.5 %shard_map.119.refs_0_ = bf16[264,768]{1,0:T(8,128)(2,1)S(1)} custom-call(bf16[136,768]{1,0:T(8,128)(2,1)S(1)} %copy-done.10, bf16[768,768]{1,0:T(8,128)(2,1)S(1)} %copy-done, bf16[768,768]{1,0:T(8,128)(2,1)S(1)} %copy-done.2), custom_call_target="tpu_custom_call" | custom-call | flops 301989888 | bytes 2949120 | tf_op jit(solution)/shard_map/pallas_call | solution.py:547
  26.3 0.6 %collective-permute-start = (bf16[264,768]{1,0:T(8,128)(2,1)S(1)}, bf16[264,768]{1,0:T(8,128)(2,1)S(1)}, u32[]{:S(2)}, u32[]{:S(2)}) collective-permute-start(bf16[264,768]{1,0:T(8,128)(2,1)S(1)} %shard_map.119.refs_0_), channel_id=1, source_target_pairs={{0,1},{1,0},{2,3},{3,2},{4,5},{5,4},{6,7},{7,6},{8,9},{9,8},{10,11... | collective-permute-start | bytes 1216520 | tf_op jit(solution)/shard_map/ppermute | solution.py:580
  26.9 0.8 %copy-done.3 = bf16[264,768]{1,0:T(8,128)(2,1)} copy-done((bf16[264,768]{1,0:T(8,128)(2,1)}, bf16[264,768]{1,0:T(8,128)(2,1)S(1)}, u32[]{:S(2)}) %copy-start.3) | copy-done | bytes 405528
  27.6 1.6 %collective-permute-start.12 = (bf16[72,768]{1,0:T(8,128)(2,1)S(1)}, bf16[72,768]{1,0:T(8,128)(2,1)S(1)}, u32[]{:S(2)}, u32[]{:S(2)}) collective-permute-start(bf16[72,768]{1,0:T(8,128)(2,1)S(1)} %shard_map.125), channel_id=1, source_target_pairs={{0,4},{1,5},{4,8},{5,9},{8,12},{9,13},{12,14},{13,15},{14,10},{15,... | collective-permute-start | bytes 331784 | tf_op jit(solution)/shard_map/ppermute | solution.py:577
  29.3 0.0 collective-permute-done.refs_1_
  29.3 0.7 %copy-done.5 = bf16[264,768]{1,0:T(8,128)(2,1)} copy-done((bf16[264,768]{1,0:T(8,128)(2,1)}, bf16[264,768]{1,0:T(8,128)(2,1)S(1)}, u32[]{:S(2)}) %copy-start.5) | copy-done | bytes 405528
  30.0 0.4 collective-permute-start.13
  30.5 2.2 %collective-permute-done.12.refs_8_ = bf16[72,768]{1,0:T(8,128)(2,1)S(1)} collective-permute-done((bf16[72,768]{1,0:T(8,128)(2,1)S(1)}, bf16[72,768]{1,0:T(8,128)(2,1)S(1)}, u32[]{:S(2)}, u32[]{:S(2)}) %collective-permute-start.12) | collective-permute-done | bytes 110624 | tf_op jit(solution)/shard_map/ppermute | solution.py:577
  32.7 2.1 %collective-permute-done.13.refs_9_ = bf16[64,768]{1,0:T(8,128)(2,1)} collective-permute-done((bf16[64,768]{1,0:T(8,128)(2,1)S(1)}, bf16[64,768]{1,0:T(8,128)(2,1)}, u32[]{:S(2)}, u32[]{:S(2)}) %collective-permute-start.13) | collective-permute-done | bytes 98336 | tf_op jit(solution)/shard_map/ppermute | solution.py:577
  34.8 0.0 collective-permute-start.15
  34.8 0.9 %copy-done.12 = bf16[128,768]{1,0:T(8,128)(2,1)S(1)} copy-done((bf16[128,768]{1,0:T(8,128)(2,1)S(1)}, bf16[128,768]{1,0:T(8,128)(2,1)}, u32[]{:S(2)}) %copy-start.12) | copy-done | bytes 196632
  35.7 1.0 %shard_map.127.refs_6_.refs_12_ = bf16[6144,256]{1,0:T(8,128)(2,1)S(1)} custom-call(s32[1]{0:T(128)} %bitcast.3.me_ref, bf16[128,768]{1,0:T(8,128)(2,1)S(1)} %copy-done.12), custom_call_target="tpu_custom_call" | custom-call | flops 50331648 | bytes 3145728 | tf_op jit(solution)/shard_map/pallas_call | solution.py:547
  36.7 0.2 copy-done.7
  37.0 0.0 copy-start.14
  37.0 0.3 shard_map.128.refs_13_
  37.3 0.4 copy-done.15
  37.7 0.7 %shard_map.129 = (f32[160,256]{1,0:T(8,128)S(1)}, f32[96,256]{1,0:T(8,128)S(1)}) custom-call(s32[1]{0:T(128)} %bitcast.3.me_ref, bf16[16,256,128]{2,1,0:T(8,128)(2,1)S(1)} %copy-done.9, bf16[16,128]{1,0:T(8,128)(2,1)S(1)} %bitcast.8), custom_call_target="tpu_custom_call" | custom-call | flops 268435456 | bytes 1310720 | tf_op jit(solution)/shard_map/pallas_call | solution.py:547
  38.4 0.0 collective-permute-done.5.refs_3_
  38.4 0.0 collective-permute-done.8.refs_5_
  38.5 0.0 copy-start.8
  38.5 0.0 copy-start.11
  38.5 2.6 %shard_map.130 = (f32[1280,256]{1,0:T(8,128)S(1)}, f32[8,256]{1,0:T(8,128)S(1)}, f32[8,256]{1,0:T(8,128)S(1)}) custom-call(bf16[264,768]{1,0:T(8,128)(2,1)S(1)} %copy-done.4, bf16[264,768]{1,0:T(8,128)(2,1)S(1)} %copy-done.6, bf16[528,768]{1,0:T(8,128)(2,1)S(1)} %shard_map.122.refs_2_, bf16[528,768]{1,0:T(8,128)(2,1)} %collective-permute-done.5.refs_3_, ...), custom_call_target="tpu_custom_call" | custom-call | flops 503316480 | bytes 5898240 | tf_op jit(solution)/shard_map/pallas_call | solution.py:547
  41.1 5.4 %shard_map.131 = bf16[16,8,768]{2,1,0:T(8,128)(2,1)} custom-call(bf16[264,768]{1,0:T(8,128)(2,1)S(1)} %copy-done.4, bf16[264,768]{1,0:T(8,128)(2,1)S(1)} %copy-done.6, bf16[528,768]{1,0:T(8,128)(2,1)S(1)} %shard_map.122.refs_2_, bf16[528,768]{1,0:T(8,128)(2,1)} %collective-permute-done.5.refs_3_, bf16[528,768]{1,0:T(8,128)(2,1)} %shard_map.123.refs_4_, ...), custom_call_target="tpu_custom_call" | custom-call | flops 100663296 | bytes 3145728 | tf_op jit(solution)/shard_map/pallas_call | solution.py:547
  (30 shorter events, 0.1 us)
Async XLA Ops:
  0.0 18.3 %copy-start = (bf16[768,768]{1,0:T(8,128)(2,1)S(1)}, bf16[768,768]{1,0:T(8,128)(2,1)}, u32[]{:S(2)}) copy-start(bf16[768,768]{1,0:T(8,128)(2,1)} %refs_17_.1) | copy-start | bytes 3538948
  0.0 9.5 %collective-permute-start.1 = (bf16[16,8,768]{2,1,0:T(8,128)(2,1)}, bf16[16,8,768]{2,1,0:T(8,128)(2,1)S(1)}, u32[]{:S(2)}, u32[]{:S(2)}) collective-permute-start(bf16[16,8,768]{2,1,0:T(8,128)(2,1)} %refs_22_.1), channel_id=1, source_target_pairs={{0,4},{1,5},{4,8},{5,9},{8,12},{9,13},{12,14},{13,15},{14,10},{15,... | collective-permute-start | bytes 589832 | tf_op jit(solution)/shard_map/ppermute | solution.py:577
  3.1 9.0 %collective-permute-start.3 = (bf16[16,8,768]{2,1,0:T(8,128)(2,1)}, bf16[16,8,768]{2,1,0:T(8,128)(2,1)S(1)}, u32[]{:S(2)}, u32[]{:S(2)}) collective-permute-start(bf16[16,8,768]{2,1,0:T(8,128)(2,1)} %refs_22_.1), channel_id=1, source_target_pairs={{0,2},{1,3},{4,0},{5,1},{8,4},{9,5},{12,8},{13,9},{14,12},{15,13},... | collective-permute-start | bytes 589832 | tf_op jit(solution)/shard_map/ppermute | solution.py:577
  5.6 4.0 %collective-permute-start.2 = (bf16[8,768]{1,0:T(8,128)(2,1)}, bf16[8,768]{1,0:T(8,128)(2,1)S(1)}, u32[]{:S(2)}, u32[]{:S(2)}) collective-permute-start(bf16[8,768]{1,0:T(8,128)(2,1)} %get-tuple-element.14.refs_9_.refs_21_), channel_id=1, source_target_pairs={{0,4},{1,5},{4,8},{5,9},{8,12},{9,13},{12,14},{13,15},{14,10},{15,... | collective-permute-start | bytes 36872 | tf_op jit(solution)/shard_map/ppermute | solution.py:577
  7.6 4.4 %collective-permute-start.4 = (bf16[8,768]{1,0:T(8,128)(2,1)}, bf16[8,768]{1,0:T(8,128)(2,1)S(1)}, u32[]{:S(2)}, u32[]{:S(2)}) collective-permute-start(bf16[8,768]{1,0:T(8,128)(2,1)} %get-tuple-element.14.refs_9_.refs_21_), channel_id=1, source_target_pairs={{0,2},{1,3},{4,0},{5,1},{8,4},{9,5},{12,8},{13,9},{14,12},{15,13},... | collective-permute-start | bytes 36872 | tf_op jit(solution)/shard_map/ppermute | solution.py:577
  9.9 5.9 %collective-permute-start.6 = (bf16[136,768]{1,0:T(8,128)(2,1)S(1)}, bf16[136,768]{1,0:T(8,128)(2,1)S(1)}, u32[]{:S(2)}, u32[]{:S(2)}) collective-permute-start(bf16[136,768]{1,0:T(8,128)(2,1)S(1)} %shard_map.120.refs_0_), channel_id=1, source_target_pairs={{0,4},{1,5},{4,8},{5,9},{8,12},{9,13},{12,14},{13,15},{14,10},{15,... | collective-permute-start | bytes 626696 | tf_op jit(solution)/shard_map/ppermute | solution.py:577
  12.4 5.9 %collective-permute-start.7 = (bf16[136,768]{1,0:T(8,128)(2,1)S(1)}, bf16[136,768]{1,0:T(8,128)(2,1)S(1)}, u32[]{:S(2)}, u32[]{:S(2)}) collective-permute-start(bf16[136,768]{1,0:T(8,128)(2,1)S(1)} %shard_map.121.refs_1_), channel_id=1, source_target_pairs={{0,2},{1,3},{4,0},{5,1},{8,4},{9,5},{12,8},{13,9},{14,12},{15,13},... | collective-permute-start | bytes 626696 | tf_op jit(solution)/shard_map/ppermute | solution.py:577
  15.9 6.7 %collective-permute-start.9 = (bf16[136,768]{1,0:T(8,128)(2,1)S(1)}, bf16[136,768]{1,0:T(8,128)(2,1)S(1)}, u32[]{:S(2)}, u32[]{:S(2)}) collective-permute-start(bf16[136,768]{1,0:T(8,128)(2,1)S(1)} %collective-permute-done.6.refs_0_), channel_id=1, source_target_pairs={{0,4},{1,5},{4,8},{5,9},{8,12},{9,13},{12,14},{13,15},{14,10},{15,... | collective-permute-start | bytes 626696 | tf_op jit(solution)/shard_map/ppermute | solution.py:577
  18.3 5.8 %collective-permute-start.10 = (bf16[136,768]{1,0:T(8,128)(2,1)S(1)}, bf16[136,768]{1,0:T(8,128)(2,1)S(1)}, u32[]{:S(2)}, u32[]{:S(2)}) collective-permute-start(bf16[136,768]{1,0:T(8,128)(2,1)S(1)} %collective-permute-done.7.refs_1_), channel_id=1, source_target_pairs={{0,2},{1,3},{4,0},{5,1},{8,4},{9,5},{12,8},{13,9},{14,12},{15,13},... | collective-permute-start | bytes 626696 | tf_op jit(solution)/shard_map/ppermute | solution.py:577
  18.3 1.3 %copy-start.1 = (bf16[768,768]{1,0:T(8,128)(2,1)S(1)}, bf16[768,768]{1,0:T(8,128)(2,1)}, u32[]{:S(2)}) copy-start(bf16[768,768]{1,0:T(8,128)(2,1)} %refs_18_.1) | copy-start | bytes 3538948
  20.4 18.0 %collective-permute-start.5 = (bf16[528,768]{1,0:T(8,128)(2,1)S(1)}, bf16[528,768]{1,0:T(8,128)(2,1)}, u32[]{:S(2)}, u32[]{:S(2)}) collective-permute-start(bf16[528,768]{1,0:T(8,128)(2,1)S(1)} %shard_map.122.refs_2_), channel_id=1, source_target_pairs={{0,1},{1,0},{2,3},{3,2},{4,5},{5,4},{6,7},{7,6},{8,9},{9,8},{10,11... | collective-permute-start | bytes 2433032 | tf_op jit(solution)/shard_map/ppermute | solution.py:580
  22.1 3.7 %copy-start.2 = (bf16[768,768]{1,0:T(8,128)(2,1)S(1)}, bf16[768,768]{1,0:T(8,128)(2,1)}, u32[]{:S(2)}) copy-start(bf16[768,768]{1,0:T(8,128)(2,1)} %refs_18_.1) | copy-start | bytes 3538948
  22.1 3.7 %copy-start.10 = (bf16[136,768]{1,0:T(8,128)(2,1)S(1)}, bf16[136,768]{1,0:T(8,128)(2,1)}, u32[]{:S(2)}) copy-start(bf16[136,768]{1,0:T(8,128)(2,1)} %get-tuple-element.13.refs_0_.pay_ref) | copy-start | bytes 626692
  22.1 16.3 %collective-permute-start.8 = (bf16[528,768]{1,0:T(8,128)(2,1)}, bf16[528,768]{1,0:T(8,128)(2,1)}, u32[]{:S(2)}, u32[]{:S(2)}) collective-permute-start(bf16[528,768]{1,0:T(8,128)(2,1)} %shard_map.123.refs_4_), channel_id=1, source_target_pairs={{0,1},{1,0},{2,3},{3,2},{4,5},{5,4},{6,7},{7,6},{8,9},{9,8},{10,11... | collective-permute-start | bytes 2433032 | tf_op jit(solution)/shard_map/ppermute | solution.py:580
  25.8 15.3 %collective-permute-start.11 = (bf16[528,768]{1,0:T(8,128)(2,1)}, bf16[528,768]{1,0:T(8,128)(2,1)}, u32[]{:S(2)}, u32[]{:S(2)}) collective-permute-start(bf16[528,768]{1,0:T(8,128)(2,1)} %shard_map.124.refs_6_), channel_id=1, source_target_pairs={{0,1},{1,0},{2,3},{3,2},{4,5},{5,4},{6,7},{7,6},{8,9},{9,8},{10,11... | collective-permute-start | bytes 2433032 | tf_op jit(solution)/shard_map/ppermute | solution.py:580
  26.3 3.0 %collective-permute-start = (bf16[264,768]{1,0:T(8,128)(2,1)S(1)}, bf16[264,768]{1,0:T(8,128)(2,1)S(1)}, u32[]{:S(2)}, u32[]{:S(2)}) collective-permute-start(bf16[264,768]{1,0:T(8,128)(2,1)S(1)} %shard_map.119.refs_0_), channel_id=1, source_target_pairs={{0,1},{1,0},{2,3},{3,2},{4,5},{5,4},{6,7},{7,6},{8,9},{9,8},{10,11... | collective-permute-start | bytes 1216520 | tf_op jit(solution)/shard_map/ppermute | solution.py:580
  26.9 0.8 %copy-start.3 = (bf16[264,768]{1,0:T(8,128)(2,1)}, bf16[264,768]{1,0:T(8,128)(2,1)S(1)}, u32[]{:S(2)}) copy-start(bf16[264,768]{1,0:T(8,128)(2,1)S(1)} %shard_map.119.refs_0_) | copy-start | bytes 1216516
  27.6 5.0 %collective-permute-start.12 = (bf16[72,768]{1,0:T(8,128)(2,1)S(1)}, bf16[72,768]{1,0:T(8,128)(2,1)S(1)}, u32[]{:S(2)}, u32[]{:S(2)}) collective-permute-start(bf16[72,768]{1,0:T(8,128)(2,1)S(1)} %shard_map.125), channel_id=1, source_target_pairs={{0,4},{1,5},{4,8},{5,9},{8,12},{9,13},{12,14},{13,15},{14,10},{15,... | collective-permute-start | bytes 331784 | tf_op jit(solution)/shard_map/ppermute | solution.py:577
  29.3 0.8 %copy-start.5 = (bf16[264,768]{1,0:T(8,128)(2,1)}, bf16[264,768]{1,0:T(8,128)(2,1)S(1)}, u32[]{:S(2)}) copy-start(bf16[264,768]{1,0:T(8,128)(2,1)S(1)} %collective-permute-done.refs_1_) | copy-start | bytes 1216516
  30.0 4.7 %collective-permute-start.13 = (bf16[64,768]{1,0:T(8,128)(2,1)S(1)}, bf16[64,768]{1,0:T(8,128)(2,1)}, u32[]{:S(2)}, u32[]{:S(2)}) collective-permute-start(bf16[64,768]{1,0:T(8,128)(2,1)S(1)} %shard_map.126), channel_id=1, source_target_pairs={{0,2},{1,3},{4,0},{5,1},{8,4},{9,5},{12,8},{13,9},{14,12},{15,13},... | collective-permute-start | bytes 294920 | tf_op jit(solution)/shard_map/ppermute | solution.py:577
  32.7 8.4 %collective-permute-start.14 = (bf16[72,768]{1,0:T(8,128)(2,1)S(1)}, bf16[72,768]{1,0:T(8,128)(2,1)}, u32[]{:S(2)}, u32[]{:S(2)}) collective-permute-start(bf16[72,768]{1,0:T(8,128)(2,1)S(1)} %collective-permute-done.12.refs_8_), channel_id=1, source_target_pairs={{0,1},{1,0},{2,3},{3,2},{4,5},{5,4},{6,7},{7,6},{8,9},{9,8},{10,11... | collective-permute-start | bytes 331784 | tf_op jit(solution)/shard_map/ppermute | solution.py:580
  34.8 6.3 %collective-permute-start.15 = (bf16[64,768]{1,0:T(8,128)(2,1)}, bf16[64,768]{1,0:T(8,128)(2,1)}, u32[]{:S(2)}, u32[]{:S(2)}) collective-permute-start(bf16[64,768]{1,0:T(8,128)(2,1)} %collective-permute-done.13.refs_9_), channel_id=1, source_target_pairs={{0,1},{1,0},{2,3},{3,2},{4,5},{5,4},{6,7},{7,6},{8,9},{9,8},{10,11... | collective-permute-start | bytes 294920 | tf_op jit(solution)/shard_map/ppermute | solution.py:580
  34.8 0.9 %copy-start.12 = (bf16[128,768]{1,0:T(8,128)(2,1)S(1)}, bf16[128,768]{1,0:T(8,128)(2,1)}, u32[]{:S(2)}) copy-start(bf16[128,768]{1,0:T(8,128)(2,1)} %get-tuple-element.15.q_ref) | copy-start | bytes 589828
  35.7 1.3 %copy-start.7 = (bf16[768,768]{1,0:T(8,128)(2,1)S(1)}, bf16[768,768]{1,0:T(8,128)(2,1)}, u32[]{:S(2)}) copy-start(bf16[768,768]{1,0:T(8,128)(2,1)} %wg_ref.1) | copy-start | bytes 3538948
  35.7 1.6 %copy-start.9 = (bf16[16,256,128]{2,1,0:T(8,128)(2,1)S(1)}, bf16[16,256,128]{2,1,0:T(8,128)(2,1)}, u32[]{:S(2)}) copy-start(bf16[16,256,128]{2,1,0:T(8,128)(2,1)} %pair_ref.1) | copy-start | bytes 3145732
  37.0 0.8 %copy-start.15 = (bf16[128,16]{0,1:T(8,128)(2,1)S(1)}, bf16[128,16]{0,1:T(8,128)(2,1)}, u32[]{:S(2)}) copy-start(bf16[128,16]{0,1:T(8,128)(2,1)} %param.22) | copy-start | bytes 12292
  37.0 1.5 %copy-start.4 = (bf16[264,768]{1,0:T(8,128)(2,1)S(1)}, bf16[264,768]{1,0:T(8,128)(2,1)}, u32[]{:S(2)}) copy-start(bf16[264,768]{1,0:T(8,128)(2,1)} %copy-done.3) | copy-start | bytes 1216516
  37.0 1.5 %copy-start.6 = (bf16[264,768]{1,0:T(8,128)(2,1)S(1)}, bf16[264,768]{1,0:T(8,128)(2,1)}, u32[]{:S(2)}) copy-start(bf16[264,768]{1,0:T(8,128)(2,1)} %copy-done.5) | copy-start | bytes 1216516
  37.0 1.5 %copy-start.13 = (bf16[8,768]{1,0:T(8,128)(2,1)S(1)}, bf16[8,768]{1,0:T(8,128)(2,1)}, u32[]{:S(2)}) copy-start(bf16[8,768]{1,0:T(8,128)(2,1)} %get-tuple-element.14.refs_9_.refs_21_) | copy-start | bytes 36868
  37.0 1.5 %copy-start.14 = (f32[66,16]{0,1:T(8,128)S(1)}, f32[66,16]{0,1:T(8,128)}, u32[]{:S(2)}) copy-start(f32[66,16]{0,1:T(8,128)} %param.23) | copy-start | bytes 12676
  38.5 2.7 %copy-start.8 = (bf16[768,768]{1,0:T(8,128)(2,1)S(1)}, bf16[768,768]{1,0:T(8,128)(2,1)}, u32[]{:S(2)}) copy-start(bf16[768,768]{1,0:T(8,128)(2,1)} %refs_23_.1) | copy-start | bytes 3538948
  38.5 2.7 %copy-start.11 = (bf16[16,8,768]{2,1,0:T(8,128)(2,1)S(1)}, bf16[16,8,768]{2,1,0:T(8,128)(2,1)}, u32[]{:S(2)}) copy-start(bf16[16,8,768]{2,1,0:T(8,128)(2,1)} %refs_22_.1) | copy-start | bytes 589828

commit v9 on v8

--- a/solution.py
+++ b/solution.py
@@ -16,32 +16,10 @@
 CORES = 2
 TILE = 256
 LANES = 128
+META_ROWS = 8
+RADIX = 128
 FULL = 60 << 20
 VMEM = pl.BlockSpec(memory_space=pltpu.VMEM)
-ANY = pl.BlockSpec(memory_space=pl.ANY)
-SMEM = pl.BlockSpec(memory_space=pltpu.SMEM)
-VMEM = pl.BlockSpec(memory_space=pltpu.VMEM)
-ANY = pl.BlockSpec(memory_space=pl.ANY)
-ANY = pl.BlockSpec(memory_space=pl.ANY)
-SMEM = pl.BlockSpec(memory_space=pltpu.SMEM)
-VMEM = pl.BlockSpec(memory_space=pltpu.VMEM)
-ANY = pl.BlockSpec(memory_space=pl.ANY)
-ANY = pl.BlockSpec(memory_space=pl.ANY)
-ANY = pl.BlockSpec(memory_space=pl.ANY)
-SMEM = pl.BlockSpec(memory_space=pltpu.SMEM)
-VMEM = pl.BlockSpec(memory_space=pltpu.VMEM)
-ANY = pl.BlockSpec(memory_space=pl.ANY)
-ANY = pl.BlockSpec(memory_space=pl.ANY)
-ANY = pl.BlockSpec(memory_space=pl.ANY)
-SMEM = pl.BlockSpec(memory_space=pltpu.SMEM)
-VMEM = pl.BlockSpec(memory_space=pltpu.VMEM)
-ANY = pl.BlockSpec(memory_space=pl.ANY)
-ANY = pl.BlockSpec(memory_space=pl.ANY)
-ANY = pl.BlockSpec(memory_space=pl.ANY)
-SMEM = pl.BlockSpec(memory_space=pltpu.SMEM)
-VMEM = pl.BlockSpec(memory_space=pltpu.VMEM)
-ANY = pl.BlockSpec(memory_space=pl.ANY)
-ANY = pl.BlockSpec(memory_space=pl.ANY)
 ANY = pl.BlockSpec(memory_space=pl.ANY)
 SMEM = pl.BlockSpec(memory_space=pltpu.SMEM)
 
@@ -74,229 +52,43 @@
     return jnp.dot(a, b, preferred_element_type=F32)
 
 
-META_ROWS = 8
-RADIX = 128
-
-
-def prep_body(single_ref, chain_ref, residue_ref, valid_ref, out_ref):
-    tokens, samples, width = single_ref.shape
-    rows = tokens * samples
-    normed = normed_rows(single_ref[...])
-    out_ref[pl.ds(0, rows), :] = matmul(sample_major(tokens, samples), normed).astype(BF16)
-    residue = residue_ref[...]
-    row = lax.broadcasted_iota(jnp.int32, (META_ROWS, tokens), 0)
-    meta = jnp.where(row == 0, chain_ref[...], 0)
-    meta = jnp.where(row == 1, residue // RADIX, meta)
-    meta = jnp.where(row == 2, residue % RADIX, meta)
-    meta = jnp.where(row == 3, valid_ref[...], meta)
+def tags_body(chain_hbm, residue_hbm, valid_hbm, out_ref, ints_ref, sems):
+    copies = []
+    for i, ref in enumerate((chain_hbm, residue_hbm, valid_hbm)):
+        copies.append(pltpu.make_async_copy(ref, ints_ref.at[i], sems.at[i]))
+        copies[i].start()
+    tokens, width = ints_ref.shape[2], out_ref.shape[1]
     token = lax.broadcasted_iota(jnp.int32, (tokens, width), 0)
     lane = lax.broadcasted_iota(jnp.int32, (tokens, width), 1)
     spread = (lane % tokens == token).astype(F32).astype(BF16)
-    tiled = matmul(meta.astype(F32).astype(BF16), spread)
-    out_ref[pl.ds(rows, META_ROWS), :] = tiled.astype(BF16)
-    meta_ref[...] = tiled.astype(BF16)
-    weight.wait()
-    q_ref[...] = matmul(data, wq_ref[...]).astype(BF16)
-
-
-def join_body(single_ref, meta_ref, out_ref):
-    tokens, samples, _ = single_ref.shape
-    rows = tokens * samples
-    normed = normed_rows(single_ref[...])
-    out_ref[pl.ds(0, rows), :] = matmul(sample_major(tokens, samples), normed).astype(BF16)
-    out_ref[pl.ds(rows, META_ROWS), :] = meta_ref[...]
-
-
-META_ROWS = 8
-RADIX = 128
-
-
-def prep_body(single_ref, chain_ref, residue_ref, valid_ref, out_ref):
-    tokens, samples, width = single_ref.shape
-    rows = tokens * samples
-    normed = normed_rows(single_ref[...])
-    out_ref[pl.ds(0, rows), :] = matmul(sample_major(tokens, samples), normed).astype(BF16)
-    residue = residue_ref[...]
-    row = lax.broadcasted_iota(jnp.int32, (META_ROWS, tokens), 0)
-    meta = jnp.where(row == 0, chain_ref[...], 0)
-    meta = jnp.where(row == 1, residue // RADIX, meta)
-    meta = jnp.where(row == 2, residue % RADIX, meta)
-    meta = jnp.where(row == 3, valid_ref[...], meta)
-    token = lax.broadcasted_iota(jnp.int32, (tokens, width), 0)
-    lane = lax.broadcasted_iota(jnp.int32, (tokens, width), 1)
-    spread = (lane % tokens == token).astype(F32).astype(BF16)
-    tiled = matmul(meta.astype(F32).astype(BF16), spread)
-    out_ref[pl.ds(rows, META_ROWS), :] = tiled.astype(BF16)
-    meta_ref[...] = tiled.astype(BF16)
-    weight.wait()
-    q_ref[...] = matmul(data, wq_ref[...]).astype(BF16)
-
-
-def join_body(single_ref, meta_ref, out_ref):
-    tokens, samples, _ = single_ref.shape
-    rows = tokens * samples
-    normed = normed_rows(single_ref[...])
-    out_ref[pl.ds(0, rows), :] = matmul(sample_major(tokens, samples), normed).astype(BF16)
-    out_ref[pl.ds(rows, META_ROWS), :] = meta_ref[...]
-
-
-META_ROWS = 8
-RADIX = 128
-
-
-def prep_body(single_ref, chain_ref, residue_ref, valid_ref, out_ref):
-    tokens, samples, width = single_ref.shape
-    rows = tokens * samples
-    normed = normed_rows(single_ref[...])
-    out_ref[pl.ds(0, rows), :] = matmul(sample_major(tokens, samples), normed).astype(BF16)
-    residue = residue_ref[...]
-    row = lax.broadcasted_iota(jnp.int32, (META_ROWS, tokens), 0)
-    meta = jnp.where(row == 0, chain_ref[...], 0)
-    meta = jnp.where(row == 1, residue // RADIX, meta)
-    meta = jnp.where(row == 2, residue % RADIX, meta)
-    meta = jnp.where(row == 3, valid_ref[...], meta)
-    token = lax.broadcasted_iota(jnp.int32, (tokens, width), 0)
-    lane = lax.broadcasted_iota(jnp.int32, (tokens, width), 1)
-    spread = (lane % tokens == token).astype(F32).astype(BF16)
-    tiled = matmul(meta.astype(F32).astype(BF16), spread)
-    out_ref[pl.ds(rows, META_ROWS), :] = tiled.astype(BF16)
-    meta_ref[...] = tiled.astype(BF16)
-    weight.wait()
-    q_ref[...] = matmul(data, wq_ref[...]).astype(BF16)
-
-
-def join_body(single_ref, meta_ref, out_ref):
-    tokens, samples, _ = single_ref.shape
-    rows = tokens * samples
-    normed = normed_rows(single_ref[...])
-    out_ref[pl.ds(0, rows), :] = matmul(sample_major(tokens, samples), normed).astype(BF16)
-    out_ref[pl.ds(rows, META_ROWS), :] = meta_ref[...]
-
-
-META_ROWS = 8
-RADIX = 128
-
-
-def prep_body(
-    single_hbm, chain_hbm, residue_hbm, valid_hbm, wq_hbm, out_ref, meta_ref, q_ref,
-    single_ref, ints_ref, wq_ref, sems,
-):
-    copies = [pltpu.make_async_copy(single_hbm, single_ref, sems.at[0])]
-    for i, ref in enumerate((chain_hbm, residue_hbm, valid_hbm)):
-        copies.append(pltpu.make_async_copy(ref, ints_ref.at[i], sems.at[i + 1]))
-    weight = pltpu.make_async_copy(wq_hbm, wq_ref, sems.at[4])
-    for copy in (*copies, weight):
-        copy.start()
-    tokens, samples, width = single_ref.shape
-    rows = tokens * samples
-    token = lax.broadcasted_iota(jnp.int32, (tokens, width), 0)
-    lane = lax.broadcasted_iota(jnp.int32, (tokens, width), 1)
-    spread = (lane % tokens == token).astype(F32).astype(BF16)
-    perm = sample_major(tokens, samples)
     for copy in copies:
         copy.wait()
-    data = matmul(perm, normed_rows(single_ref[...])).astype(BF16)
-    out_ref[pl.ds(0, rows), :] = data
     residue = ints_ref[1]
     row = lax.broadcasted_iota(jnp.int32, (META_ROWS, tokens), 0)
     meta = jnp.where(row == 0, ints_ref[0], 0)
     meta = jnp.where(row == 1, residue // RADIX, meta)
     meta = jnp.where(row == 2, residue % RADIX, meta)
     meta = jnp.where(row == 3, ints_ref[2], meta)
-    tiled = matmul(meta.astype(F32).astype(BF16), spread)
-    out_ref[pl.ds(rows, META_ROWS), :] = tiled.astype(BF16)
-    meta_ref[...] = tiled.astype(BF16)
-    weight.wait()
-    q_ref[...] = matmul(data, wq_ref[...]).astype(BF16)
-
-
-def join_body(single_ref, meta_ref, out_ref):
+    out_ref[...] = matmul(meta.astype(F32).astype(BF16), spread).astype(BF16)
+
+
+def prep_body(
+    single_hbm, meta_hbm, wq_hbm, out_ref, q_ref, single_ref, meta_ref, wq_ref, sems
+):
+    copies = []
+    moves = ((single_hbm, single_ref), (meta_hbm, meta_ref), (wq_hbm, wq_ref))
+    for i, (source, target) in enumerate(moves):
+        copies.append(pltpu.make_async_copy(source, target, sems.at[i]))
+        copies[i].start()
     tokens, samples, _ = single_ref.shape
     rows = tokens * samples
-    normed = normed_rows(single_ref[...])
-    out_ref[pl.ds(0, rows), :] = matmul(sample_major(tokens, samples), normed).astype(BF16)
-    out_ref[pl.ds(rows, META_ROWS), :] = meta_ref[...]
-
-
-META_ROWS = 8
-RADIX = 128
-
-
-def prep_body(single_hbm, chain_hbm, residue_hbm, valid_hbm, out_ref, meta_ref, single_ref, ints_ref, sems):
-    copies = [pltpu.make_async_copy(single_hbm, single_ref, sems.at[0])]
-    for i, ref in enumerate((chain_hbm, residue_hbm, valid_hbm)):
-        copies.append(pltpu.make_async_copy(ref, ints_ref.at[i], sems.at[i + 1]))
-    weight = pltpu.make_async_copy(wq_hbm, wq_ref, sems.at[4])
-    for copy in (*copies, weight):
-        copy.start()
-    tokens, samples, width = single_ref.shape
-    rows = tokens * samples
-    token = lax.broadcasted_iota(jnp.int32, (tokens, width), 0)
-    lane = lax.broadcasted_iota(jnp.int32, (tokens, width), 1)
-    spread = (lane % tokens == token).astype(F32).astype(BF16)
     perm = sample_major(tokens, samples)
-    for copy in copies:
-        copy.wait()
+    copies[0].wait()
     data = matmul(perm, normed_rows(single_ref[...])).astype(BF16)
     out_ref[pl.ds(0, rows), :] = data
-    residue = ints_ref[1]
-    row = lax.broadcasted_iota(jnp.int32, (META_ROWS, tokens), 0)
-    meta = jnp.where(row == 0, ints_ref[0], 0)
-    meta = jnp.where(row == 1, residue // RADIX, meta)
-    meta = jnp.where(row == 2, residue % RADIX, meta)
-    meta = jnp.where(row == 3, ints_ref[2], meta)
-    tiled = matmul(meta.astype(F32).astype(BF16), spread)
-    out_ref[pl.ds(rows, META_ROWS), :] = tiled.astype(BF16)
-    meta_ref[...] = tiled.astype(BF16)
-    weight.wait()
-    q_ref[...] = matmul(data, wq_ref[...]).astype(BF16)
-
-
-def join_body(single_ref, meta_ref, out_ref):
-    tokens, samples, _ = single_ref.shape
-    rows = tokens * samples
-    normed = normed_rows(single_ref[...])
-    out_ref[pl.ds(0, rows), :] = matmul(sample_major(tokens, samples), normed).astype(BF16)
+    copies[1].wait()
     out_ref[pl.ds(rows, META_ROWS), :] = meta_ref[...]
-    meta_ref[...] = tiled.astype(BF16)
-    weight.wait()
-    q_ref[...] = matmul(data, wq_ref[...]).astype(BF16)
-
-
-META_ROWS = 8
-RADIX = 128
-
-
-def prep_body(
-    single_hbm, chain_hbm, residue_hbm, valid_hbm, wq_hbm, out_ref, meta_ref, q_ref,
-    single_ref, ints_ref, wq_ref, sems,
-):
-    copies = [pltpu.make_async_copy(single_hbm, single_ref, sems.at[0])]
-    for i, ref in enumerate((chain_hbm, residue_hbm, valid_hbm)):
-        copies.append(pltpu.make_async_copy(ref, ints_ref.at[i], sems.at[i + 1]))
-    weight = pltpu.make_async_copy(wq_hbm, wq_ref, sems.at[4])
-    for copy in (*copies, weight):
-        copy.start()
-    tokens, samples, width = single_ref.shape
-    rows = tokens * samples
-    token = lax.broadcasted_iota(jnp.int32, (tokens, width), 0)
-    lane = lax.broadcasted_iota(jnp.int32, (tokens, width), 1)
-    spread = (lane % tokens == token).astype(F32).astype(BF16)
-    perm = sample_major(tokens, samples)
-    for copy in copies:
-        copy.wait()
-    data = matmul(perm, normed_rows(single_ref[...])).astype(BF16)
-    out_ref[pl.ds(0, rows), :] = data
-    residue = ints_ref[1]
-    row = lax.broadcasted_iota(jnp.int32, (META_ROWS, tokens), 0)
-    meta = jnp.where(row == 0, ints_ref[0], 0)
-    meta = jnp.where(row == 1, residue // RADIX, meta)
-    meta = jnp.where(row == 2, residue % RADIX, meta)
-    meta = jnp.where(row == 3, ints_ref[2], meta)
-    tiled = matmul(meta.astype(F32).astype(BF16), spread)
-    out_ref[pl.ds(rows, META_ROWS), :] = tiled.astype(BF16)
-    meta_ref[...] = tiled.astype(BF16)
-    weight.wait()
+    copies[2].wait()
     q_ref[...] = matmul(data, wq_ref[...]).astype(BF16)
 
 
@@ -493,10 +285,11 @@
     kv_refs, lasts = refs[:-19], refs[-19:-15]
     tokens, samples, width = single_ref.shape
     rows = tokens * samples
-    half = rows // 2
     hs = width // heads
-    metas = kv_metas(kv_refs[split:], rows) + [r[pl.ds(half, META_ROWS), :] for r in (lasts[0], lasts[2])]
-    data = jnp.concatenate([r[pl.ds(0, half), :] for r in lasts], axis=0)
+    share = lasts[0].shape[0] - META_ROWS
+    metas = kv_metas(kv_refs[split:], rows) + [r[pl.ds(share, META_ROWS), :] for r in (lasts[0], lasts[2])]
+    sizes = (share, rows - share) * 2
+    data = jnp.concatenate([r[pl.ds(0, n), :] for r, n in zip(lasts, sizes)], axis=0)
     k_last = matmul(data, wk_ref[...]).astype(BF16)
     v_last = matmul(data, wv_ref[...]).astype(BF16)
     bias = full_bias(own_ref[...], metas, tokens, pair_ref, tab_ref, pad_ref)
@@ -587,20 +380,25 @@
     cw = ring(single, 1)
     ccw = ring(single, -1)
     blocks = jax.ShapeDtypeStruct((rows + META_ROWS, width), BF16)
-    payload, meta, query = call(
+    meta = call(
+        tags_body,
+        jax.ShapeDtypeStruct((META_ROWS, width), BF16),
+        tuple(v.reshape(1, tokens) for v in (chain, residue, valid)),
+        in_specs=[ANY] * 3,
+        scratch=[pltpu.VMEM((3, 1, tokens), jnp.int32), pltpu.SemaphoreType.DMA((3,))],
+        moved=2 * META_ROWS * width,
+        limit=FULL,
+    )
+    payload, query = call(
         prep_body,
-        (
-            blocks,
-            jax.ShapeDtypeStruct((META_ROWS, width), BF16),
-            jax.ShapeDtypeStruct((rows, width), BF16),
-        ),
-        (single, *(v.reshape(1, tokens) for v in (chain, residue, valid)), w_query),
-        in_specs=[ANY] * 5,
+        (blocks, jax.ShapeDtypeStruct((rows, width), BF16)),
+        (single, meta, w_query),
+        in_specs=[ANY] * 3,
         scratch=[
             pltpu.VMEM(single.shape, BF16),
-            pltpu.VMEM((3, 1, tokens), jnp.int32),
+            pltpu.VMEM(meta.shape, BF16),
             pltpu.VMEM((width, width), BF16),
-            pltpu.SemaphoreType.DMA((5,)),
+            pltpu.SemaphoreType.DMA((3,)),
         ],
         flops=2 * rows * width * width,
         moved=6 * rows * width + 2 * width * width,
@@ -641,13 +439,13 @@
             moved=4 * width * width + 6 * n * rows * width,
         )
 
-    def piece(value, at, meta):
-        count = rows // 2 + (META_ROWS if meta else 0)
+    def piece(value, at, size, meta):
+        count = size + (META_ROWS if meta else 0)
 
         def body(in_ref, out_ref):
-            out_ref[pl.ds(0, rows // 2), :] = in_ref[pl.ds(at, rows // 2), :]
+            out_ref[pl.ds(0, size), :] = in_ref[pl.ds(at, size), :]
             if meta:
-                out_ref[pl.ds(rows // 2, META_ROWS), :] = in_ref[pl.ds(rows, META_ROWS), :]
+                out_ref[pl.ds(size, META_ROWS), :] = in_ref[pl.ds(rows, META_ROWS), :]
 
         shape = jax.ShapeDtypeStruct((count, width), BF16)
         return call(body, shape, (value,), moved=2 * rows * width)
@@ -662,6 +460,7 @@
         moved=2 * pair.size + 4 * total * lines,
         limit=(6 << 20) + 4 * pair.size,
     )
+    share = samples * 3 // 4 * tokens
     kvs = [kv([payload])]
     kvs.append(flip(kvs[-1]))
     for k in range(1, half):
@@ -669,8 +468,8 @@
             cw_next = ring(cw, 1)
             ccw_next = ring(ccw, -1)
         else:
-            cw_next = ring(piece(cw, 0, True), 1)
-            ccw_next = ring(piece(ccw, rows // 2, False), -1)
+            cw_next = ring(piece(cw, 0, share, True), 1)
+            ccw_next = ring(piece(ccw, share, rows - share, False), -1)
         kvs.append(kv([cw, ccw]))
         kvs.append(flip(kvs[-1]))
         cw, ccw = cw_next, ccw_next
@@ -722,14 +521,10 @@
         P(),
     )
 
-    step = jax.shard_map(
+    return jax.shard_map(
         shards,
         mesh=mesh,
         in_specs=placed,
         out_specs=P(("groups", "tok"), None, None),
         check_vma=False,
     )
-    return step
-    return step
-    return step
-    return step

time: 46.8 us -> 53 us (1.13)
  local copies, waits for them, and re-layouts: 4.37 us -> 7.9 us
  Pallas kernels: 18.1 us -> 20.1 us
  starting transfers between devices: 12.4 us -> 14.1 us
  waiting for transfers between devices: 11.5 us -> 10.4 us
    unnamed x32 -> x40, local copies, waits for them, and re-layouts: 4.37 us -> 7.9 us
    pallas_call x14 -> x15, Pallas kernels: 18.1 us -> 20.1 us  [call(): pl.pallas_call(body, out_shape=out_shape, in_specs=in_specs or [VMEM] * l...]
    ppermute x10, starting transfers between devices: 11.3 us -> 12.7 us  [ring(): return lax.ppermute(value, 'tok', pairs)]
    ppermute x10, waiting for transfers between devices: 11.5 us -> 10.4 us  [ring(): return lax.ppermute(value, 'tok', pairs)]
  transfers between devices with their start and end apart: 16 -> 16, of which waited for: 6 -> 4; matrix products, arithmetic and copies ran while one was open for 0% -> 0% of each run, Pallas kernels for 27% -> 28%
where the time goes in v9:
time: 53 us; the launch traced here: 52.7 us
  Pallas kernels  20.1 us (38%)
  starting transfers between devices  14.1 us (27%)
  waiting for transfers between devices  10.4 us (20%)
  local copies, waits for them, and re-layouts  7.9 us (15%)
    pallas_call x15, Pallas kernels, call(): pl.pallas_call(body, out_shape=out_shape, in_specs=in_specs or [VMEM] * l...  20.1 us
    ppermute x10, starting transfers between devices, ring(): return lax.ppermute(value, 'tok', pairs)  12.7 us
    ppermute x10, waiting for transfers between devices, ring(): return lax.ppermute(value, 'tok', pairs)  10.4 us
    unnamed x40, local copies, waits for them, and re-layouts  7.9 us
    ppermute x6, starting transfers between devices, flip(): return lax.ppermute(value, 'tok', [(d, d ^ 1) for d in range(devices)])  1.37 us
  transfers between devices with their start and end apart: 16, of which 4 were waited for; matrix products, arithmetic and copies ran while one was open for 0% of the time, Pallas kernels for 28%

profile of v9, /device:TPU:0, one launch (start us, length us, event | category | flops | bytes accessed | tf_op | source)
XLA Modules:
  0.0 52.7 jit_solution(5412048504094842174)
XLA Ops:
  0.0 3.0 %collective-permute-start.3 = (bf16[16,8,768]{2,1,0:T(8,128)(2,1)}, bf16[16,8,768]{2,1,0:T(8,128)(2,1)S(1)}, u32[]{:S(2)}, u32[]{:S(2)}) collective-permute-start(bf16[16,8,768]{2,1,0:T(8,128)(2,1)} %refs_22_.1), channel_id=1, source_target_pairs={{0,2},{1,3},{4,0},{5,1},{8,4},{9,5},{12,8},{13,9},{14,12},{15,13},... | collective-permute-start | bytes 589832 | tf_op jit(solution)/shard_map/ppermute | solution.py:370
  3.0 0.1 collective-permute-start.1
  3.1 1.4 %shard_map.118.meta_hbm.refs_9_.refs_21_ = bf16[8,768]{1,0:T(8,128)(2,1)} custom-call(s32[1,16]{1,0:T(1,128)} %bitcast.9, s32[1,16]{1,0:T(1,128)} %bitcast.10, s32[1,16]{1,0:T(1,128)} %bitcast.11), custom_call_target="tpu_custom_call" | custom-call | bytes 12288 | tf_op jit(solution)/shard_map/pallas_call | solution.py:340
  4.5 2.0 %collective-permute-start.4 = (bf16[8,768]{1,0:T(8,128)(2,1)}, bf16[8,768]{1,0:T(8,128)(2,1)S(1)}, u32[]{:S(2)}, u32[]{:S(2)}) collective-permute-start(bf16[8,768]{1,0:T(8,128)(2,1)} %shard_map.118.meta_hbm.refs_9_.refs_21_), channel_id=1, source_target_pairs={{0,2},{1,3},{4,0},{5,1},{8,4},{9,5},{12,8},{13,9},{14,12},{15,13},... | collective-permute-start | bytes 36872 | tf_op jit(solution)/shard_map/ppermute | solution.py:370
  6.5 0.1 collective-permute-start.2
  6.6 1.8 %collective-permute-done.4.meta_ref = bf16[8,768]{1,0:T(8,128)(2,1)S(1)} collective-permute-done((bf16[8,768]{1,0:T(8,128)(2,1)}, bf16[8,768]{1,0:T(8,128)(2,1)S(1)}, u32[]{:S(2)}, u32[]{:S(2)}) %collective-permute-start.4) | collective-permute-done | bytes 12320 | tf_op jit(solution)/shard_map/ppermute | solution.py:370
  8.5 0.0 collective-permute-done.3.single_ref
  8.5 0.4 shard_map.122.refs_1_
  8.9 2.0 %collective-permute-start.7 = (bf16[136,768]{1,0:T(8,128)(2,1)S(1)}, bf16[136,768]{1,0:T(8,128)(2,1)S(1)}, u32[]{:S(2)}, u32[]{:S(2)}) collective-permute-start(bf16[136,768]{1,0:T(8,128)(2,1)S(1)} %shard_map.122.refs_1_), channel_id=1, source_target_pairs={{0,2},{1,3},{4,0},{5,1},{8,4},{9,5},{12,8},{13,9},{14,12},{15,13},... | collective-permute-start | bytes 626696 | tf_op jit(solution)/shard_map/ppermute | solution.py:370
  10.9 0.0 collective-permute-done.2.meta_ref
  10.9 0.0 collective-permute-done.1.single_ref
  10.9 0.4 shard_map.121.refs_0_
  11.3 0.1 collective-permute-start.6
  11.4 3.8 %collective-permute-done.7.refs_1_ = bf16[136,768]{1,0:T(8,128)(2,1)S(1)} collective-permute-done((bf16[136,768]{1,0:T(8,128)(2,1)S(1)}, bf16[136,768]{1,0:T(8,128)(2,1)S(1)}, u32[]{:S(2)}, u32[]{:S(2)}) %collective-permute-start.7) | collective-permute-done | bytes 208928 | tf_op jit(solution)/shard_map/ppermute | solution.py:370
  15.2 1.5 %collective-permute-start.10 = (bf16[136,768]{1,0:T(8,128)(2,1)S(1)}, bf16[136,768]{1,0:T(8,128)(2,1)S(1)}, u32[]{:S(2)}, u32[]{:S(2)}) collective-permute-start(bf16[136,768]{1,0:T(8,128)(2,1)S(1)} %collective-permute-done.7.refs_1_), channel_id=1, source_target_pairs={{0,2},{1,3},{4,0},{5,1},{8,4},{9,5},{12,8},{13,9},{14,12},{15,13},... | collective-permute-start | bytes 626696 | tf_op jit(solution)/shard_map/ppermute | solution.py:370
  16.7 0.5 collective-permute-done.6.refs_0_
  17.2 0.3 collective-permute-start.9
  17.4 1.3 %copy-done = bf16[768,768]{1,0:T(8,128)(2,1)S(1)} copy-done((bf16[768,768]{1,0:T(8,128)(2,1)S(1)}, bf16[768,768]{1,0:T(8,128)(2,1)}, u32[]{:S(2)}) %copy-start) | copy-done | bytes 1179672
  18.7 1.3 %copy-done.2 = bf16[768,768]{1,0:T(8,128)(2,1)S(1)} copy-done((bf16[768,768]{1,0:T(8,128)(2,1)S(1)}, bf16[768,768]{1,0:T(8,128)(2,1)}, u32[]{:S(2)}) %copy-start.2) | copy-done | bytes 1179672
  20.0 0.8 %shard_map.123.refs_2_ = bf16[528,768]{1,0:T(8,128)(2,1)S(1)} custom-call(bf16[136,768]{1,0:T(8,128)(2,1)S(1)} %shard_map.121.refs_0_, bf16[136,768]{1,0:T(8,128)(2,1)S(1)} %shard_map.122.refs_1_, bf16[768,768]{1,0:T(8,128)(2,1)S(1)} %copy-done, bf16[768,768]{1,0:T(8,128)(2,1)S(1)} %copy-done.2), custom_call_target="tpu_custom_call" | custom-call | flops 603979776 | bytes 3538944 | tf_op jit(solution)/shard_map/pallas_call | solution.py:340
  20.8 0.1 collective-permute-start.5
  20.8 1.7 %shard_map.124.refs_4_ = bf16[528,768]{1,0:T(8,128)(2,1)} custom-call(bf16[136,768]{1,0:T(8,128)(2,1)S(1)} %collective-permute-done.6.refs_0_, bf16[136,768]{1,0:T(8,128)(2,1)S(1)} %collective-permute-done.7.refs_1_, bf16[768,768]{1,0:T(8,128)(2,1)S(1)} %copy-done, bf16[768,768]{1,0:T(8,128)(2,1)S(1)} %copy-done.2), custom_call_target="tpu_custom_call" | custom-call | flops 603979776 | bytes 3538944 | tf_op jit(solution)/shard_map/pallas_call | solution.py:340
  22.5 0.5 collective-permute-start.8
  23.0 1.7 %shard_map.125.refs_6_ = bf16[528,768]{1,0:T(8,128)(2,1)} custom-call(bf16[136,768]{1,0:T(8,128)(2,1)S(1)} %collective-permute-done.9.refs_0_.in_ref, bf16[136,768]{1,0:T(8,128)(2,1)S(1)} %collective-permute-done.10.refs_1_.in_ref, bf16[768,768]{1,0:T(8,128)(2,1)S(1)} %copy-done, bf16[768,768]{1,0:T(8,128)(2,1)S(1)} %copy-done.2), custom_call_target="tpu_custom_call" | custom-call | flops 603979776 | bytes 3538944 | tf_op jit(solution)/shard_map/pallas_call | solution.py:340
  24.7 0.7 %copy-done.13 = bf16[136,768]{1,0:T(8,128)(2,1)} copy-done((bf16[136,768]{1,0:T(8,128)(2,1)}, bf16[136,768]{1,0:T(8,128)(2,1)S(1)}, u32[]{:S(2)}) %copy-start.13) | copy-done | bytes 208920
  25.4 0.0 collective-permute-start.11
  25.4 2.5 %shard_map.119 = (bf16[136,768]{1,0:T(8,128)(2,1)}, bf16[128,768]{1,0:T(8,128)(2,1)}) custom-call(bf16[16,8,768]{2,1,0:T(8,128)(2,1)} %refs_22_.1, bf16[8,768]{1,0:T(8,128)(2,1)} %shard_map.118.meta_hbm.refs_9_.refs_21_, bf16[768,768]{1,0:T(8,128)(2,1)} %wq_hbm.1), custom_call_target="tpu_custom_call" | custom-call | flops 150994944 | bytes 1769472 | tf_op jit(solution)/shard_map/pallas_call | solution.py:340
  28.0 0.9 %copy-done.11 = bf16[136,768]{1,0:T(8,128)(2,1)S(1)} copy-done((bf16[136,768]{1,0:T(8,128)(2,1)S(1)}, bf16[136,768]{1,0:T(8,128)(2,1)}, u32[]{:S(2)}) %copy-start.11) | copy-done | bytes 208920
  28.9 0.5 shard_map.120.refs_0_
  29.4 0.0 copy-start.19
  29.4 0.5 collective-permute-start
  29.9 0.8 %copy-done.4 = bf16[264,768]{1,0:T(8,128)(2,1)} copy-done((bf16[264,768]{1,0:T(8,128)(2,1)}, bf16[264,768]{1,0:T(8,128)(2,1)S(1)}, u32[]{:S(2)}) %copy-start.4) | copy-done | bytes 405528
  30.7 1.9 %collective-permute-start.12 = (bf16[104,768]{1,0:T(8,128)(2,1)S(1)}, bf16[104,768]{1,0:T(8,128)(2,1)S(1)}, u32[]{:S(2)}, u32[]{:S(2)}) collective-permute-start(bf16[104,768]{1,0:T(8,128)(2,1)S(1)} %shard_map.126), channel_id=1, source_target_pairs={{0,4},{1,5},{4,8},{5,9},{8,12},{9,13},{12,14},{13,15},{14,10},{15,... | collective-permute-start | bytes 479240 | tf_op jit(solution)/shard_map/ppermute | solution.py:370
  32.6 4.3 %collective-permute-done.12.refs_8_ = bf16[104,768]{1,0:T(8,128)(2,1)S(1)} collective-permute-done((bf16[104,768]{1,0:T(8,128)(2,1)S(1)}, bf16[104,768]{1,0:T(8,128)(2,1)S(1)}, u32[]{:S(2)}, u32[]{:S(2)}) %collective-permute-start.12) | collective-permute-done | bytes 159776 | tf_op jit(solution)/shard_map/ppermute | solution.py:370
  36.9 0.6 %shard_map.127 = bf16[32,768]{1,0:T(8,128)(2,1)} custom-call(bf16[136,768]{1,0:T(8,128)(2,1)S(1)} %collective-permute-done.10.refs_1_.in_ref), custom_call_target="tpu_custom_call" | custom-call | bytes 196608 | tf_op jit(solution)/shard_map/pallas_call | solution.py:340
  37.5 0.8 %copy-done.6 = bf16[264,768]{1,0:T(8,128)(2,1)} copy-done((bf16[264,768]{1,0:T(8,128)(2,1)}, bf16[264,768]{1,0:T(8,128)(2,1)S(1)}, u32[]{:S(2)}) %copy-start.6) | copy-done | bytes 405528
  38.3 1.7 %collective-permute-start.13 = (bf16[32,768]{1,0:T(8,128)(2,1)}, bf16[32,768]{1,0:T(8,128)(2,1)}, u32[]{:S(2)}, u32[]{:S(2)}) collective-permute-start(bf16[32,768]{1,0:T(8,128)(2,1)} %shard_map.127), channel_id=1, source_target_pairs={{0,2},{1,3},{4,0},{5,1},{8,4},{9,5},{12,8},{13,9},{14,12},{15,13},... | collective-permute-start | bytes 147464 | tf_op jit(solution)/shard_map/ppermute | solution.py:370
  40.0 1.3 %copy-done.8 = bf16[768,768]{1,0:T(8,128)(2,1)S(1)} copy-done((bf16[768,768]{1,0:T(8,128)(2,1)S(1)}, bf16[768,768]{1,0:T(8,128)(2,1)}, u32[]{:S(2)}) %copy-start.8) | copy-done | bytes 1179672
  41.3 0.3 shard_map.129.refs_13_
  41.6 0.9 %copy-done.10 = bf16[16,256,128]{2,1,0:T(8,128)(2,1)S(1)} copy-done((bf16[16,256,128]{2,1,0:T(8,128)(2,1)S(1)}, bf16[16,256,128]{2,1,0:T(8,128)(2,1)}, u32[]{:S(2)}) %copy-start.10) | copy-done | bytes 1048600
  42.5 0.7 %shard_map.130 = (f32[160,256]{1,0:T(8,128)S(1)}, f32[96,256]{1,0:T(8,128)S(1)}) custom-call(s32[1]{0:T(128)} %bitcast.3.me_ref, bf16[16,256,128]{2,1,0:T(8,128)(2,1)S(1)} %copy-done.10, bf16[16,128]{1,0:T(8,128)(2,1)S(1)} %bitcast.8), custom_call_target="tpu_custom_call" | custom-call | flops 268435456 | bytes 1310720 | tf_op jit(solution)/shard_map/pallas_call | solution.py:340
  43.2 0.3 collective-permute-start.15
  43.5 0.0 copy-start.18
  43.5 1.0 %shard_map.128.refs_6_.refs_12_ = bf16[6144,256]{1,0:T(8,128)(2,1)S(1)} custom-call(s32[1]{0:T(128)} %bitcast.3.me_ref, bf16[128,768]{1,0:T(8,128)(2,1)S(1)} %copy-done.16), custom_call_target="tpu_custom_call" | custom-call | flops 50331648 | bytes 3145728 | tf_op jit(solution)/shard_map/pallas_call | solution.py:340
  44.6 0.0 copy-done.7
  44.6 0.0 copy-start.15
  44.6 2.6 %shard_map.131 = (f32[1280,256]{1,0:T(8,128)S(1)}, f32[8,256]{1,0:T(8,128)S(1)}, f32[8,256]{1,0:T(8,128)S(1)}) custom-call(bf16[264,768]{1,0:T(8,128)(2,1)S(1)} %copy-done.5, bf16[264,768]{1,0:T(8,128)(2,1)S(1)} %copy-done.7, bf16[528,768]{1,0:T(8,128)(2,1)S(1)} %shard_map.123.refs_2_, bf16[528,768]{1,0:T(8,128)(2,1)} %collective-permute-done.5.refs_3_, ...), custom_call_target="tpu_custom_call" | custom-call | flops 503316480 | bytes 5898240 | tf_op jit(solution)/shard_map/pallas_call | solution.py:340
  47.3 5.4 %shard_map.132 = bf16[16,8,768]{2,1,0:T(8,128)(2,1)} custom-call(bf16[264,768]{1,0:T(8,128)(2,1)S(1)} %copy-done.5, bf16[264,768]{1,0:T(8,128)(2,1)S(1)} %copy-done.7, bf16[528,768]{1,0:T(8,128)(2,1)S(1)} %shard_map.123.refs_2_, bf16[528,768]{1,0:T(8,128)(2,1)} %collective-permute-done.5.refs_3_, bf16[528,768]{1,0:T(8,128)(2,1)} %shard_map.124.refs_4_, ...), custom_call_target="tpu_custom_call" | custom-call | flops 100663296 | bytes 3145728 | tf_op jit(solution)/shard_map/pallas_call | solution.py:340
  (39 shorter events, 0.1 us)
Async XLA Ops:
  0.0 8.5 %collective-permute-start.3 = (bf16[16,8,768]{2,1,0:T(8,128)(2,1)}, bf16[16,8,768]{2,1,0:T(8,128)(2,1)S(1)}, u32[]{:S(2)}, u32[]{:S(2)}) collective-permute-start(bf16[16,8,768]{2,1,0:T(8,128)(2,1)} %refs_22_.1), channel_id=1, source_target_pairs={{0,2},{1,3},{4,0},{5,1},{8,4},{9,5},{12,8},{13,9},{14,12},{15,13},... | collective-permute-start | bytes 589832 | tf_op jit(solution)/shard_map/ppermute | solution.py:370
  3.0 7.9 %collective-permute-start.1 = (bf16[16,8,768]{2,1,0:T(8,128)(2,1)}, bf16[16,8,768]{2,1,0:T(8,128)(2,1)S(1)}, u32[]{:S(2)}, u32[]{:S(2)}) collective-permute-start(bf16[16,8,768]{2,1,0:T(8,128)(2,1)} %refs_22_.1), channel_id=1, source_target_pairs={{0,4},{1,5},{4,8},{5,9},{8,12},{9,13},{12,14},{13,15},{14,10},{15,... | collective-permute-start | bytes 589832 | tf_op jit(solution)/shard_map/ppermute | solution.py:370
  4.5 4.0 %collective-permute-start.4 = (bf16[8,768]{1,0:T(8,128)(2,1)}, bf16[8,768]{1,0:T(8,128)(2,1)S(1)}, u32[]{:S(2)}, u32[]{:S(2)}) collective-permute-start(bf16[8,768]{1,0:T(8,128)(2,1)} %shard_map.118.meta_hbm.refs_9_.refs_21_), channel_id=1, source_target_pairs={{0,2},{1,3},{4,0},{5,1},{8,4},{9,5},{12,8},{13,9},{14,12},{15,13},... | collective-permute-start | bytes 36872 | tf_op jit(solution)/shard_map/ppermute | solution.py:370
  6.5 4.4 %collective-permute-start.2 = (bf16[8,768]{1,0:T(8,128)(2,1)}, bf16[8,768]{1,0:T(8,128)(2,1)S(1)}, u32[]{:S(2)}, u32[]{:S(2)}) collective-permute-start(bf16[8,768]{1,0:T(8,128)(2,1)} %shard_map.118.meta_hbm.refs_9_.refs_21_), channel_id=1, source_target_pairs={{0,4},{1,5},{4,8},{5,9},{8,12},{9,13},{12,14},{13,15},{14,10},{15,... | collective-permute-start | bytes 36872 | tf_op jit(solution)/shard_map/ppermute | solution.py:370
  8.9 6.4 %collective-permute-start.7 = (bf16[136,768]{1,0:T(8,128)(2,1)S(1)}, bf16[136,768]{1,0:T(8,128)(2,1)S(1)}, u32[]{:S(2)}, u32[]{:S(2)}) collective-permute-start(bf16[136,768]{1,0:T(8,128)(2,1)S(1)} %shard_map.122.refs_1_), channel_id=1, source_target_pairs={{0,2},{1,3},{4,0},{5,1},{8,4},{9,5},{12,8},{13,9},{14,12},{15,13},... | collective-permute-start | bytes 626696 | tf_op jit(solution)/shard_map/ppermute | solution.py:370
  11.3 5.9 %collective-permute-start.6 = (bf16[136,768]{1,0:T(8,128)(2,1)S(1)}, bf16[136,768]{1,0:T(8,128)(2,1)S(1)}, u32[]{:S(2)}, u32[]{:S(2)}) collective-permute-start(bf16[136,768]{1,0:T(8,128)(2,1)S(1)} %shard_map.121.refs_0_), channel_id=1, source_target_pairs={{0,4},{1,5},{4,8},{5,9},{8,12},{9,13},{12,14},{13,15},{14,10},{15,... | collective-permute-start | bytes 626696 | tf_op jit(solution)/shard_map/ppermute | solution.py:370
  15.2 7.8 %collective-permute-start.10 = (bf16[136,768]{1,0:T(8,128)(2,1)S(1)}, bf16[136,768]{1,0:T(8,128)(2,1)S(1)}, u32[]{:S(2)}, u32[]{:S(2)}) collective-permute-start(bf16[136,768]{1,0:T(8,128)(2,1)S(1)} %collective-permute-done.7.refs_1_), channel_id=1, source_target_pairs={{0,2},{1,3},{4,0},{5,1},{8,4},{9,5},{12,8},{13,9},{14,12},{15,13},... | collective-permute-start | bytes 626696 | tf_op jit(solution)/shard_map/ppermute | solution.py:370
  17.2 5.9 %collective-permute-start.9 = (bf16[136,768]{1,0:T(8,128)(2,1)S(1)}, bf16[136,768]{1,0:T(8,128)(2,1)S(1)}, u32[]{:S(2)}, u32[]{:S(2)}) collective-permute-start(bf16[136,768]{1,0:T(8,128)(2,1)S(1)} %collective-permute-done.6.refs_0_), channel_id=1, source_target_pairs={{0,4},{1,5},{4,8},{5,9},{8,12},{9,13},{12,14},{13,15},{14,10},{15,... | collective-permute-start | bytes 626696 | tf_op jit(solution)/shard_map/ppermute | solution.py:370
  17.4 1.3 %copy-start = (bf16[768,768]{1,0:T(8,128)(2,1)S(1)}, bf16[768,768]{1,0:T(8,128)(2,1)}, u32[]{:S(2)}) copy-start(bf16[768,768]{1,0:T(8,128)(2,1)} %refs_17_.1) | copy-start | bytes 3538948
  18.7 1.3 %copy-start.2 = (bf16[768,768]{1,0:T(8,128)(2,1)S(1)}, bf16[768,768]{1,0:T(8,128)(2,1)}, u32[]{:S(2)}) copy-start(bf16[768,768]{1,0:T(8,128)(2,1)} %refs_18_.1) | copy-start | bytes 3538948
  20.8 23.8 %collective-permute-start.5 = (bf16[528,768]{1,0:T(8,128)(2,1)S(1)}, bf16[528,768]{1,0:T(8,128)(2,1)}, u32[]{:S(2)}, u32[]{:S(2)}) collective-permute-start(bf16[528,768]{1,0:T(8,128)(2,1)S(1)} %shard_map.123.refs_2_), channel_id=1, source_target_pairs={{0,1},{1,0},{2,3},{3,2},{4,5},{5,4},{6,7},{7,6},{8,9},{9,8},{10,11... | collective-permute-start | bytes 2433032 | tf_op jit(solution)/shard_map/ppermute | solution.py:373
  22.5 22.0 %collective-permute-start.8 = (bf16[528,768]{1,0:T(8,128)(2,1)}, bf16[528,768]{1,0:T(8,128)(2,1)}, u32[]{:S(2)}, u32[]{:S(2)}) collective-permute-start(bf16[528,768]{1,0:T(8,128)(2,1)} %shard_map.124.refs_4_), channel_id=1, source_target_pairs={{0,1},{1,0},{2,3},{3,2},{4,5},{5,4},{6,7},{7,6},{8,9},{9,8},{10,11... | collective-permute-start | bytes 2433032 | tf_op jit(solution)/shard_map/ppermute | solution.py:373
  23.0 4.9 %copy-start.3 = (bf16[768,768]{1,0:T(8,128)(2,1)S(1)}, bf16[768,768]{1,0:T(8,128)(2,1)}, u32[]{:S(2)}) copy-start(bf16[768,768]{1,0:T(8,128)(2,1)} %refs_18_.1) | copy-start | bytes 3538948
  24.7 0.7 %copy-start.13 = (bf16[136,768]{1,0:T(8,128)(2,1)}, bf16[136,768]{1,0:T(8,128)(2,1)S(1)}, u32[]{:S(2)}) copy-start(bf16[136,768]{1,0:T(8,128)(2,1)S(1)} %collective-permute-done.9.refs_0_.in_ref) | copy-start | bytes 626692
  25.4 2.6 %copy-start.1 = (bf16[768,768]{1,0:T(8,128)(2,1)S(1)}, bf16[768,768]{1,0:T(8,128)(2,1)}, u32[]{:S(2)}) copy-start(bf16[768,768]{1,0:T(8,128)(2,1)} %refs_17_.1) | copy-start | bytes 3538948
  25.4 21.9 %collective-permute-start.11 = (bf16[528,768]{1,0:T(8,128)(2,1)}, bf16[528,768]{1,0:T(8,128)(2,1)}, u32[]{:S(2)}, u32[]{:S(2)}) collective-permute-start(bf16[528,768]{1,0:T(8,128)(2,1)} %shard_map.125.refs_6_), channel_id=1, source_target_pairs={{0,1},{1,0},{2,3},{3,2},{4,5},{5,4},{6,7},{7,6},{8,9},{9,8},{10,11... | collective-permute-start | bytes 2433032 | tf_op jit(solution)/shard_map/ppermute | solution.py:373
  28.0 0.9 %copy-start.11 = (bf16[136,768]{1,0:T(8,128)(2,1)S(1)}, bf16[136,768]{1,0:T(8,128)(2,1)}, u32[]{:S(2)}) copy-start(bf16[136,768]{1,0:T(8,128)(2,1)} %get-tuple-element.12.refs_0_.pay_ref) | copy-start | bytes 626692
  28.9 1.8 %copy-start.14 = (bf16[136,768]{1,0:T(8,128)(2,1)S(1)}, bf16[136,768]{1,0:T(8,128)(2,1)}, u32[]{:S(2)}) copy-start(bf16[136,768]{1,0:T(8,128)(2,1)} %copy-done.13) | copy-start | bytes 626692
  28.9 11.1 %copy-start.12 = (bf16[136,768]{1,0:T(8,128)(2,1)S(1)}, bf16[136,768]{1,0:T(8,128)(2,1)}, u32[]{:S(2)}) copy-start(bf16[136,768]{1,0:T(8,128)(2,1)} %get-tuple-element.12.refs_0_.pay_ref) | copy-start | bytes 626692
  29.4 12.2 %copy-start.19 = (bf16[128,16]{0,1:T(8,128)(2,1)S(1)}, bf16[128,16]{0,1:T(8,128)(2,1)}, u32[]{:S(2)}) copy-start(bf16[128,16]{0,1:T(8,128)(2,1)} %param.22) | copy-start | bytes 12292
  29.4 8.1 %collective-permute-start = (bf16[264,768]{1,0:T(8,128)(2,1)S(1)}, bf16[264,768]{1,0:T(8,128)(2,1)S(1)}, u32[]{:S(2)}, u32[]{:S(2)}) collective-permute-start(bf16[264,768]{1,0:T(8,128)(2,1)S(1)} %shard_map.120.refs_0_), channel_id=1, source_target_pairs={{0,1},{1,0},{2,3},{3,2},{4,5},{5,4},{6,7},{7,6},{8,9},{9,8},{10,11... | collective-permute-start | bytes 1216520 | tf_op jit(solution)/shard_map/ppermute | solution.py:373
  29.9 0.8 %copy-start.4 = (bf16[264,768]{1,0:T(8,128)(2,1)}, bf16[264,768]{1,0:T(8,128)(2,1)S(1)}, u32[]{:S(2)}) copy-start(bf16[264,768]{1,0:T(8,128)(2,1)S(1)} %shard_map.120.refs_0_) | copy-start | bytes 1216516
  30.7 6.2 %collective-permute-start.12 = (bf16[104,768]{1,0:T(8,128)(2,1)S(1)}, bf16[104,768]{1,0:T(8,128)(2,1)S(1)}, u32[]{:S(2)}, u32[]{:S(2)}) collective-permute-start(bf16[104,768]{1,0:T(8,128)(2,1)S(1)} %shard_map.126), channel_id=1, source_target_pairs={{0,4},{1,5},{4,8},{5,9},{8,12},{9,13},{12,14},{13,15},{14,10},{15,... | collective-permute-start | bytes 479240 | tf_op jit(solution)/shard_map/ppermute | solution.py:370
  36.9 10.4 %collective-permute-start.14 = (bf16[104,768]{1,0:T(8,128)(2,1)S(1)}, bf16[104,768]{1,0:T(8,128)(2,1)}, u32[]{:S(2)}, u32[]{:S(2)}) collective-permute-start(bf16[104,768]{1,0:T(8,128)(2,1)S(1)} %collective-permute-done.12.refs_8_), channel_id=1, source_target_pairs={{0,1},{1,0},{2,3},{3,2},{4,5},{5,4},{6,7},{7,6},{8,9},{9,8},{10,11... | collective-permute-start | bytes 479240 | tf_op jit(solution)/shard_map/ppermute | solution.py:373
  37.5 0.8 %copy-start.6 = (bf16[264,768]{1,0:T(8,128)(2,1)}, bf16[264,768]{1,0:T(8,128)(2,1)S(1)}, u32[]{:S(2)}) copy-start(bf16[264,768]{1,0:T(8,128)(2,1)S(1)} %collective-permute-done.refs_1_) | copy-start | bytes 1216516
  38.3 4.9 %collective-permute-start.13 = (bf16[32,768]{1,0:T(8,128)(2,1)}, bf16[32,768]{1,0:T(8,128)(2,1)}, u32[]{:S(2)}, u32[]{:S(2)}) collective-permute-start(bf16[32,768]{1,0:T(8,128)(2,1)} %shard_map.127), channel_id=1, source_target_pairs={{0,2},{1,3},{4,0},{5,1},{8,4},{9,5},{12,8},{13,9},{14,12},{15,13},... | collective-permute-start | bytes 147464 | tf_op jit(solution)/shard_map/ppermute | solution.py:370
  40.0 1.3 %copy-start.8 = (bf16[768,768]{1,0:T(8,128)(2,1)S(1)}, bf16[768,768]{1,0:T(8,128)(2,1)}, u32[]{:S(2)}) copy-start(bf16[768,768]{1,0:T(8,128)(2,1)} %wg_ref.1) | copy-start | bytes 3538948
  41.3 1.2 %copy-start.10 = (bf16[16,256,128]{2,1,0:T(8,128)(2,1)S(1)}, bf16[16,256,128]{2,1,0:T(8,128)(2,1)}, u32[]{:S(2)}) copy-start(bf16[16,256,128]{2,1,0:T(8,128)(2,1)} %pair_ref.1) | copy-start | bytes 3145732
  41.3 2.2 %copy-start.16 = (bf16[128,768]{1,0:T(8,128)(2,1)S(1)}, bf16[128,768]{1,0:T(8,128)(2,1)}, u32[]{:S(2)}) copy-start(bf16[128,768]{1,0:T(8,128)(2,1)} %get-tuple-element.13.q_ref) | copy-start | bytes 589828
  43.2 4.1 %collective-permute-start.15 = (bf16[32,768]{1,0:T(8,128)(2,1)}, bf16[32,768]{1,0:T(8,128)(2,1)S(1)}, u32[]{:S(2)}, u32[]{:S(2)}) collective-permute-start(bf16[32,768]{1,0:T(8,128)(2,1)} %collective-permute-done.13.refs_9_), channel_id=1, source_target_pairs={{0,1},{1,0},{2,3},{3,2},{4,5},{5,4},{6,7},{7,6},{8,9},{9,8},{10,11... | collective-permute-start | bytes 147464 | tf_op jit(solution)/shard_map/ppermute | solution.py:373
  43.5 1.1 %copy-start.5 = (bf16[264,768]{1,0:T(8,128)(2,1)S(1)}, bf16[264,768]{1,0:T(8,128)(2,1)}, u32[]{:S(2)}) copy-start(bf16[264,768]{1,0:T(8,128)(2,1)} %copy-done.4) | copy-start | bytes 1216516
  43.5 1.1 %copy-start.7 = (bf16[264,768]{1,0:T(8,128)(2,1)S(1)}, bf16[264,768]{1,0:T(8,128)(2,1)}, u32[]{:S(2)}) copy-start(bf16[264,768]{1,0:T(8,128)(2,1)} %copy-done.6) | copy-start | bytes 1216516
  43.5 1.1 %copy-start.17 = (bf16[8,768]{1,0:T(8,128)(2,1)S(1)}, bf16[8,768]{1,0:T(8,128)(2,1)}, u32[]{:S(2)}) copy-start(bf16[8,768]{1,0:T(8,128)(2,1)} %shard_map.118.meta_hbm.refs_9_.refs_21_) | copy-start | bytes 36868
  43.5 1.1 %copy-start.18 = (f32[66,16]{0,1:T(8,128)S(1)}, f32[66,16]{0,1:T(8,128)}, u32[]{:S(2)}) copy-start(f32[66,16]{0,1:T(8,128)} %param.23) | copy-start | bytes 12676
  44.6 2.7 %copy-start.9 = (bf16[768,768]{1,0:T(8,128)(2,1)S(1)}, bf16[768,768]{1,0:T(8,128)(2,1)}, u32[]{:S(2)}) copy-start(bf16[768,768]{1,0:T(8,128)(2,1)} %refs_23_.1) | copy-start | bytes 3538948
  44.6 2.7 %copy-start.15 = (bf16[16,8,768]{2,1,0:T(8,128)(2,1)S(1)}, bf16[16,8,768]{2,1,0:T(8,128)(2,1)}, u32[]{:S(2)}) copy-start(bf16[16,8,768]{2,1,0:T(8,128)(2,1)} %refs_22_.1) | copy-start | bytes 589828

commit v10 on v9

--- a/solution.py
+++ b/solution.py
@@ -52,43 +52,36 @@
     return jnp.dot(a, b, preferred_element_type=F32)
 
 
-def tags_body(chain_hbm, residue_hbm, valid_hbm, out_ref, ints_ref, sems):
-    copies = []
+def prep_body(
+    single_hbm, chain_hbm, residue_hbm, valid_hbm, wq_hbm, out_ref, meta_ref, q_ref,
+    single_ref, ints_ref, wq_ref, sems,
+):
+    copies = [pltpu.make_async_copy(single_hbm, single_ref, sems.at[0])]
     for i, ref in enumerate((chain_hbm, residue_hbm, valid_hbm)):
-        copies.append(pltpu.make_async_copy(ref, ints_ref.at[i], sems.at[i]))
-        copies[i].start()
-    tokens, width = ints_ref.shape[2], out_ref.shape[1]
+        copies.append(pltpu.make_async_copy(ref, ints_ref.at[i], sems.at[i + 1]))
+    weight = pltpu.make_async_copy(wq_hbm, wq_ref, sems.at[4])
+    for copy in (*copies, weight):
+        copy.start()
+    tokens, samples, width = single_ref.shape
+    rows = tokens * samples
     token = lax.broadcasted_iota(jnp.int32, (tokens, width), 0)
     lane = lax.broadcasted_iota(jnp.int32, (tokens, width), 1)
     spread = (lane % tokens == token).astype(F32).astype(BF16)
+    perm = sample_major(tokens, samples)
     for copy in copies:
         copy.wait()
+    data = matmul(perm, normed_rows(single_ref[...])).astype(BF16)
+    out_ref[pl.ds(0, rows), :] = data
     residue = ints_ref[1]
     row = lax.broadcasted_iota(jnp.int32, (META_ROWS, tokens), 0)
     meta = jnp.where(row == 0, ints_ref[0], 0)
     meta = jnp.where(row == 1, residue // RADIX, meta)
     meta = jnp.where(row == 2, residue % RADIX, meta)
     meta = jnp.where(row == 3, ints_ref[2], meta)
-    out_ref[...] = matmul(meta.astype(F32).astype(BF16), spread).astype(BF16)
-
-
-def prep_body(
-    single_hbm, meta_hbm, wq_hbm, out_ref, q_ref, single_ref, meta_ref, wq_ref, sems
-):
-    copies = []
-    moves = ((single_hbm, single_ref), (meta_hbm, meta_ref), (wq_hbm, wq_ref))
-    for i, (source, target) in enumerate(moves):
-        copies.append(pltpu.make_async_copy(source, target, sems.at[i]))
-        copies[i].start()
-    tokens, samples, _ = single_ref.shape
-    rows = tokens * samples
-    perm = sample_major(tokens, samples)
-    copies[0].wait()
-    data = matmul(perm, normed_rows(single_ref[...])).astype(BF16)
-    out_ref[pl.ds(0, rows), :] = data
-    copies[1].wait()
-    out_ref[pl.ds(rows, META_ROWS), :] = meta_ref[...]
-    copies[2].wait()
+    tiled = matmul(meta.astype(F32).astype(BF16), spread)
+    out_ref[pl.ds(rows, META_ROWS), :] = tiled.astype(BF16)
+    meta_ref[...] = tiled.astype(BF16)
+    weight.wait()
     q_ref[...] = matmul(data, wq_ref[...]).astype(BF16)
 
 
@@ -380,25 +373,20 @@
     cw = ring(single, 1)
     ccw = ring(single, -1)
     blocks = jax.ShapeDtypeStruct((rows + META_ROWS, width), BF16)
-    meta = call(
-        tags_body,
-        jax.ShapeDtypeStruct((META_ROWS, width), BF16),
-        tuple(v.reshape(1, tokens) for v in (chain, residue, valid)),
-        in_specs=[ANY] * 3,
-        scratch=[pltpu.VMEM((3, 1, tokens), jnp.int32), pltpu.SemaphoreType.DMA((3,))],
-        moved=2 * META_ROWS * width,
-        limit=FULL,
-    )
-    payload, query = call(
+    payload, meta, query = call(
         prep_body,
-        (blocks, jax.ShapeDtypeStruct((rows, width), BF16)),
-        (single, meta, w_query),
-        in_specs=[ANY] * 3,
+        (
+            blocks,
+            jax.ShapeDtypeStruct((META_ROWS, width), BF16),
+            jax.ShapeDtypeStruct((rows, width), BF16),
+        ),
+        (single, *(v.reshape(1, tokens) for v in (chain, residue, valid)), w_query),
+        in_specs=[ANY] * 5,
         scratch=[
             pltpu.VMEM(single.shape, BF16),
-            pltpu.VMEM(meta.shape, BF16),
+            pltpu.VMEM((3, 1, tokens), jnp.int32),
             pltpu.VMEM((width, width), BF16),
-            pltpu.SemaphoreType.DMA((3,)),
+            pltpu.SemaphoreType.DMA((5,)),
         ],
         flops=2 * rows * width * width,
         moved=6 * rows * width + 2 * width * width,

time: 53 us -> 49.1 us (0.926)
  local copies, waits for them, and re-layouts: 7.9 us -> 4.99 us
  waiting for transfers between devices: 10.4 us -> 12.4 us
  starting transfers between devices: 14.1 us -> 12.5 us
  Pallas kernels: 20.1 us -> 18.7 us
    unnamed x40 -> x32, local copies, waits for them, and re-layouts: 7.9 us -> 4.99 us
    ppermute x10, waiting for transfers between devices: 10.4 us -> 12.4 us  [ring(): return lax.ppermute(value, 'tok', pairs)]
    pallas_call x15 -> x14, Pallas kernels: 20.1 us -> 18.7 us  [call(): pl.pallas_call(body, out_shape=out_shape, in_specs=in_specs or [VMEM] * l...]
    ppermute x10, starting transfers between devices: 12.7 us -> 11.4 us  [ring(): return lax.ppermute(value, 'tok', pairs)]
  transfers between devices with their start and end apart: 16 -> 16, of which waited for: 4 -> 6; matrix products, arithmetic and copies ran while one was open for 0% -> 0% of each run, Pallas kernels for 28% -> 27%
where the time goes in v10:
time: 49.1 us; the launch traced here: 48.8 us
  Pallas kernels  18.7 us (38%)
  starting transfers between devices  12.5 us (25%)
  waiting for transfers between devices  12.4 us (25%)
  local copies, waits for them, and re-layouts  4.99 us (10%)
    pallas_call x14, Pallas kernels, call(): pl.pallas_call(body, out_shape=out_shape, in_specs=in_specs or [VMEM] * l...  18.7 us
    ppermute x10, waiting for transfers between devices, ring(): return lax.ppermute(value, 'tok', pairs)  12.4 us
    ppermute x10, starting transfers between devices, ring(): return lax.ppermute(value, 'tok', pairs)  11.4 us
    unnamed x32, local copies, waits for them, and re-layouts  4.99 us
    ppermute x6, starting transfers between devices, flip(): return lax.ppermute(value, 'tok', [(d, d ^ 1) for d in range(devices)])  1.14 us
  transfers between devices with their start and end apart: 16, of which 6 were waited for; matrix products, arithmetic and copies ran while one was open for 0% of the time, Pallas kernels for 27%

profile of v10, /device:TPU:0, one launch (start us, length us, event | category | flops | bytes accessed | tf_op | source)
XLA Modules:
  0.0 48.8 jit_solution(12904394868467362832)
XLA Ops:
  0.0 3.1 %collective-permute-start.1 = (bf16[16,8,768]{2,1,0:T(8,128)(2,1)}, bf16[16,8,768]{2,1,0:T(8,128)(2,1)S(1)}, u32[]{:S(2)}, u32[]{:S(2)}) collective-permute-start(bf16[16,8,768]{2,1,0:T(8,128)(2,1)} %refs_22_.1), channel_id=1, source_target_pairs={{0,4},{1,5},{4,8},{5,9},{8,12},{9,13},{12,14},{13,15},{14,10},{15,... | collective-permute-start | bytes 589832 | tf_op jit(solution)/shard_map/ppermute | solution.py:363
  3.1 0.0 collective-permute-start.3
  3.1 2.5 %shard_map.118 = (bf16[136,768]{1,0:T(8,128)(2,1)}, bf16[8,768]{1,0:T(8,128)(2,1)}, bf16[128,768]{1,0:T(8,128)(2,1)}) custom-call(bf16[16,8,768]{2,1,0:T(8,128)(2,1)} %refs_22_.1, s32[1,16]{1,0:T(1,128)} %bitcast.9, s32[1,16]{1,0:T(1,128)} %bitcast.10, s32[1,16]{1,0:T(1,128)} %bitcast.11, bf16[768,768]{1,0:T(8,128)(2,1)} %wq_hbm.1), custom_call_target="tpu_custom_call" | custom-call | flops 150994944 | bytes 1769472 | tf_op jit(solution)/shard_map/pallas_call | solution.py:333
  5.6 2.1 %collective-permute-start.2 = (bf16[8,768]{1,0:T(8,128)(2,1)}, bf16[8,768]{1,0:T(8,128)(2,1)S(1)}, u32[]{:S(2)}, u32[]{:S(2)}) collective-permute-start(bf16[8,768]{1,0:T(8,128)(2,1)} %get-tuple-element.14.refs_9_.refs_21_), channel_id=1, source_target_pairs={{0,4},{1,5},{4,8},{5,9},{8,12},{9,13},{12,14},{13,15},{14,10},{15,... | collective-permute-start | bytes 36872 | tf_op jit(solution)/shard_map/ppermute | solution.py:363
  7.6 0.0 collective-permute-start.4
  7.7 1.9 %collective-permute-done.2.meta_ref = bf16[8,768]{1,0:T(8,128)(2,1)S(1)} collective-permute-done((bf16[8,768]{1,0:T(8,128)(2,1)}, bf16[8,768]{1,0:T(8,128)(2,1)S(1)}, u32[]{:S(2)}, u32[]{:S(2)}) %collective-permute-start.2) | collective-permute-done | bytes 12320 | tf_op jit(solution)/shard_map/ppermute | solution.py:363
  9.5 0.4 shard_map.120.refs_0_
  9.9 2.1 %collective-permute-start.6 = (bf16[136,768]{1,0:T(8,128)(2,1)S(1)}, bf16[136,768]{1,0:T(8,128)(2,1)S(1)}, u32[]{:S(2)}, u32[]{:S(2)}) collective-permute-start(bf16[136,768]{1,0:T(8,128)(2,1)S(1)} %shard_map.120.refs_0_), channel_id=1, source_target_pairs={{0,4},{1,5},{4,8},{5,9},{8,12},{9,13},{12,14},{13,15},{14,10},{15,... | collective-permute-start | bytes 626696 | tf_op jit(solution)/shard_map/ppermute | solution.py:363
  12.0 0.0 collective-permute-done.4.meta_ref
  12.0 0.0 collective-permute-done.3.single_ref
  12.0 0.4 shard_map.121.refs_1_
  12.4 0.1 collective-permute-start.7
  12.5 3.4 %collective-permute-done.6.refs_0_ = bf16[136,768]{1,0:T(8,128)(2,1)S(1)} collective-permute-done((bf16[136,768]{1,0:T(8,128)(2,1)S(1)}, bf16[136,768]{1,0:T(8,128)(2,1)S(1)}, u32[]{:S(2)}, u32[]{:S(2)}) %collective-permute-start.6) | collective-permute-done | bytes 208928 | tf_op jit(solution)/shard_map/ppermute | solution.py:363
  15.9 1.9 %collective-permute-start.9 = (bf16[136,768]{1,0:T(8,128)(2,1)S(1)}, bf16[136,768]{1,0:T(8,128)(2,1)S(1)}, u32[]{:S(2)}, u32[]{:S(2)}) collective-permute-start(bf16[136,768]{1,0:T(8,128)(2,1)S(1)} %collective-permute-done.6.refs_0_), channel_id=1, source_target_pairs={{0,4},{1,5},{4,8},{5,9},{8,12},{9,13},{12,14},{13,15},{14,10},{15,... | collective-permute-start | bytes 626696 | tf_op jit(solution)/shard_map/ppermute | solution.py:363
  17.8 0.5 collective-permute-done.7.refs_1_
  18.3 0.0 collective-permute-start.10
  18.3 1.3 %copy-done.1 = bf16[768,768]{1,0:T(8,128)(2,1)S(1)} copy-done((bf16[768,768]{1,0:T(8,128)(2,1)S(1)}, bf16[768,768]{1,0:T(8,128)(2,1)}, u32[]{:S(2)}) %copy-start.1) | copy-done | bytes 1179672
  19.6 0.8 %shard_map.122.refs_2_ = bf16[528,768]{1,0:T(8,128)(2,1)S(1)} custom-call(bf16[136,768]{1,0:T(8,128)(2,1)S(1)} %shard_map.120.refs_0_, bf16[136,768]{1,0:T(8,128)(2,1)S(1)} %shard_map.121.refs_1_, bf16[768,768]{1,0:T(8,128)(2,1)S(1)} %copy-done, bf16[768,768]{1,0:T(8,128)(2,1)S(1)} %copy-done.1), custom_call_target="tpu_custom_call" | custom-call | flops 603979776 | bytes 3538944 | tf_op jit(solution)/shard_map/pallas_call | solution.py:333
  20.4 0.1 collective-permute-start.5
  20.4 1.7 %shard_map.123.refs_4_ = bf16[528,768]{1,0:T(8,128)(2,1)} custom-call(bf16[136,768]{1,0:T(8,128)(2,1)S(1)} %collective-permute-done.6.refs_0_, bf16[136,768]{1,0:T(8,128)(2,1)S(1)} %collective-permute-done.7.refs_1_, bf16[768,768]{1,0:T(8,128)(2,1)S(1)} %copy-done, bf16[768,768]{1,0:T(8,128)(2,1)S(1)} %copy-done.1), custom_call_target="tpu_custom_call" | custom-call | flops 603979776 | bytes 3538944 | tf_op jit(solution)/shard_map/pallas_call | solution.py:333
  22.1 0.5 %collective-permute-start.8 = (bf16[528,768]{1,0:T(8,128)(2,1)}, bf16[528,768]{1,0:T(8,128)(2,1)}, u32[]{:S(2)}, u32[]{:S(2)}) collective-permute-start(bf16[528,768]{1,0:T(8,128)(2,1)} %shard_map.123.refs_4_), channel_id=1, source_target_pairs={{0,1},{1,0},{2,3},{3,2},{4,5},{5,4},{6,7},{7,6},{8,9},{9,8},{10,11... | collective-permute-start | bytes 2433032 | tf_op jit(solution)/shard_map/ppermute | solution.py:366
  22.6 0.0 collective-permute-done.9.refs_0_.in_ref
  22.6 1.5 %collective-permute-done.10.refs_1_.in_ref = bf16[136,768]{1,0:T(8,128)(2,1)S(1)} collective-permute-done((bf16[136,768]{1,0:T(8,128)(2,1)S(1)}, bf16[136,768]{1,0:T(8,128)(2,1)S(1)}, u32[]{:S(2)}, u32[]{:S(2)}) %collective-permute-start.10) | collective-permute-done | bytes 208928 | tf_op jit(solution)/shard_map/ppermute | solution.py:363
  24.1 1.7 %shard_map.124.refs_6_ = bf16[528,768]{1,0:T(8,128)(2,1)} custom-call(bf16[136,768]{1,0:T(8,128)(2,1)S(1)} %collective-permute-done.9.refs_0_.in_ref, bf16[136,768]{1,0:T(8,128)(2,1)S(1)} %collective-permute-done.10.refs_1_.in_ref, bf16[768,768]{1,0:T(8,128)(2,1)S(1)} %copy-done, bf16[768,768]{1,0:T(8,128)(2,1)S(1)} %copy-done.1), custom_call_target="tpu_custom_call" | custom-call | flops 603979776 | bytes 3538944 | tf_op jit(solution)/shard_map/pallas_call | solution.py:333
  25.8 0.5 %shard_map.119.refs_0_ = bf16[264,768]{1,0:T(8,128)(2,1)S(1)} custom-call(bf16[136,768]{1,0:T(8,128)(2,1)S(1)} %copy-done.10, bf16[768,768]{1,0:T(8,128)(2,1)S(1)} %copy-done, bf16[768,768]{1,0:T(8,128)(2,1)S(1)} %copy-done.2), custom_call_target="tpu_custom_call" | custom-call | flops 301989888 | bytes 2949120 | tf_op jit(solution)/shard_map/pallas_call | solution.py:333
  26.3 0.0 copy-start.15
  26.3 0.6 %collective-permute-start = (bf16[264,768]{1,0:T(8,128)(2,1)S(1)}, bf16[264,768]{1,0:T(8,128)(2,1)S(1)}, u32[]{:S(2)}, u32[]{:S(2)}) collective-permute-start(bf16[264,768]{1,0:T(8,128)(2,1)S(1)} %shard_map.119.refs_0_), channel_id=1, source_target_pairs={{0,1},{1,0},{2,3},{3,2},{4,5},{5,4},{6,7},{7,6},{8,9},{9,8},{10,11... | collective-permute-start | bytes 1216520 | tf_op jit(solution)/shard_map/ppermute | solution.py:366
  26.9 0.8 %copy-done.3 = bf16[264,768]{1,0:T(8,128)(2,1)} copy-done((bf16[264,768]{1,0:T(8,128)(2,1)}, bf16[264,768]{1,0:T(8,128)(2,1)S(1)}, u32[]{:S(2)}) %copy-start.3) | copy-done | bytes 405528
  27.7 1.6 %collective-permute-start.12 = (bf16[104,768]{1,0:T(8,128)(2,1)S(1)}, bf16[104,768]{1,0:T(8,128)(2,1)S(1)}, u32[]{:S(2)}, u32[]{:S(2)}) collective-permute-start(bf16[104,768]{1,0:T(8,128)(2,1)S(1)} %shard_map.125), channel_id=1, source_target_pairs={{0,4},{1,5},{4,8},{5,9},{8,12},{9,13},{12,14},{13,15},{14,10},{15,... | collective-permute-start | bytes 479240 | tf_op jit(solution)/shard_map/ppermute | solution.py:363
  29.3 4.5 %collective-permute-done.12.refs_8_ = bf16[104,768]{1,0:T(8,128)(2,1)S(1)} collective-permute-done((bf16[104,768]{1,0:T(8,128)(2,1)S(1)}, bf16[104,768]{1,0:T(8,128)(2,1)S(1)}, u32[]{:S(2)}, u32[]{:S(2)}) %collective-permute-start.12) | collective-permute-done | bytes 159776 | tf_op jit(solution)/shard_map/ppermute | solution.py:363
  33.7 0.6 %shard_map.126 = bf16[32,768]{1,0:T(8,128)(2,1)} custom-call(bf16[136,768]{1,0:T(8,128)(2,1)S(1)} %collective-permute-done.10.refs_1_.in_ref), custom_call_target="tpu_custom_call" | custom-call | bytes 196608 | tf_op jit(solution)/shard_map/pallas_call | solution.py:333
  34.4 0.0 collective-permute-done.refs_1_
  34.4 0.8 %copy-done.5 = bf16[264,768]{1,0:T(8,128)(2,1)} copy-done((bf16[264,768]{1,0:T(8,128)(2,1)}, bf16[264,768]{1,0:T(8,128)(2,1)S(1)}, u32[]{:S(2)}) %copy-start.5) | copy-done | bytes 405528
  35.1 0.5 %collective-permute-start.13 = (bf16[32,768]{1,0:T(8,128)(2,1)}, bf16[32,768]{1,0:T(8,128)(2,1)}, u32[]{:S(2)}, u32[]{:S(2)}) collective-permute-start(bf16[32,768]{1,0:T(8,128)(2,1)} %shard_map.126), channel_id=1, source_target_pairs={{0,2},{1,3},{4,0},{5,1},{8,4},{9,5},{12,8},{13,9},{14,12},{15,13},... | collective-permute-start | bytes 147464 | tf_op jit(solution)/shard_map/ppermute | solution.py:363
  35.6 1.3 %copy-done.7 = bf16[768,768]{1,0:T(8,128)(2,1)S(1)} copy-done((bf16[768,768]{1,0:T(8,128)(2,1)S(1)}, bf16[768,768]{1,0:T(8,128)(2,1)}, u32[]{:S(2)}) %copy-start.7) | copy-done | bytes 1179672
  36.9 0.3 shard_map.128.refs_13_
  37.3 0.9 %copy-done.9 = bf16[16,256,128]{2,1,0:T(8,128)(2,1)S(1)} copy-done((bf16[16,256,128]{2,1,0:T(8,128)(2,1)S(1)}, bf16[16,256,128]{2,1,0:T(8,128)(2,1)}, u32[]{:S(2)}) %copy-start.9) | copy-done | bytes 1048600
  38.1 0.7 %shard_map.129 = (f32[160,256]{1,0:T(8,128)S(1)}, f32[96,256]{1,0:T(8,128)S(1)}) custom-call(s32[1]{0:T(128)} %bitcast.3.me_ref, bf16[16,256,128]{2,1,0:T(8,128)(2,1)S(1)} %copy-done.9, bf16[16,128]{1,0:T(8,128)(2,1)S(1)} %bitcast.8), custom_call_target="tpu_custom_call" | custom-call | flops 268435456 | bytes 1310720 | tf_op jit(solution)/shard_map/pallas_call | solution.py:333
  38.8 0.8 %collective-permute-done.13.refs_9_ = bf16[32,768]{1,0:T(8,128)(2,1)} collective-permute-done((bf16[32,768]{1,0:T(8,128)(2,1)}, bf16[32,768]{1,0:T(8,128)(2,1)}, u32[]{:S(2)}, u32[]{:S(2)}) %collective-permute-start.13) | collective-permute-done | bytes 49184 | tf_op jit(solution)/shard_map/ppermute | solution.py:363
  39.6 0.0 copy-start.14
  39.6 1.0 %shard_map.127.refs_6_.refs_12_ = bf16[6144,256]{1,0:T(8,128)(2,1)S(1)} custom-call(s32[1]{0:T(128)} %bitcast.3.me_ref, bf16[128,768]{1,0:T(8,128)(2,1)S(1)} %copy-done.12), custom_call_target="tpu_custom_call" | custom-call | flops 50331648 | bytes 3145728 | tf_op jit(solution)/shard_map/pallas_call | solution.py:333
  40.7 0.0 collective-permute-done.5.refs_3_
  40.7 0.0 copy-done.6
  40.7 0.0 copy-start.8
  40.8 0.0 copy-start.11
  40.8 2.6 %shard_map.130 = (f32[1280,256]{1,0:T(8,128)S(1)}, f32[8,256]{1,0:T(8,128)S(1)}, f32[8,256]{1,0:T(8,128)S(1)}) custom-call(bf16[264,768]{1,0:T(8,128)(2,1)S(1)} %copy-done.4, bf16[264,768]{1,0:T(8,128)(2,1)S(1)} %copy-done.6, bf16[528,768]{1,0:T(8,128)(2,1)S(1)} %shard_map.122.refs_2_, bf16[528,768]{1,0:T(8,128)(2,1)} %collective-permute-done.5.refs_3_, ...), custom_call_target="tpu_custom_call" | custom-call | flops 503316480 | bytes 5898240 | tf_op jit(solution)/shard_map/pallas_call | solution.py:333
  43.4 0.0 collective-permute-done.15.refs_11_
  43.4 5.4 %shard_map.131 = bf16[16,8,768]{2,1,0:T(8,128)(2,1)} custom-call(bf16[264,768]{1,0:T(8,128)(2,1)S(1)} %copy-done.4, bf16[264,768]{1,0:T(8,128)(2,1)S(1)} %copy-done.6, bf16[528,768]{1,0:T(8,128)(2,1)S(1)} %shard_map.122.refs_2_, bf16[528,768]{1,0:T(8,128)(2,1)} %collective-permute-done.5.refs_3_, bf16[528,768]{1,0:T(8,128)(2,1)} %shard_map.123.refs_4_, ...), custom_call_target="tpu_custom_call" | custom-call | flops 100663296 | bytes 3145728 | tf_op jit(solution)/shard_map/pallas_call | solution.py:333
  (30 shorter events, 0.1 us)
Async XLA Ops:
  0.0 18.3 %copy-start = (bf16[768,768]{1,0:T(8,128)(2,1)S(1)}, bf16[768,768]{1,0:T(8,128)(2,1)}, u32[]{:S(2)}) copy-start(bf16[768,768]{1,0:T(8,128)(2,1)} %refs_17_.1) | copy-start | bytes 3538948
  0.0 9.5 %collective-permute-start.1 = (bf16[16,8,768]{2,1,0:T(8,128)(2,1)}, bf16[16,8,768]{2,1,0:T(8,128)(2,1)S(1)}, u32[]{:S(2)}, u32[]{:S(2)}) collective-permute-start(bf16[16,8,768]{2,1,0:T(8,128)(2,1)} %refs_22_.1), channel_id=1, source_target_pairs={{0,4},{1,5},{4,8},{5,9},{8,12},{9,13},{12,14},{13,15},{14,10},{15,... | collective-permute-start | bytes 589832 | tf_op jit(solution)/shard_map/ppermute | solution.py:363
  3.1 9.0 %collective-permute-start.3 = (bf16[16,8,768]{2,1,0:T(8,128)(2,1)}, bf16[16,8,768]{2,1,0:T(8,128)(2,1)S(1)}, u32[]{:S(2)}, u32[]{:S(2)}) collective-permute-start(bf16[16,8,768]{2,1,0:T(8,128)(2,1)} %refs_22_.1), channel_id=1, source_target_pairs={{0,2},{1,3},{4,0},{5,1},{8,4},{9,5},{12,8},{13,9},{14,12},{15,13},... | collective-permute-start | bytes 589832 | tf_op jit(solution)/shard_map/ppermute | solution.py:363
  5.6 4.0 %collective-permute-start.2 = (bf16[8,768]{1,0:T(8,128)(2,1)}, bf16[8,768]{1,0:T(8,128)(2,1)S(1)}, u32[]{:S(2)}, u32[]{:S(2)}) collective-permute-start(bf16[8,768]{1,0:T(8,128)(2,1)} %get-tuple-element.14.refs_9_.refs_21_), channel_id=1, source_target_pairs={{0,4},{1,5},{4,8},{5,9},{8,12},{9,13},{12,14},{13,15},{14,10},{15,... | collective-permute-start | bytes 36872 | tf_op jit(solution)/shard_map/ppermute | solution.py:363
  7.6 4.4 %collective-permute-start.4 = (bf16[8,768]{1,0:T(8,128)(2,1)}, bf16[8,768]{1,0:T(8,128)(2,1)S(1)}, u32[]{:S(2)}, u32[]{:S(2)}) collective-permute-start(bf16[8,768]{1,0:T(8,128)(2,1)} %get-tuple-element.14.refs_9_.refs_21_), channel_id=1, source_target_pairs={{0,2},{1,3},{4,0},{5,1},{8,4},{9,5},{12,8},{13,9},{14,12},{15,13},... | collective-permute-start | bytes 36872 | tf_op jit(solution)/shard_map/ppermute | solution.py:363
  9.9 5.9 %collective-permute-start.6 = (bf16[136,768]{1,0:T(8,128)(2,1)S(1)}, bf16[136,768]{1,0:T(8,128)(2,1)S(1)}, u32[]{:S(2)}, u32[]{:S(2)}) collective-permute-start(bf16[136,768]{1,0:T(8,128)(2,1)S(1)} %shard_map.120.refs_0_), channel_id=1, source_target_pairs={{0,4},{1,5},{4,8},{5,9},{8,12},{9,13},{12,14},{13,15},{14,10},{15,... | collective-permute-start | bytes 626696 | tf_op jit(solution)/shard_map/ppermute | solution.py:363
  12.4 5.9 %collective-permute-start.7 = (bf16[136,768]{1,0:T(8,128)(2,1)S(1)}, bf16[136,768]{1,0:T(8,128)(2,1)S(1)}, u32[]{:S(2)}, u32[]{:S(2)}) collective-permute-start(bf16[136,768]{1,0:T(8,128)(2,1)S(1)} %shard_map.121.refs_1_), channel_id=1, source_target_pairs={{0,2},{1,3},{4,0},{5,1},{8,4},{9,5},{12,8},{13,9},{14,12},{15,13},... | collective-permute-start | bytes 626696 | tf_op jit(solution)/shard_map/ppermute | solution.py:363
  15.9 6.7 %collective-permute-start.9 = (bf16[136,768]{1,0:T(8,128)(2,1)S(1)}, bf16[136,768]{1,0:T(8,128)(2,1)S(1)}, u32[]{:S(2)}, u32[]{:S(2)}) collective-permute-start(bf16[136,768]{1,0:T(8,128)(2,1)S(1)} %collective-permute-done.6.refs_0_), channel_id=1, source_target_pairs={{0,4},{1,5},{4,8},{5,9},{8,12},{9,13},{12,14},{13,15},{14,10},{15,... | collective-permute-start | bytes 626696 | tf_op jit(solution)/shard_map/ppermute | solution.py:363
  18.3 5.8 %collective-permute-start.10 = (bf16[136,768]{1,0:T(8,128)(2,1)S(1)}, bf16[136,768]{1,0:T(8,128)(2,1)S(1)}, u32[]{:S(2)}, u32[]{:S(2)}) collective-permute-start(bf16[136,768]{1,0:T(8,128)(2,1)S(1)} %collective-permute-done.7.refs_1_), channel_id=1, source_target_pairs={{0,2},{1,3},{4,0},{5,1},{8,4},{9,5},{12,8},{13,9},{14,12},{15,13},... | collective-permute-start | bytes 626696 | tf_op jit(solution)/shard_map/ppermute | solution.py:363
  18.3 1.3 %copy-start.1 = (bf16[768,768]{1,0:T(8,128)(2,1)S(1)}, bf16[768,768]{1,0:T(8,128)(2,1)}, u32[]{:S(2)}) copy-start(bf16[768,768]{1,0:T(8,128)(2,1)} %refs_18_.1) | copy-start | bytes 3538948
  20.4 20.3 %collective-permute-start.5 = (bf16[528,768]{1,0:T(8,128)(2,1)S(1)}, bf16[528,768]{1,0:T(8,128)(2,1)}, u32[]{:S(2)}, u32[]{:S(2)}) collective-permute-start(bf16[528,768]{1,0:T(8,128)(2,1)S(1)} %shard_map.122.refs_2_), channel_id=1, source_target_pairs={{0,1},{1,0},{2,3},{3,2},{4,5},{5,4},{6,7},{7,6},{8,9},{9,8},{10,11... | collective-permute-start | bytes 2433032 | tf_op jit(solution)/shard_map/ppermute | solution.py:366
  22.1 3.7 %copy-start.2 = (bf16[768,768]{1,0:T(8,128)(2,1)S(1)}, bf16[768,768]{1,0:T(8,128)(2,1)}, u32[]{:S(2)}) copy-start(bf16[768,768]{1,0:T(8,128)(2,1)} %refs_18_.1) | copy-start | bytes 3538948
  22.1 3.7 %copy-start.10 = (bf16[136,768]{1,0:T(8,128)(2,1)S(1)}, bf16[136,768]{1,0:T(8,128)(2,1)}, u32[]{:S(2)}) copy-start(bf16[136,768]{1,0:T(8,128)(2,1)} %get-tuple-element.13.refs_0_.pay_ref) | copy-start | bytes 626692
  22.1 18.6 %collective-permute-start.8 = (bf16[528,768]{1,0:T(8,128)(2,1)}, bf16[528,768]{1,0:T(8,128)(2,1)}, u32[]{:S(2)}, u32[]{:S(2)}) collective-permute-start(bf16[528,768]{1,0:T(8,128)(2,1)} %shard_map.123.refs_4_), channel_id=1, source_target_pairs={{0,1},{1,0},{2,3},{3,2},{4,5},{5,4},{6,7},{7,6},{8,9},{9,8},{10,11... | collective-permute-start | bytes 2433032 | tf_op jit(solution)/shard_map/ppermute | solution.py:366
  25.8 17.6 %collective-permute-start.11 = (bf16[528,768]{1,0:T(8,128)(2,1)}, bf16[528,768]{1,0:T(8,128)(2,1)}, u32[]{:S(2)}, u32[]{:S(2)}) collective-permute-start(bf16[528,768]{1,0:T(8,128)(2,1)} %shard_map.124.refs_6_), channel_id=1, source_target_pairs={{0,1},{1,0},{2,3},{3,2},{4,5},{5,4},{6,7},{7,6},{8,9},{9,8},{10,11... | collective-permute-start | bytes 2433032 | tf_op jit(solution)/shard_map/ppermute | solution.py:366
  26.3 11.0 %copy-start.15 = (bf16[128,16]{0,1:T(8,128)(2,1)S(1)}, bf16[128,16]{0,1:T(8,128)(2,1)}, u32[]{:S(2)}) copy-start(bf16[128,16]{0,1:T(8,128)(2,1)} %param.22) | copy-start | bytes 12292
  26.3 8.1 %collective-permute-start = (bf16[264,768]{1,0:T(8,128)(2,1)S(1)}, bf16[264,768]{1,0:T(8,128)(2,1)S(1)}, u32[]{:S(2)}, u32[]{:S(2)}) collective-permute-start(bf16[264,768]{1,0:T(8,128)(2,1)S(1)} %shard_map.119.refs_0_), channel_id=1, source_target_pairs={{0,1},{1,0},{2,3},{3,2},{4,5},{5,4},{6,7},{7,6},{8,9},{9,8},{10,11... | collective-permute-start | bytes 1216520 | tf_op jit(solution)/shard_map/ppermute | solution.py:366
  26.9 0.8 %copy-start.3 = (bf16[264,768]{1,0:T(8,128)(2,1)}, bf16[264,768]{1,0:T(8,128)(2,1)S(1)}, u32[]{:S(2)}) copy-start(bf16[264,768]{1,0:T(8,128)(2,1)S(1)} %shard_map.119.refs_0_) | copy-start | bytes 1216516
  27.7 6.1 %collective-permute-start.12 = (bf16[104,768]{1,0:T(8,128)(2,1)S(1)}, bf16[104,768]{1,0:T(8,128)(2,1)S(1)}, u32[]{:S(2)}, u32[]{:S(2)}) collective-permute-start(bf16[104,768]{1,0:T(8,128)(2,1)S(1)} %shard_map.125), channel_id=1, source_target_pairs={{0,4},{1,5},{4,8},{5,9},{8,12},{9,13},{12,14},{13,15},{14,10},{15,... | collective-permute-start | bytes 479240 | tf_op jit(solution)/shard_map/ppermute | solution.py:363
  33.7 9.7 %collective-permute-start.14 = (bf16[104,768]{1,0:T(8,128)(2,1)S(1)}, bf16[104,768]{1,0:T(8,128)(2,1)}, u32[]{:S(2)}, u32[]{:S(2)}) collective-permute-start(bf16[104,768]{1,0:T(8,128)(2,1)S(1)} %collective-permute-done.12.refs_8_), channel_id=1, source_target_pairs={{0,1},{1,0},{2,3},{3,2},{4,5},{5,4},{6,7},{7,6},{8,9},{9,8},{10,11... | collective-permute-start | bytes 479240 | tf_op jit(solution)/shard_map/ppermute | solution.py:366
  34.4 0.8 %copy-start.5 = (bf16[264,768]{1,0:T(8,128)(2,1)}, bf16[264,768]{1,0:T(8,128)(2,1)S(1)}, u32[]{:S(2)}) copy-start(bf16[264,768]{1,0:T(8,128)(2,1)S(1)} %collective-permute-done.refs_1_) | copy-start | bytes 1216516
  35.1 4.5 %collective-permute-start.13 = (bf16[32,768]{1,0:T(8,128)(2,1)}, bf16[32,768]{1,0:T(8,128)(2,1)}, u32[]{:S(2)}, u32[]{:S(2)}) collective-permute-start(bf16[32,768]{1,0:T(8,128)(2,1)} %shard_map.126), channel_id=1, source_target_pairs={{0,2},{1,3},{4,0},{5,1},{8,4},{9,5},{12,8},{13,9},{14,12},{15,13},... | collective-permute-start | bytes 147464 | tf_op jit(solution)/shard_map/ppermute | solution.py:363
  35.6 1.3 %copy-start.7 = (bf16[768,768]{1,0:T(8,128)(2,1)S(1)}, bf16[768,768]{1,0:T(8,128)(2,1)}, u32[]{:S(2)}) copy-start(bf16[768,768]{1,0:T(8,128)(2,1)} %wg_ref.1) | copy-start | bytes 3538948
  36.9 1.2 %copy-start.9 = (bf16[16,256,128]{2,1,0:T(8,128)(2,1)S(1)}, bf16[16,256,128]{2,1,0:T(8,128)(2,1)}, u32[]{:S(2)}) copy-start(bf16[16,256,128]{2,1,0:T(8,128)(2,1)} %pair_ref.1) | copy-start | bytes 3145732
  36.9 2.7 %copy-start.12 = (bf16[128,768]{1,0:T(8,128)(2,1)S(1)}, bf16[128,768]{1,0:T(8,128)(2,1)}, u32[]{:S(2)}) copy-start(bf16[128,768]{1,0:T(8,128)(2,1)} %get-tuple-element.15.q_ref) | copy-start | bytes 589828
  39.6 3.8 %collective-permute-start.15 = (bf16[32,768]{1,0:T(8,128)(2,1)}, bf16[32,768]{1,0:T(8,128)(2,1)S(1)}, u32[]{:S(2)}, u32[]{:S(2)}) collective-permute-start(bf16[32,768]{1,0:T(8,128)(2,1)} %collective-permute-done.13.refs_9_), channel_id=1, source_target_pairs={{0,1},{1,0},{2,3},{3,2},{4,5},{5,4},{6,7},{7,6},{8,9},{9,8},{10,11... | collective-permute-start | bytes 147464 | tf_op jit(solution)/shard_map/ppermute | solution.py:366
  39.6 1.1 %copy-start.4 = (bf16[264,768]{1,0:T(8,128)(2,1)S(1)}, bf16[264,768]{1,0:T(8,128)(2,1)}, u32[]{:S(2)}) copy-start(bf16[264,768]{1,0:T(8,128)(2,1)} %copy-done.3) | copy-start | bytes 1216516
  39.6 1.1 %copy-start.6 = (bf16[264,768]{1,0:T(8,128)(2,1)S(1)}, bf16[264,768]{1,0:T(8,128)(2,1)}, u32[]{:S(2)}) copy-start(bf16[264,768]{1,0:T(8,128)(2,1)} %copy-done.5) | copy-start | bytes 1216516
  39.6 1.1 %copy-start.13 = (bf16[8,768]{1,0:T(8,128)(2,1)S(1)}, bf16[8,768]{1,0:T(8,128)(2,1)}, u32[]{:S(2)}) copy-start(bf16[8,768]{1,0:T(8,128)(2,1)} %get-tuple-element.14.refs_9_.refs_21_) | copy-start | bytes 36868
  39.6 1.1 %copy-start.14 = (f32[66,16]{0,1:T(8,128)S(1)}, f32[66,16]{0,1:T(8,128)}, u32[]{:S(2)}) copy-start(f32[66,16]{0,1:T(8,128)} %param.23) | copy-start | bytes 12676
  40.7 2.7 %copy-start.8 = (bf16[768,768]{1,0:T(8,128)(2,1)S(1)}, bf16[768,768]{1,0:T(8,128)(2,1)}, u32[]{:S(2)}) copy-start(bf16[768,768]{1,0:T(8,128)(2,1)} %refs_23_.1) | copy-start | bytes 3538948
  40.8 2.7 %copy-start.11 = (bf16[16,8,768]{2,1,0:T(8,128)(2,1)S(1)}, bf16[16,8,768]{2,1,0:T(8,128)(2,1)}, u32[]{:S(2)}) copy-start(bf16[16,8,768]{2,1,0:T(8,128)(2,1)} %refs_22_.1) | copy-start | bytes 589828

commit v11 on v10

--- a/solution.py
+++ b/solution.py
@@ -270,19 +270,26 @@
         exp_ref[pl.ds(s * count, count), :] = weights
 
 
+def last_body(first_ref, second_ref, wk_ref, wv_ref, out_ref):
+    rows = out_ref.shape[0] // 2
+    share = rows - second_ref.shape[0]
+    data = jnp.concatenate([first_ref[pl.ds(0, share), :], second_ref[...]], axis=0)
+    out_ref[pl.ds(0, rows), :] = matmul(data, wk_ref[...]).astype(BF16)
+    out_ref[pl.ds(rows, rows), :] = matmul(data, wv_ref[...]).astype(BF16)
+
+
 def finish_body(heads, scale, split, *refs):
     (
         q_ref, gate_ref, exp_ref, top_ref, mass_ref, wk_ref, wv_ref, pair_ref, tab_ref, own_ref,
         single_ref, wo_ref, out_ref, pad_ref, weight_ref,
     ) = refs[-15:]
-    kv_refs, lasts = refs[:-19], refs[-19:-15]
+    kv_refs, lasts, mine_ref = refs[:-19], refs[-19:-16], refs[-16]
     tokens, samples, width = single_ref.shape
     rows = tokens * samples
     hs = width // heads
     share = lasts[0].shape[0] - META_ROWS
-    metas = kv_metas(kv_refs[split:], rows) + [r[pl.ds(share, META_ROWS), :] for r in (lasts[0], lasts[2])]
-    sizes = (share, rows - share) * 2
-    data = jnp.concatenate([r[pl.ds(0, n), :] for r, n in zip(lasts, sizes)], axis=0)
+    metas = kv_metas(kv_refs[split:], rows) + [r[pl.ds(share, META_ROWS), :] for r in lasts[:2]]
+    data = jnp.concatenate([lasts[1][pl.ds(0, share), :], lasts[2][...]], axis=0)
     k_last = matmul(data, wk_ref[...]).astype(BF16)
     v_last = matmul(data, wv_ref[...]).astype(BF16)
     bias = full_bias(own_ref[...], metas, tokens, pair_ref, tab_ref, pad_ref)
@@ -290,9 +297,9 @@
     lane_head = lax.broadcasted_iota(jnp.int32, (tokens, width), 1) // hs
     lines = heads * tokens
     for s in range(samples):
-        new = [slice(u * rows + s * tokens, u * rows + (s + 1) * tokens) for u in range(2)]
+        new = slice(s * tokens, (s + 1) * tokens)
         keys = gather(kv_refs[split:], rows, s * tokens, tokens, False)
-        keys = jnp.concatenate(keys + [k_last[n] for n in new], axis=0)
+        keys = jnp.concatenate(keys + [mine_ref[pl.ds(s * tokens, tokens), :], k_last[new]], axis=0)
         scores = matmul(keys, q_ref[pl.ds(s * width, width), :]) * scale + bias
         before = top_ref[pl.ds(s, 1), :]
         top = jnp.maximum(jnp.max(scores, axis=0, keepdims=True), before)
@@ -305,9 +312,9 @@
         weight_ref[pl.ds(s * lines, lines), :] = jnp.transpose(weights).astype(BF16)
     gated = []
     for s in range(samples):
-        new = [slice(u * rows + s * tokens, u * rows + (s + 1) * tokens) for u in range(2)]
+        new = slice(s * tokens, (s + 1) * tokens)
         values = gather(kv_refs, rows, s * tokens, tokens, True)
-        values = jnp.concatenate(values + [v_last[n] for n in new], axis=0)
+        values = jnp.concatenate(values + [mine_ref[pl.ds(rows + s * tokens, tokens), :], v_last[new]], axis=0)
         pieces = {}
         for h0, h1, start in head_windows(width, hs):
             here = pl.ds(s * lines + h0 * tokens, (h1 + 1 - h0) * tokens)
@@ -479,11 +486,18 @@
         scratch=pad,
     )
     cw_other, ccw_other = flip(cw), flip(ccw)
+    mine = call(
+        last_body,
+        jax.ShapeDtypeStruct((2 * rows, width), BF16),
+        (cw, ccw, w_key, w_value),
+        flops=4 * rows * width * width,
+        moved=4 * width * width + 6 * rows * width,
+    )
     return call(
         functools.partial(finish_body, heads, scale, split),
         jax.ShapeDtypeStruct(single.shape, BF16),
         (
-            *kvs, cw, ccw, cw_other, ccw_other, query, gate, *first, w_key, w_value,
+            *kvs, cw, cw_other, ccw_other, mine, query, gate, *first, w_key, w_value,
             pair_bias[1], table, meta, single, w_out,
         ),
         flops=4 * rows * total * width,

time: 49.1 us -> 49.5 us (level)
  Pallas kernels: 18.7 us -> 19.6 us
  waiting for transfers between devices: 12.4 us -> 11.7 us
    pallas_call x14 -> x15, Pallas kernels: 18.7 us -> 19.6 us  [call(): pl.pallas_call(body, out_shape=out_shape, in_specs=in_specs or [VMEM] * l...]
    ppermute x10, waiting for transfers between devices: 12.4 us -> 11.6 us  [ring(): return lax.ppermute(value, 'tok', pairs)]
  transfers between devices with their start and end apart: 16 -> 16, of which waited for: 6 -> 5; matrix products, arithmetic and copies ran while one was open for 0% -> 0% of each run, Pallas kernels for 27% -> 30%
where the time goes in v11:
time: 49.5 us; the launch traced here: 49.2 us
  Pallas kernels  19.6 us (40%)
  starting transfers between devices  12.8 us (26%)
  waiting for transfers between devices  11.7 us (24%)
  local copies, waits for them, and re-layouts  4.87 us (10%)
    pallas_call x15, Pallas kernels, call(): pl.pallas_call(body, out_shape=out_shape, in_specs=in_specs or [VMEM] * l...  19.6 us
    ppermute x10, waiting for transfers between devices, ring(): return lax.ppermute(value, 'tok', pairs)  11.6 us
    ppermute x10, starting transfers between devices, ring(): return lax.ppermute(value, 'tok', pairs)  11.4 us
    unnamed x32, local copies, waits for them, and re-layouts  4.87 us
    ppermute x6, starting transfers between devices, flip(): return lax.ppermute(value, 'tok', [(d, d ^ 1) for d in range(devices)])  1.44 us
  transfers between devices with their start and end apart: 16, of which 5 were waited for; matrix products, arithmetic and copies ran while one was open for 0% of the time, Pallas kernels for 30%

profile of v11, /device:TPU:0, one launch (start us, length us, event | category | flops | bytes accessed | tf_op | source)
XLA Modules:
  0.0 49.2 jit_solution(7509545004362042618)
XLA Ops:
  0.0 3.1 %collective-permute-start.1 = (bf16[16,8,768]{2,1,0:T(8,128)(2,1)}, bf16[16,8,768]{2,1,0:T(8,128)(2,1)S(1)}, u32[]{:S(2)}, u32[]{:S(2)}) collective-permute-start(bf16[16,8,768]{2,1,0:T(8,128)(2,1)} %refs_22_.1), channel_id=1, source_target_pairs={{0,4},{1,5},{4,8},{5,9},{8,12},{9,13},{12,14},{13,15},{14,10},{15,... | collective-permute-start | bytes 589832 | tf_op jit(solution)/shard_map/ppermute | solution.py:370
  3.1 0.0 collective-permute-start.3
  3.1 2.5 %shard_map.118 = (bf16[136,768]{1,0:T(8,128)(2,1)}, bf16[8,768]{1,0:T(8,128)(2,1)}, bf16[128,768]{1,0:T(8,128)(2,1)}) custom-call(bf16[16,8,768]{2,1,0:T(8,128)(2,1)} %refs_22_.1, s32[1,16]{1,0:T(1,128)} %bitcast.9, s32[1,16]{1,0:T(1,128)} %bitcast.10, s32[1,16]{1,0:T(1,128)} %bitcast.11, bf16[768,768]{1,0:T(8,128)(2,1)} %wq_hbm.1), custom_call_target="tpu_custom_call" | custom-call | flops 150994944 | bytes 1769472 | tf_op jit(solution)/shard_map/pallas_call | solution.py:340
  5.6 2.1 %collective-permute-start.2 = (bf16[8,768]{1,0:T(8,128)(2,1)}, bf16[8,768]{1,0:T(8,128)(2,1)S(1)}, u32[]{:S(2)}, u32[]{:S(2)}) collective-permute-start(bf16[8,768]{1,0:T(8,128)(2,1)} %get-tuple-element.14.refs_9_.refs_21_), channel_id=1, source_target_pairs={{0,4},{1,5},{4,8},{5,9},{8,12},{9,13},{12,14},{13,15},{14,10},{15,... | collective-permute-start | bytes 36872 | tf_op jit(solution)/shard_map/ppermute | solution.py:370
  7.6 0.0 collective-permute-start.4
  7.7 1.9 %collective-permute-done.2.meta_ref = bf16[8,768]{1,0:T(8,128)(2,1)S(1)} collective-permute-done((bf16[8,768]{1,0:T(8,128)(2,1)}, bf16[8,768]{1,0:T(8,128)(2,1)S(1)}, u32[]{:S(2)}, u32[]{:S(2)}) %collective-permute-start.2) | collective-permute-done | bytes 12320 | tf_op jit(solution)/shard_map/ppermute | solution.py:370
  9.5 0.4 shard_map.120.refs_0_
  9.9 2.1 %collective-permute-start.6 = (bf16[136,768]{1,0:T(8,128)(2,1)S(1)}, bf16[136,768]{1,0:T(8,128)(2,1)S(1)}, u32[]{:S(2)}, u32[]{:S(2)}) collective-permute-start(bf16[136,768]{1,0:T(8,128)(2,1)S(1)} %shard_map.120.refs_0_), channel_id=1, source_target_pairs={{0,4},{1,5},{4,8},{5,9},{8,12},{9,13},{12,14},{13,15},{14,10},{15,... | collective-permute-start | bytes 626696 | tf_op jit(solution)/shard_map/ppermute | solution.py:370
  12.0 0.0 collective-permute-done.4.meta_ref
  12.0 0.0 collective-permute-done.3.single_ref
  12.0 0.4 shard_map.121.refs_1_
  12.4 0.1 collective-permute-start.7
  12.5 3.4 %collective-permute-done.6.refs_0_ = bf16[136,768]{1,0:T(8,128)(2,1)S(1)} collective-permute-done((bf16[136,768]{1,0:T(8,128)(2,1)S(1)}, bf16[136,768]{1,0:T(8,128)(2,1)S(1)}, u32[]{:S(2)}, u32[]{:S(2)}) %collective-permute-start.6) | collective-permute-done | bytes 208928 | tf_op jit(solution)/shard_map/ppermute | solution.py:370
  15.9 1.9 %collective-permute-start.9 = (bf16[136,768]{1,0:T(8,128)(2,1)S(1)}, bf16[136,768]{1,0:T(8,128)(2,1)S(1)}, u32[]{:S(2)}, u32[]{:S(2)}) collective-permute-start(bf16[136,768]{1,0:T(8,128)(2,1)S(1)} %collective-permute-done.6.refs_0_), channel_id=1, source_target_pairs={{0,4},{1,5},{4,8},{5,9},{8,12},{9,13},{12,14},{13,15},{14,10},{15,... | collective-permute-start | bytes 626696 | tf_op jit(solution)/shard_map/ppermute | solution.py:370
  17.8 0.5 collective-permute-done.7.refs_1_
  18.3 0.0 collective-permute-start.10
  18.3 1.3 %copy-done.1 = bf16[768,768]{1,0:T(8,128)(2,1)S(1)} copy-done((bf16[768,768]{1,0:T(8,128)(2,1)S(1)}, bf16[768,768]{1,0:T(8,128)(2,1)}, u32[]{:S(2)}) %copy-start.1) | copy-done | bytes 1179672
  19.6 0.8 %shard_map.122.refs_2_ = bf16[528,768]{1,0:T(8,128)(2,1)S(1)} custom-call(bf16[136,768]{1,0:T(8,128)(2,1)S(1)} %shard_map.120.refs_0_, bf16[136,768]{1,0:T(8,128)(2,1)S(1)} %shard_map.121.refs_1_, bf16[768,768]{1,0:T(8,128)(2,1)S(1)} %copy-done, bf16[768,768]{1,0:T(8,128)(2,1)S(1)} %copy-done.1), custom_call_target="tpu_custom_call" | custom-call | flops 603979776 | bytes 3538944 | tf_op jit(solution)/shard_map/pallas_call | solution.py:340
  20.4 0.1 collective-permute-start.5
  20.4 1.7 %shard_map.123.refs_4_ = bf16[528,768]{1,0:T(8,128)(2,1)} custom-call(bf16[136,768]{1,0:T(8,128)(2,1)S(1)} %collective-permute-done.6.refs_0_, bf16[136,768]{1,0:T(8,128)(2,1)S(1)} %collective-permute-done.7.refs_1_, bf16[768,768]{1,0:T(8,128)(2,1)S(1)} %copy-done, bf16[768,768]{1,0:T(8,128)(2,1)S(1)} %copy-done.1), custom_call_target="tpu_custom_call" | custom-call | flops 603979776 | bytes 3538944 | tf_op jit(solution)/shard_map/pallas_call | solution.py:340
  22.1 0.5 %collective-permute-start.8 = (bf16[528,768]{1,0:T(8,128)(2,1)}, bf16[528,768]{1,0:T(8,128)(2,1)}, u32[]{:S(2)}, u32[]{:S(2)}) collective-permute-start(bf16[528,768]{1,0:T(8,128)(2,1)} %shard_map.123.refs_4_), channel_id=1, source_target_pairs={{0,1},{1,0},{2,3},{3,2},{4,5},{5,4},{6,7},{7,6},{8,9},{9,8},{10,11... | collective-permute-start | bytes 2433032 | tf_op jit(solution)/shard_map/ppermute | solution.py:373
  22.6 0.0 collective-permute-done.9.refs_0_.in_ref
  22.6 1.5 %collective-permute-done.10.refs_1_.in_ref = bf16[136,768]{1,0:T(8,128)(2,1)S(1)} collective-permute-done((bf16[136,768]{1,0:T(8,128)(2,1)S(1)}, bf16[136,768]{1,0:T(8,128)(2,1)S(1)}, u32[]{:S(2)}, u32[]{:S(2)}) %collective-permute-start.10) | collective-permute-done | bytes 208928 | tf_op jit(solution)/shard_map/ppermute | solution.py:370
  24.1 1.7 %shard_map.124.refs_6_ = bf16[528,768]{1,0:T(8,128)(2,1)} custom-call(bf16[136,768]{1,0:T(8,128)(2,1)S(1)} %collective-permute-done.9.refs_0_.in_ref, bf16[136,768]{1,0:T(8,128)(2,1)S(1)} %collective-permute-done.10.refs_1_.in_ref, bf16[768,768]{1,0:T(8,128)(2,1)S(1)} %copy-done, bf16[768,768]{1,0:T(8,128)(2,1)S(1)} %copy-done.1), custom_call_target="tpu_custom_call" | custom-call | flops 603979776 | bytes 3538944 | tf_op jit(solution)/shard_map/pallas_call | solution.py:340
  25.8 0.5 shard_map.119.refs_0_
  26.3 0.6 %collective-permute-start = (bf16[264,768]{1,0:T(8,128)(2,1)S(1)}, bf16[264,768]{1,0:T(8,128)(2,1)S(1)}, u32[]{:S(2)}, u32[]{:S(2)}) collective-permute-start(bf16[264,768]{1,0:T(8,128)(2,1)S(1)} %shard_map.119.refs_0_), channel_id=1, source_target_pairs={{0,1},{1,0},{2,3},{3,2},{4,5},{5,4},{6,7},{7,6},{8,9},{9,8},{10,11... | collective-permute-start | bytes 1216520 | tf_op jit(solution)/shard_map/ppermute | solution.py:373
  26.9 0.8 %copy-done.3 = bf16[264,768]{1,0:T(8,128)(2,1)} copy-done((bf16[264,768]{1,0:T(8,128)(2,1)}, bf16[264,768]{1,0:T(8,128)(2,1)S(1)}, u32[]{:S(2)}) %copy-start.3) | copy-done | bytes 405528
  27.6 1.6 %collective-permute-start.12 = (bf16[104,768]{1,0:T(8,128)(2,1)S(1)}, bf16[104,768]{1,0:T(8,128)(2,1)S(1)}, u32[]{:S(2)}, u32[]{:S(2)}) collective-permute-start(bf16[104,768]{1,0:T(8,128)(2,1)S(1)} %shard_map.125), channel_id=1, source_target_pairs={{0,4},{1,5},{4,8},{5,9},{8,12},{9,13},{12,14},{13,15},{14,10},{15,... | collective-permute-start | bytes 479240 | tf_op jit(solution)/shard_map/ppermute | solution.py:370
  29.3 4.5 %collective-permute-done.12.first_ref.refs_8_ = bf16[104,768]{1,0:T(8,128)(2,1)S(1)} collective-permute-done((bf16[104,768]{1,0:T(8,128)(2,1)S(1)}, bf16[104,768]{1,0:T(8,128)(2,1)S(1)}, u32[]{:S(2)}, u32[]{:S(2)}) %collective-permute-start.12) | collective-permute-done | bytes 159776 | tf_op jit(solution)/shard_map/ppermute | solution.py:370
  33.7 0.0 collective-permute-start.13
  33.7 0.6 %shard_map.126 = bf16[32,768]{1,0:T(8,128)(2,1)} custom-call(bf16[136,768]{1,0:T(8,128)(2,1)S(1)} %collective-permute-done.10.refs_1_.in_ref), custom_call_target="tpu_custom_call" | custom-call | bytes 196608 | tf_op jit(solution)/shard_map/pallas_call | solution.py:340
  34.4 0.0 collective-permute-done.refs_1_
  34.4 0.8 %copy-done.5 = bf16[264,768]{1,0:T(8,128)(2,1)} copy-done((bf16[264,768]{1,0:T(8,128)(2,1)}, bf16[264,768]{1,0:T(8,128)(2,1)S(1)}, u32[]{:S(2)}) %copy-start.5) | copy-done | bytes 405528
  35.1 0.5 %collective-permute-start.14 = (bf16[32,768]{1,0:T(8,128)(2,1)}, bf16[32,768]{1,0:T(8,128)(2,1)}, u32[]{:S(2)}, u32[]{:S(2)}) collective-permute-start(bf16[32,768]{1,0:T(8,128)(2,1)} %shard_map.126), channel_id=1, source_target_pairs={{0,2},{1,3},{4,0},{5,1},{8,4},{9,5},{12,8},{13,9},{14,12},{15,13},... | collective-permute-start | bytes 147464 | tf_op jit(solution)/shard_map/ppermute | solution.py:370
  35.6 0.9 %copy-done.12 = bf16[128,768]{1,0:T(8,128)(2,1)S(1)} copy-done((bf16[128,768]{1,0:T(8,128)(2,1)S(1)}, bf16[128,768]{1,0:T(8,128)(2,1)}, u32[]{:S(2)}) %copy-start.12) | copy-done | bytes 196632
  36.6 1.0 %shard_map.128.refs_6_.refs_12_ = bf16[6144,256]{1,0:T(8,128)(2,1)S(1)} custom-call(s32[1]{0:T(128)} %bitcast.3.me_ref, bf16[128,768]{1,0:T(8,128)(2,1)S(1)} %copy-done.12), custom_call_target="tpu_custom_call" | custom-call | flops 50331648 | bytes 3145728 | tf_op jit(solution)/shard_map/pallas_call | solution.py:340
  37.6 0.2 copy-done.8
  37.8 0.3 shard_map.129.refs_13_
  38.2 0.9 %copy-done.9 = bf16[16,256,128]{2,1,0:T(8,128)(2,1)S(1)} copy-done((bf16[16,256,128]{2,1,0:T(8,128)(2,1)S(1)}, bf16[16,256,128]{2,1,0:T(8,128)(2,1)}, u32[]{:S(2)}) %copy-start.9) | copy-done | bytes 1048600
  39.1 0.7 %shard_map.130 = (f32[160,256]{1,0:T(8,128)S(1)}, f32[96,256]{1,0:T(8,128)S(1)}) custom-call(s32[1]{0:T(128)} %bitcast.3.me_ref, bf16[16,256,128]{2,1,0:T(8,128)(2,1)S(1)} %copy-done.9, bf16[16,128]{1,0:T(8,128)(2,1)S(1)} %bitcast.8), custom_call_target="tpu_custom_call" | custom-call | flops 268435456 | bytes 1310720 | tf_op jit(solution)/shard_map/pallas_call | solution.py:340
  39.8 0.0 copy-start.14
  39.8 0.0 collective-permute-done.14.second_ref
  39.8 0.3 collective-permute-start.15
  40.1 1.3 %shard_map.127.refs_11_ = bf16[256,768]{1,0:T(8,128)(2,1)S(1)} custom-call(bf16[104,768]{1,0:T(8,128)(2,1)S(1)} %collective-permute-done.12.first_ref.refs_8_, bf16[32,768]{1,0:T(8,128)(2,1)} %collective-permute-done.14.second_ref, bf16[768,768]{1,0:T(8,128)(2,1)S(1)} %copy-done, bf16[768,768]{1,0:T(8,128)(2,1)S(1)} %copy-done.2), custom_call_target="tpu_custom_call" | custom-call | flops 301989888 | bytes 2949120 | tf_op jit(solution)/shard_map/pallas_call | solution.py:340
  41.4 0.0 copy-start.7
  41.5 0.0 copy-start.11
  41.5 2.6 %shard_map.131 = (f32[1280,256]{1,0:T(8,128)S(1)}, f32[8,256]{1,0:T(8,128)S(1)}, f32[8,256]{1,0:T(8,128)S(1)}) custom-call(bf16[264,768]{1,0:T(8,128)(2,1)S(1)} %copy-done.4, bf16[264,768]{1,0:T(8,128)(2,1)S(1)} %copy-done.6, bf16[528,768]{1,0:T(8,128)(2,1)S(1)} %shard_map.122.refs_2_, bf16[528,768]{1,0:T(8,128)(2,1)} %collective-permute-done.5.refs_3_, ...), custom_call_target="tpu_custom_call" | custom-call | flops 503316480 | bytes 5898240 | tf_op jit(solution)/shard_map/pallas_call | solution.py:340
  44.1 5.1 %shard_map.132 = bf16[16,8,768]{2,1,0:T(8,128)(2,1)} custom-call(bf16[264,768]{1,0:T(8,128)(2,1)S(1)} %copy-done.4, bf16[264,768]{1,0:T(8,128)(2,1)S(1)} %copy-done.6, bf16[528,768]{1,0:T(8,128)(2,1)S(1)} %shard_map.122.refs_2_, bf16[528,768]{1,0:T(8,128)(2,1)} %collective-permute-done.5.refs_3_, bf16[528,768]{1,0:T(8,128)(2,1)} %shard_map.123.refs_4_, ...), custom_call_target="tpu_custom_call" | custom-call | flops 100663296 | bytes 3145728 | tf_op jit(solution)/shard_map/pallas_call | solution.py:340
  (31 shorter events, 0.1 us)
Async XLA Ops:
  0.0 18.3 %copy-start = (bf16[768,768]{1,0:T(8,128)(2,1)S(1)}, bf16[768,768]{1,0:T(8,128)(2,1)}, u32[]{:S(2)}) copy-start(bf16[768,768]{1,0:T(8,128)(2,1)} %refs_17_.1) | copy-start | bytes 3538948
  0.0 9.5 %collective-permute-start.1 = (bf16[16,8,768]{2,1,0:T(8,128)(2,1)}, bf16[16,8,768]{2,1,0:T(8,128)(2,1)S(1)}, u32[]{:S(2)}, u32[]{:S(2)}) collective-permute-start(bf16[16,8,768]{2,1,0:T(8,128)(2,1)} %refs_22_.1), channel_id=1, source_target_pairs={{0,4},{1,5},{4,8},{5,9},{8,12},{9,13},{12,14},{13,15},{14,10},{15,... | collective-permute-start | bytes 589832 | tf_op jit(solution)/shard_map/ppermute | solution.py:370
  3.1 9.0 %collective-permute-start.3 = (bf16[16,8,768]{2,1,0:T(8,128)(2,1)}, bf16[16,8,768]{2,1,0:T(8,128)(2,1)S(1)}, u32[]{:S(2)}, u32[]{:S(2)}) collective-permute-start(bf16[16,8,768]{2,1,0:T(8,128)(2,1)} %refs_22_.1), channel_id=1, source_target_pairs={{0,2},{1,3},{4,0},{5,1},{8,4},{9,5},{12,8},{13,9},{14,12},{15,13},... | collective-permute-start | bytes 589832 | tf_op jit(solution)/shard_map/ppermute | solution.py:370
  5.6 4.0 %collective-permute-start.2 = (bf16[8,768]{1,0:T(8,128)(2,1)}, bf16[8,768]{1,0:T(8,128)(2,1)S(1)}, u32[]{:S(2)}, u32[]{:S(2)}) collective-permute-start(bf16[8,768]{1,0:T(8,128)(2,1)} %get-tuple-element.14.refs_9_.refs_21_), channel_id=1, source_target_pairs={{0,4},{1,5},{4,8},{5,9},{8,12},{9,13},{12,14},{13,15},{14,10},{15,... | collective-permute-start | bytes 36872 | tf_op jit(solution)/shard_map/ppermute | solution.py:370
  7.6 4.4 %collective-permute-start.4 = (bf16[8,768]{1,0:T(8,128)(2,1)}, bf16[8,768]{1,0:T(8,128)(2,1)S(1)}, u32[]{:S(2)}, u32[]{:S(2)}) collective-permute-start(bf16[8,768]{1,0:T(8,128)(2,1)} %get-tuple-element.14.refs_9_.refs_21_), channel_id=1, source_target_pairs={{0,2},{1,3},{4,0},{5,1},{8,4},{9,5},{12,8},{13,9},{14,12},{15,13},... | collective-permute-start | bytes 36872 | tf_op jit(solution)/shard_map/ppermute | solution.py:370
  9.9 5.9 %collective-permute-start.6 = (bf16[136,768]{1,0:T(8,128)(2,1)S(1)}, bf16[136,768]{1,0:T(8,128)(2,1)S(1)}, u32[]{:S(2)}, u32[]{:S(2)}) collective-permute-start(bf16[136,768]{1,0:T(8,128)(2,1)S(1)} %shard_map.120.refs_0_), channel_id=1, source_target_pairs={{0,4},{1,5},{4,8},{5,9},{8,12},{9,13},{12,14},{13,15},{14,10},{15,... | collective-permute-start | bytes 626696 | tf_op jit(solution)/shard_map/ppermute | solution.py:370
  12.4 5.9 %collective-permute-start.7 = (bf16[136,768]{1,0:T(8,128)(2,1)S(1)}, bf16[136,768]{1,0:T(8,128)(2,1)S(1)}, u32[]{:S(2)}, u32[]{:S(2)}) collective-permute-start(bf16[136,768]{1,0:T(8,128)(2,1)S(1)} %shard_map.121.refs_1_), channel_id=1, source_target_pairs={{0,2},{1,3},{4,0},{5,1},{8,4},{9,5},{12,8},{13,9},{14,12},{15,13},... | collective-permute-start | bytes 626696 | tf_op jit(solution)/shard_map/ppermute | solution.py:370
  15.9 6.7 %collective-permute-start.9 = (bf16[136,768]{1,0:T(8,128)(2,1)S(1)}, bf16[136,768]{1,0:T(8,128)(2,1)S(1)}, u32[]{:S(2)}, u32[]{:S(2)}) collective-permute-start(bf16[136,768]{1,0:T(8,128)(2,1)S(1)} %collective-permute-done.6.refs_0_), channel_id=1, source_target_pairs={{0,4},{1,5},{4,8},{5,9},{8,12},{9,13},{12,14},{13,15},{14,10},{15,... | collective-permute-start | bytes 626696 | tf_op jit(solution)/shard_map/ppermute | solution.py:370
  18.3 5.8 %collective-permute-start.10 = (bf16[136,768]{1,0:T(8,128)(2,1)S(1)}, bf16[136,768]{1,0:T(8,128)(2,1)S(1)}, u32[]{:S(2)}, u32[]{:S(2)}) collective-permute-start(bf16[136,768]{1,0:T(8,128)(2,1)S(1)} %collective-permute-done.7.refs_1_), channel_id=1, source_target_pairs={{0,2},{1,3},{4,0},{5,1},{8,4},{9,5},{12,8},{13,9},{14,12},{15,13},... | collective-permute-start | bytes 626696 | tf_op jit(solution)/shard_map/ppermute | solution.py:370
  18.3 1.3 %copy-start.1 = (bf16[768,768]{1,0:T(8,128)(2,1)S(1)}, bf16[768,768]{1,0:T(8,128)(2,1)}, u32[]{:S(2)}) copy-start(bf16[768,768]{1,0:T(8,128)(2,1)} %refs_18_.1) | copy-start | bytes 3538948
  20.4 21.0 %collective-permute-start.5 = (bf16[528,768]{1,0:T(8,128)(2,1)S(1)}, bf16[528,768]{1,0:T(8,128)(2,1)}, u32[]{:S(2)}, u32[]{:S(2)}) collective-permute-start(bf16[528,768]{1,0:T(8,128)(2,1)S(1)} %shard_map.122.refs_2_), channel_id=1, source_target_pairs={{0,1},{1,0},{2,3},{3,2},{4,5},{5,4},{6,7},{7,6},{8,9},{9,8},{10,11... | collective-permute-start | bytes 2433032 | tf_op jit(solution)/shard_map/ppermute | solution.py:373
  22.1 3.7 %copy-start.2 = (bf16[768,768]{1,0:T(8,128)(2,1)S(1)}, bf16[768,768]{1,0:T(8,128)(2,1)}, u32[]{:S(2)}) copy-start(bf16[768,768]{1,0:T(8,128)(2,1)} %refs_18_.1) | copy-start | bytes 3538948
  22.1 3.7 %copy-start.10 = (bf16[136,768]{1,0:T(8,128)(2,1)S(1)}, bf16[136,768]{1,0:T(8,128)(2,1)}, u32[]{:S(2)}) copy-start(bf16[136,768]{1,0:T(8,128)(2,1)} %get-tuple-element.13.refs_0_.pay_ref) | copy-start | bytes 626692
  22.1 19.3 %collective-permute-start.8 = (bf16[528,768]{1,0:T(8,128)(2,1)}, bf16[528,768]{1,0:T(8,128)(2,1)}, u32[]{:S(2)}, u32[]{:S(2)}) collective-permute-start(bf16[528,768]{1,0:T(8,128)(2,1)} %shard_map.123.refs_4_), channel_id=1, source_target_pairs={{0,1},{1,0},{2,3},{3,2},{4,5},{5,4},{6,7},{7,6},{8,9},{9,8},{10,11... | collective-permute-start | bytes 2433032 | tf_op jit(solution)/shard_map/ppermute | solution.py:373
  25.8 18.3 %collective-permute-start.11 = (bf16[528,768]{1,0:T(8,128)(2,1)}, bf16[528,768]{1,0:T(8,128)(2,1)}, u32[]{:S(2)}, u32[]{:S(2)}) collective-permute-start(bf16[528,768]{1,0:T(8,128)(2,1)} %shard_map.124.refs_6_), channel_id=1, source_target_pairs={{0,1},{1,0},{2,3},{3,2},{4,5},{5,4},{6,7},{7,6},{8,9},{9,8},{10,11... | collective-permute-start | bytes 2433032 | tf_op jit(solution)/shard_map/ppermute | solution.py:373
  26.3 8.1 %collective-permute-start = (bf16[264,768]{1,0:T(8,128)(2,1)S(1)}, bf16[264,768]{1,0:T(8,128)(2,1)S(1)}, u32[]{:S(2)}, u32[]{:S(2)}) collective-permute-start(bf16[264,768]{1,0:T(8,128)(2,1)S(1)} %shard_map.119.refs_0_), channel_id=1, source_target_pairs={{0,1},{1,0},{2,3},{3,2},{4,5},{5,4},{6,7},{7,6},{8,9},{9,8},{10,11... | collective-permute-start | bytes 1216520 | tf_op jit(solution)/shard_map/ppermute | solution.py:373
  26.9 0.8 %copy-start.3 = (bf16[264,768]{1,0:T(8,128)(2,1)}, bf16[264,768]{1,0:T(8,128)(2,1)S(1)}, u32[]{:S(2)}) copy-start(bf16[264,768]{1,0:T(8,128)(2,1)S(1)} %shard_map.119.refs_0_) | copy-start | bytes 1216516
  27.6 6.1 %collective-permute-start.12 = (bf16[104,768]{1,0:T(8,128)(2,1)S(1)}, bf16[104,768]{1,0:T(8,128)(2,1)S(1)}, u32[]{:S(2)}, u32[]{:S(2)}) collective-permute-start(bf16[104,768]{1,0:T(8,128)(2,1)S(1)} %shard_map.125), channel_id=1, source_target_pairs={{0,4},{1,5},{4,8},{5,9},{8,12},{9,13},{12,14},{13,15},{14,10},{15,... | collective-permute-start | bytes 479240 | tf_op jit(solution)/shard_map/ppermute | solution.py:370
  33.7 10.4 %collective-permute-start.13 = (bf16[104,768]{1,0:T(8,128)(2,1)S(1)}, bf16[104,768]{1,0:T(8,128)(2,1)}, u32[]{:S(2)}, u32[]{:S(2)}) collective-permute-start(bf16[104,768]{1,0:T(8,128)(2,1)S(1)} %collective-permute-done.12.first_ref.refs_8_), channel_id=1, source_target_pairs={{0,1},{1,0},{2,3},{3,2},{4,5},{5,4},{6,7},{7,6},{8,9},{9,8},{10,11... | collective-permute-start | bytes 479240 | tf_op jit(solution)/shard_map/ppermute | solution.py:373
  34.4 0.8 %copy-start.5 = (bf16[264,768]{1,0:T(8,128)(2,1)}, bf16[264,768]{1,0:T(8,128)(2,1)S(1)}, u32[]{:S(2)}) copy-start(bf16[264,768]{1,0:T(8,128)(2,1)S(1)} %collective-permute-done.refs_1_) | copy-start | bytes 1216516
  35.1 4.7 %collective-permute-start.14 = (bf16[32,768]{1,0:T(8,128)(2,1)}, bf16[32,768]{1,0:T(8,128)(2,1)}, u32[]{:S(2)}, u32[]{:S(2)}) collective-permute-start(bf16[32,768]{1,0:T(8,128)(2,1)} %shard_map.126), channel_id=1, source_target_pairs={{0,2},{1,3},{4,0},{5,1},{8,4},{9,5},{12,8},{13,9},{14,12},{15,13},... | collective-permute-start | bytes 147464 | tf_op jit(solution)/shard_map/ppermute | solution.py:370
  35.6 0.9 %copy-start.12 = (bf16[128,768]{1,0:T(8,128)(2,1)S(1)}, bf16[128,768]{1,0:T(8,128)(2,1)}, u32[]{:S(2)}) copy-start(bf16[128,768]{1,0:T(8,128)(2,1)} %get-tuple-element.15.q_ref) | copy-start | bytes 589828
  36.6 1.3 %copy-start.8 = (bf16[768,768]{1,0:T(8,128)(2,1)S(1)}, bf16[768,768]{1,0:T(8,128)(2,1)}, u32[]{:S(2)}) copy-start(bf16[768,768]{1,0:T(8,128)(2,1)} %wg_ref.1) | copy-start | bytes 3538948
  37.8 1.2 %copy-start.9 = (bf16[16,256,128]{2,1,0:T(8,128)(2,1)S(1)}, bf16[16,256,128]{2,1,0:T(8,128)(2,1)}, u32[]{:S(2)}) copy-start(bf16[16,256,128]{2,1,0:T(8,128)(2,1)} %pair_ref.1) | copy-start | bytes 3145732
  37.8 1.2 %copy-start.15 = (bf16[128,16]{0,1:T(8,128)(2,1)S(1)}, bf16[128,16]{0,1:T(8,128)(2,1)}, u32[]{:S(2)}) copy-start(bf16[128,16]{0,1:T(8,128)(2,1)} %param.22) | copy-start | bytes 12292
  39.7 1.7 %copy-start.4 = (bf16[264,768]{1,0:T(8,128)(2,1)S(1)}, bf16[264,768]{1,0:T(8,128)(2,1)}, u32[]{:S(2)}) copy-start(bf16[264,768]{1,0:T(8,128)(2,1)} %copy-done.3) | copy-start | bytes 1216516
  39.7 1.7 %copy-start.6 = (bf16[264,768]{1,0:T(8,128)(2,1)S(1)}, bf16[264,768]{1,0:T(8,128)(2,1)}, u32[]{:S(2)}) copy-start(bf16[264,768]{1,0:T(8,128)(2,1)} %copy-done.5) | copy-start | bytes 1216516
  39.8 1.7 %copy-start.13 = (bf16[8,768]{1,0:T(8,128)(2,1)S(1)}, bf16[8,768]{1,0:T(8,128)(2,1)}, u32[]{:S(2)}) copy-start(bf16[8,768]{1,0:T(8,128)(2,1)} %get-tuple-element.14.refs_9_.refs_21_) | copy-start | bytes 36868
  39.8 1.7 %copy-start.14 = (f32[66,16]{0,1:T(8,128)S(1)}, f32[66,16]{0,1:T(8,128)}, u32[]{:S(2)}) copy-start(f32[66,16]{0,1:T(8,128)} %param.23) | copy-start | bytes 12676
  39.8 4.3 %collective-permute-start.15 = (bf16[32,768]{1,0:T(8,128)(2,1)}, bf16[32,768]{1,0:T(8,128)(2,1)S(1)}, u32[]{:S(2)}, u32[]{:S(2)}) collective-permute-start(bf16[32,768]{1,0:T(8,128)(2,1)} %collective-permute-done.14.second_ref), channel_id=1, source_target_pairs={{0,1},{1,0},{2,3},{3,2},{4,5},{5,4},{6,7},{7,6},{8,9},{9,8},{10,11... | collective-permute-start | bytes 147464 | tf_op jit(solution)/shard_map/ppermute | solution.py:373
  41.4 2.7 %copy-start.7 = (bf16[768,768]{1,0:T(8,128)(2,1)S(1)}, bf16[768,768]{1,0:T(8,128)(2,1)}, u32[]{:S(2)}) copy-start(bf16[768,768]{1,0:T(8,128)(2,1)} %refs_23_.1) | copy-start | bytes 3538948
  41.5 2.7 %copy-start.11 = (bf16[16,8,768]{2,1,0:T(8,128)(2,1)S(1)}, bf16[16,8,768]{2,1,0:T(8,128)(2,1)}, u32[]{:S(2)}) copy-start(bf16[16,8,768]{2,1,0:T(8,128)(2,1)} %refs_22_.1) | copy-start | bytes 589828
